TPU v7x, 128 devices: a whole 4x4x4 slice. The times are simulated.
128 devices in a mesh: member: 32 (over x, z, core), mp: 4 (over y).
Axes of the slice: x: 4, y: 4, z: 4, core: 2. Of those that a mesh axis runs over, the one named last changes fastest.
Arguments:
- latents: bfloat16 [128, 1024, 1024], P('member', 'mp'), may hold values from -6 to 6
- w_first: bfloat16 [1024, 2048], P(None, 'mp'), may hold values from -0.1875 to 0.1875
- w_second: bfloat16 [2048, 1024], P('mp'), may hold values from -0.125 to 0.125
- readout_matrix: bfloat16 [1024, 768], P(None, 'mp'), may hold values from -0.1875 to 0.1875
- observed: float32 [1024, 768], P(('mp', 'member')), may hold values from -9 to 9
- obs_index: int32 [1024], P(('mp', 'member')), may hold values from 0 to 1023, as said below
- valid_mask: int32 [1024], P(('mp', 'member')), may hold values from 0 to 1
Outputs:
- grad_first: float32 [1024, 2048], P(('member', 'mp'))
- grad_second: float32 [2048, 1024], P(('member', 'mp'))
- grad_head: float32 [1024, 768], P(('member', 'mp'))
- loss: float32 [], replicated
Inputs may be any that keep to these rules, and one draw needn't show every extreme that they name: obs_index[p] names a record of the same aligned block of 8 patches as p.
All inputs are finite; a program needn't handle non-finite values.
Results may differ from a plain program's by a relative error of at most 0.006.
Values may be sent and summed in bfloat16 or wider, within the bound.
No kernel may reach another device: no remote copies, remote signals or barrier semaphores. Data moves between devices by JAX's collectives and lax.ppermute only.
A program may use at most 128 MiB of HBM per device.

v0:
```python
import functools

import jax
import jax.numpy as jnp
from jax import lax
from jax.experimental import pallas as pl
from jax.experimental.pallas import tpu as pltpu
from jax.sharding import Mesh
from jax.sharding import PartitionSpec as P

SMOOTHING = 1.0
LOSS_SCALE = 4096.0
RING = 4
PAIR_LOW = ((0, 1), (1, 0), (2, 3), (3, 2))
PAIR_HIGH = ((0, 3), (3, 0), (1, 2), (2, 1))
ROOT_2_PI = 0.7978845608028654
CUBIC = 0.044715
LANES = 256
MIB = 1 << 20
F32 = jnp.float32
BF16 = jnp.bfloat16


def shift(x, axis, by):
    size = lax.axis_size(axis)
    return lax.ppermute(x, axis, [(i, (i + by) % size) for i in range(size)])


def dot(a, b, contract=((1,), (0,))):
    return lax.dot_general(a, b, (contract, ((), ())), preferred_element_type=F32)


def params(cells):
    return pltpu.CompilerParams(
        dimension_semantics=("arbitrary",) * cells, vmem_limit_bytes=56 * MIB
    )


def forward_kernel(first_call, last_call, block_rows, sizes, *refs):
    width, half, head_rows = sizes
    place, tokens, mine, theirs = refs[:4]
    refs = refs[4:]
    if first_call:
        total_in = None
        slope, hidden, second, head, total = refs
    elif last_call:
        total_in, _, _, _, head_in, slope, hidden, second, head, residual, forecast = refs
    else:
        total_in, _, _, _, _, slope, hidden, second, head, total = refs
    block, core = place[0], place[1]
    chunks = width // LANES
    start = width
    head_start = start + chunks * half

    @pl.when(pl.program_id(0) == 0)
    def _():
        if last_call:
            head[...] = head_in[...]
        for pack, side in ((mine, core), (theirs, 1 - core)):
            second[side] = pack[start : start + chunks * half, :]
            for e in range(2):
                piece = pack[head_start + e * head_rows : head_start + (e + 1) * head_rows, :]
                lane = pl.multiple_of(side * (width // 2) + e * LANES, LANES)
                row = pl.multiple_of(block * head_rows, 64) if last_call else 0
                head[pl.ds(row, head_rows), pl.ds(lane, LANES)] = piece

    rows = tokens[...]
    base = rows.astype(F32) if first_call else total_in[...]
    sums = [base[:, q * LANES : (q + 1) * LANES] for q in range(chunks)]
    for pack, side in ((mine, core), (theirs, 1 - core)):
        x = dot(rows, pack[:width, :])
        sq = x * x
        t = jnp.tanh(ROOT_2_PI * (x + CUBIC * x * sq))
        up = 0.5 * (1.0 + t)
        active = (x * up).astype(BF16)
        lane = pl.multiple_of(side * half, half)
        slope[:, pl.ds(lane, half)] = up + (0.5 * ROOT_2_PI) * x * (1.0 - t * t) * (
            1.0 + (3.0 * CUBIC) * sq
        )
        hidden[:, pl.ds(lane, half)] = active
        for q in range(chunks):
            sums[q] = sums[q] + dot(active, pack[start + q * half : start + (q + 1) * half, :])
    full = jnp.concatenate(sums, 1)
    if last_call:
        rounded = full.astype(BF16)
        residual[...] = rounded
        forecast[...] = dot(rounded, head[...], ((1,), (1,))).astype(BF16)
    else:
        total[...] = full


def forward_part(place, tokens, mine, theirs, carried, out_width, last_call):
    rows, width = tokens.shape
    half = LANES
    hid = 2 * half * RING
    head_rows = out_width // RING
    first_call = carried is None
    block_rows = min(rows, 256)
    whole = lambda shape: pl.BlockSpec(shape, lambda i, s: (0,) * len(shape))
    by_rows = lambda cols: pl.BlockSpec((block_rows, cols), lambda i, s: (i, 0))
    in_place = pl.BlockSpec(memory_space=pl.ANY)
    in_specs = [by_rows(width), whole(mine.shape), whole(theirs.shape)]
    args = [tokens, mine, theirs]
    aliases = {}
    if not first_call:
        slope, hidden, second, head, total = carried
        args += [total, slope, hidden, second, head]
        in_specs += [by_rows(width), in_place, in_place, in_place]
        in_specs += [whole((out_width, width)) if last_call else in_place]
        aliases = {5: 0, 6: 1, 7: 2}
        if not last_call:
            aliases = {**aliases, 8: 3, 4: 4}
    column = pl.BlockSpec((block_rows, 2 * half), lambda i, s: (i, s[0]))
    out_specs = [
        column,
        column,
        pl.BlockSpec((2, width * half // LANES, LANES), lambda i, s: (s[0], 0, 0)),
        whole((out_width, width))
        if last_call
        else pl.BlockSpec((head_rows, width), lambda i, s: (s[0], 0)),
    ]
    out_shape = [
        jax.ShapeDtypeStruct((rows, hid), F32),
        jax.ShapeDtypeStruct((rows, hid), BF16),
        jax.ShapeDtypeStruct((2 * RING, width * half // LANES, LANES), BF16),
        jax.ShapeDtypeStruct((out_width, width), BF16),
    ]
    if last_call:
        out_specs += [by_rows(width), by_rows(out_width)]
        out_shape += [
            jax.ShapeDtypeStruct((rows, width), BF16),
            jax.ShapeDtypeStruct((rows, out_width), BF16),
        ]
    else:
        out_specs += [by_rows(width)]
        out_shape += [jax.ShapeDtypeStruct((rows, width), F32)]
    return pl.pallas_call(
        functools.partial(
            forward_kernel, first_call, last_call, block_rows, (width, half, head_rows)
        ),
        grid_spec=pltpu.PrefetchScalarGridSpec(
            num_scalar_prefetch=1,
            grid=(rows // block_rows,),
            in_specs=in_specs,
            out_specs=out_specs,
        ),
        out_shape=out_shape,
        input_output_aliases=aliases,
        compiler_params=params(1),
        cost_estimate=pl.CostEstimate(
            flops=8 * rows * width * half, bytes_accessed=12 * MIB, transcendentals=rows * 2 * half
        ),
        name="forward_part",
    )(place, *args)


def store_halves(core, parts, keep, send):
    n, _, rows, cols = parts.shape
    zero = parts[:, 0].reshape(n * rows, cols).astype(BF16)
    one = parts[:, 1].reshape(n * rows, cols).astype(BF16)

    @pl.when(core == 0)
    def _():
        keep[0] = zero
        send[0] = one

    @pl.when(core == 1)
    def _():
        keep[0] = one
        send[0] = zero


def early_kernel(place, hidden_t, resid_grad, residual_t, grad_rows, keep, send):
    second = dot(hidden_t[...], resid_grad[...])
    head = dot(residual_t[...], grad_rows[...])
    width, out_width = second.shape[1], head.shape[1]
    second = second.reshape(RING, 2, RING, -1, width)
    head = head.reshape(RING, 2, RING, -1, out_width)
    blank = jnp.zeros((*head.shape[:4], width - out_width), F32)
    both = jnp.concatenate([second, jnp.concatenate([head, blank], 4)], 3)
    both = both.reshape(RING, 2, -1, width)
    store_halves(place[1], both, keep, send)


def early_grads(place, hidden_t, resid_grad, residual_t, grad_rows):
    hid, rows = hidden_t.shape
    width, out_width = residual_t.shape[0], grad_rows.shape[1]
    lines = (hid + width) // RING // 2
    gray = lambda i: 2 * ((i // 2 + i) % 2) + i // 2
    out = pl.BlockSpec((1, lines, width), lambda i, s: (gray(i), 0, 0))
    return pl.pallas_call(
        early_kernel,
        grid_spec=pltpu.PrefetchScalarGridSpec(
            num_scalar_prefetch=1,
            grid=(RING,),
            in_specs=[
                pl.BlockSpec((hid // RING, rows), lambda i, s: (i, 0)),
                pl.BlockSpec((rows, width), lambda i, s: (0, 0)),
                pl.BlockSpec((width // RING, rows), lambda i, s: (i, 0)),
                pl.BlockSpec((rows, out_width), lambda i, s: (0, 0)),
            ],
            out_specs=[out, out],
        ),
        out_shape=[jax.ShapeDtypeStruct((RING, lines, width), BF16)] * 2,
        compiler_params=params(1),
        cost_estimate=pl.CostEstimate(
            flops=2 * rows * width * (hid + out_width), bytes_accessed=18 * MIB, transcendentals=0
        ),
        name="early_grads",
    )(place, hidden_t, resid_grad, residual_t, grad_rows)


def late_kernel(place, resid_grad, second, slope, tokens_t, keep, send):
    grad = resid_grad[...]
    width = grad.shape[1]
    total = None
    for q in range(width // LANES):
        term = dot(
            grad[:, q * LANES : (q + 1) * LANES],
            second[0, q * LANES : (q + 1) * LANES, :],
            ((1,), (1,)),
        )
        total = term if total is None else total + term
    preact_grad = (slope[...] * total).astype(BF16)
    first = dot(tokens_t[...], preact_grad)
    parts = first.reshape(16, 2, RING, -1, LANES)
    parts = jnp.stack([parts[:, :, i] for i in (0, 3, 1, 2)], 2)
    store_halves(place[1], parts.reshape(16, 2, -1, LANES), keep, send)


def late_grads(place, resid_grad, second, slope, tokens_t):
    rows, width = resid_grad.shape
    hid = slope.shape[1]
    per = width // LANES
    out = pl.BlockSpec((1, width // 2, LANES), lambda j, s: (j // per, 0, j % per))
    return pl.pallas_call(
        late_kernel,
        grid_spec=pltpu.PrefetchScalarGridSpec(
            num_scalar_prefetch=1,
            grid=(hid // LANES,),
            in_specs=[
                pl.BlockSpec((rows, width), lambda j, s: (0, 0)),
                pl.BlockSpec((1, *second.shape[1:]), lambda j, s: (j, 0, 0)),
                pl.BlockSpec((rows, LANES), lambda j, s: (0, j)),
                pl.BlockSpec((width, rows), lambda j, s: (0, 0)),
            ],
            out_specs=[out, out],
        ),
        out_shape=[jax.ShapeDtypeStruct((hid // width, width // 2, width), BF16)] * 2,
        compiler_params=params(1),
        cost_estimate=pl.CostEstimate(
            flops=4 * rows * width * hid, bytes_accessed=20 * MIB, transcendentals=0
        ),
        name="late_grads",
    )(place, resid_grad, second, slope, tokens_t)


def add(a, b):
    return (a.astype(F32) + b.astype(F32)).astype(BF16)


def take(x, index, axis):
    return lax.dynamic_index_in_dim(x, index, axis, keepdims=False)


def ring_bits(axis):
    here = lax.axis_index(axis)
    high = here // 2
    return (high + here) % 2, high


def ring_sum(a, b, axis):
    low, high = ring_bits(axis)
    a_in = lax.ppermute(take(a, 1 - low, 0), axis, PAIR_LOW)
    b_in = lax.ppermute(take(b, 1 - high, 1), axis, PAIR_HIGH)
    a = add(take(a, low, 0), a_in)
    b = add(take(b, high, 1), b_in)
    a_in = lax.ppermute(take(a, 1 - high, 0), axis, PAIR_HIGH)
    b_in = lax.ppermute(take(b, 1 - low, 0), axis, PAIR_LOW)
    return add(take(a, high, 0), a_in), add(take(b, low, 0), b_in)


def terms(value):
    first = lax.reduce_precision(value, 8, 7)
    second = lax.reduce_precision(value - first, 8, 7)
    third = value - first - second
    return first, second, third


def pick(flag, one, zero):
    return jnp.where(flag == 1, one, zero)


def packed(first, second, head):
    columns = lambda v: [v[:, i : i + LANES] for i in range(0, v.shape[1], LANES)]
    return jnp.concatenate([first, *columns(second), *columns(head)], 0)


def score(samples, target, valid_mask):
    count = samples.shape[0]
    wide = samples.astype(F32)
    gram = jnp.einsum("mpo,npo->pmn", samples, samples, preferred_element_type=F32)
    squares = jnp.sum(wide * wide, axis=2).T
    dist_sq = squares[:, :, None] + squares[:, None, :] - 2.0 * gram
    spread = jnp.sqrt(dist_sq + SMOOTHING)
    kernel = 1.0 / spread
    kernel_sum = jnp.sum(kernel, axis=2)
    pulled = jnp.einsum("pmn,npo->mpo", kernel, wide, precision=lax.Precision.HIGHEST)
    offset = wide - target[None]
    error_norm = jnp.sqrt(jnp.sum(offset * offset, axis=2) + SMOOTHING)
    repulse = wide * kernel_sum.T[:, :, None] - pulled
    validity = valid_mask.astype(F32)
    grad_raw = (
        LOSS_SCALE
        * validity[None, :, None]
        * (offset / (count * error_norm[:, :, None]) - repulse / (count * count))
    ).astype(BF16)
    scores = validity * (
        jnp.mean(error_norm, axis=0) - jnp.sum(spread, axis=(1, 2)) / (2.0 * count * count)
    )
    return grad_raw, jnp.sum(scores), jnp.sum(validity)


def per_device(latents, w_first, w_second, readout_matrix, observed, obs_index, valid_mask):
    members, patches, width = latents.shape
    out_width = observed.shape[1]
    core = lax.axis_index("c")
    here = lax.axis_index("y")
    own = obs_index.shape[0]
    rows = members * patches
    shard = w_first.shape[1]
    half = shard // 2

    head_shard = readout_matrix.T

    def half_of(side):
        return packed(
            lax.dynamic_slice_in_dim(w_first, side * half, half, 1),
            lax.dynamic_slice_in_dim(w_second, side * half, half, 0),
            lax.dynamic_slice_in_dim(head_shard, side * (width // 2), width // 2, 1),
        )

    mine = half_of(core)
    right = shift(mine, "y", 1)
    left = shift(mine, "y", -1)
    lines = mine.shape[0] // 2
    far = [shift(right[:lines], "y", 1), shift(left[lines:], "y", -1)]
    right_other = shift(right, "c", 1)
    left_other = shift(left, "c", 1)
    far = jnp.concatenate(far, 0)
    far_other = shift(far, "c", 1)

    tokens = (
        latents.reshape(members, 16, 2, own, width).transpose(2, 1, 0, 3, 4).reshape(rows, width)
    )
    place = lambda off: jnp.stack([(here + off) % RING, core]).astype(jnp.int32)
    run = functools.partial(forward_part, out_width=out_width)
    carried = run(place(0), tokens, mine, half_of(1 - core), carried=None, last_call=False)
    carried = run(place(3), tokens, right, right_other, carried=carried, last_call=False)
    carried = run(place(1), tokens, left, left_other, carried=carried, last_call=False)
    slope, hidden, second, head, residual, forecast = run(
        place(2), tokens, far, far_other, carried=carried, last_call=True
    )

    forecast = forecast.reshape(2, 16, members * own, out_width)
    theirs = shift(take(forecast, 1 - core, 0), "c", 1)
    pair = jnp.concatenate([take(forecast, core, 0), theirs], 1)
    pair, hidden, residual, tokens = lax.optimization_barrier((pair, hidden, residual, tokens))
    gathered = lax.all_to_all(pair, ("x", "z"), 0, 0, tiled=True)
    samples = gathered.reshape(16 * 2 * members, own, out_width)
    hidden_t, residual_t, tokens_t = hidden.T, residual.T, tokens.T

    device = ((here * 4 + lax.axis_index("x")) * 4 + lax.axis_index("z")) * 2 + core
    target = jnp.take(observed, obs_index - device * own, axis=0)
    grad_raw, score_part, count_part = score(samples, target, valid_mask)

    line = jnp.arange(8)[:, None]
    sums = jnp.where(line == 0, score_part, count_part) + jnp.zeros((8, 128))
    sums = sums + shift(sums, "c", 1)
    sums = sums + shift(sums, "x", 1)
    sums = sums + shift(sums, "x", 2)
    riders = jnp.zeros((8, width - out_width))
    for i, value in enumerate(terms(sums[0, 0]) + terms(sums[1, 0])):
        riders = jnp.where(line == i, value, riders)
    riders = jnp.broadcast_to(riders.astype(BF16), (16, *riders.shape))

    returned = lax.all_to_all(
        grad_raw.reshape(16, 2 * members * own, out_width), ("x", "z"), 0, 0, tiled=True
    ).reshape(16, 2, members * own, out_width)
    back = shift(returned[:, 1], "c", 1)
    grad_rows = jnp.where(
        core == 0, jnp.stack([returned[:, 0], back]), jnp.stack([back, returned[:, 0]])
    ).reshape(rows, out_width)

    at = place(0)
    resid_grad = dot(grad_rows, head).astype(BF16)
    keep, send = early_grads(at, hidden_t, resid_grad, residual_t, grad_rows)
    early = add(keep, shift(send, "c", 1)).reshape(2, 2, 2, -1, width)
    keep, send = late_grads(at, resid_grad, second, slope, tokens_t)
    late = add(keep, shift(send, "c", 1)).reshape(2, 16, 2, 2, -1, width)
    a, b = ring_sum(early[:, :, 0], early[:, :, 1], "x")
    early = jnp.concatenate([a, b]).reshape(16, -1, width)
    n_second = shard * RING // 128
    early = lax.dynamic_update_slice(early, riders, (0, n_second, out_width))
    early = lax.all_to_all(early, ("z", "y"), 0, 0, tiled=True)
    late = late.transpose(0, 2, 3, 1, 4, 5)
    a, b = ring_sum(late[0], late[1], "y")
    late = lax.all_to_all(jnp.concatenate([a, b], 1), ("x", "z"), 0, 0, tiled=True)
    early = jnp.sum(early.astype(F32), 0)
    late = jnp.sum(late.astype(F32), 0)
    ride = early[n_second : n_second + 8, out_width]
    score_total = ride[0] + ride[1] + ride[2]
    valid_total = jnp.maximum(ride[3] + ride[4] + ride[5], 1.0)
    scale = 1.0 / valid_total
    n_first = late.shape[0] // 2
    return (
        jnp.concatenate([late[:n_first], late[n_first:]], 1) * scale,
        early[:n_second] * scale,
        early[n_second:, :out_width] * scale,
        score_total / valid_total,
    )


def solution(mesh):
    grid = Mesh(mesh.devices.reshape(4, 4, 2, 4), ("x", "z", "c", "y"))
    rows = P(("y", "x", "z", "c"))
    shares = P(("x", "z", "c", "y"), None)
    return jax.shard_map(
        per_device,
        mesh=grid,
        in_specs=(
            P(("x", "z", "c"), "y", None),
            P(None, "y"),
            P("y", None),
            P(None, "y"),
            rows,
            rows,
            rows,
        ),
        out_specs=(shares, shares, shares, P()),
        check_vma=False,
    )
```

profile of v0, /device:TPU:0, one launch (start us, length us, event | category | flops | bytes accessed | tf_op | source)
XLA Modules:
  0.0 326.5 jit_solution(10912441574681721203)
XLA Ops:
  0.7 2.4 dynamic-slice_dynamic-update-slice_fusion
  3.7 0.8 dynamic-slice_dynamic-update-slice_fusion.4
  5.2 0.8 dynamic-slice_dynamic-update-slice_fusion.2
  7.3 0.7 slice_dynamic-update-slice_fusion.1
  8.1 1.7 collective-permute-start
  9.7 1.6 collective-permute-start.2
  11.3 27.4 %collective-permute-done.refs_2_ = bf16[2432,256]{1,0:T(8,128)(2,1)S(1)} collective-permute-done((bf16[2432,256]{1,0:T(8,128)(2,1)}, bf16[2432,256]{1,0:T(8,128)(2,1)S(1)}, u32[]{:S(2)}, u32[]{:S(2)}) %collective-permute-start) | collective-permute-done | bytes 1245216 | tf_op jit(solution)/shard_map/ppermute | solution.py:26
  38.8 0.9 slice.146
  40.0 0.9 slice.147
  40.9 2.9 collective-permute-start.3
  43.9 3.2 copy.50
  47.6 8.6 %collective-permute-done.1 = bf16[1216,256]{1,0:T(8,128)(2,1)S(1)} collective-permute-done((bf16[1216,256]{1,0:T(8,128)(2,1)}, bf16[1216,256]{1,0:T(8,128)(2,1)S(1)}, u32[]{:S(2)}, u32[]{:S(2)}) %collective-permute-start.1) | collective-permute-done | bytes 622624 | tf_op jit(solution)/shard_map/ppermute | solution.py:26
  56.5 1.1 constant_dynamic-update-slice_fusion.refs_2_
  60.9 8.9 %forward_part.4 = (f32[1024,2048]{1,0:T(8,128)}, bf16[1024,2048]{1,0:T(8,128)(2,1)}, bf16[8,1024,256]{2,1,0:T(8,128)(2,1)}, bf16[768,1024]{1,0:T(8,128)(2,1)}, f32[1024,1024]{1,0:T(8,128)}) custom-call(s32[2]{0:T(128)} %pad_add_fusion.refs_0_.place, bf16[1024,1024]{1,0:T(8,128)(2,1)} %bitcast.100, bf16[2432,256]{1,0:T(8,128)(2,1)} %get-tuple-element.105.refs_2_, ...), custom_call_target="tpu_custom_call" | custom-call | flops 2147483648 | bytes 12582912 | tf_op jit(solution)/shard_map/forward_part/pallas_call | solution.py:137
  69.8 9.8 %forward_part.5 = (f32[1024,2048]{1,0:T(8,128)}, bf16[1024,2048]{1,0:T(8,128)(2,1)}, bf16[8,1024,256]{2,1,0:T(8,128)(2,1)}, bf16[768,1024]{1,0:T(8,128)(2,1)}, f32[1024,1024]{1,0:T(8,128)}) custom-call(s32[2]{0:T(128)} %pad_add_fusion.3.refs_0_, ...), custom_call_target="tpu_custom_call", output_to_operand_aliasing={{0}: (5, {}), {1}: (6, {}), {2}: (7, {}), {3}: (8, {}), {4}... | custom-call | flops 2147483648 | bytes 12582912 | tf_op jit(solution)/shard_map/forward_part/pallas_call | solution.py:137
  79.6 1.0 copy-done.10
  80.6 9.7 %forward_part.6 = (f32[1024,2048]{1,0:T(8,128)}, bf16[1024,2048]{1,0:T(8,128)(2,1)}, bf16[8,1024,256]{2,1,0:T(8,128)(2,1)}, bf16[768,1024]{1,0:T(8,128)(2,1)}, f32[1024,1024]{1,0:T(8,128)}) custom-call(s32[2]{0:T(128)} %pad_add_fusion.2.refs_0_, ...), custom_call_target="tpu_custom_call", output_to_operand_aliasing={{0}: (5, {}), {1}: (6, {}), {2}: (7, {}), {3}: (8, {}), {4}... | custom-call | flops 2147483648 | bytes 12582912 | tf_op jit(solution)/shard_map/forward_part/pallas_call | solution.py:137
  90.4 1.0 copy-done.9
  91.4 11.2 %forward_part.7 = (f32[1024,2048]{1,0:T(8,128)}, bf16[1024,2048]{1,0:T(8,128)(2,1)}, bf16[8,1024,256]{2,1,0:T(8,128)(2,1)}, bf16[768,1024]{1,0:T(8,128)(2,1)}, b...) custom-call(s32[2]{0:T(128)} %pad_add_fusion.1.refs_0_, ...), custom_call_target="tpu_custom_call", output_to_operand_aliasing={{0}: (5, {}), {1}: (6, {}), {2}: (7, {})} | custom-call | flops 2147483648 | bytes 12582912 | tf_op jit(solution)/shard_map/forward_part/pallas_call | solution.py:137
  102.6 1.5 dynamic-slice_bitcast_fusion.3
  104.5 1.9 collective-permute-done.7
  106.5 1.3 pad_maximum_fusion
  107.7 7.9 %all-to-all-start = ((bf16[16,64,768]{2,1,0:T(8,128)(2,1)}), bf16[16,64,768]{2,1,0:T(8,128)(2,1)S(1)}, u32[]{:S(2)}, u32[]{:S(2)}) async-start(bf16[16,64,768]{2,1,0:T(8,128)(2,1)} %pad_maximum_fusion), calls=%async_computation | async-start | bytes 3145728 | tf_op jit(solution)/shard_map/all_to_all | solution.py:369
  116.4 24.0 %all-to-all-done = bf16[16,64,768]{2,1,0:T(8,128)(2,1)S(1)} async-done(((bf16[16,64,768]{2,1,0:T(8,128)(2,1)}), bf16[16,64,768]{2,1,0:T(8,128)(2,1)S(1)}, u32[]{:S(2)}, u32[]{:S(2)}) %all-to-all-start) | async-done | bytes 1572896 | tf_op jit(solution)/shard_map/all_to_all | solution.py:369
  140.6 0.7 fusion.6
  141.7 0.9 fusion.34
  143.2 2.8 fusion.8
  146.0 0.9 copy.60
  146.9 24.7 %all_to_all.20 = bf16[16,64,768]{2,1,0:T(8,128)(2,1)S(1)} all-to-all(bf16[16,64,768]{2,1,0:T(8,128)(2,1)S(1)} %bitcast.109), channel_id=1, replica_groups=mesh['x'=4,'z'=4,'c'=2,'y'=4] {'x','z'}, dimensions={0} | all-to-all | bytes 3145728 | tf_op jit(solution)/shard_map/all_to_all | solution.py:387
  171.6 1.0 slice_bitcast_fusion.1
  172.6 0.9 copy-done.2
  173.5 2.6 copy.62
  176.1 1.8 maximum_select_fusion
  178.0 3.2 convolution_convert_fusion.resid_grad
  181.1 23.1 %late_grads.1 = (bf16[2,512,1024]{2,1,0:T(8,128)(2,1)}, bf16[2,512,1024]{2,1,0:T(8,128)(2,1)}) custom-call(s32[2]{0:T(128)} %pad_add_fusion.refs_0_.place, bf16[1024,1024]{1,0:T(8,128)(2,1)} %convolution_convert_fusion.resid_grad, bf16[8,1024,256]{2,1,0:T(8,128)(2,1)} %get-tuple-element.53.second, f32[1024,2048]{1,0:T(8,128)} %get-tuple-element.54.slope, ...), custom_call_target="tpu_custom_call" | custom-call | flops 8589934592 | bytes 20971520 | tf_op jit(solution)/shard_map/late_grads/pallas_call | solution.py:236
  204.3 6.6 %copy.64 = bf16[1024,2048]{0,1:T(8,128)(2,1)} copy(bf16[1024,2048]{1,0:T(8,128)(2,1)} %get-tuple-element.58) | data formatting | bytes 8388608 | tf_op jit(solution)/shard_map/optimization_barrier | solution.py:368
  210.9 2.6 copy.65
  213.5 12.0 %early_grads.1 = (bf16[4,384,1024]{2,1,0:T(8,128)(2,1)}, bf16[4,384,1024]{2,1,0:T(8,128)(2,1)}) custom-call(s32[2]{0:T(128)} %pad_add_fusion.refs_0_.place, bf16[2048,1024]{1,0:T(8,128)(2,1)} %bitcast.112, bf16[1024,1024]{1,0:T(8,128)(2,1)} %convolution_convert_fusion.resid_grad, bf16[1024,1024]{1,0:T(8,128)(2,1)} %bitcast.115, bf16[1024,768]{1,0:T(8,128)(2,1)} %bitcast.118), custom_call_target="tpu_custom_call" | custom-call | flops 5905580032 | bytes 18874368 | tf_op jit(solution)/shard_map/early_grads/pallas_call | solution.py:191
  225.8 1.3 compare_select_fusion.2
  227.4 3.8 %collective-permute-done.19 = f32[8,128]{1,0:T(8,128)S(1)} collective-permute-done((f32[8,128]{1,0:T(8,128)S(1)}, f32[8,128]{1,0:T(8,128)S(1)}, u32[]{:S(2)}, u32[]{:S(2)}) %collective-permute-start.19) | collective-permute-done | bytes 4128 | tf_op jit(solution)/shard_map/ppermute | solution.py:26
  231.7 4.4 %collective-permute-done.20 = f32[8,128]{1,0:T(8,128)S(1)} collective-permute-done((f32[8,128]{1,0:T(8,128)S(1)}, f32[8,128]{1,0:T(8,128)S(1)}, u32[]{:S(2)}, u32[]{:S(2)}) %collective-permute-start.20) | collective-permute-done | bytes 4128 | tf_op jit(solution)/shard_map/ppermute | solution.py:26
  236.2 5.0 %collective-permute-done.21 = f32[8,128]{1,0:T(8,128)S(1)} collective-permute-done((f32[8,128]{1,0:T(8,128)S(1)}, f32[8,128]{1,0:T(8,128)S(1)}, u32[]{:S(2)}, u32[]{:S(2)}) %collective-permute-start.21) | collective-permute-done | bytes 4128 | tf_op jit(solution)/shard_map/ppermute | solution.py:26
  241.2 2.6 add_convert_fusion.1
  244.2 1.1 collective-permute-start.10
  253.7 2.0 select_convert_fusion
  255.8 2.7 collective-permute-start.12
  258.7 4.4 %add_convert_fusion = bf16[4,384,1024]{2,1,0:T(8,128)(2,1)S(1)} fusion(bf16[4,384,1024]{2,1,0:T(8,128)(2,1)} %collective-permute-done.14, bf16[4,384,1024]{2,1,0:T(8,128)(2,1)} %get-tuple-element.60), kind=kLoop, calls=%fused_computation.1 | loop fusion | flops 6291456 | bytes 9437184 | tf_op jit(solution)/shard_map/convert_element_type | solution.py:259
  263.6 1.4 collective-permute-start.11
  265.1 0.9 collective-permute-start.17
  266.0 5.5 %collective-permute-done.12 = bf16[2,16,8,1024]{3,2,0,1:T(8,128)(2,1)S(1)} collective-permute-done((bf16[2,16,8,1024]{3,2,0,1:T(8,128)(2,1)S(1)}, bf16[2,16,8,1024]{3,2,0,1:T(8,128)(2,1)S(1)}, u32[]{:S(2)}, u32[]{:S(2)}) %collective-permute-start.12) | collective-permute-done | bytes 524320 | tf_op jit(solution)/shard_map/ppermute | solution.py:275
  271.7 1.2 collective-permute-start.13
  272.9 1.4 collective-permute-done.11
  274.3 6.5 %collective-permute-done.15 = bf16[2,192,1024]{2,1,0:T(8,128)(2,1)S(1)} collective-permute-done((bf16[2,192,1024]{2,1,0:T(8,128)(2,1)S(1)}, bf16[2,192,1024]{2,1,0:T(8,128)(2,1)S(1)}, u32[]{:S(2)}, u32[]{:S(2)}) %collective-permute-start.15) | collective-permute-done | bytes 786464 | tf_op jit(solution)/shard_map/ppermute | solution.py:274
  281.5 1.9 collective-permute-done.17
  283.7 0.8 dynamic-slice_bitcast_fusion.5
  284.5 1.7 collective-permute-start.18
  286.2 0.8 pad_maximum_fusion.2
  287.1 3.6 %all-to-all-start.2 = ((bf16[16,16,1024]{2,1,0:T(8,128)(2,1)}), bf16[16,16,1024]{2,1,0:T(8,128)(2,1)S(1)}, u32[]{:S(2)}, u32[]{:S(2)}) async-start(bf16[16,16,1024]{2,1,0:T(8,128)(2,1)} %pad_maximum_fusion.2), calls=%async_computation.2 | async-start | bytes 1048576 | tf_op jit(solution)/shard_map/all_to_all | solution.py:408
  290.7 1.3 collective-permute-done.16
  292.1 3.2 collective-permute-done.18
  295.4 1.0 pad_maximum_fusion.1
  297.1 3.7 %all-to-all-done.2 = bf16[16,16,1024]{2,1,0:T(8,128)(2,1)S(1)} async-done(((bf16[16,16,1024]{2,1,0:T(8,128)(2,1)}), bf16[16,16,1024]{2,1,0:T(8,128)(2,1)S(1)}, u32[]{:S(2)}, u32[]{:S(2)}) %all-to-all-start.2) | async-done | bytes 524320 | tf_op jit(solution)/shard_map/all_to_all | solution.py:408
  300.7 6.4 %all-to-all-start.3 = ((bf16[16,24,1024]{2,1,0:T(8,128)(2,1)}), bf16[16,24,1024]{2,1,0:T(8,128)(2,1)S(1)}, u32[]{:S(2)}, u32[]{:S(2)}) async-start(bf16[16,24,1024]{2,1,0:T(8,128)(2,1)} %broadcast_dynamic-update-slice_fusion), calls=%async_computation.3 | async-start | bytes 1572864 | tf_op jit(solution)/shard_map/all_to_all | solution.py:405
  307.2 11.5 %all-to-all-done.3 = bf16[16,24,1024]{2,1,0:T(8,128)(2,1)S(1)} async-done(((bf16[16,24,1024]{2,1,0:T(8,128)(2,1)}), bf16[16,24,1024]{2,1,0:T(8,128)(2,1)S(1)}, u32[]{:S(2)}, u32[]{:S(2)}) %all-to-all-start.3) | async-done | bytes 786464 | tf_op jit(solution)/shard_map/all_to_all | solution.py:405
  (110 shorter events, 18.1 us)
Async XLA Ops:
  0.6 115.1 %copy-start = (f32[8,768]{1,0:T(8,128)S(1)}, f32[8,768]{1,0:T(8,128)}, u32[]{:S(2)}) copy-start(f32[8,768]{1,0:T(8,128)} %param.11) | copy-start | bytes 73732
  0.6 2.4 copy-start.11
  3.0 3.6 %copy-start.12 = (bf16[1024,192]{0,1:T(8,128)(2,1)S(1)}, bf16[1024,192]{0,1:T(8,128)(2,1)}, u32[]{:S(2)}) copy-start(bf16[1024,192]{0,1:T(8,128)(2,1)} %param.10) | copy-start | bytes 1179652
  8.1 30.7 %collective-permute-start = (bf16[2432,256]{1,0:T(8,128)(2,1)}, bf16[2432,256]{1,0:T(8,128)(2,1)S(1)}, u32[]{:S(2)}, u32[]{:S(2)}) collective-permute-start(bf16[2432,256]{1,0:T(8,128)(2,1)} %get-tuple-element.105.refs_2_), channel_id=1, source_target_pairs={{0,1},{1,2},{2,3},{3,0},{4,5},{5,6},{6,7},{7,4},{8,9},{9,10},{10,1... | collective-permute-start | bytes 3735560 | tf_op jit(solution)/shard_map/ppermute | solution.py:26
  9.7 30.3 %collective-permute-start.2 = (bf16[2432,256]{1,0:T(8,128)(2,1)}, bf16[2432,256]{1,0:T(8,128)(2,1)S(1)}, u32[]{:S(2)}, u32[]{:S(2)}) collective-permute-start(bf16[2432,256]{1,0:T(8,128)(2,1)} %get-tuple-element.105.refs_2_), channel_id=1, source_target_pairs={{0,3},{1,0},{2,1},{3,2},{4,7},{5,4},{6,5},{7,6},{8,11},{9,8},{10,9... | collective-permute-start | bytes 3735560 | tf_op jit(solution)/shard_map/ppermute | solution.py:26
  38.8 8.3 %copy-start.4 = (bf16[2432,256]{1,0:T(8,128)(2,1)}, bf16[2432,256]{1,0:T(8,128)(2,1)S(1)}, u32[]{:S(2)}) copy-start(bf16[2432,256]{1,0:T(8,128)(2,1)S(1)} %collective-permute-done.refs_2_) | copy-start | bytes 3735556
  39.7 16.5 %collective-permute-start.1 = (bf16[1216,256]{1,0:T(8,128)(2,1)}, bf16[1216,256]{1,0:T(8,128)(2,1)S(1)}, u32[]{:S(2)}, u32[]{:S(2)}) collective-permute-start(bf16[1216,256]{1,0:T(8,128)(2,1)} %slice.146), channel_id=1, source_target_pairs={{0,1},{1,2},{2,3},{3,0},{4,5},{5,6},{6,7},{7,4},{8,9},{9,10},{10,1... | collective-permute-start | bytes 1867784 | tf_op jit(solution)/shard_map/ppermute | solution.py:26
  40.0 7.1 %copy-start.3 = (bf16[2432,256]{1,0:T(8,128)(2,1)}, bf16[2432,256]{1,0:T(8,128)(2,1)S(1)}, u32[]{:S(2)}) copy-start(bf16[2432,256]{1,0:T(8,128)(2,1)S(1)} %collective-permute-done.2.refs_2_) | copy-start | bytes 3735556
  40.9 15.5 %collective-permute-start.3 = (bf16[1216,256]{1,0:T(8,128)(2,1)}, bf16[1216,256]{1,0:T(8,128)(2,1)}, u32[]{:S(2)}, u32[]{:S(2)}) collective-permute-start(bf16[1216,256]{1,0:T(8,128)(2,1)} %slice.147), channel_id=1, source_target_pairs={{0,3},{1,0},{2,1},{3,2},{4,7},{5,4},{6,5},{7,6},{8,11},{9,8},{10,9... | collective-permute-start | bytes 1867784 | tf_op jit(solution)/shard_map/ppermute | solution.py:26
  47.1 22.8 %collective-permute-start.6 = (bf16[2432,256]{1,0:T(8,128)(2,1)S(1)}, bf16[2432,256]{1,0:T(8,128)(2,1)}, u32[]{:S(2)}, u32[]{:S(2)}) collective-permute-start(bf16[2432,256]{1,0:T(8,128)(2,1)S(1)} %collective-permute-done.refs_2_), channel_id=1, source_target_pairs={{0,4},{4,0},{1,5},{5,1},{2,6},{6,2},{3,7},{7,3},{8,12},{12,8},{9,1... | collective-permute-start | bytes 3735560 | tf_op jit(solution)/shard_map/ppermute | solution.py:26
  47.1 32.5 %collective-permute-start.5 = (bf16[2432,256]{1,0:T(8,128)(2,1)S(1)}, bf16[2432,256]{1,0:T(8,128)(2,1)S(1)}, u32[]{:S(2)}, u32[]{:S(2)}) collective-permute-start(bf16[2432,256]{1,0:T(8,128)(2,1)S(1)} %collective-permute-done.2.refs_2_), channel_id=1, source_target_pairs={{0,4},{4,0},{1,5},{5,1},{2,6},{6,2},{3,7},{7,3},{8,12},{12,8},{9,1... | collective-permute-start | bytes 3735560 | tf_op jit(solution)/shard_map/ppermute | solution.py:26
  57.6 12.2 %copy-start.5 = (bf16[2432,256]{1,0:T(8,128)(2,1)}, bf16[2432,256]{1,0:T(8,128)(2,1)S(1)}, u32[]{:S(2)}) copy-start(bf16[2432,256]{1,0:T(8,128)(2,1)S(1)} %constant_dynamic-update-slice_fusion.refs_2_) | copy-start | bytes 3735556
  57.6 32.8 %collective-permute-start.4 = (bf16[2432,256]{1,0:T(8,128)(2,1)S(1)}, bf16[2432,256]{1,0:T(8,128)(2,1)S(1)}, u32[]{:S(2)}, u32[]{:S(2)}) collective-permute-start(bf16[2432,256]{1,0:T(8,128)(2,1)S(1)} %constant_dynamic-update-slice_fusion.refs_2_), channel_id=1, source_target_pairs={{0,4},{4,0},{1,5},{5,1},{2,6},{6,2},{3,7},{7,3},{8,12},{12,8},{9,1... | collective-permute-start | bytes 3735560 | tf_op jit(solution)/shard_map/ppermute | solution.py:26
  79.6 1.0 copy-start.10
  90.4 1.0 copy-start.9
  104.1 2.4 collective-permute-start.7
  107.7 8.0 %copy-start.13 = (s32[8]{0:T(128)S(1)}, s32[8]{0:T(128)}, u32[]{:S(2)}) copy-start(s32[8]{0:T(128)} %param.12) | copy-start | bytes 100
  107.7 32.7 %all-to-all-start = ((bf16[16,64,768]{2,1,0:T(8,128)(2,1)}), bf16[16,64,768]{2,1,0:T(8,128)(2,1)S(1)}, u32[]{:S(2)}, u32[]{:S(2)}) async-start(bf16[16,64,768]{2,1,0:T(8,128)(2,1)} %pad_maximum_fusion), calls=%async_computation | async-start | bytes 3145728 | tf_op jit(solution)/shard_map/all_to_all | solution.py:369
  141.7 0.9 copy-start.14
  171.6 1.9 copy-start.2
  172.6 3.4 %collective-permute-start.8 = (bf16[16,32,768]{2,1,0:T(8,128)(2,1)}, bf16[16,32,768]{2,1,0:T(8,128)(2,1)}, u32[]{:S(2)}, u32[]{:S(2)}) collective-permute-start(bf16[16,32,768]{2,1,0:T(8,128)(2,1)} %get-tuple-element.75), channel_id=1, source_target_pairs={{0,4},{4,0},{1,5},{5,1},{2,6},{6,2},{3,7},{7,3},{8,12},{12,8},{9,1... | collective-permute-start | bytes 2359304 | tf_op jit(solution)/shard_map/ppermute | solution.py:26
  176.1 1.9 copy-start.15
  177.9 3.2 copy-start.8
  204.2 6.6 %copy-start.7 = (bf16[1024,1024]{1,0:T(8,128)(2,1)S(1)}, bf16[1024,1024]{1,0:T(8,128)(2,1)}, u32[]{:S(2)}) copy-start(bf16[1024,1024]{1,0:T(8,128)(2,1)} %get-tuple-element.59) | copy-start | bytes 6291460
  204.2 37.0 %collective-permute-start.9 = (bf16[2,512,1024]{2,1,0:T(8,128)(2,1)}, bf16[2,512,1024]{2,1,0:T(8,128)(2,1)}, u32[]{:S(2)}, u32[]{:S(2)}) collective-permute-start(bf16[2,512,1024]{2,1,0:T(8,128)(2,1)} %get-tuple-element.57), channel_id=1, source_target_pairs={{0,4},{4,0},{1,5},{5,1},{2,6},{6,2},{3,7},{7,3},{8,12},{12,8},{9,1... | collective-permute-start | bytes 6291464 | tf_op jit(solution)/shard_map/ppermute | solution.py:26
  213.5 27.8 %copy-start.6 = (bf16[2,512,1024]{2,1,0:T(8,128)(2,1)S(1)}, bf16[2,512,1024]{2,1,0:T(8,128)(2,1)}, u32[]{:S(2)}) copy-start(bf16[2,512,1024]{2,1,0:T(8,128)(2,1)} %get-tuple-element.56) | copy-start | bytes 6291460
  225.5 33.2 %collective-permute-start.14 = (bf16[4,384,1024]{2,1,0:T(8,128)(2,1)}, bf16[4,384,1024]{2,1,0:T(8,128)(2,1)}, u32[]{:S(2)}, u32[]{:S(2)}) collective-permute-start(bf16[4,384,1024]{2,1,0:T(8,128)(2,1)} %get-tuple-element.61), channel_id=1, source_target_pairs={{0,4},{4,0},{1,5},{5,1},{2,6},{6,2},{3,7},{7,3},{8,12},{12,8},{9,1... | collective-permute-start | bytes 9437192 | tf_op jit(solution)/shard_map/ppermute | solution.py:26
  227.2 3.9 %collective-permute-start.19 = (f32[8,128]{1,0:T(8,128)S(1)}, f32[8,128]{1,0:T(8,128)S(1)}, u32[]{:S(2)}, u32[]{:S(2)}) collective-permute-start(f32[8,128]{1,0:T(8,128)S(1)} %add.246), channel_id=1, source_target_pairs={{0,4},{4,0},{1,5},{5,1},{2,6},{6,2},{3,7},{7,3},{8,12},{12,8},{9,1... | collective-permute-start | bytes 12296 | tf_op jit(solution)/shard_map/ppermute | solution.py:26
  231.2 4.8 %collective-permute-start.20 = (f32[8,128]{1,0:T(8,128)S(1)}, f32[8,128]{1,0:T(8,128)S(1)}, u32[]{:S(2)}, u32[]{:S(2)}) collective-permute-start(f32[8,128]{1,0:T(8,128)S(1)} %broadcast_add_fusion), channel_id=1, source_target_pairs={{0,32},{32,64},{64,96},{96,0},{1,33},{33,65},{65,97},{97,1},{2,34}... | collective-permute-start | bytes 12296 | tf_op jit(solution)/shard_map/ppermute | solution.py:26
  236.1 5.1 %collective-permute-start.21 = (f32[8,128]{1,0:T(8,128)S(1)}, f32[8,128]{1,0:T(8,128)S(1)}, u32[]{:S(2)}, u32[]{:S(2)}) collective-permute-start(f32[8,128]{1,0:T(8,128)S(1)} %fusion.43), channel_id=1, source_target_pairs={{0,64},{32,96},{64,0},{96,32},{1,65},{33,97},{65,1},{97,33},{2,66}... | collective-permute-start | bytes 12296 | tf_op jit(solution)/shard_map/ppermute | solution.py:26
  244.2 14.3 %collective-permute-start.10 = (bf16[2,16,8,1024]{3,2,1,0:T(8,128)(2,1)S(1)}, bf16[2,16,8,1024]{3,2,1,0:T(8,128)(2,1)S(1)}, u32[]{:S(2)}, u32[]{:S(2)}) collective-permute-start(bf16[2,16,8,1024]{3,2,1,0:T(8,128)(2,1)S(1)} %bitcast.119), channel_id=1, source_target_pairs={{0,1},{1,0},{2,3},{3,2},{4,5},{5,4},{6,7},{7,6},{8,9},{9,8},{10,11... | collective-permute-start | bytes 1572872 | tf_op jit(solution)/shard_map/ppermute | solution.py:274
  255.8 15.7 %collective-permute-start.12 = (bf16[2,16,8,1024]{3,2,0,1:T(8,128)(2,1)S(1)}, bf16[2,16,8,1024]{3,2,0,1:T(8,128)(2,1)S(1)}, u32[]{:S(2)}, u32[]{:S(2)}) collective-permute-start(bf16[2,16,8,1024]{3,2,0,1:T(8,128)(2,1)S(1)} %dynamic-slice_bitcast_fusion.4), channel_id=1, source_target_pairs={{0,3},{3,0},{1,2},{2,1},{4,7},{7,4},{5,6},{6,5},{8,11},{11,8},{9,1... | collective-permute-start | bytes 1572872 | tf_op jit(solution)/shard_map/ppermute | solution.py:275
  263.5 17.3 %collective-permute-start.15 = (bf16[2,192,1024]{2,1,0:T(8,128)(2,1)S(1)}, bf16[2,192,1024]{2,1,0:T(8,128)(2,1)S(1)}, u32[]{:S(2)}, u32[]{:S(2)}) collective-permute-start(bf16[2,192,1024]{2,1,0:T(8,128)(2,1)S(1)} %dynamic-slice_bitcast_fusion.1), channel_id=1, source_target_pairs={{0,32},{32,0},{64,96},{96,64},{1,33},{33,1},{65,97},{97,65},{2,34}... | collective-permute-start | bytes 2359304 | tf_op jit(solution)/shard_map/ppermute | solution.py:274
  263.6 10.6 %collective-permute-start.11 = (bf16[16,8,1024]{2,1,0:T(8,128)(2,1)S(1)}, bf16[16,8,1024]{2,1,0:T(8,128)(2,1)S(1)}, u32[]{:S(2)}, u32[]{:S(2)}) collective-permute-start(bf16[16,8,1024]{2,1,0:T(8,128)(2,1)S(1)} %dynamic-slice_bitcast_fusion.8), channel_id=1, source_target_pairs={{0,3},{3,0},{1,2},{2,1},{4,7},{7,4},{5,6},{6,5},{8,11},{11,8},{9,1... | collective-permute-start | bytes 786440 | tf_op jit(solution)/shard_map/ppermute | solution.py:278
  265.1 18.3 %collective-permute-start.17 = (bf16[2,192,1024]{2,1,0:T(8,128)(2,1)S(1)}, bf16[2,192,1024]{2,1,0:T(8,128)(2,1)S(1)}, u32[]{:S(2)}, u32[]{:S(2)}) collective-permute-start(bf16[2,192,1024]{2,1,0:T(8,128)(2,1)S(1)} %dynamic-slice_bitcast_fusion), channel_id=1, source_target_pairs={{0,96},{96,0},{32,64},{64,32},{1,97},{97,1},{33,65},{65,33},{2,98}... | collective-permute-start | bytes 2359304 | tf_op jit(solution)/shard_map/ppermute | solution.py:275
  271.7 14.5 %collective-permute-start.13 = (bf16[16,8,1024]{2,1,0:T(8,128)(2,1)S(1)}, bf16[16,8,1024]{2,1,0:T(8,128)(2,1)S(1)}, u32[]{:S(2)}, u32[]{:S(2)}) collective-permute-start(bf16[16,8,1024]{2,1,0:T(8,128)(2,1)S(1)} %dynamic-slice_bitcast_fusion.7), channel_id=1, source_target_pairs={{0,1},{1,0},{2,3},{3,2},{4,5},{5,4},{6,7},{7,6},{8,9},{9,8},{10,11... | collective-permute-start | bytes 786440 | tf_op jit(solution)/shard_map/ppermute | solution.py:279
  281.2 10.8 %collective-permute-start.16 = (bf16[192,1024]{1,0:T(8,128)(2,1)S(1)}, bf16[192,1024]{1,0:T(8,128)(2,1)S(1)}, u32[]{:S(2)}, u32[]{:S(2)}) collective-permute-start(bf16[192,1024]{1,0:T(8,128)(2,1)S(1)} %dynamic-slice_bitcast_fusion.6), channel_id=1, source_target_pairs={{0,96},{96,0},{32,64},{64,32},{1,97},{97,1},{33,65},{65,33},{2,98}... | collective-permute-start | bytes 1179656 | tf_op jit(solution)/shard_map/ppermute | solution.py:278
  284.5 10.8 %collective-permute-start.18 = (bf16[192,1024]{1,0:T(8,128)(2,1)}, bf16[192,1024]{1,0:T(8,128)(2,1)S(1)}, u32[]{:S(2)}, u32[]{:S(2)}) collective-permute-start(bf16[192,1024]{1,0:T(8,128)(2,1)} %dynamic-slice_bitcast_fusion.5), channel_id=1, source_target_pairs={{0,32},{32,0},{64,96},{96,64},{1,33},{33,1},{65,97},{97,65},{2,34}... | collective-permute-start | bytes 1179656 | tf_op jit(solution)/shard_map/ppermute | solution.py:279
  287.1 13.6 %all-to-all-start.2 = ((bf16[16,16,1024]{2,1,0:T(8,128)(2,1)}), bf16[16,16,1024]{2,1,0:T(8,128)(2,1)S(1)}, u32[]{:S(2)}, u32[]{:S(2)}) async-start(bf16[16,16,1024]{2,1,0:T(8,128)(2,1)} %pad_maximum_fusion.2), calls=%async_computation.2 | async-start | bytes 1048576 | tf_op jit(solution)/shard_map/all_to_all | solution.py:408
  296.4 28.9 %copy-start.1 = (f32[8,768]{1,0:T(8,128)S(1)}, f32[8,768]{1,0:T(8,128)}, u32[]{:S(2)}) copy-start(f32[8,768]{1,0:T(8,128)} %param.11) | copy-start | bytes 73732
  300.7 18.0 %all-to-all-start.3 = ((bf16[16,24,1024]{2,1,0:T(8,128)(2,1)}), bf16[16,24,1024]{2,1,0:T(8,128)(2,1)S(1)}, u32[]{:S(2)}, u32[]{:S(2)}) async-start(bf16[16,24,1024]{2,1,0:T(8,128)(2,1)} %broadcast_dynamic-update-slice_fusion), calls=%async_computation.3 | async-start | bytes 1572864 | tf_op jit(solution)/shard_map/all_to_all | solution.py:405
where the time goes:
time: 328 us; the launch traced here: 326 us
  waiting for transfers between devices  110 us (34%)
  Pallas kernels  74.7 us (23%)
  local copies, waits for them, and re-layouts  37 us (11%)
  starting transfers between devices  35.9 us (11%)
  blocking collectives  24.7 us (8%)
  other arithmetic  23.5 us (7%)
  between operations  13.4 us (4%)
  matrix products  6.9 us (2%)
    ppermute x14, waiting for transfers between devices, shift(): return lax.ppermute(x, axis, [(i, (i + by) % size) for i in range(size)])  51.4 us
    pallas_call x4, Pallas kernels, forward_part(): pl.pallas_call(functools.partial(forward_kernel, first_call, last_call, b...  39.6 us
    all_to_all x1, blocking collectives, per_device(): lax.all_to_all(grad_raw.reshape(16, 2 * members * own, out_width), ('x',...  24.7 us
    all_to_all x1, waiting for transfers between devices, per_device(): gathered = lax.all_to_all(pair, ('x', 'z'), 0, 0, tiled=True)  24 us
    pallas_call x1, Pallas kernels, late_grads(): pl.pallas_call(late_kernel, grid_spec=pltpu.PrefetchScalarGridSpec(num_sc...  23.1 us
    pallas_call x1, Pallas kernels, early_grads(): pl.pallas_call(early_kernel, grid_spec=pltpu.PrefetchScalarGridSpec(num_s...  12 us
    optimization_barrier x3, local copies, waits for them, and re-layouts, per_device(): lax.optimization_barrier((pair, hidden, residual, tokens))  11.7 us
    all_to_all x1, waiting for transfers between devices, per_device(): early = lax.all_to_all(early, ('z', 'y'), 0, 0, tiled=True)  11.5 us
  transfers between devices with their start and end apart: 25, of which 16 were waited for; matrix products, arithmetic and copies ran while one was open for 12% of the time, Pallas kernels for 12%

commit v1 on v0

--- a/solution.py
+++ b/solution.py
@@ -57,7 +57,11 @@
         if last_call:
             head[...] = head_in[...]
         for pack, side in ((mine, core), (theirs, 1 - core)):
-            second[side] = pack[start : start + chunks * half, :]
+            below = pl.multiple_of(side * half, half)
+            for q in range(chunks):
+                second[pl.ds(below, half), q * LANES : (q + 1) * LANES] = pack[
+                    start + q * half : start + (q + 1) * half, :
+                ]
             for e in range(2):
                 piece = pack[head_start + e * head_rows : head_start + (e + 1) * head_rows, :]
                 lane = pl.multiple_of(side * (width // 2) + e * LANES, LANES)
@@ -114,7 +118,7 @@
     out_specs = [
         column,
         column,
-        pl.BlockSpec((2, width * half // LANES, LANES), lambda i, s: (s[0], 0, 0)),
+        pl.BlockSpec((2 * half, width), lambda i, s: (s[0], 0)),
         whole((out_width, width))
         if last_call
         else pl.BlockSpec((head_rows, width), lambda i, s: (s[0], 0)),
@@ -122,7 +126,7 @@
     out_shape = [
         jax.ShapeDtypeStruct((rows, hid), F32),
         jax.ShapeDtypeStruct((rows, hid), BF16),
-        jax.ShapeDtypeStruct((2 * RING, width * half // LANES, LANES), BF16),
+        jax.ShapeDtypeStruct((hid, width), BF16),
         jax.ShapeDtypeStruct((out_width, width), BF16),
     ]
     if last_call:
@@ -170,21 +174,21 @@
         send[0] = zero
 
 
-def early_kernel(place, hidden_t, resid_grad, residual_t, grad_rows, keep, send):
-    second = dot(hidden_t[...], resid_grad[...])
-    head = dot(residual_t[...], grad_rows[...])
+def early_kernel(place, hidden, resid_grad, residual, grad_rows, riders, keep, send):
+    second = dot(hidden[...], resid_grad[...], ((0,), (0,)))
+    head = dot(residual[...], grad_rows[...], ((0,), (0,)))
     width, out_width = second.shape[1], head.shape[1]
     second = second.reshape(RING, 2, RING, -1, width)
     head = head.reshape(RING, 2, RING, -1, out_width)
-    blank = jnp.zeros((*head.shape[:4], width - out_width), F32)
+    blank = jnp.broadcast_to(riders[...], (*head.shape[:4], width - out_width))
     both = jnp.concatenate([second, jnp.concatenate([head, blank], 4)], 3)
     both = both.reshape(RING, 2, -1, width)
     store_halves(place[1], both, keep, send)
 
 
-def early_grads(place, hidden_t, resid_grad, residual_t, grad_rows):
-    hid, rows = hidden_t.shape
-    width, out_width = residual_t.shape[0], grad_rows.shape[1]
+def early_grads(place, hidden, resid_grad, residual, grad_rows, riders):
+    rows, hid = hidden.shape
+    width, out_width = residual.shape[1], grad_rows.shape[1]
     lines = (hid + width) // RING // 2
     gray = lambda i: 2 * ((i // 2 + i) % 2) + i // 2
     out = pl.BlockSpec((1, lines, width), lambda i, s: (gray(i), 0, 0))
@@ -194,10 +198,11 @@
             num_scalar_prefetch=1,
             grid=(RING,),
             in_specs=[
-                pl.BlockSpec((hid // RING, rows), lambda i, s: (i, 0)),
+                pl.BlockSpec((rows, hid // RING), lambda i, s: (0, i)),
                 pl.BlockSpec((rows, width), lambda i, s: (0, 0)),
-                pl.BlockSpec((width // RING, rows), lambda i, s: (i, 0)),
+                pl.BlockSpec((rows, width // RING), lambda i, s: (0, i)),
                 pl.BlockSpec((rows, out_width), lambda i, s: (0, 0)),
+                pl.BlockSpec(riders.shape, lambda i, s: (0, 0)),
             ],
             out_specs=[out, out],
         ),
@@ -207,52 +212,44 @@
             flops=2 * rows * width * (hid + out_width), bytes_accessed=18 * MIB, transcendentals=0
         ),
         name="early_grads",
-    )(place, hidden_t, resid_grad, residual_t, grad_rows)
-
-
-def late_kernel(place, resid_grad, second, slope, tokens_t, keep, send):
-    grad = resid_grad[...]
-    width = grad.shape[1]
-    total = None
-    for q in range(width // LANES):
-        term = dot(
-            grad[:, q * LANES : (q + 1) * LANES],
-            second[0, q * LANES : (q + 1) * LANES, :],
-            ((1,), (1,)),
-        )
-        total = term if total is None else total + term
-    preact_grad = (slope[...] * total).astype(BF16)
-    first = dot(tokens_t[...], preact_grad)
-    parts = first.reshape(16, 2, RING, -1, LANES)
+    )(place, hidden, resid_grad, residual, grad_rows, riders)
+
+
+def late_kernel(place, resid_grad, second, slope, tokens, keep, send):
+    hidden_grad = dot(resid_grad[...], second[...], ((1,), (1,)))
+    preact_grad = (slope[...] * hidden_grad).astype(BF16)
+    first = dot(tokens[...], preact_grad, ((0,), (0,)))
+    cols = first.shape[1]
+    parts = first.reshape(16, 2, RING, -1, cols)
     parts = jnp.stack([parts[:, :, i] for i in (0, 3, 1, 2)], 2)
-    store_halves(place[1], parts.reshape(16, 2, -1, LANES), keep, send)
-
-
-def late_grads(place, resid_grad, second, slope, tokens_t):
+    store_halves(place[1], parts.reshape(16, 2, -1, cols), keep, send)
+
+
+def late_grads(place, part, resid_grad, second, slope, tokens):
     rows, width = resid_grad.shape
-    hid = slope.shape[1]
-    per = width // LANES
-    out = pl.BlockSpec((1, width // 2, LANES), lambda j, s: (j // per, 0, j % per))
+    tile = 2 * LANES
+    steps = width // tile
+    out = pl.BlockSpec((1, width // 2, tile), lambda j, s: (0, 0, j))
     return pl.pallas_call(
         late_kernel,
         grid_spec=pltpu.PrefetchScalarGridSpec(
             num_scalar_prefetch=1,
-            grid=(hid // LANES,),
+            grid=(steps,),
             in_specs=[
                 pl.BlockSpec((rows, width), lambda j, s: (0, 0)),
-                pl.BlockSpec((1, *second.shape[1:]), lambda j, s: (j, 0, 0)),
-                pl.BlockSpec((rows, LANES), lambda j, s: (0, j)),
-                pl.BlockSpec((width, rows), lambda j, s: (0, 0)),
+                pl.BlockSpec((tile, width), lambda j, s: (part * steps + j, 0)),
+                pl.BlockSpec((rows, tile), lambda j, s: (0, part * steps + j)),
+                pl.BlockSpec((rows, width), lambda j, s: (0, 0)),
             ],
             out_specs=[out, out],
         ),
-        out_shape=[jax.ShapeDtypeStruct((hid // width, width // 2, width), BF16)] * 2,
+        out_shape=[jax.ShapeDtypeStruct((1, width // 2, width), BF16)] * 2,
         compiler_params=params(1),
         cost_estimate=pl.CostEstimate(
-            flops=4 * rows * width * hid, bytes_accessed=20 * MIB, transcendentals=0
+            flops=4 * rows * width * width, bytes_accessed=12 * MIB, transcendentals=0
         ),
         name="late_grads",
-    )(place, resid_grad, second, slope, tokens_t)
+    )(place, resid_grad, second, slope, tokens)
 
 
 def add(a, b):
@@ -269,15 +266,27 @@
     return (high + here) % 2, high
 
 
-def ring_sum(a, b, axis):
+def ring_chain(axis, low_first):
     low, high = ring_bits(axis)
-    a_in = lax.ppermute(take(a, 1 - low, 0), axis, PAIR_LOW)
-    b_in = lax.ppermute(take(b, 1 - high, 1), axis, PAIR_HIGH)
-    a = add(take(a, low, 0), a_in)
-    b = add(take(b, high, 1), b_in)
-    a_in = lax.ppermute(take(a, 1 - high, 0), axis, PAIR_HIGH)
-    b_in = lax.ppermute(take(b, 1 - low, 0), axis, PAIR_LOW)
-    return add(take(a, high, 0), a_in), add(take(b, low, 0), b_in)
+    if low_first:
+        steps = ((PAIR_LOW, low, 0), (PAIR_HIGH, high, 0))
+    else:
+        steps = ((PAIR_HIGH, high, 1), (PAIR_LOW, low, 0))
+    return [(pairs, axis, bit, dim) for pairs, bit, dim in steps]
+
+
+def outgoing(x, step):
+    _, _, bit, dim = step
+    return take(x, 1 - bit, dim)
+
+
+def swapped(x, sent, step):
+    pairs, axis, bit, dim = step
+    return add(take(x, bit, dim), lax.ppermute(sent, axis, pairs))
+
+
+def tie(*arrays):
+    return lax.optimization_barrier(arrays)
 
 
 def terms(value):
@@ -291,9 +300,39 @@
     return jnp.where(flag == 1, one, zero)
 
 
-def packed(first, second, head):
-    columns = lambda v: [v[:, i : i + LANES] for i in range(0, v.shape[1], LANES)]
-    return jnp.concatenate([first, *columns(second), *columns(head)], 0)
+def pack_kernel(side, first, second, head, out):
+    width, half = first.shape
+    out[:width, :] = first[...]
+    at = width
+    for q in range(second.shape[1] // LANES):
+        out[at : at + half, :] = second[:, q * LANES : (q + 1) * LANES]
+        at += half
+    turned = head[...].astype(F32).T.astype(BF16)
+    for e in range(turned.shape[1] // LANES):
+        out[at : at + turned.shape[0], :] = turned[:, e * LANES : (e + 1) * LANES]
+        at += turned.shape[0]
+
+
+def packed(side, first, second, head):
+    width, shard = first.shape
+    half = shard // 2
+    lines = width + half * width // LANES + head.shape[1] * width // 2 // LANES
+    return pl.pallas_call(
+        pack_kernel,
+        grid_spec=pltpu.PrefetchScalarGridSpec(
+            num_scalar_prefetch=1,
+            grid=(1,),
+            in_specs=[
+                pl.BlockSpec((width, half), lambda i, s: (0, s[0])),
+                pl.BlockSpec((half, width), lambda i, s: (s[0], 0)),
+                pl.BlockSpec((width // 2, head.shape[1]), lambda i, s: (s[0], 0)),
+            ],
+            out_specs=pl.BlockSpec((lines, LANES), lambda i, s: (0, 0)),
+        ),
+        out_shape=jax.ShapeDtypeStruct((lines, LANES), BF16),
+        compiler_params=params(1),
+        name="packed",
+    )(side, first, second, head)
 
 
 def score(samples, target, valid_mask):
@@ -331,33 +370,28 @@
     shard = w_first.shape[1]
     half = shard // 2
 
-    head_shard = readout_matrix.T
-
-    def half_of(side):
-        return packed(
-            lax.dynamic_slice_in_dim(w_first, side * half, half, 1),
-            lax.dynamic_slice_in_dim(w_second, side * half, half, 0),
-            lax.dynamic_slice_in_dim(head_shard, side * (width // 2), width // 2, 1),
-        )
-
-    mine = half_of(core)
+    side = jnp.reshape(core, (1,)).astype(jnp.int32)
+    mine = packed(side, w_first, w_second, readout_matrix)
     right = shift(mine, "y", 1)
     left = shift(mine, "y", -1)
     lines = mine.shape[0] // 2
+    latents, other_side, mine = tie(latents, 1 - side, mine)
+    tokens = (
+        latents.reshape(members, 16, 2, own, width).transpose(2, 1, 0, 3, 4).reshape(rows, width)
+    )
+    theirs = packed(other_side, w_first, w_second, readout_matrix)
+    place = lambda off: jnp.stack([(here + off) % RING, core]).astype(jnp.int32)
+    run = functools.partial(forward_part, out_width=out_width)
+    carried = run(place(0), tokens, mine, theirs, carried=None, last_call=False)
+    right, left, *carried = tie(right, left, *carried)
     far = [shift(right[:lines], "y", 1), shift(left[lines:], "y", -1)]
     right_other = shift(right, "c", 1)
     left_other = shift(left, "c", 1)
-    far = jnp.concatenate(far, 0)
-    far_other = shift(far, "c", 1)
-
-    tokens = (
-        latents.reshape(members, 16, 2, own, width).transpose(2, 1, 0, 3, 4).reshape(rows, width)
-    )
-    place = lambda off: jnp.stack([(here + off) % RING, core]).astype(jnp.int32)
-    run = functools.partial(forward_part, out_width=out_width)
-    carried = run(place(0), tokens, mine, half_of(1 - core), carried=None, last_call=False)
     carried = run(place(3), tokens, right, right_other, carried=carried, last_call=False)
     carried = run(place(1), tokens, left, left_other, carried=carried, last_call=False)
+    near, past, *carried = tie(*far, *carried)
+    far = jnp.concatenate([near, past], 0)
+    far_other = shift(far, "c", 1)
     slope, hidden, second, head, residual, forecast = run(
         place(2), tokens, far, far_other, carried=carried, last_call=True
     )
@@ -365,24 +399,20 @@
     forecast = forecast.reshape(2, 16, members * own, out_width)
     theirs = shift(take(forecast, 1 - core, 0), "c", 1)
     pair = jnp.concatenate([take(forecast, core, 0), theirs], 1)
-    pair, hidden, residual, tokens = lax.optimization_barrier((pair, hidden, residual, tokens))
+    device = ((here * 4 + lax.axis_index("x")) * 4 + lax.axis_index("z")) * 2 + core
+    target = jnp.take(observed, obs_index - device * own, axis=0)
+    pair, target = tie(pair, target)
     gathered = lax.all_to_all(pair, ("x", "z"), 0, 0, tiled=True)
     samples = gathered.reshape(16 * 2 * members, own, out_width)
-    hidden_t, residual_t, tokens_t = hidden.T, residual.T, tokens.T
-
-    device = ((here * 4 + lax.axis_index("x")) * 4 + lax.axis_index("z")) * 2 + core
-    target = jnp.take(observed, obs_index - device * own, axis=0)
     grad_raw, score_part, count_part = score(samples, target, valid_mask)
 
-    line = jnp.arange(8)[:, None]
-    sums = jnp.where(line == 0, score_part, count_part) + jnp.zeros((8, 128))
-    sums = sums + shift(sums, "c", 1)
-    sums = sums + shift(sums, "x", 1)
-    sums = sums + shift(sums, "x", 2)
-    riders = jnp.zeros((8, width - out_width))
-    for i, value in enumerate(terms(sums[0, 0]) + terms(sums[1, 0])):
+    shape = (8, width - out_width)
+    line = lax.broadcasted_iota(jnp.int32, shape, 0)
+    lane = lax.broadcasted_iota(jnp.int32, shape, 1)
+    riders = jnp.where(line == 3, count_part, 0.0)
+    for i, value in enumerate(terms(score_part)):
         riders = jnp.where(line == i, value, riders)
-    riders = jnp.broadcast_to(riders.astype(BF16), (16, *riders.shape))
+    riders = jnp.where(lane == 2 * lax.axis_index("x") + core, riders, 0.0)
 
     returned = lax.all_to_all(
         grad_raw.reshape(16, 2 * members * own, out_width), ("x", "z"), 0, 0, tiled=True
@@ -394,23 +424,42 @@
 
     at = place(0)
     resid_grad = dot(grad_rows, head).astype(BF16)
-    keep, send = early_grads(at, hidden_t, resid_grad, residual_t, grad_rows)
-    early = add(keep, shift(send, "c", 1)).reshape(2, 2, 2, -1, width)
-    keep, send = late_grads(at, resid_grad, second, slope, tokens_t)
-    late = add(keep, shift(send, "c", 1)).reshape(2, 16, 2, 2, -1, width)
-    a, b = ring_sum(early[:, :, 0], early[:, :, 1], "x")
-    early = jnp.concatenate([a, b]).reshape(16, -1, width)
-    n_second = shard * RING // 128
-    early = lax.dynamic_update_slice(early, riders, (0, n_second, out_width))
+    early = early_grads(at, hidden, resid_grad, residual, grad_rows, riders)
+    resid_grad, *early = tie(resid_grad, *early)
+    early = add(early[0], shift(early[1], "c", 1)).reshape(2, 2, 2, -1, width)
+    flows = [
+        (early[:, :, 0], ring_chain("x", True)),
+        (early[:, :, 1], ring_chain("x", False)),
+    ]
+    late = late_grads(at, 0, resid_grad, second, slope, tokens)
+    sent = [outgoing(x, steps[0]) for x, steps in flows]
+    resid_grad, *rest = tie(resid_grad, *sent, *late)
+    sent, late = rest[:2], rest[2:]
+    early = [swapped(x, s, steps[0]) for (x, steps), s in zip(flows, sent)]
+    a = add(late[0], shift(late[1], "c", 1)).reshape(16, 2, 2, -1, width)
+    a = a.transpose(1, 2, 0, 3, 4)
+    late = late_grads(at, 1, resid_grad, second, slope, tokens)
+    a_steps, b_steps = ring_chain("y", True), ring_chain("y", False)
+    a_sent = outgoing(a, a_steps[0])
+    a_sent, *late = tie(a_sent, *late)
+    a = swapped(a, a_sent, a_steps[0])
+    b = add(late[0], shift(late[1], "c", 1)).reshape(16, 2, 2, -1, width)
+    b = b.transpose(1, 2, 0, 3, 4)
+    early = [
+        swapped(x, outgoing(x, steps[1]), steps[1]) for x, (_, steps) in zip(early, flows)
+    ]
+    b = swapped(b, outgoing(b, b_steps[0]), b_steps[0])
+    a = swapped(a, outgoing(a, a_steps[1]), a_steps[1])
+    b = swapped(b, outgoing(b, b_steps[1]), b_steps[1])
+    early = jnp.concatenate(early).reshape(16, -1, width)
     early = lax.all_to_all(early, ("z", "y"), 0, 0, tiled=True)
-    late = late.transpose(0, 2, 3, 1, 4, 5)
-    a, b = ring_sum(late[0], late[1], "y")
     late = lax.all_to_all(jnp.concatenate([a, b], 1), ("x", "z"), 0, 0, tiled=True)
     early = jnp.sum(early.astype(F32), 0)
     late = jnp.sum(late.astype(F32), 0)
-    ride = early[n_second : n_second + 8, out_width]
+    n_second = shard * RING // 128
+    ride = jnp.sum(early[n_second : n_second + 8, out_width:], 1)
     score_total = ride[0] + ride[1] + ride[2]
-    valid_total = jnp.maximum(ride[3] + ride[4] + ride[5], 1.0)
+    valid_total = jnp.maximum(ride[3], 1.0)
     scale = 1.0 / valid_total
     n_first = late.shape[0] // 2
     return (

time: 328 us -> 278 us (0.85)
  waiting for transfers between devices: 110 us -> 67 us
  blocking collectives: 24.7 us -> 55.8 us
  local copies, waits for them, and re-layouts: 37 us -> 18.8 us
  starting transfers between devices: 35.9 us -> 23.3 us
  between operations: 13.4 us -> 8.51 us
  other arithmetic: 23.5 us -> 19.3 us
    ppermute x14 -> x12, waiting for transfers between devices: 51.4 us -> 15.9 us  [shift(): return lax.ppermute(x, axis, [(i, (i + by) % size) for i in range(size)])]
    all_to_all x0 -> x1, blocking collectives: none -> 30.7 us  [per_device(): gathered = lax.all_to_all(pair, ('x', 'z'), 0, 0, tiled=True)]
    all_to_all x1 -> x0, waiting for transfers between devices: 24 us -> none  [per_device(): gathered = lax.all_to_all(pair, ('x', 'z'), 0, 0, tiled=True)]
    ppermute x8, waiting for transfers between devices: 19.8 us -> 43 us  [swapped(): return add(take(x, bit, dim), lax.ppermute(sent, axis, pairs))]
    optimization_barrier x3 -> x0, local copies, waits for them, and re-layouts: 11.7 us -> none  [per_device(): lax.optimization_barrier((pair, hidden, residual, tokens))]
    all_to_all x1, waiting for transfers between devices: 11.5 us -> 2.51 us  [per_device(): early = lax.all_to_all(early, ('z', 'y'), 0, 0, tiled=True)]
    all_to_all x1 -> x0, starting transfers between devices: 7.92 us -> none  [per_device(): gathered = lax.all_to_all(pair, ('x', 'z'), 0, 0, tiled=True)]
    pallas_call x0 -> x2, Pallas kernels: none -> 4.93 us  [packed(): pl.pallas_call(pack_kernel, grid_spec=pltpu.PrefetchScalarGridSpec(num_sc...]
  transfers between devices with their start and end apart: 25 -> 22, of which waited for: 16 -> 11; matrix products, arithmetic and copies ran while one was open for 12% -> 7% of each run, Pallas kernels for 12% -> 18%
where the time goes in v1:
time: 278 us; the launch traced here: 276 us
  Pallas kernels  76.9 us (28%)
  waiting for transfers between devices  67 us (24%)
  blocking collectives  55.8 us (20%)
  starting transfers between devices  23.3 us (8%)
  other arithmetic  19.3 us (7%)
  local copies, waits for them, and re-layouts  18.8 us (7%)
  between operations  8.51 us (3%)
  matrix products  6.87 us (2%)
    ppermute x8, waiting for transfers between devices, swapped(): return add(take(x, bit, dim), lax.ppermute(sent, axis, pairs))  43 us
    pallas_call x4, Pallas kernels, forward_part(): pl.pallas_call(functools.partial(forward_kernel, first_call, last_call, b...  39.7 us
    all_to_all x1, blocking collectives, per_device(): gathered = lax.all_to_all(pair, ('x', 'z'), 0, 0, tiled=True)  30.7 us
    all_to_all x1, blocking collectives, per_device(): lax.all_to_all(grad_raw.reshape(16, 2 * members * own, out_width), ('x',...  25.1 us
    pallas_call x2, Pallas kernels, late_grads(): pl.pallas_call(late_kernel, grid_spec=pltpu.PrefetchScalarGridSpec(num_sc...  20 us
    ppermute x12, waiting for transfers between devices, shift(): return lax.ppermute(x, axis, [(i, (i + by) % size) for i in range(size)])  15.9 us
    pallas_call x1, Pallas kernels, early_grads(): pl.pallas_call(early_kernel, grid_spec=pltpu.PrefetchScalarGridSpec(num_s...  12.2 us
    convert_element_type x11, other arithmetic, add(): return (a.astype(F32) + b.astype(F32)).astype(BF16)  8.29 us
  transfers between devices with their start and end apart: 22, of which 11 were waited for; matrix products, arithmetic and copies ran while one was open for 7% of the time, Pallas kernels for 18%

profile of v1, /device:TPU:0, one launch (start us, length us, event | category | flops | bytes accessed | tf_op | source)
XLA Modules:
  0.0 276.4 jit_solution(246303845200688696)
XLA Ops:
  0.7 2.0 copy.32.head
  2.7 2.5 packed.2.refs_2_
  5.2 1.7 collective-permute-start
  6.8 1.6 collective-permute-start.1
  8.4 3.2 %copy.33 = bf16[4,16,2,8,1024]{4,3,0,1,2:T(8,128)(2,1)} copy(bf16[4,16,2,8,1024]{4,3,2,1,0:T(8,128)(2,1)} %bitcast.115) | data formatting | bytes 4194304 | tf_op jit(solution)/shard_map/reshape | solution.py:380
  11.6 2.4 packed.3.refs_3_
  14.7 9.0 %forward_part.4 = (f32[1024,2048]{1,0:T(8,128)}, bf16[1024,2048]{1,0:T(8,128)(2,1)}, bf16[2048,1024]{1,0:T(8,128)(2,1)}, bf16[768,1024]{1,0:T(8,128)(2,1)}, f32[1024,1024]{1,0:T(8,128)}) custom-call(s32[2]{0:T(128)} %pad_add_fusion.1.refs_0_.place, bf16[1024,1024]{1,0:T(8,128)(2,1)} %bitcast.100, bf16[2432,256]{1,0:T(8,128)(2,1)} %packed.2.refs_2_, ...), custom_call_target="tpu_custom_call" | custom-call | flops 2147483648 | bytes 12582912 | tf_op jit(solution)/shard_map/forward_part/pallas_call | solution.py:141
  23.7 12.2 %collective-permute-done.refs_2_ = bf16[2432,256]{1,0:T(8,128)(2,1)S(1)} collective-permute-done((bf16[2432,256]{1,0:T(8,128)(2,1)}, bf16[2432,256]{1,0:T(8,128)(2,1)S(1)}, u32[]{:S(2)}, u32[]{:S(2)}) %collective-permute-start) | collective-permute-done | bytes 1245216 | tf_op jit(solution)/shard_map/ppermute | solution.py:26
  36.5 1.6 collective-permute-start.2
  38.1 1.7 collective-permute-start.3
  39.8 0.6 pad_add_fusion.3.refs_0_
  41.1 9.8 %forward_part.5 = (f32[1024,2048]{1,0:T(8,128)}, bf16[1024,2048]{1,0:T(8,128)(2,1)}, bf16[2048,1024]{1,0:T(8,128)(2,1)}, bf16[768,1024]{1,0:T(8,128)(2,1)}, f32[1024,1024]{1,0:T(8,128)}) custom-call(s32[2]{0:T(128)} %pad_add_fusion.3.refs_0_, ...), custom_call_target="tpu_custom_call", output_to_operand_aliasing={{0}: (5, {}), {1}: (6, {}), {2}: (7, {}), {3}: (8, {}), {4}... | custom-call | flops 2147483648 | bytes 12582912 | tf_op jit(solution)/shard_map/forward_part/pallas_call | solution.py:141
  50.8 9.8 %forward_part.6 = (f32[1024,2048]{1,0:T(8,128)}, bf16[1024,2048]{1,0:T(8,128)(2,1)}, bf16[2048,1024]{1,0:T(8,128)(2,1)}, bf16[768,1024]{1,0:T(8,128)(2,1)}, f32[1024,1024]{1,0:T(8,128)}) custom-call(s32[2]{0:T(128)} %pad_add_fusion.2.refs_0_, ...), custom_call_target="tpu_custom_call", output_to_operand_aliasing={{0}: (5, {}), {1}: (6, {}), {2}: (7, {}), {3}: (8, {}), {4}... | custom-call | flops 2147483648 | bytes 12582912 | tf_op jit(solution)/shard_map/forward_part/pallas_call | solution.py:141
  60.8 0.8 pad_add_fusion.refs_0_
  61.6 2.2 collective-permute-done.6.refs_3_
  63.8 1.0 copy-done.10
  64.8 11.2 %forward_part.7 = (f32[1024,2048]{1,0:T(8,128)}, bf16[1024,2048]{1,0:T(8,128)(2,1)}, bf16[2048,1024]{1,0:T(8,128)(2,1)}, bf16[768,1024]{1,0:T(8,128)(2,1)}, bf16...) custom-call(s32[2]{0:T(128)} %pad_add_fusion.refs_0_, ...), custom_call_target="tpu_custom_call", output_to_operand_aliasing={{0}: (5, {}), {1}: (6, {}), {2}: (7, {})} | custom-call | flops 2147483648 | bytes 12582912 | tf_op jit(solution)/shard_map/forward_part/pallas_call | solution.py:141
  76.0 1.5 dynamic-slice_bitcast_fusion.3
  78.4 1.5 collective-permute-done.7
  80.0 30.7 %all_to_all.20 = bf16[16,64,768]{2,1,0:T(8,128)(2,1)S(1)} all-to-all(bf16[16,64,768]{2,1,0:T(8,128)(2,1)S(1)} %pad_maximum_fusion), channel_id=1, replica_groups=mesh['x'=4,'z'=4,'c'=2,'y'=4] {'x','z'}, dimensions={0} | all-to-all | bytes 3145728 | tf_op jit(solution)/shard_map/all_to_all | solution.py:405
  110.9 0.7 fusion.6
  112.0 0.9 fusion.34
  112.9 0.6 multiply_reduce_fusion
  113.5 2.8 %fusion.8 = bf16[128,8,768]{2,0,1:T(8,128)(2,1)S(1)} fusion(f32[128,8]{0,1:T(8,128)S(1)} %bitcast.121, f32[128,8]{0,1:T(8,128)S(1)} %copy.37, f32[8,768]{1,0:T(8,128)S(1)} %broadcast_select_fusion, f32[8]{0:T(128)S(1)} %get-tuple-element.142, bf16[128,8,768]{2,1,0:T(8,128)(2,1)S(1)} %bitcast.111, f32[8,128,128]{1,2,0:T(8,128)S(1)} %get-tuple-element.143), kind=kOutput, calls=%fused_computation.14 | convolution fusion | flops 1215168512 | bytes 3702816 | tf_op jit(solution)/shard_map/pmn,npo->mpo/dot_general | solution.py:347
  116.3 0.9 copy.44
  117.2 25.1 %all_to_all.21 = bf16[16,64,768]{2,1,0:T(8,128)(2,1)S(1)} all-to-all(bf16[16,64,768]{2,1,0:T(8,128)(2,1)S(1)} %bitcast.109), channel_id=1, replica_groups=mesh['x'=4,'z'=4,'c'=2,'y'=4] {'x','z'}, dimensions={0} | all-to-all | bytes 3145728 | tf_op jit(solution)/shard_map/all_to_all | solution.py:417
  146.2 0.7 compare_select_fusion.1
  146.8 1.9 select_select_fusion.riders
  149.1 1.6 copy-done.15
  150.7 3.1 %convolution_convert_fusion.resid_grad = bf16[1024,1024]{1,0:T(8,128)(2,1)} fusion(bf16[1024,768]{1,0:T(8,128)(2,1)S(1)} %bitcast.117, bf16[768,1024]{1,0:T(8,128)(2,1)S(1)} %copy-done.15), kind=kOutput, calls=%fused_computation.17 | convolution fusion | flops 1611661312 | bytes 5242880 | tf_op jit(solution)/shard_map/dot_general | solution.py:30
  153.8 12.2 %early_grads.1 = (bf16[4,384,1024]{2,1,0:T(8,128)(2,1)}, bf16[4,384,1024]{2,1,0:T(8,128)(2,1)}) custom-call(s32[2]{0:T(128)} %pad_add_fusion.1.refs_0_.place, bf16[1024,2048]{1,0:T(8,128)(2,1)} %get-tuple-element.97.hidden, bf16[1024,1024]{1,0:T(8,128)(2,1)} %convolution_convert_fusion.resid_grad, bf16[1024,1024]{1,0:T(8,128)(2,1)} %get-tuple-element.98.residual, ...), custom_call_target="tpu_custom_call" | custom-call | flops 5905580032 | bytes 18874368 | tf_op jit(solution)/shard_map/early_grads/pallas_call | solution.py:195
  166.5 10.1 %late_grads.2 = (bf16[1,512,1024]{2,1,0:T(8,128)(2,1)}, bf16[1,512,1024]{2,1,0:T(8,128)(2,1)}) custom-call(s32[2]{0:T(128)} %pad_add_fusion.1.refs_0_.place, bf16[1024,1024]{1,0:T(8,128)(2,1)} %convolution_convert_fusion.resid_grad, bf16[2048,1024]{1,0:T(8,128)(2,1)} %get-tuple-element.104.second, f32[1024,2048]{1,0:T(8,128)} %get-tuple-element.105.slope, ...), custom_call_target="tpu_custom_call" | custom-call | flops 4294967296 | bytes 12582912 | tf_op jit(solution)/shard_map/late_grads/pallas_call | solution.py:233
  176.6 1.6 add_convert_fusion
  178.5 1.0 dynamic-slice_bitcast_fusion
  179.5 0.9 dynamic-slice_bitcast_fusion.1
  180.5 1.6 collective-permute-start.18
  182.1 9.9 %late_grads.3 = (bf16[1,512,1024]{2,1,0:T(8,128)(2,1)}, bf16[1,512,1024]{2,1,0:T(8,128)(2,1)}) custom-call(s32[2]{0:T(128)} %pad_add_fusion.1.refs_0_.place, bf16[1024,1024]{1,0:T(8,128)(2,1)} %convolution_convert_fusion.resid_grad, bf16[2048,1024]{1,0:T(8,128)(2,1)} %get-tuple-element.104.second, f32[1024,2048]{1,0:T(8,128)} %get-tuple-element.105.slope, ...), custom_call_target="tpu_custom_call" | custom-call | flops 4294967296 | bytes 12582912 | tf_op jit(solution)/shard_map/late_grads/pallas_call | solution.py:233
  191.9 8.3 %collective-permute-done.16 = bf16[2,192,1024]{2,1,0:T(8,128)(2,1)} collective-permute-done((bf16[2,192,1024]{2,1,0:T(8,128)(2,1)}, bf16[2,192,1024]{2,1,0:T(8,128)(2,1)}, u32[]{:S(2)}, u32[]{:S(2)}) %collective-permute-start.16) | collective-permute-done | bytes 786464 | tf_op jit(solution)/shard_map/ppermute | solution.py:285
  200.3 1.4 fusion.10
  201.7 0.9 dynamic-slice_bitcast_fusion.6
  202.6 1.1 collective-permute-start.17
  203.7 1.6 add_convert_fusion.2
  205.3 0.9 constant_dynamic-slice_fusion.1
  206.3 0.8 copy.75
  207.4 0.8 dynamic-slice_bitcast_fusion.5
  208.5 5.8 %collective-permute-done.17 = bf16[192,1024]{1,0:T(8,128)(2,1)} collective-permute-done((bf16[192,1024]{1,0:T(8,128)(2,1)}, bf16[192,1024]{1,0:T(8,128)(2,1)}, u32[]{:S(2)}, u32[]{:S(2)}) %collective-permute-start.17) | collective-permute-done | bytes 393248 | tf_op jit(solution)/shard_map/ppermute | solution.py:285
  214.3 1.1 fusion.29
  215.5 4.5 %collective-permute-done.19 = bf16[192,1024]{1,0:T(8,128)(2,1)S(1)} collective-permute-done((bf16[192,1024]{1,0:T(8,128)(2,1)}, bf16[192,1024]{1,0:T(8,128)(2,1)S(1)}, u32[]{:S(2)}, u32[]{:S(2)}) %collective-permute-start.19) | collective-permute-done | bytes 393248 | tf_op jit(solution)/shard_map/ppermute | solution.py:285
  220.1 2.7 collective-permute-done.11
  223.0 1.5 add_convert_fusion.1
  224.5 0.9 dynamic-slice_bitcast_fusion.4
  225.4 1.6 collective-permute-start.14
  227.0 1.8 collective-permute-start.12
  228.7 0.9 pad_maximum_fusion.1
  229.7 3.6 %all-to-all-start.3 = ((bf16[16,24,1024]{2,1,0:T(8,128)(2,1)}), bf16[16,24,1024]{2,1,0:T(8,128)(2,1)S(1)}, u32[]{:S(2)}, u32[]{:S(2)}) async-start(bf16[16,24,1024]{2,1,0:T(8,128)(2,1)} %bitcast.46), calls=%async_computation.3 | async-start | bytes 1572864 | tf_op jit(solution)/shard_map/all_to_all | solution.py:455
  233.3 18.2 %collective-permute-done.12 = bf16[16,8,1024]{2,1,0:T(8,128)(2,1)S(1)} collective-permute-done((bf16[16,8,1024]{2,1,0:T(8,128)(2,1)S(1)}, bf16[16,8,1024]{2,1,0:T(8,128)(2,1)S(1)}, u32[]{:S(2)}, u32[]{:S(2)}) %collective-permute-start.12) | collective-permute-done | bytes 262176 | tf_op jit(solution)/shard_map/ppermute | solution.py:285
  251.9 2.5 all-to-all-done.3
  254.7 3.6 %collective-permute-done.15 = bf16[16,8,1024]{2,1,0:T(8,128)(2,1)S(1)} collective-permute-done((bf16[16,8,1024]{2,1,0:T(8,128)(2,1)S(1)}, bf16[16,8,1024]{2,1,0:T(8,128)(2,1)S(1)}, u32[]{:S(2)}, u32[]{:S(2)}) %collective-permute-start.15) | collective-permute-done | bytes 262176 | tf_op jit(solution)/shard_map/ppermute | solution.py:285
  258.3 0.9 pad_maximum_fusion.2
  259.2 5.3 %all-to-all-start.2 = ((bf16[16,16,1024]{2,1,0:T(8,128)(2,1)}), bf16[16,16,1024]{2,1,0:T(8,128)(2,1)S(1)}, u32[]{:S(2)}, u32[]{:S(2)}) async-start(bf16[16,16,1024]{2,1,0:T(8,128)(2,1)} %pad_maximum_fusion.2), calls=%async_computation.2 | async-start | bytes 1048576 | tf_op jit(solution)/shard_map/all_to_all | solution.py:456
  267.7 0.6 slice_multiply_fusion.1
  268.4 0.6 slice_multiply_fusion
  269.0 5.6 %all-to-all-done.2 = bf16[16,16,1024]{2,1,0:T(8,128)(2,1)S(1)} async-done(((bf16[16,16,1024]{2,1,0:T(8,128)(2,1)}), bf16[16,16,1024]{2,1,0:T(8,128)(2,1)S(1)}, u32[]{:S(2)}, u32[]{:S(2)}) %all-to-all-start.2) | async-done | bytes 524320 | tf_op jit(solution)/shard_map/all_to_all | solution.py:456
  274.7 0.6 maximum_multiply_fusion
  (90 shorter events, 7.2 us)
Async XLA Ops:
  0.6 77.1 %copy-start = (f32[8,768]{1,0:T(8,128)S(1)}, f32[8,768]{1,0:T(8,128)}, u32[]{:S(2)}) copy-start(f32[8,768]{1,0:T(8,128)} %param.11) | copy-start | bytes 73732
  5.2 30.7 %collective-permute-start = (bf16[2432,256]{1,0:T(8,128)(2,1)}, bf16[2432,256]{1,0:T(8,128)(2,1)S(1)}, u32[]{:S(2)}, u32[]{:S(2)}) collective-permute-start(bf16[2432,256]{1,0:T(8,128)(2,1)} %packed.2.refs_2_), channel_id=1, source_target_pairs={{0,1},{1,2},{2,3},{3,0},{4,5},{5,6},{6,7},{7,4},{8,9},{9,10},{10,1... | collective-permute-start | bytes 3735560 | tf_op jit(solution)/shard_map/ppermute | solution.py:26
  6.8 29.0 %collective-permute-start.1 = (bf16[2432,256]{1,0:T(8,128)(2,1)}, bf16[2432,256]{1,0:T(8,128)(2,1)S(1)}, u32[]{:S(2)}, u32[]{:S(2)}) collective-permute-start(bf16[2432,256]{1,0:T(8,128)(2,1)} %packed.2.refs_2_), channel_id=1, source_target_pairs={{0,3},{1,0},{2,1},{3,2},{4,7},{5,4},{6,5},{7,6},{8,11},{9,8},{10,9... | collective-permute-start | bytes 3735560 | tf_op jit(solution)/shard_map/ppermute | solution.py:26
  35.8 5.2 %copy-start.6 = (bf16[2432,256]{1,0:T(8,128)(2,1)}, bf16[2432,256]{1,0:T(8,128)(2,1)S(1)}, u32[]{:S(2)}) copy-start(bf16[2432,256]{1,0:T(8,128)(2,1)S(1)} %collective-permute-done.refs_2_) | copy-start | bytes 3735556
  35.9 15.0 %copy-start.5 = (bf16[2432,256]{1,0:T(8,128)(2,1)}, bf16[2432,256]{1,0:T(8,128)(2,1)S(1)}, u32[]{:S(2)}) copy-start(bf16[2432,256]{1,0:T(8,128)(2,1)S(1)} %collective-permute-done.1.refs_2_) | copy-start | bytes 3735556
  35.9 5.2 %collective-permute-start.5 = (bf16[2432,256]{1,0:T(8,128)(2,1)S(1)}, bf16[2432,256]{1,0:T(8,128)(2,1)}, u32[]{:S(2)}, u32[]{:S(2)}) collective-permute-start(bf16[2432,256]{1,0:T(8,128)(2,1)S(1)} %collective-permute-done.refs_2_), channel_id=1, source_target_pairs={{0,4},{4,0},{1,5},{5,1},{2,6},{6,2},{3,7},{7,3},{8,12},{12,8},{9,1... | collective-permute-start | bytes 3735560 | tf_op jit(solution)/shard_map/ppermute | solution.py:26
  35.9 14.9 %collective-permute-start.4 = (bf16[2432,256]{1,0:T(8,128)(2,1)S(1)}, bf16[2432,256]{1,0:T(8,128)(2,1)}, u32[]{:S(2)}, u32[]{:S(2)}) collective-permute-start(bf16[2432,256]{1,0:T(8,128)(2,1)S(1)} %collective-permute-done.1.refs_2_), channel_id=1, source_target_pairs={{0,4},{4,0},{1,5},{5,1},{2,6},{6,2},{3,7},{7,3},{8,12},{12,8},{9,1... | collective-permute-start | bytes 3735560 | tf_op jit(solution)/shard_map/ppermute | solution.py:26
  36.5 24.1 %collective-permute-start.2 = (bf16[1216,256]{1,0:T(8,128)(2,1)S(1)}, bf16[1216,256]{1,0:T(8,128)(2,1)S(1)}, u32[]{:S(2)}, u32[]{:S(2)}) collective-permute-start(bf16[1216,256]{1,0:T(8,128)(2,1)S(1)} %slice.46), channel_id=1, source_target_pairs={{0,1},{1,2},{2,3},{3,0},{4,5},{5,6},{6,7},{7,4},{8,9},{9,10},{10,1... | collective-permute-start | bytes 1867784 | tf_op jit(solution)/shard_map/ppermute | solution.py:26
  38.1 22.5 %collective-permute-start.3 = (bf16[1216,256]{1,0:T(8,128)(2,1)S(1)}, bf16[1216,256]{1,0:T(8,128)(2,1)S(1)}, u32[]{:S(2)}, u32[]{:S(2)}) collective-permute-start(bf16[1216,256]{1,0:T(8,128)(2,1)S(1)} %slice.47), channel_id=1, source_target_pairs={{0,3},{1,0},{2,1},{3,2},{4,7},{5,4},{6,5},{7,6},{8,11},{9,8},{10,9... | collective-permute-start | bytes 1867784 | tf_op jit(solution)/shard_map/ppermute | solution.py:26
  60.7 3.0 %copy-start.7 = (bf16[2432,256]{1,0:T(8,128)(2,1)}, bf16[2432,256]{1,0:T(8,128)(2,1)S(1)}, u32[]{:S(2)}) copy-start(bf16[2432,256]{1,0:T(8,128)(2,1)S(1)} %constant_dynamic-update-slice_fusion.refs_2_) | copy-start | bytes 3735556
  60.7 3.0 %collective-permute-start.6 = (bf16[2432,256]{1,0:T(8,128)(2,1)S(1)}, bf16[2432,256]{1,0:T(8,128)(2,1)S(1)}, u32[]{:S(2)}, u32[]{:S(2)}) collective-permute-start(bf16[2432,256]{1,0:T(8,128)(2,1)S(1)} %constant_dynamic-update-slice_fusion.refs_2_), channel_id=1, source_target_pairs={{0,4},{4,0},{1,5},{5,1},{2,6},{6,2},{3,7},{7,3},{8,12},{12,8},{9,1... | collective-permute-start | bytes 3735560 | tf_op jit(solution)/shard_map/ppermute | solution.py:26
  63.8 1.0 copy-start.10
  76.0 1.7 copy-start.13
  77.5 2.4 collective-permute-start.7
  112.0 0.9 copy-start.14
  142.5 6.3 %collective-permute-start.8 = (bf16[16,32,768]{2,1,0:T(8,128)(2,1)S(1)}, bf16[16,32,768]{2,1,0:T(8,128)(2,1)S(1)}, u32[]{:S(2)}, u32[]{:S(2)}) collective-permute-start(bf16[16,32,768]{2,1,0:T(8,128)(2,1)S(1)} %get-tuple-element.129), channel_id=1, source_target_pairs={{0,4},{4,0},{1,5},{5,1},{2,6},{6,2},{3,7},{7,3},{8,12},{12,8},{9,1... | collective-permute-start | bytes 2359304 | tf_op jit(solution)/shard_map/ppermute | solution.py:26
  148.8 1.9 copy-start.15
  149.0 4.8 %copy-start.9 = (bf16[2,16,32,768]{3,2,1,0:T(8,128)(2,1)}, bf16[2,16,32,768]{3,2,1,0:T(8,128)(2,1)S(1)}, u32[]{:S(2)}) copy-start(bf16[2,16,32,768]{3,2,1,0:T(8,128)(2,1)S(1)} %maximum_select_fusion) | copy-start | bytes 4718596
  166.0 10.6 %collective-permute-start.9 = (bf16[4,384,1024]{2,1,0:T(8,128)(2,1)}, bf16[4,384,1024]{2,1,0:T(8,128)(2,1)S(1)}, u32[]{:S(2)}, u32[]{:S(2)}) collective-permute-start(bf16[4,384,1024]{2,1,0:T(8,128)(2,1)} %get-tuple-element.103), channel_id=1, source_target_pairs={{0,4},{4,0},{1,5},{5,1},{2,6},{6,2},{3,7},{7,3},{8,12},{12,8},{9,1... | collective-permute-start | bytes 9437192 | tf_op jit(solution)/shard_map/ppermute | solution.py:26
  166.5 10.1 %copy-start.4 = (bf16[4,384,1024]{2,1,0:T(8,128)(2,1)S(1)}, bf16[4,384,1024]{2,1,0:T(8,128)(2,1)}, u32[]{:S(2)}) copy-start(bf16[4,384,1024]{2,1,0:T(8,128)(2,1)} %get-tuple-element.102) | copy-start | bytes 9437188
  180.4 19.8 %collective-permute-start.16 = (bf16[2,192,1024]{2,1,0:T(8,128)(2,1)}, bf16[2,192,1024]{2,1,0:T(8,128)(2,1)}, u32[]{:S(2)}, u32[]{:S(2)}) collective-permute-start(bf16[2,192,1024]{2,1,0:T(8,128)(2,1)} %dynamic-slice_bitcast_fusion.1), channel_id=1, source_target_pairs={{0,32},{32,0},{64,96},{96,64},{1,33},{33,1},{65,97},{97,65},{2,34}... | collective-permute-start | bytes 2359304 | tf_op jit(solution)/shard_map/ppermute | solution.py:285
  180.4 23.2 %collective-permute-start.10 = (bf16[1,512,1024]{2,1,0:T(8,128)(2,1)}, bf16[1,512,1024]{2,1,0:T(8,128)(2,1)}, u32[]{:S(2)}, u32[]{:S(2)}) collective-permute-start(bf16[1,512,1024]{2,1,0:T(8,128)(2,1)} %get-tuple-element.109), channel_id=1, source_target_pairs={{0,4},{4,0},{1,5},{5,1},{2,6},{6,2},{3,7},{7,3},{8,12},{12,8},{9,1... | collective-permute-start | bytes 3145736 | tf_op jit(solution)/shard_map/ppermute | solution.py:26
  180.5 26.6 %collective-permute-start.18 = (bf16[2,192,1024]{2,1,0:T(8,128)(2,1)}, bf16[2,192,1024]{2,1,0:T(8,128)(2,1)S(1)}, u32[]{:S(2)}, u32[]{:S(2)}) collective-permute-start(bf16[2,192,1024]{2,1,0:T(8,128)(2,1)} %dynamic-slice_bitcast_fusion), channel_id=1, source_target_pairs={{0,96},{96,0},{32,64},{64,32},{1,97},{97,1},{33,65},{65,33},{2,98}... | collective-permute-start | bytes 2359304 | tf_op jit(solution)/shard_map/ppermute | solution.py:285
  191.9 11.7 %copy-start.11 = (bf16[1,512,1024]{2,1,0:T(8,128)(2,1)S(1)}, bf16[1,512,1024]{2,1,0:T(8,128)(2,1)}, u32[]{:S(2)}) copy-start(bf16[1,512,1024]{2,1,0:T(8,128)(2,1)} %get-tuple-element.108) | copy-start | bytes 3145732
  201.7 2.0 copy-start.2
  202.6 11.7 %collective-permute-start.17 = (bf16[192,1024]{1,0:T(8,128)(2,1)}, bf16[192,1024]{1,0:T(8,128)(2,1)}, u32[]{:S(2)}, u32[]{:S(2)}) collective-permute-start(bf16[192,1024]{1,0:T(8,128)(2,1)} %dynamic-slice_bitcast_fusion.6), channel_id=1, source_target_pairs={{0,96},{96,0},{32,64},{64,32},{1,97},{97,1},{33,65},{65,33},{2,98}... | collective-permute-start | bytes 1179656 | tf_op jit(solution)/shard_map/ppermute | solution.py:285
  207.1 7.2 %copy-start.3 = (bf16[2,192,1024]{2,1,0:T(8,128)(2,1)S(1)}, bf16[2,192,1024]{2,1,0:T(8,128)(2,1)}, u32[]{:S(2)}) copy-start(bf16[2,192,1024]{2,1,0:T(8,128)(2,1)} %copy-done.2) | copy-start | bytes 2359300
  207.1 15.9 %collective-permute-start.13 = (bf16[1,512,1024]{2,1,0:T(8,128)(2,1)}, bf16[1,512,1024]{2,1,0:T(8,128)(2,1)}, u32[]{:S(2)}, u32[]{:S(2)}) collective-permute-start(bf16[1,512,1024]{2,1,0:T(8,128)(2,1)} %get-tuple-element.115), channel_id=1, source_target_pairs={{0,4},{4,0},{1,5},{5,1},{2,6},{6,2},{3,7},{7,3},{8,12},{12,8},{9,1... | collective-permute-start | bytes 3145736 | tf_op jit(solution)/shard_map/ppermute | solution.py:26
  207.4 15.3 %copy-start.8 = (bf16[16,1,2,8,1024]{4,3,2,1,0:T(8,128)(2,1)S(1)}, bf16[16,1,2,8,1024]{4,3,2,1,0:T(8,128)(2,1)}, u32[]{:S(2)}) copy-start(bf16[16,1,2,8,1024]{4,3,2,1,0:T(8,128)(2,1)} %get-tuple-element.132) | copy-start | bytes 1572868
  208.2 11.7 %collective-permute-start.19 = (bf16[192,1024]{1,0:T(8,128)(2,1)}, bf16[192,1024]{1,0:T(8,128)(2,1)S(1)}, u32[]{:S(2)}, u32[]{:S(2)}) collective-permute-start(bf16[192,1024]{1,0:T(8,128)(2,1)} %dynamic-slice_bitcast_fusion.5), channel_id=1, source_target_pairs={{0,32},{32,0},{64,96},{96,64},{1,33},{33,1},{65,97},{97,65},{2,34}... | collective-permute-start | bytes 1179656 | tf_op jit(solution)/shard_map/ppermute | solution.py:285
  208.2 14.5 %collective-permute-start.11 = (bf16[2,16,8,1024]{3,2,1,0:T(8,128)(2,1)}, bf16[2,16,8,1024]{3,2,1,0:T(8,128)(2,1)S(1)}, u32[]{:S(2)}, u32[]{:S(2)}) collective-permute-start(bf16[2,16,8,1024]{3,2,1,0:T(8,128)(2,1)} %bitcast.98), channel_id=1, source_target_pairs={{0,1},{1,0},{2,3},{3,2},{4,5},{5,4},{6,7},{7,6},{8,9},{9,8},{10,11... | collective-permute-start | bytes 1572872 | tf_op jit(solution)/shard_map/ppermute | solution.py:285
  215.5 7.5 %copy-start.12 = (bf16[1,512,1024]{2,1,0:T(8,128)(2,1)S(1)}, bf16[1,512,1024]{2,1,0:T(8,128)(2,1)}, u32[]{:S(2)}) copy-start(bf16[1,512,1024]{2,1,0:T(8,128)(2,1)} %get-tuple-element.114) | copy-start | bytes 3145732
  225.4 26.2 %collective-permute-start.14 = (bf16[2,16,8,1024]{3,2,0,1:T(8,128)(2,1)}, bf16[2,16,8,1024]{3,2,0,1:T(8,128)(2,1)S(1)}, u32[]{:S(2)}, u32[]{:S(2)}) collective-permute-start(bf16[2,16,8,1024]{3,2,0,1:T(8,128)(2,1)} %dynamic-slice_bitcast_fusion.4), channel_id=1, source_target_pairs={{0,3},{3,0},{1,2},{2,1},{4,7},{7,4},{5,6},{6,5},{8,11},{11,8},{9,1... | collective-permute-start | bytes 1572872 | tf_op jit(solution)/shard_map/ppermute | solution.py:285
  227.0 24.5 %collective-permute-start.12 = (bf16[16,8,1024]{2,1,0:T(8,128)(2,1)S(1)}, bf16[16,8,1024]{2,1,0:T(8,128)(2,1)S(1)}, u32[]{:S(2)}, u32[]{:S(2)}) collective-permute-start(bf16[16,8,1024]{2,1,0:T(8,128)(2,1)S(1)} %dynamic-slice_bitcast_fusion.8), channel_id=1, source_target_pairs={{0,3},{3,0},{1,2},{2,1},{4,7},{7,4},{5,6},{6,5},{8,11},{11,8},{9,1... | collective-permute-start | bytes 786440 | tf_op jit(solution)/shard_map/ppermute | solution.py:285
  229.7 24.7 %all-to-all-start.3 = ((bf16[16,24,1024]{2,1,0:T(8,128)(2,1)}), bf16[16,24,1024]{2,1,0:T(8,128)(2,1)S(1)}, u32[]{:S(2)}, u32[]{:S(2)}) async-start(bf16[16,24,1024]{2,1,0:T(8,128)(2,1)} %bitcast.46), calls=%async_computation.3 | async-start | bytes 1572864 | tf_op jit(solution)/shard_map/all_to_all | solution.py:455
  251.8 6.5 %collective-permute-start.15 = (bf16[16,8,1024]{2,1,0:T(8,128)(2,1)S(1)}, bf16[16,8,1024]{2,1,0:T(8,128)(2,1)S(1)}, u32[]{:S(2)}, u32[]{:S(2)}) collective-permute-start(bf16[16,8,1024]{2,1,0:T(8,128)(2,1)S(1)} %dynamic-slice_bitcast_fusion.7), channel_id=1, source_target_pairs={{0,1},{1,0},{2,3},{3,2},{4,5},{5,4},{6,7},{7,6},{8,9},{9,8},{10,11... | collective-permute-start | bytes 786440 | tf_op jit(solution)/shard_map/ppermute | solution.py:285
  258.3 17.0 %copy-start.1 = (f32[8,768]{1,0:T(8,128)S(1)}, f32[8,768]{1,0:T(8,128)}, u32[]{:S(2)}) copy-start(f32[8,768]{1,0:T(8,128)} %param.11) | copy-start | bytes 73732
  259.2 15.4 %all-to-all-start.2 = ((bf16[16,16,1024]{2,1,0:T(8,128)(2,1)}), bf16[16,16,1024]{2,1,0:T(8,128)(2,1)S(1)}, u32[]{:S(2)}, u32[]{:S(2)}) async-start(bf16[16,16,1024]{2,1,0:T(8,128)(2,1)} %pad_maximum_fusion.2), calls=%async_computation.2 | async-start | bytes 1048576 | tf_op jit(solution)/shard_map/all_to_all | solution.py:456

commit v2 on v1

--- a/solution.py
+++ b/solution.py
@@ -174,19 +174,32 @@
         send[0] = zero
 
 
-def early_kernel(place, hidden, resid_grad, residual, grad_rows, riders, keep, send):
+def riders(place, scalars, shape):
+    line = lax.broadcasted_iota(jnp.int32, shape, 0)
+    lane = lax.broadcasted_iota(jnp.int32, shape, 1)
+    score = jnp.full(shape, scalars[0], F32)
+    out = jnp.where(line == 3, scalars[1], 0.0)
+    for i in range(3):
+        term = score.astype(BF16).astype(F32)
+        out = jnp.where(line == i, term, out)
+        score = score - term
+    return jnp.where(lane == 2 * place[2] + place[1], out, 0.0)
+
+
+def early_kernel(place, hidden, resid_grad, residual, grad_rows, scalars, keep, send):
     second = dot(hidden[...], resid_grad[...], ((0,), (0,)))
     head = dot(residual[...], grad_rows[...], ((0,), (0,)))
     width, out_width = second.shape[1], head.shape[1]
     second = second.reshape(RING, 2, RING, -1, width)
     head = head.reshape(RING, 2, RING, -1, out_width)
-    blank = jnp.broadcast_to(riders[...], (*head.shape[:4], width - out_width))
+    blank = riders(place, scalars, (head.shape[3], width - out_width))
+    blank = jnp.broadcast_to(blank, (*head.shape[:3], *blank.shape))
     both = jnp.concatenate([second, jnp.concatenate([head, blank], 4)], 3)
     both = both.reshape(RING, 2, -1, width)
     store_halves(place[1], both, keep, send)
 
 
-def early_grads(place, hidden, resid_grad, residual, grad_rows, riders):
+def early_grads(place, hidden, resid_grad, residual, grad_rows, scalars):
     rows, hid = hidden.shape
     width, out_width = residual.shape[1], grad_rows.shape[1]
     lines = (hid + width) // RING // 2
@@ -202,7 +215,7 @@
                 pl.BlockSpec((rows, width), lambda i, s: (0, 0)),
                 pl.BlockSpec((rows, width // RING), lambda i, s: (0, i)),
                 pl.BlockSpec((rows, out_width), lambda i, s: (0, 0)),
-                pl.BlockSpec(riders.shape, lambda i, s: (0, 0)),
+                pl.BlockSpec(memory_space=pltpu.SMEM),
             ],
             out_specs=[out, out],
         ),
@@ -212,7 +225,7 @@
             flops=2 * rows * width * (hid + out_width), bytes_accessed=18 * MIB, transcendentals=0
         ),
         name="early_grads",
-    )(place, hidden, resid_grad, residual, grad_rows, riders)
+    )(place, hidden, resid_grad, residual, grad_rows, scalars)
 
 
 def late_kernel(place, resid_grad, second, slope, tokens, keep, send):
@@ -280,24 +293,25 @@
     return take(x, 1 - bit, dim)
 
 
-def swapped(x, sent, step):
-    pairs, axis, bit, dim = step
-    return add(take(x, bit, dim), lax.ppermute(sent, axis, pairs))
+def sent_along(x, step):
+    return lax.ppermute(x, step[1], step[0])
+
+
+def kept_plus(x, arrived, step):
+    _, _, bit, dim = step
+    return add(take(x, bit, dim), arrived)
+
+
+def by_ring(x):
+    return x.reshape(16, 2, 2, -1, x.shape[-1]).transpose(1, 2, 0, 3, 4)
 
 
 def tie(*arrays):
     return lax.optimization_barrier(arrays)
 
 
-def terms(value):
-    first = lax.reduce_precision(value, 8, 7)
-    second = lax.reduce_precision(value - first, 8, 7)
-    third = value - first - second
-    return first, second, third
-
-
-def pick(flag, one, zero):
-    return jnp.where(flag == 1, one, zero)
+def after(x, *others):
+    return lax.optimization_barrier((x, *others))[0]
 
 
 def pack_kernel(side, first, second, head, out):
@@ -377,16 +391,17 @@
     lines = mine.shape[0] // 2
     latents, other_side, mine = tie(latents, 1 - side, mine)
     tokens = (
-        latents.reshape(members, 16, 2, own, width).transpose(2, 1, 0, 3, 4).reshape(rows, width)
+        latents.reshape(members, 32, own, width).transpose(1, 0, 2, 3).reshape(rows, width)
     )
     theirs = packed(other_side, w_first, w_second, readout_matrix)
-    place = lambda off: jnp.stack([(here + off) % RING, core]).astype(jnp.int32)
+    place = lambda off: jnp.stack([(here + off) % RING, core, lax.axis_index("x")]).astype(jnp.int32)
     run = functools.partial(forward_part, out_width=out_width)
     carried = run(place(0), tokens, mine, theirs, carried=None, last_call=False)
     right, left, *carried = tie(right, left, *carried)
-    far = [shift(right[:lines], "y", 1), shift(left[lines:], "y", -1)]
-    right_other = shift(right, "c", 1)
-    left_other = shift(left, "c", 1)
+    far = [right[:lines], left[lines:]]
+    right_other = shift(after(right, *far), "c", 1)
+    left_other = shift(after(left, *far), "c", 1)
+    far = [shift(far[0], "y", 1), shift(far[1], "y", -1)]
     carried = run(place(3), tokens, right, right_other, carried=carried, last_call=False)
     carried = run(place(1), tokens, left, left_other, carried=carried, last_call=False)
     near, past, *carried = tie(*far, *carried)
@@ -396,62 +411,55 @@
         place(2), tokens, far, far_other, carried=carried, last_call=True
     )
 
-    forecast = forecast.reshape(2, 16, members * own, out_width)
-    theirs = shift(take(forecast, 1 - core, 0), "c", 1)
-    pair = jnp.concatenate([take(forecast, core, 0), theirs], 1)
+    group = ("x", "z", "c")
     device = ((here * 4 + lax.axis_index("x")) * 4 + lax.axis_index("z")) * 2 + core
     target = jnp.take(observed, obs_index - device * own, axis=0)
-    pair, target = tie(pair, target)
-    gathered = lax.all_to_all(pair, ("x", "z"), 0, 0, tiled=True)
-    samples = gathered.reshape(16 * 2 * members, own, out_width)
+    forecast, target = tie(forecast.reshape(32, members * own, out_width), target)
+    gathered = lax.all_to_all(forecast, group, 0, 0, tiled=True)
+    samples = gathered.reshape(32 * members, own, out_width)
     grad_raw, score_part, count_part = score(samples, target, valid_mask)
-
-    shape = (8, width - out_width)
-    line = lax.broadcasted_iota(jnp.int32, shape, 0)
-    lane = lax.broadcasted_iota(jnp.int32, shape, 1)
-    riders = jnp.where(line == 3, count_part, 0.0)
-    for i, value in enumerate(terms(score_part)):
-        riders = jnp.where(line == i, value, riders)
-    riders = jnp.where(lane == 2 * lax.axis_index("x") + core, riders, 0.0)
-
-    returned = lax.all_to_all(
-        grad_raw.reshape(16, 2 * members * own, out_width), ("x", "z"), 0, 0, tiled=True
-    ).reshape(16, 2, members * own, out_width)
-    back = shift(returned[:, 1], "c", 1)
-    grad_rows = jnp.where(
-        core == 0, jnp.stack([returned[:, 0], back]), jnp.stack([back, returned[:, 0]])
+    grad_rows = lax.all_to_all(
+        grad_raw.reshape(32, members * own, out_width), group, 0, 0, tiled=True
     ).reshape(rows, out_width)
 
     at = place(0)
+    scalars = jnp.stack([score_part, count_part])
     resid_grad = dot(grad_rows, head).astype(BF16)
-    early = early_grads(at, hidden, resid_grad, residual, grad_rows, riders)
-    resid_grad, *early = tie(resid_grad, *early)
-    early = add(early[0], shift(early[1], "c", 1)).reshape(2, 2, 2, -1, width)
-    flows = [
-        (early[:, :, 0], ring_chain("x", True)),
-        (early[:, :, 1], ring_chain("x", False)),
+    early = early_grads(at, hidden, resid_grad, residual, grad_rows, scalars)
+    early_in = shift(early[1], "c", 1)
+    late = late_grads(at, 0, after(resid_grad, early[1]), second, slope, tokens)
+    a_in = shift(late[1], "c", 1)
+    x_steps = [ring_chain("x", True), ring_chain("x", False)]
+    y_steps = [ring_chain("y", True), ring_chain("y", False)]
+    early = add(after(early[0], late[1]), early_in).reshape(2, 2, 2, -1, width)
+    early = [early[:, :, 0], early[:, :, 1]]
+    early_sent = [outgoing(x, steps[0]) for x, steps in zip(early, x_steps)]
+    early_in = [sent_along(x, steps[0]) for x, steps in zip(early_sent, x_steps)]
+    a = by_ring(add(after(late[0], *early_sent), a_in))
+    a_sent = outgoing(a, y_steps[0][0])
+    a_in = sent_along(a_sent, y_steps[0][0])
+    late = late_grads(at, 1, after(resid_grad, a_sent), second, slope, tokens)
+    b_in = shift(after(late[1], a_in, *early_in), "c", 1)
+    a = kept_plus(a, a_in, y_steps[0][0])
+    a_sent = outgoing(a, y_steps[0][1])
+    a_in = sent_along(a_sent, y_steps[0][1])
+    b = by_ring(add(after(late[0], a_sent), b_in))
+    b_sent = outgoing(b, y_steps[1][0])
+    b_in = sent_along(b_sent, y_steps[1][0])
+    early = [
+        kept_plus(x, after(v, b_sent), steps[0]) for x, v, steps in zip(early, early_in, x_steps)
     ]
-    late = late_grads(at, 0, resid_grad, second, slope, tokens)
-    sent = [outgoing(x, steps[0]) for x, steps in flows]
-    resid_grad, *rest = tie(resid_grad, *sent, *late)
-    sent, late = rest[:2], rest[2:]
-    early = [swapped(x, s, steps[0]) for (x, steps), s in zip(flows, sent)]
-    a = add(late[0], shift(late[1], "c", 1)).reshape(16, 2, 2, -1, width)
-    a = a.transpose(1, 2, 0, 3, 4)
-    late = late_grads(at, 1, resid_grad, second, slope, tokens)
-    a_steps, b_steps = ring_chain("y", True), ring_chain("y", False)
-    a_sent = outgoing(a, a_steps[0])
-    a_sent, *late = tie(a_sent, *late)
-    a = swapped(a, a_sent, a_steps[0])
-    b = add(late[0], shift(late[1], "c", 1)).reshape(16, 2, 2, -1, width)
-    b = b.transpose(1, 2, 0, 3, 4)
+    early_sent = [outgoing(x, steps[1]) for x, steps in zip(early, x_steps)]
+    early_in = [sent_along(x, steps[1]) for x, steps in zip(early_sent, x_steps)]
+    b = kept_plus(b, after(b_in, *early_sent), y_steps[1][0])
+    b_sent = outgoing(b, y_steps[1][1])
+    b_in = sent_along(b_sent, y_steps[1][1])
     early = [
-        swapped(x, outgoing(x, steps[1]), steps[1]) for x, (_, steps) in zip(early, flows)
+        kept_plus(x, after(v, b_sent), steps[1]) for x, v, steps in zip(early, early_in, x_steps)
     ]
-    b = swapped(b, outgoing(b, b_steps[0]), b_steps[0])
-    a = swapped(a, outgoing(a, a_steps[1]), a_steps[1])
-    b = swapped(b, outgoing(b, b_steps[1]), b_steps[1])
     early = jnp.concatenate(early).reshape(16, -1, width)
+    a = kept_plus(a, after(a_in, early), y_steps[0][1])
+    b = kept_plus(b, b_in, y_steps[1][1])
     early = lax.all_to_all(early, ("z", "y"), 0, 0, tiled=True)
     late = lax.all_to_all(jnp.concatenate([a, b], 1), ("x", "z"), 0, 0, tiled=True)
     early = jnp.sum(early.astype(F32), 0)

time: 278 us -> 256 us (0.921)
  blocking collectives: 55.8 us -> 30.5 us
  starting transfers between devices: 23.3 us -> 29.4 us
  between operations: 8.51 us -> 4.99 us
  local copies, waits for them, and re-layouts: 18.8 us -> 15.6 us
    all_to_all x2 -> x1, blocking collectives: 55.8 us -> 30.5 us  [per_device(): gathered = lax.all_to_all(forecast, group, 0, 0, tiled=True)]
    all_to_all x0 -> x1, waiting for transfers between devices: none -> 21.2 us  [per_device(): lax.all_to_all(grad_raw.reshape(32, members * own, out_width), group, 0,...]
    ppermute x8, waiting for transfers between devices: 43 us -> 28.3 us  [sent_along(): return lax.ppermute(x, step[1], step[0])]
    all_to_all x0 -> x1, starting transfers between devices: none -> 4.23 us  [per_device(): lax.all_to_all(grad_raw.reshape(32, members * own, out_width), group, 0,...]
    convert_element_type x11, other arithmetic: 8.29 us -> 11.9 us  [add(): return (a.astype(F32) + b.astype(F32)).astype(BF16)]
    squeeze x8 -> x6, local copies, waits for them, and re-layouts: 5.98 us -> 2.64 us  [take(): return lax.dynamic_index_in_dim(x, index, axis, keepdims=False)]
    select_n x3 -> x0, other arithmetic: 2.83 us -> none  [the longest x1 1.93 us: per_device(): riders = jnp.where(lane == 2 * lax.axis_index('x') + core, riders, 0.0)]
    ppermute x12 -> x10, waiting for transfers between devices: 15.9 us -> 13.9 us  [shift(): return lax.ppermute(x, axis, [(i, (i + by) % size) for i in range(size)])]
  transfers between devices with their start and end apart: 22 -> 21, of which waited for: 11 -> 9; matrix products, arithmetic and copies ran while one was open for 7% -> 10% of each run, Pallas kernels for 18% -> 20%
where the time goes in v2:
time: 256 us; the launch traced here: 255 us
  Pallas kernels  77 us (30%)
  waiting for transfers between devices  68.8 us (27%)
  blocking collectives  30.5 us (12%)
  starting transfers between devices  29.4 us (11%)
  other arithmetic  21.9 us (9%)
  local copies, waits for them, and re-layouts  15.6 us (6%)
  matrix products  6.83 us (3%)
  between operations  4.99 us (2%)
    pallas_call x4, Pallas kernels, forward_part(): pl.pallas_call(functools.partial(forward_kernel, first_call, last_call, b...  39.8 us
    all_to_all x1, blocking collectives, per_device(): gathered = lax.all_to_all(forecast, group, 0, 0, tiled=True)  30.5 us
    ppermute x8, waiting for transfers between devices, sent_along(): return lax.ppermute(x, step[1], step[0])  28.3 us
    all_to_all x1, waiting for transfers between devices, per_device(): lax.all_to_all(grad_raw.reshape(32, members * own, out_width), group, 0,...  21.2 us
    pallas_call x2, Pallas kernels, late_grads(): pl.pallas_call(late_kernel, grid_spec=pltpu.PrefetchScalarGridSpec(num_sc...  20 us
    ppermute x10, waiting for transfers between devices, shift(): return lax.ppermute(x, axis, [(i, (i + by) % size) for i in range(size)])  13.9 us
    pallas_call x1, Pallas kernels, early_grads(): pl.pallas_call(early_kernel, grid_spec=pltpu.PrefetchScalarGridSpec(num_s...  12.1 us
    convert_element_type x11, other arithmetic, add(): return (a.astype(F32) + b.astype(F32)).astype(BF16)  11.9 us
  transfers between devices with their start and end apart: 21, of which 9 were waited for; matrix products, arithmetic and copies ran while one was open for 10% of the time, Pallas kernels for 20%

profile of v2, /device:TPU:0, one launch (start us, length us, event | category | flops | bytes accessed | tf_op | source)
XLA Modules:
  0.0 255.1 jit_solution(10169317807003991746)
XLA Ops:
  0.7 2.0 copy.32.head
  2.7 2.5 packed.2.refs_2_
  5.2 1.7 collective-permute-start
  6.9 1.6 collective-permute-start.1
  8.5 3.2 %copy.33 = bf16[4,32,8,1024]{3,2,0,1:T(8,128)(2,1)} copy(bf16[4,32,8,1024]{3,2,1,0:T(8,128)(2,1)} %bitcast.104) | data formatting | bytes 4194304 | tf_op jit(solution)/shard_map/reshape | solution.py:394
  11.6 2.4 packed.3.refs_3_
  14.1 0.6 add_add_fusion.refs_0_.place
  14.7 9.1 %forward_part.4 = (f32[1024,2048]{1,0:T(8,128)}, bf16[1024,2048]{1,0:T(8,128)(2,1)}, bf16[2048,1024]{1,0:T(8,128)(2,1)}, bf16[768,1024]{1,0:T(8,128)(2,1)}, f32[1024,1024]{1,0:T(8,128)}) custom-call(s32[3]{0:T(128)} %add_add_fusion.refs_0_.place, bf16[1024,1024]{1,0:T(8,128)(2,1)} %bitcast.91, bf16[2432,256]{1,0:T(8,128)(2,1)} %packed.2.refs_2_, ...), custom_call_target="tpu_custom_call" | custom-call | flops 2147483648 | bytes 12582912 | tf_op jit(solution)/shard_map/forward_part/pallas_call | solution.py:141
  23.7 12.2 %collective-permute-done.refs_2_ = bf16[2432,256]{1,0:T(8,128)(2,1)S(1)} collective-permute-done((bf16[2432,256]{1,0:T(8,128)(2,1)}, bf16[2432,256]{1,0:T(8,128)(2,1)S(1)}, u32[]{:S(2)}, u32[]{:S(2)}) %collective-permute-start) | collective-permute-done | bytes 1245216 | tf_op jit(solution)/shard_map/ppermute | solution.py:26
  35.9 1.0 slice.39
  37.6 1.6 collective-permute-start.2
  39.1 1.7 collective-permute-start.3
  40.8 0.7 add_add_fusion.3.refs_0_
  41.4 0.7 add_add_fusion.2.refs_0_
  42.1 9.7 %forward_part.5 = (f32[1024,2048]{1,0:T(8,128)}, bf16[1024,2048]{1,0:T(8,128)(2,1)}, bf16[2048,1024]{1,0:T(8,128)(2,1)}, bf16[768,1024]{1,0:T(8,128)(2,1)}, f32[1024,1024]{1,0:T(8,128)}) custom-call(s32[3]{0:T(128)} %add_add_fusion.3.refs_0_, ...), custom_call_target="tpu_custom_call", output_to_operand_aliasing={{0}: (5, {}), {1}: (6, {}), {2}: (7, {}), {3}: (8, {}), {4}... | custom-call | flops 2147483648 | bytes 12582912 | tf_op jit(solution)/shard_map/forward_part/pallas_call | solution.py:141
  51.9 9.8 %forward_part.6 = (f32[1024,2048]{1,0:T(8,128)}, bf16[1024,2048]{1,0:T(8,128)(2,1)}, bf16[2048,1024]{1,0:T(8,128)(2,1)}, bf16[768,1024]{1,0:T(8,128)(2,1)}, f32[1024,1024]{1,0:T(8,128)}) custom-call(s32[3]{0:T(128)} %add_add_fusion.2.refs_0_, ...), custom_call_target="tpu_custom_call", output_to_operand_aliasing={{0}: (5, {}), {1}: (6, {}), {2}: (7, {}), {3}: (8, {}), {4}... | custom-call | flops 2147483648 | bytes 12582912 | tf_op jit(solution)/shard_map/forward_part/pallas_call | solution.py:141
  62.3 0.6 gather_fusion
  62.9 0.7 add_add_fusion.1.refs_0_
  63.6 1.2 collective-permute-done.6.refs_3_
  64.8 1.1 copy-done.12
  65.8 11.3 %forward_part.7 = (f32[1024,2048]{1,0:T(8,128)}, bf16[1024,2048]{1,0:T(8,128)(2,1)}, bf16[2048,1024]{1,0:T(8,128)(2,1)}, bf16[768,1024]{1,0:T(8,128)(2,1)}, bf16...) custom-call(s32[3]{0:T(128)} %add_add_fusion.1.refs_0_, ...), custom_call_target="tpu_custom_call", output_to_operand_aliasing={{0}: (5, {}), {1}: (6, {}), {2}: (7, {})} | custom-call | flops 2147483648 | bytes 12582912 | tf_op jit(solution)/shard_map/forward_part/pallas_call | solution.py:141
  77.1 30.5 %all_to_all.20 = bf16[32,32,768]{2,1,0:T(8,128)(2,1)S(1)} all-to-all(bf16[32,32,768]{2,1,0:T(8,128)(2,1)} %bitcast.107), channel_id=1, replica_groups=mesh['x'=4,'z'=4,'c'=2,'y'=4] {'x','z','c'}, dimensions={0} | all-to-all | bytes 3145728 | tf_op jit(solution)/shard_map/all_to_all | solution.py:418
  107.9 0.8 fusion.6
  109.0 0.9 fusion.34
  109.9 0.6 multiply_reduce_fusion
  110.5 2.8 %fusion.8 = bf16[128,8,768]{2,0,1:T(8,128)(2,1)S(1)} fusion(f32[128,8]{0,1:T(8,128)S(1)} %bitcast.110, f32[128,8]{0,1:T(8,128)S(1)} %copy.37, f32[8,768]{1,0:T(8,128)S(1)} %broadcast_select_fusion, f32[8]{0:T(128)S(1)} %get-tuple-element.144, bf16[128,8,768]{2,1,0:T(8,128)(2,1)S(1)} %bitcast.100, f32[8,128,128]{1,2,0:T(8,128)S(1)} %get-tuple-element.145), kind=kOutput, calls=%fused_computation.14 | convolution fusion | flops 1215168512 | bytes 3702816 | tf_op jit(solution)/shard_map/pmn,npo->mpo/dot_general | solution.py:361
  113.3 2.0 copy.44
  115.3 4.2 %all-to-all-start.1 = ((bf16[32,32,768]{2,1,0:T(8,128)(2,1)}), bf16[32,32,768]{2,1,0:T(8,128)(2,1)S(1)}, u32[]{:S(2)}, u32[]{:S(2)}) async-start(bf16[32,32,768]{2,1,0:T(8,128)(2,1)} %bitcast.16), calls=%async_computation.1 | async-start | bytes 3145728 | tf_op jit(solution)/shard_map/all_to_all | solution.py:421
  119.6 1.9 pad_maximum_fusion.2.scalars
  121.5 21.2 %all-to-all-done.1 = bf16[32,32,768]{2,1,0:T(8,128)(2,1)S(1)} async-done(((bf16[32,32,768]{2,1,0:T(8,128)(2,1)}), bf16[32,32,768]{2,1,0:T(8,128)(2,1)S(1)}, u32[]{:S(2)}, u32[]{:S(2)}) %all-to-all-start.1) | async-done | bytes 1572896 | tf_op jit(solution)/shard_map/all_to_all | solution.py:421
  142.7 3.1 %convolution_convert_fusion.resid_grad = bf16[1024,1024]{1,0:T(8,128)(2,1)} fusion(bf16[1024,768]{1,0:T(8,128)(2,1)S(1)} %bitcast.105, bf16[768,1024]{1,0:T(8,128)(2,1)S(1)} %copy-done.18), kind=kOutput, calls=%fused_computation.17 | convolution fusion | flops 1611661312 | bytes 5242880 | tf_op jit(solution)/shard_map/dot_general | solution.py:30
  145.8 12.1 %early_grads.1 = (bf16[4,384,1024]{2,1,0:T(8,128)(2,1)}, bf16[4,384,1024]{2,1,0:T(8,128)(2,1)}) custom-call(s32[3]{0:T(128)} %add_add_fusion.refs_0_.place, bf16[1024,2048]{1,0:T(8,128)(2,1)} %get-tuple-element.102.hidden, bf16[1024,1024]{1,0:T(8,128)(2,1)} %convolution_convert_fusion.resid_grad, bf16[1024,1024]{1,0:T(8,128)(2,1)} %get-tuple-element.103.residual, ...), custom_call_target="tpu_custom_call" | custom-call | flops 5905580032 | bytes 18874368 | tf_op jit(solution)/shard_map/early_grads/pallas_call | solution.py:208
  158.0 10.1 %late_grads.2 = (bf16[1,512,1024]{2,1,0:T(8,128)(2,1)}, bf16[1,512,1024]{2,1,0:T(8,128)(2,1)}) custom-call(s32[3]{0:T(128)} %add_add_fusion.refs_0_.place, bf16[1024,1024]{1,0:T(8,128)(2,1)} %convolution_convert_fusion.resid_grad, bf16[2048,1024]{1,0:T(8,128)(2,1)} %get-tuple-element.106.second, f32[1024,2048]{1,0:T(8,128)} %get-tuple-element.107.slope, ...), custom_call_target="tpu_custom_call" | custom-call | flops 4294967296 | bytes 12582912 | tf_op jit(solution)/shard_map/late_grads/pallas_call | solution.py:246
  168.6 1.6 add_convert_fusion
  170.6 0.8 collective-permute-start.12
  172.1 0.9 constant_dynamic-slice_fusion.1
  173.5 9.9 %late_grads.3 = (bf16[1,512,1024]{2,1,0:T(8,128)(2,1)}, bf16[1,512,1024]{2,1,0:T(8,128)(2,1)}) custom-call(s32[3]{0:T(128)} %add_add_fusion.refs_0_.place, bf16[1024,1024]{1,0:T(8,128)(2,1)} %convolution_convert_fusion.resid_grad, bf16[2048,1024]{1,0:T(8,128)(2,1)} %get-tuple-element.106.second, f32[1024,2048]{1,0:T(8,128)} %get-tuple-element.107.slope, ...), custom_call_target="tpu_custom_call" | custom-call | flops 4294967296 | bytes 12582912 | tf_op jit(solution)/shard_map/late_grads/pallas_call | solution.py:246
  183.4 3.7 %collective-permute-done.9 = bf16[2,16,8,1024]{3,2,1,0:T(8,128)(2,1)S(1)} collective-permute-done((bf16[2,16,8,1024]{3,2,1,0:T(8,128)(2,1)S(1)}, bf16[2,16,8,1024]{3,2,1,0:T(8,128)(2,1)S(1)}, u32[]{:S(2)}, u32[]{:S(2)}) %collective-permute-start.9) | collective-permute-done | bytes 524320 | tf_op jit(solution)/shard_map/ppermute | solution.py:297
  187.1 4.4 %collective-permute-done.12 = bf16[2,192,1024]{2,1,0:T(8,128)(2,1)} collective-permute-done((bf16[2,192,1024]{2,1,0:T(8,128)(2,1)S(1)}, bf16[2,192,1024]{2,1,0:T(8,128)(2,1)}, u32[]{:S(2)}, u32[]{:S(2)}) %collective-permute-start.12) | collective-permute-done | bytes 786464 | tf_op jit(solution)/shard_map/ppermute | solution.py:297
  191.5 1.5 fusion.27
  193.0 0.8 dynamic-slice_bitcast_fusion.6
  194.5 1.5 add_convert_fusion.1
  196.0 0.9 dynamic-slice_bitcast_fusion.2
  197.0 1.7 collective-permute-start.15
  198.7 1.4 fusion.10
  200.1 1.7 fusion.9
  201.9 2.0 collective-permute-start.14
  203.9 1.5 collective-permute-start.10
  205.4 7.8 %collective-permute-done.15 = bf16[2,16,8,1024]{3,2,0,1:T(8,128)(2,1)} collective-permute-done((bf16[2,16,8,1024]{3,2,0,1:T(8,128)(2,1)}, bf16[2,16,8,1024]{3,2,0,1:T(8,128)(2,1)}, u32[]{:S(2)}, u32[]{:S(2)}) %collective-permute-start.15) | collective-permute-done | bytes 524320 | tf_op jit(solution)/shard_map/ppermute | solution.py:297
  213.3 1.4 fusion.26
  214.7 0.7 dynamic-slice_bitcast_fusion.5
  215.4 1.1 fusion.29
  216.7 0.9 pad_maximum_fusion
  217.6 3.6 %all-to-all-start.3 = ((bf16[16,24,1024]{2,1,0:T(8,128)(2,1)}), bf16[16,24,1024]{2,1,0:T(8,128)(2,1)S(1)}, u32[]{:S(2)}, u32[]{:S(2)}) async-start(bf16[16,24,1024]{2,1,0:T(8,128)(2,1)} %bitcast.44), calls=%async_computation.3 | async-start | bytes 1572864 | tf_op jit(solution)/shard_map/all_to_all | solution.py:463
  221.3 1.9 collective-permute-start.17
  223.2 1.0 fusion.31
  224.2 12.4 %collective-permute-done.17 = bf16[16,8,1024]{2,1,0:T(8,128)(2,1)S(1)} collective-permute-done((bf16[16,8,1024]{2,1,0:T(8,128)(2,1)}, bf16[16,8,1024]{2,1,0:T(8,128)(2,1)S(1)}, u32[]{:S(2)}, u32[]{:S(2)}) %collective-permute-start.17) | collective-permute-done | bytes 262176 | tf_op jit(solution)/shard_map/ppermute | solution.py:297
  236.7 0.9 pad_maximum_fusion.1
  237.6 5.6 %all-to-all-start.2 = ((bf16[16,16,1024]{2,1,0:T(8,128)(2,1)}), bf16[16,16,1024]{2,1,0:T(8,128)(2,1)S(1)}, u32[]{:S(2)}, u32[]{:S(2)}) async-start(bf16[16,16,1024]{2,1,0:T(8,128)(2,1)} %pad_maximum_fusion.1), calls=%async_computation.2 | async-start | bytes 1048576 | tf_op jit(solution)/shard_map/all_to_all | solution.py:464
  243.4 0.6 fusion.38
  246.7 0.6 slice_multiply_fusion.1
  247.3 0.6 slice_multiply_fusion
  247.9 5.3 %all-to-all-done.2 = bf16[16,16,1024]{2,1,0:T(8,128)(2,1)S(1)} async-done(((bf16[16,16,1024]{2,1,0:T(8,128)(2,1)}), bf16[16,16,1024]{2,1,0:T(8,128)(2,1)S(1)}, u32[]{:S(2)}, u32[]{:S(2)}) %all-to-all-start.2) | async-done | bytes 524320 | tf_op jit(solution)/shard_map/all_to_all | solution.py:464
  253.3 0.6 maximum_multiply_fusion
  (84 shorter events, 5.1 us)
Async XLA Ops:
  0.6 61.7 %copy-start = (f32[8,768]{1,0:T(8,128)S(1)}, f32[8,768]{1,0:T(8,128)}, u32[]{:S(2)}) copy-start(f32[8,768]{1,0:T(8,128)} %param.11) | copy-start | bytes 73732
  5.2 30.7 %collective-permute-start = (bf16[2432,256]{1,0:T(8,128)(2,1)}, bf16[2432,256]{1,0:T(8,128)(2,1)S(1)}, u32[]{:S(2)}, u32[]{:S(2)}) collective-permute-start(bf16[2432,256]{1,0:T(8,128)(2,1)} %packed.2.refs_2_), channel_id=1, source_target_pairs={{0,1},{1,2},{2,3},{3,0},{4,5},{5,6},{6,7},{7,4},{8,9},{9,10},{10,1... | collective-permute-start | bytes 3735560 | tf_op jit(solution)/shard_map/ppermute | solution.py:26
  6.9 29.0 %collective-permute-start.1 = (bf16[2432,256]{1,0:T(8,128)(2,1)}, bf16[2432,256]{1,0:T(8,128)(2,1)S(1)}, u32[]{:S(2)}, u32[]{:S(2)}) collective-permute-start(bf16[2432,256]{1,0:T(8,128)(2,1)} %packed.2.refs_2_), channel_id=1, source_target_pairs={{0,3},{1,0},{2,1},{3,2},{4,7},{5,4},{6,5},{7,6},{8,11},{9,8},{10,9... | collective-permute-start | bytes 3735560 | tf_op jit(solution)/shard_map/ppermute | solution.py:26
  35.9 6.2 %copy-start.7 = (bf16[2432,256]{1,0:T(8,128)(2,1)}, bf16[2432,256]{1,0:T(8,128)(2,1)S(1)}, u32[]{:S(2)}) copy-start(bf16[2432,256]{1,0:T(8,128)(2,1)S(1)} %collective-permute-done.refs_2_) | copy-start | bytes 3735556
  35.9 15.9 %copy-start.6 = (bf16[2432,256]{1,0:T(8,128)(2,1)}, bf16[2432,256]{1,0:T(8,128)(2,1)S(1)}, u32[]{:S(2)}) copy-start(bf16[2432,256]{1,0:T(8,128)(2,1)S(1)} %collective-permute-done.1.refs_2_) | copy-start | bytes 3735556
  37.0 5.1 %collective-permute-start.5 = (bf16[2432,256]{1,0:T(8,128)(2,1)S(1)}, bf16[2432,256]{1,0:T(8,128)(2,1)}, u32[]{:S(2)}, u32[]{:S(2)}) collective-permute-start(bf16[2432,256]{1,0:T(8,128)(2,1)S(1)} %collective-permute-done.refs_2_), channel_id=1, source_target_pairs={{0,4},{4,0},{1,5},{5,1},{2,6},{6,2},{3,7},{7,3},{8,12},{12,8},{9,1... | collective-permute-start | bytes 3735560 | tf_op jit(solution)/shard_map/ppermute | solution.py:26
  37.1 14.8 %collective-permute-start.4 = (bf16[2432,256]{1,0:T(8,128)(2,1)S(1)}, bf16[2432,256]{1,0:T(8,128)(2,1)}, u32[]{:S(2)}, u32[]{:S(2)}) collective-permute-start(bf16[2432,256]{1,0:T(8,128)(2,1)S(1)} %collective-permute-done.1.refs_2_), channel_id=1, source_target_pairs={{0,4},{4,0},{1,5},{5,1},{2,6},{6,2},{3,7},{7,3},{8,12},{12,8},{9,1... | collective-permute-start | bytes 3735560 | tf_op jit(solution)/shard_map/ppermute | solution.py:26
  37.6 24.1 %collective-permute-start.2 = (bf16[1216,256]{1,0:T(8,128)(2,1)}, bf16[1216,256]{1,0:T(8,128)(2,1)S(1)}, u32[]{:S(2)}, u32[]{:S(2)}) collective-permute-start(bf16[1216,256]{1,0:T(8,128)(2,1)} %slice.39), channel_id=1, source_target_pairs={{0,1},{1,2},{2,3},{3,0},{4,5},{5,6},{6,7},{7,4},{8,9},{9,10},{10,1... | collective-permute-start | bytes 1867784 | tf_op jit(solution)/shard_map/ppermute | solution.py:26
  39.1 22.5 %collective-permute-start.3 = (bf16[1216,256]{1,0:T(8,128)(2,1)S(1)}, bf16[1216,256]{1,0:T(8,128)(2,1)S(1)}, u32[]{:S(2)}, u32[]{:S(2)}) collective-permute-start(bf16[1216,256]{1,0:T(8,128)(2,1)S(1)} %slice.40), channel_id=1, source_target_pairs={{0,3},{1,0},{2,1},{3,2},{4,7},{5,4},{6,5},{7,6},{8,11},{9,8},{10,9... | collective-permute-start | bytes 1867784 | tf_op jit(solution)/shard_map/ppermute | solution.py:26
  61.6 0.7 copy-start.16
  61.8 3.0 %copy-start.8 = (bf16[2432,256]{1,0:T(8,128)(2,1)}, bf16[2432,256]{1,0:T(8,128)(2,1)S(1)}, u32[]{:S(2)}) copy-start(bf16[2432,256]{1,0:T(8,128)(2,1)S(1)} %constant_dynamic-update-slice_fusion.refs_2_) | copy-start | bytes 3735556
  61.8 3.0 %collective-permute-start.6 = (bf16[2432,256]{1,0:T(8,128)(2,1)S(1)}, bf16[2432,256]{1,0:T(8,128)(2,1)S(1)}, u32[]{:S(2)}, u32[]{:S(2)}) collective-permute-start(bf16[2432,256]{1,0:T(8,128)(2,1)S(1)} %constant_dynamic-update-slice_fusion.refs_2_), channel_id=1, source_target_pairs={{0,4},{4,0},{1,5},{5,1},{2,6},{6,2},{3,7},{7,3},{8,12},{12,8},{9,1... | collective-permute-start | bytes 3735560 | tf_op jit(solution)/shard_map/ppermute | solution.py:26
  64.8 1.1 copy-start.12
  109.0 0.9 copy-start.17
  115.3 27.4 %copy-start.18 = (bf16[768,1024]{1,0:T(8,128)(2,1)S(1)}, bf16[768,1024]{1,0:T(8,128)(2,1)}, u32[]{:S(2)}) copy-start(bf16[768,1024]{1,0:T(8,128)(2,1)} %get-tuple-element.101) | copy-start | bytes 4718596
  115.3 27.4 %all-to-all-start.1 = ((bf16[32,32,768]{2,1,0:T(8,128)(2,1)}), bf16[32,32,768]{2,1,0:T(8,128)(2,1)S(1)}, u32[]{:S(2)}, u32[]{:S(2)}) async-start(bf16[32,32,768]{2,1,0:T(8,128)(2,1)} %bitcast.16), calls=%async_computation.1 | async-start | bytes 3145728 | tf_op jit(solution)/shard_map/all_to_all | solution.py:421
  142.7 3.1 %copy-start.11 = (bf16[32,32,768]{2,1,0:T(8,128)(2,1)}, bf16[32,32,768]{2,1,0:T(8,128)(2,1)S(1)}, u32[]{:S(2)}) copy-start(bf16[32,32,768]{2,1,0:T(8,128)(2,1)S(1)} %all-to-all-done.1) | copy-start | bytes 4718596
  157.9 10.6 %collective-permute-start.7 = (bf16[4,384,1024]{2,1,0:T(8,128)(2,1)}, bf16[4,384,1024]{2,1,0:T(8,128)(2,1)S(1)}, u32[]{:S(2)}, u32[]{:S(2)}) collective-permute-start(bf16[4,384,1024]{2,1,0:T(8,128)(2,1)} %get-tuple-element.104), channel_id=1, source_target_pairs={{0,4},{4,0},{1,5},{5,1},{2,6},{6,2},{3,7},{7,3},{8,12},{12,8},{9,1... | collective-permute-start | bytes 9437192 | tf_op jit(solution)/shard_map/ppermute | solution.py:26
  158.0 10.5 %copy-start.5 = (bf16[4,384,1024]{2,1,0:T(8,128)(2,1)S(1)}, bf16[4,384,1024]{2,1,0:T(8,128)(2,1)}, u32[]{:S(2)}) copy-start(bf16[4,384,1024]{2,1,0:T(8,128)(2,1)} %get-tuple-element.111) | copy-start | bytes 9437188
  168.1 3.4 %collective-permute-start.8 = (bf16[1,512,1024]{2,1,0:T(8,128)(2,1)}, bf16[1,512,1024]{2,1,0:T(8,128)(2,1)S(1)}, u32[]{:S(2)}, u32[]{:S(2)}) collective-permute-start(bf16[1,512,1024]{2,1,0:T(8,128)(2,1)} %get-tuple-element.110), channel_id=1, source_target_pairs={{0,4},{4,0},{1,5},{5,1},{2,6},{6,2},{3,7},{7,3},{8,12},{12,8},{9,1... | collective-permute-start | bytes 3145736 | tf_op jit(solution)/shard_map/ppermute | solution.py:26
  170.5 1.2 copy-start.14
  170.6 20.9 %collective-permute-start.12 = (bf16[2,192,1024]{2,1,0:T(8,128)(2,1)S(1)}, bf16[2,192,1024]{2,1,0:T(8,128)(2,1)}, u32[]{:S(2)}, u32[]{:S(2)}) collective-permute-start(bf16[2,192,1024]{2,1,0:T(8,128)(2,1)S(1)} %dynamic-slice_bitcast_fusion), channel_id=1, source_target_pairs={{0,96},{96,0},{32,64},{64,32},{1,97},{97,1},{33,65},{65,33},{2,98}... | collective-permute-start | bytes 2359304 | tf_op jit(solution)/shard_map/ppermute | solution.py:297
  171.5 20.0 %collective-permute-start.11 = (bf16[2,192,1024]{2,1,0:T(8,128)(2,1)S(1)}, bf16[2,192,1024]{2,1,0:T(8,128)(2,1)}, u32[]{:S(2)}, u32[]{:S(2)}) collective-permute-start(bf16[2,192,1024]{2,1,0:T(8,128)(2,1)S(1)} %dynamic-slice_bitcast_fusion.1), channel_id=1, source_target_pairs={{0,32},{32,0},{64,96},{96,64},{1,33},{33,1},{65,97},{97,65},{2,34}... | collective-permute-start | bytes 2359304 | tf_op jit(solution)/shard_map/ppermute | solution.py:297
  173.1 14.0 %collective-permute-start.9 = (bf16[2,16,8,1024]{3,2,1,0:T(8,128)(2,1)S(1)}, bf16[2,16,8,1024]{3,2,1,0:T(8,128)(2,1)S(1)}, u32[]{:S(2)}, u32[]{:S(2)}) collective-permute-start(bf16[2,16,8,1024]{3,2,1,0:T(8,128)(2,1)S(1)} %bitcast.108), channel_id=1, source_target_pairs={{0,1},{1,0},{2,3},{3,2},{4,5},{5,4},{6,7},{7,6},{8,9},{9,8},{10,11... | collective-permute-start | bytes 1572872 | tf_op jit(solution)/shard_map/ppermute | solution.py:297
  187.1 4.4 %copy-start.15 = (bf16[2,16,8,1024]{3,2,1,0:T(8,128)(2,1)}, bf16[2,16,8,1024]{3,2,1,0:T(8,128)(2,1)S(1)}, u32[]{:S(2)}) copy-start(bf16[2,16,8,1024]{3,2,1,0:T(8,128)(2,1)S(1)} %collective-permute-done.9) | copy-start | bytes 1572868
  191.5 3.0 %collective-permute-start.13 = (bf16[1,512,1024]{2,1,0:T(8,128)(2,1)}, bf16[1,512,1024]{2,1,0:T(8,128)(2,1)}, u32[]{:S(2)}, u32[]{:S(2)}) collective-permute-start(bf16[1,512,1024]{2,1,0:T(8,128)(2,1)} %get-tuple-element.117), channel_id=1, source_target_pairs={{0,4},{4,0},{1,5},{5,1},{2,6},{6,2},{3,7},{7,3},{8,12},{12,8},{9,1... | collective-permute-start | bytes 3145736 | tf_op jit(solution)/shard_map/ppermute | solution.py:26
  191.5 3.0 %copy-start.13 = (bf16[1,512,1024]{2,1,0:T(8,128)(2,1)S(1)}, bf16[1,512,1024]{2,1,0:T(8,128)(2,1)}, u32[]{:S(2)}) copy-start(bf16[1,512,1024]{2,1,0:T(8,128)(2,1)} %get-tuple-element.115) | copy-start | bytes 3145732
  193.0 0.9 copy-start.9
  196.0 5.8 %copy-start.2 = (bf16[1,512,1024]{2,1,0:T(8,128)(2,1)}, bf16[1,512,1024]{2,1,0:T(8,128)(2,1)S(1)}, u32[]{:S(2)}) copy-start(bf16[1,512,1024]{2,1,0:T(8,128)(2,1)S(1)} %add_convert_fusion.1) | copy-start | bytes 3145732
  197.0 16.3 %collective-permute-start.15 = (bf16[2,16,8,1024]{3,2,0,1:T(8,128)(2,1)}, bf16[2,16,8,1024]{3,2,0,1:T(8,128)(2,1)}, u32[]{:S(2)}, u32[]{:S(2)}) collective-permute-start(bf16[2,16,8,1024]{3,2,0,1:T(8,128)(2,1)} %dynamic-slice_bitcast_fusion.2), channel_id=1, source_target_pairs={{0,3},{3,0},{1,2},{2,1},{4,7},{7,4},{5,6},{6,5},{8,11},{11,8},{9,1... | collective-permute-start | bytes 1572872 | tf_op jit(solution)/shard_map/ppermute | solution.py:297
  200.1 1.8 copy-start.3
  201.9 13.5 %copy-start.4 = (bf16[2,192,1024]{2,1,0:T(8,128)(2,1)S(1)}, bf16[2,192,1024]{2,1,0:T(8,128)(2,1)}, u32[]{:S(2)}) copy-start(bf16[2,192,1024]{2,1,0:T(8,128)(2,1)} %copy-done.3) | copy-start | bytes 2359300
  201.9 13.5 %collective-permute-start.14 = (bf16[192,1024]{1,0:T(8,128)(2,1)S(1)}, bf16[192,1024]{1,0:T(8,128)(2,1)}, u32[]{:S(2)}, u32[]{:S(2)}) collective-permute-start(bf16[192,1024]{1,0:T(8,128)(2,1)S(1)} %get-tuple-element.147), channel_id=1, source_target_pairs={{0,96},{96,0},{32,64},{64,32},{1,97},{97,1},{33,65},{65,33},{2,98}... | collective-permute-start | bytes 1179656 | tf_op jit(solution)/shard_map/ppermute | solution.py:297
  203.9 19.3 %collective-permute-start.10 = (bf16[16,8,1024]{2,1,0:T(8,128)(2,1)}, bf16[16,8,1024]{2,1,0:T(8,128)(2,1)}, u32[]{:S(2)}, u32[]{:S(2)}) collective-permute-start(bf16[16,8,1024]{2,1,0:T(8,128)(2,1)} %dynamic-slice_bitcast_fusion.6), channel_id=1, source_target_pairs={{0,3},{3,0},{1,2},{2,1},{4,7},{7,4},{5,6},{6,5},{8,11},{11,8},{9,1... | collective-permute-start | bytes 786440 | tf_op jit(solution)/shard_map/ppermute | solution.py:297
  205.4 11.1 %collective-permute-start.16 = (bf16[192,1024]{1,0:T(8,128)(2,1)S(1)}, bf16[192,1024]{1,0:T(8,128)(2,1)S(1)}, u32[]{:S(2)}, u32[]{:S(2)}) collective-permute-start(bf16[192,1024]{1,0:T(8,128)(2,1)S(1)} %get-tuple-element.146), channel_id=1, source_target_pairs={{0,32},{32,0},{64,96},{96,64},{1,33},{33,1},{65,97},{97,65},{2,34}... | collective-permute-start | bytes 1179656 | tf_op jit(solution)/shard_map/ppermute | solution.py:297
  216.5 6.7 %copy-start.10 = (bf16[2,16,8,1024]{3,2,1,0:T(8,128)(2,1)S(1)}, bf16[2,16,8,1024]{3,2,1,0:T(8,128)(2,1)}, u32[]{:S(2)}) copy-start(bf16[2,16,8,1024]{3,2,1,0:T(8,128)(2,1)} %copy-done.9) | copy-start | bytes 1572868
  217.6 19.9 %all-to-all-start.3 = ((bf16[16,24,1024]{2,1,0:T(8,128)(2,1)}), bf16[16,24,1024]{2,1,0:T(8,128)(2,1)S(1)}, u32[]{:S(2)}, u32[]{:S(2)}) async-start(bf16[16,24,1024]{2,1,0:T(8,128)(2,1)} %bitcast.44), calls=%async_computation.3 | async-start | bytes 1572864 | tf_op jit(solution)/shard_map/all_to_all | solution.py:463
  221.3 15.4 %collective-permute-start.17 = (bf16[16,8,1024]{2,1,0:T(8,128)(2,1)}, bf16[16,8,1024]{2,1,0:T(8,128)(2,1)S(1)}, u32[]{:S(2)}, u32[]{:S(2)}) collective-permute-start(bf16[16,8,1024]{2,1,0:T(8,128)(2,1)} %dynamic-slice_bitcast_fusion.5), channel_id=1, source_target_pairs={{0,1},{1,0},{2,3},{3,2},{4,5},{5,4},{6,7},{7,6},{8,9},{9,8},{10,11... | collective-permute-start | bytes 786440 | tf_op jit(solution)/shard_map/ppermute | solution.py:297
  236.6 17.3 %copy-start.1 = (f32[8,768]{1,0:T(8,128)S(1)}, f32[8,768]{1,0:T(8,128)}, u32[]{:S(2)}) copy-start(f32[8,768]{1,0:T(8,128)} %param.11) | copy-start | bytes 73732
  237.6 15.7 %all-to-all-start.2 = ((bf16[16,16,1024]{2,1,0:T(8,128)(2,1)}), bf16[16,16,1024]{2,1,0:T(8,128)(2,1)S(1)}, u32[]{:S(2)}, u32[]{:S(2)}) async-start(bf16[16,16,1024]{2,1,0:T(8,128)(2,1)} %pad_maximum_fusion.1), calls=%async_computation.2 | async-start | bytes 1048576 | tf_op jit(solution)/shard_map/all_to_all | solution.py:464

commit v3 on v2

--- a/solution.py
+++ b/solution.py
@@ -30,10 +30,8 @@
     return lax.dot_general(a, b, (contract, ((), ())), preferred_element_type=F32)
 
 
-def params(cells):
-    return pltpu.CompilerParams(
-        dimension_semantics=("arbitrary",) * cells, vmem_limit_bytes=56 * MIB
-    )
+def params(mib):
+    return pltpu.CompilerParams(dimension_semantics=("arbitrary",), vmem_limit_bytes=mib * MIB)
 
 
 def forward_kernel(first_call, last_call, block_rows, sizes, *refs):
@@ -100,7 +98,9 @@
     head_rows = out_width // RING
     first_call = carried is None
     block_rows = min(rows, 256)
-    whole = lambda shape: pl.BlockSpec(shape, lambda i, s: (0,) * len(shape))
+    whole = lambda shape: pl.BlockSpec(
+        shape, lambda i, s: (0,) * len(shape), pipeline_mode=pl.Buffered(1)
+    )
     by_rows = lambda cols: pl.BlockSpec((block_rows, cols), lambda i, s: (i, 0))
     in_place = pl.BlockSpec(memory_space=pl.ANY)
     in_specs = [by_rows(width), whole(mine.shape), whole(theirs.shape)]
@@ -150,12 +150,16 @@
         ),
         out_shape=out_shape,
         input_output_aliases=aliases,
-        compiler_params=params(1),
+        compiler_params=params(24),
         cost_estimate=pl.CostEstimate(
             flops=8 * rows * width * half, bytes_accessed=12 * MIB, transcendentals=rows * 2 * half
         ),
         name="forward_part",
     )(place, *args)
+
+
+def once(shape):
+    return pl.BlockSpec(shape, lambda i, s: (0, 0), pipeline_mode=pl.Buffered(1))
 
 
 def store_halves(core, parts, keep, send):
@@ -212,15 +216,15 @@
             grid=(RING,),
             in_specs=[
                 pl.BlockSpec((rows, hid // RING), lambda i, s: (0, i)),
-                pl.BlockSpec((rows, width), lambda i, s: (0, 0)),
+                once((rows, width)),
                 pl.BlockSpec((rows, width // RING), lambda i, s: (0, i)),
-                pl.BlockSpec((rows, out_width), lambda i, s: (0, 0)),
+                once((rows, out_width)),
                 pl.BlockSpec(memory_space=pltpu.SMEM),
             ],
             out_specs=[out, out],
         ),
         out_shape=[jax.ShapeDtypeStruct((RING, lines, width), BF16)] * 2,
-        compiler_params=params(1),
+        compiler_params=params(32),
         cost_estimate=pl.CostEstimate(
             flops=2 * rows * width * (hid + out_width), bytes_accessed=18 * MIB, transcendentals=0
         ),
@@ -249,15 +253,15 @@
             num_scalar_prefetch=1,
             grid=(steps,),
             in_specs=[
-                pl.BlockSpec((rows, width), lambda j, s: (0, 0)),
+                once((rows, width)),
                 pl.BlockSpec((tile, width), lambda j, s: (part * steps + j, 0)),
                 pl.BlockSpec((rows, tile), lambda j, s: (0, part * steps + j)),
-                pl.BlockSpec((rows, width), lambda j, s: (0, 0)),
+                once((rows, width)),
             ],
             out_specs=[out, out],
         ),
         out_shape=[jax.ShapeDtypeStruct((1, width // 2, width), BF16)] * 2,
-        compiler_params=params(1),
+        compiler_params=params(28),
         cost_estimate=pl.CostEstimate(
             flops=4 * rows * width * width, bytes_accessed=12 * MIB, transcendentals=0
         ),
@@ -321,16 +325,15 @@
     for q in range(second.shape[1] // LANES):
         out[at : at + half, :] = second[:, q * LANES : (q + 1) * LANES]
         at += half
-    turned = head[...].astype(F32).T.astype(BF16)
-    for e in range(turned.shape[1] // LANES):
-        out[at : at + turned.shape[0], :] = turned[:, e * LANES : (e + 1) * LANES]
-        at += turned.shape[0]
+    for e in range(head.shape[1] // LANES):
+        out[at : at + head.shape[0], :] = head[:, e * LANES : (e + 1) * LANES]
+        at += head.shape[0]
 
 
 def packed(side, first, second, head):
     width, shard = first.shape
     half = shard // 2
-    lines = width + half * width // LANES + head.shape[1] * width // 2 // LANES
+    lines = width + half * width // LANES + head.shape[0] * width // 2 // LANES
     return pl.pallas_call(
         pack_kernel,
         grid_spec=pltpu.PrefetchScalarGridSpec(
@@ -339,12 +342,12 @@
             in_specs=[
                 pl.BlockSpec((width, half), lambda i, s: (0, s[0])),
                 pl.BlockSpec((half, width), lambda i, s: (s[0], 0)),
-                pl.BlockSpec((width // 2, head.shape[1]), lambda i, s: (s[0], 0)),
+                pl.BlockSpec((head.shape[0], width // 2), lambda i, s: (0, s[0])),
             ],
             out_specs=pl.BlockSpec((lines, LANES), lambda i, s: (0, 0)),
         ),
         out_shape=jax.ShapeDtypeStruct((lines, LANES), BF16),
-        compiler_params=params(1),
+        compiler_params=params(8),
         name="packed",
     )(side, first, second, head)
 
@@ -385,7 +388,8 @@
     half = shard // 2
 
     side = jnp.reshape(core, (1,)).astype(jnp.int32)
-    mine = packed(side, w_first, w_second, readout_matrix)
+    turned = readout_matrix.T
+    mine = packed(side, w_first, w_second, turned)
     right = shift(mine, "y", 1)
     left = shift(mine, "y", -1)
     lines = mine.shape[0] // 2
@@ -393,7 +397,7 @@
     tokens = (
         latents.reshape(members, 32, own, width).transpose(1, 0, 2, 3).reshape(rows, width)
     )
-    theirs = packed(other_side, w_first, w_second, readout_matrix)
+    theirs = packed(other_side, w_first, w_second, turned)
     place = lambda off: jnp.stack([(here + off) % RING, core, lax.axis_index("x")]).astype(jnp.int32)
     run = functools.partial(forward_part, out_width=out_width)
     carried = run(place(0), tokens, mine, theirs, carried=None, last_call=False)

time: 256 us -> 292 us (1.14)
  local copies, waits for them, and re-layouts: 15.6 us -> 72.5 us
  Pallas kernels: 77 us -> 55.2 us
    unnamed x41 -> x110, local copies, waits for them, and re-layouts: 3.86 us -> 60.2 us
    pallas_call x4, Pallas kernels: 39.8 us -> 29.9 us  [forward_part(): pl.pallas_call(functools.partial(forward_kernel, first_call, last_call, b...]
    pallas_call x2, Pallas kernels: 20 us -> 12.9 us  [late_grads(): pl.pallas_call(late_kernel, grid_spec=pltpu.PrefetchScalarGridSpec(num_sc...]
    ppermute x10, waiting for transfers between devices: 13.9 us -> 9.19 us  [shift(): return lax.ppermute(x, axis, [(i, (i + by) % size) for i in range(size)])]
    pallas_call x2, Pallas kernels: 5 us -> 1.28 us  [packed(): pl.pallas_call(pack_kernel, grid_spec=pltpu.PrefetchScalarGridSpec(num_sc...]
  transfers between devices with their start and end apart: 21 -> 21, of which waited for: 9 -> 11; matrix products, arithmetic and copies ran while one was open for 10% -> 8% of each run, Pallas kernels for 20% -> 12%
where the time goes in v3:
time: 292 us; the launch traced here: 291 us
  local copies, waits for them, and re-layouts  72.5 us (25%)
  waiting for transfers between devices  66.4 us (23%)
  Pallas kernels  55.2 us (19%)
  starting transfers between devices  31.9 us (11%)
  blocking collectives  30.3 us (10%)
  other arithmetic  19.9 us (7%)
  matrix products  9.57 us (3%)
  between operations  4.99 us (2%)
    unnamed x110, local copies, waits for them, and re-layouts  60.2 us
    all_to_all x1, blocking collectives, per_device(): gathered = lax.all_to_all(forecast, group, 0, 0, tiled=True)  30.3 us
    ppermute x8, waiting for transfers between devices, sent_along(): return lax.ppermute(x, step[1], step[0])  30.2 us
    pallas_call x4, Pallas kernels, forward_part(): pl.pallas_call(functools.partial(forward_kernel, first_call, last_call, b...  29.9 us
    all_to_all x1, waiting for transfers between devices, per_device(): lax.all_to_all(grad_raw.reshape(32, members * own, out_width), group, 0,...  21.7 us
    pallas_call x2, Pallas kernels, late_grads(): pl.pallas_call(late_kernel, grid_spec=pltpu.PrefetchScalarGridSpec(num_sc...  12.9 us
    convert_element_type x11, other arithmetic, add(): return (a.astype(F32) + b.astype(F32)).astype(BF16)  12.7 us
    pallas_call x1, Pallas kernels, early_grads(): pl.pallas_call(early_kernel, grid_spec=pltpu.PrefetchScalarGridSpec(num_s...  11.1 us
  transfers between devices with their start and end apart: 21, of which 11 were waited for; matrix products, arithmetic and copies ran while one was open for 8% of the time, Pallas kernels for 12%

profile of v3, /device:TPU:0, one launch (start us, length us, event | category | flops | bytes accessed | tf_op | source)
XLA Modules:
  0.0 290.9 jit_solution(7164915795027466147)
XLA Ops:
  5.3 1.7 collective-permute-start
  7.0 1.6 collective-permute-start.1
  8.5 1.9 copy.30
  12.0 1.3 copy-done.38
  13.3 6.9 %forward_part.4 = (f32[1024,2048]{1,0:T(8,128)S(1)}, bf16[1024,2048]{1,0:T(8,128)(2,1)S(1)}, bf16[2048,1024]{1,0:T(8,128)(2,1)S(1)}, bf16[768,1024]{1,0:T(8,128)(2,1)S(1)}, f32[1024,1024]{1,0:T(8,128)S(1)}) custom-call(s32[3]{0:T(128)S(1)} %add_add_fusion.refs_0_.place, bf16[1024,1024]{1,0:T(8,128)(2,1)S(1)} %bitcast.94, bf16[2432,256]{1,0:T(8,128)(2,1)} %packed.2.refs_2_, ...), custom_call_target="tpu_custom_call" | custom-call | flops 2147483648 | bytes 12582912 | tf_op jit(solution)/shard_map/forward_part/pallas_call | solution.py:141
  20.2 3.3 %copy-done.2 = f32[1024,2048]{1,0:T(8,128)} copy-done((f32[1024,2048]{1,0:T(8,128)}, f32[1024,2048]{1,0:T(8,128)S(1)}, u32[]{:S(2)}) %copy-start.2) | copy-done | bytes 8388632
  23.5 2.0 copy-done.6
  25.5 1.9 copy-done.12
  27.5 2.1 copy-done.18
  30.7 5.4 %collective-permute-done.refs_2_ = bf16[2432,256]{1,0:T(8,128)(2,1)} collective-permute-done((bf16[2432,256]{1,0:T(8,128)(2,1)}, bf16[2432,256]{1,0:T(8,128)(2,1)}, u32[]{:S(2)}, u32[]{:S(2)}) %collective-permute-start) | collective-permute-done | bytes 1245216 | tf_op jit(solution)/shard_map/ppermute | solution.py:26
  36.1 2.0 slice.39
  39.4 1.5 collective-permute-start.2
  40.9 1.7 collective-permute-start.3
  43.9 3.4 %copy-done.3 = f32[1024,2048]{1,0:T(8,128)S(1)} copy-done((f32[1024,2048]{1,0:T(8,128)S(1)}, f32[1024,2048]{1,0:T(8,128)}, u32[]{:S(2)}) %copy-start.3) | copy-done | bytes 8388632
  47.3 2.2 copy-done.7
  49.5 2.2 copy-done.13
  51.7 2.2 copy-done.19
  53.9 1.4 copy-done.23
  55.3 7.4 %forward_part.5 = (f32[1024,2048]{1,0:T(8,128)S(1)}, bf16[1024,2048]{1,0:T(8,128)(2,1)S(1)}, bf16[2048,1024]{1,0:T(8,128)(2,1)S(1)}, bf16[768,1024]{1,0:T(8,128)(2,1)S(1)}, f32[1024,1024]{1,0:T(8,128)S(1)}) custom-call(s32[3]{0:T(128)S(1)} %add_add_fusion.3.refs_0_, ...), custom_call_target="tpu_custom_call", output_to_operand_aliasing={{0}: (5, {}), {1}: (6, {}), {2}: (7, {}), {3}: (8, {}), {4}... | custom-call | flops 2147483648 | bytes 12582912 | tf_op jit(solution)/shard_map/forward_part/pallas_call | solution.py:141
  62.8 7.1 %forward_part.6 = (f32[1024,2048]{1,0:T(8,128)S(1)}, bf16[1024,2048]{1,0:T(8,128)(2,1)S(1)}, bf16[2048,1024]{1,0:T(8,128)(2,1)S(1)}, bf16[768,1024]{1,0:T(8,128)(2,1)S(1)}, f32[1024,1024]{1,0:T(8,128)S(1)}) custom-call(s32[3]{0:T(128)S(1)} %add_add_fusion.2.refs_0_, ...), custom_call_target="tpu_custom_call", output_to_operand_aliasing={{0}: (5, {}), {1}: (6, {}), {2}: (7, {}), {3}: (8, {}), {4}... | custom-call | flops 2147483648 | bytes 12582912 | tf_op jit(solution)/shard_map/forward_part/pallas_call | solution.py:141
  69.9 3.3 %copy-done.4 = f32[1024,2048]{1,0:T(8,128)} copy-done((f32[1024,2048]{1,0:T(8,128)}, f32[1024,2048]{1,0:T(8,128)S(1)}, u32[]{:S(2)}) %copy-start.4) | copy-done | bytes 8388632
  73.2 2.0 copy-done.8
  75.1 1.9 copy-done.14
  77.1 2.1 copy-done.20
  81.8 1.9 collective-permute-done.6.refs_3_
  83.6 2.2 copy-done.9
  85.8 2.2 copy-done.15
  88.0 2.2 copy-done.21
  90.2 1.4 copy-done.25
  91.6 8.5 %forward_part.7 = (f32[1024,2048]{1,0:T(8,128)}, bf16[1024,2048]{1,0:T(8,128)(2,1)S(1)}, bf16[2048,1024]{1,0:T(8,128)(2,1)S(1)}, bf16[768,1024]{1,0:T(8,128)(2,1...) custom-call(s32[3]{0:T(128)S(1)} %add_add_fusion.1.refs_0_, ...), custom_call_target="tpu_custom_call", output_to_operand_aliasing={{0}: (5, {}), {1}: (6, {}), {2}: (7, {})} | custom-call | flops 2147483648 | bytes 12582912 | tf_op jit(solution)/shard_map/forward_part/pallas_call | solution.py:141
  100.1 1.9 copy-done.16
  103.2 30.3 %all_to_all.20 = bf16[32,32,768]{2,1,0:T(8,128)(2,1)S(1)} all-to-all(bf16[32,32,768]{2,1,0:T(8,128)(2,1)S(1)} %bitcast.100), channel_id=1, replica_groups=mesh['x'=4,'z'=4,'c'=2,'y'=4] {'x','z','c'}, dimensions={0} | all-to-all | bytes 3145728 | tf_op jit(solution)/shard_map/all_to_all | solution.py:422
  135.0 3.0 %fusion.34 = (f32[8]{0:T(128)S(1)}, f32[8,128]{1,0:T(8,128)S(1)}, f32[8,128,128]{1,2,0:T(8,128)S(1)}) fusion(bf16[128,8,768]{2,1,0:T(8,128)(2,1)} %bitcast.106, f32[8,128]{1,0:T(8,128)S(1)} %copy.34), kind=kOutput, calls=%fused_computation.78 | convolution fusion | flops 202243072 | bytes 2105376 | tf_op jit(solution)/shard_map/mpo,npo->pmn/dot_general | solution.py:358
  138.5 2.8 fusion.8
  141.4 2.0 copy.40
  143.4 4.7 %all-to-all-start.1 = ((bf16[32,32,768]{2,1,0:T(8,128)(2,1)}), bf16[32,32,768]{2,1,0:T(8,128)(2,1)}, u32[]{:S(2)}, u32[]{:S(2)}) async-start(bf16[32,32,768]{2,1,0:T(8,128)(2,1)} %bitcast.105), calls=%async_computation.1 | async-start | bytes 3145728 | tf_op jit(solution)/shard_map/all_to_all | solution.py:425
  148.1 1.4 pad_maximum_fusion.2.scalars
  149.4 21.7 %all-to-all-done.1 = bf16[32,32,768]{2,1,0:T(8,128)(2,1)} async-done(((bf16[32,32,768]{2,1,0:T(8,128)(2,1)}), bf16[32,32,768]{2,1,0:T(8,128)(2,1)}, u32[]{:S(2)}, u32[]{:S(2)}) %all-to-all-start.1) | async-done | bytes 1572896 | tf_op jit(solution)/shard_map/all_to_all | solution.py:425
  171.2 3.8 %convolution_convert_fusion.resid_grad = bf16[1024,1024]{1,0:T(8,128)(2,1)S(1)} fusion(bf16[1024,768]{1,0:T(8,128)(2,1)} %bitcast.18.grad_rows, bf16[768,1024]{1,0:T(8,128)(2,1)} %copy-done.41), kind=kOutput, calls=%fused_computation.17 | convolution fusion | flops 1611661312 | bytes 5242880 | tf_op jit(solution)/shard_map/dot_general | solution.py:30
  175.0 11.1 %early_grads.1 = (bf16[4,384,1024]{2,1,0:T(8,128)(2,1)S(1)}, bf16[4,384,1024]{2,1,0:T(8,128)(2,1)}) custom-call(s32[3]{0:T(128)S(1)} %add_add_fusion.refs_0_.place, bf16[1024,2048]{1,0:T(8,128)(2,1)S(1)} %copy-done.17, bf16[1024,1024]{1,0:T(8,128)(2,1)S(1)} %convolution_convert_fusion.resid_grad, bf16[1024,1024]{1,0:T(8,128)(2,1)S(1)} %copy-done.40, ...), custom_call_target="tpu_custom_call" | custom-call | flops 5905580032 | bytes 18874368 | tf_op jit(solution)/shard_map/early_grads/pallas_call | solution.py:212
  186.2 1.7 copy-done.33
  187.8 3.4 %copy-done.5 = f32[1024,2048]{1,0:T(8,128)S(1)} copy-done((f32[1024,2048]{1,0:T(8,128)S(1)}, f32[1024,2048]{1,0:T(8,128)}, u32[]{:S(2)}) %copy-start.5) | copy-done | bytes 8388632
  191.2 2.2 copy-done.11
  193.4 1.6 copy-done.27
  195.0 6.1 %late_grads.2 = (bf16[1,512,1024]{2,1,0:T(8,128)(2,1)S(1)}, bf16[1,512,1024]{2,1,0:T(8,128)(2,1)S(1)}) custom-call(s32[3]{0:T(128)S(1)} %add_add_fusion.refs_0_.place, bf16[1024,1024]{1,0:T(8,128)(2,1)S(1)} %copy-done.27, bf16[2048,1024]{1,0:T(8,128)(2,1)S(1)} %copy-done.11, f32[1024,2048]{1,0:T(8,128)S(1)} %copy-done.5, bf16[1024,1024]{1,0:T(8,128)(2,1)S(1)} %bitcast.98), custom_call_target="tpu_custom_call" | custom-call | flops 4294967296 | bytes 12582912 | tf_op jit(solution)/shard_map/late_grads/pallas_call | solution.py:250
  201.9 2.9 %add_convert_fusion = bf16[4,384,1024]{2,1,0:T(8,128)(2,1)S(1)} fusion(bf16[4,384,1024]{2,1,0:T(8,128)(2,1)} %collective-permute-done.7, bf16[4,384,1024]{2,1,0:T(8,128)(2,1)S(1)} %copy-done.34), kind=kLoop, calls=%fused_computation.1 | loop fusion | flops 6291456 | bytes 9437184 | tf_op jit(solution)/shard_map/convert_element_type | solution.py:273
  207.7 1.6 collective-permute-start.9
  210.4 6.8 %late_grads.3 = (bf16[1,512,1024]{2,1,0:T(8,128)(2,1)S(1)}, bf16[1,512,1024]{2,1,0:T(8,128)(2,1)}) custom-call(s32[3]{0:T(128)S(1)} %add_add_fusion.refs_0_.place, bf16[1024,1024]{1,0:T(8,128)(2,1)S(1)} %copy-done.28, bf16[2048,1024]{1,0:T(8,128)(2,1)S(1)} %copy-done.11, f32[1024,2048]{1,0:T(8,128)S(1)} %bitcast.93, bf16[1024,1024]{1,0:T(8,128)(2,1)S(1)} %bitcast.99), custom_call_target="tpu_custom_call" | custom-call | flops 4294967296 | bytes 12582912 | tf_op jit(solution)/shard_map/late_grads/pallas_call | solution.py:250
  217.2 4.4 %collective-permute-done.9 = bf16[2,16,8,1024]{3,2,1,0:T(8,128)(2,1)S(1)} collective-permute-done((bf16[2,16,8,1024]{3,2,1,0:T(8,128)(2,1)S(1)}, bf16[2,16,8,1024]{3,2,1,0:T(8,128)(2,1)S(1)}, u32[]{:S(2)}, u32[]{:S(2)}) %collective-permute-start.9) | collective-permute-done | bytes 524320 | tf_op jit(solution)/shard_map/ppermute | solution.py:301
  221.7 4.5 %collective-permute-done.12 = bf16[2,192,1024]{2,1,0:T(8,128)(2,1)} collective-permute-done((bf16[2,192,1024]{2,1,0:T(8,128)(2,1)S(1)}, bf16[2,192,1024]{2,1,0:T(8,128)(2,1)}, u32[]{:S(2)}, u32[]{:S(2)}) %collective-permute-start.12) | collective-permute-done | bytes 786464 | tf_op jit(solution)/shard_map/ppermute | solution.py:301
  226.2 1.4 fusion.27
  229.2 1.6 add_convert_fusion.1
  231.7 2.9 collective-permute-start.15
  234.5 1.4 fusion.10
  235.9 1.4 fusion.9
  238.3 1.9 collective-permute-start.14
  240.6 7.3 %collective-permute-done.15 = bf16[2,16,8,1024]{3,2,0,1:T(8,128)(2,1)S(1)} collective-permute-done((bf16[2,16,8,1024]{3,2,0,1:T(8,128)(2,1)}, bf16[2,16,8,1024]{3,2,0,1:T(8,128)(2,1)S(1)}, u32[]{:S(2)}, u32[]{:S(2)}) %collective-permute-start.15) | collective-permute-done | bytes 524320 | tf_op jit(solution)/shard_map/ppermute | solution.py:301
  247.9 1.2 fusion.26
  249.1 1.6 collective-permute-done.14
  253.0 4.0 %all-to-all-start.3 = ((bf16[16,24,1024]{2,1,0:T(8,128)(2,1)}), bf16[16,24,1024]{2,1,0:T(8,128)(2,1)S(1)}, u32[]{:S(2)}, u32[]{:S(2)}) async-start(bf16[16,24,1024]{2,1,0:T(8,128)(2,1)} %bitcast.45), calls=%async_computation.3 | async-start | bytes 1572864 | tf_op jit(solution)/shard_map/all_to_all | solution.py:467
  257.0 1.9 collective-permute-start.17
  259.9 12.4 %collective-permute-done.17 = bf16[16,8,1024]{2,1,0:T(8,128)(2,1)S(1)} collective-permute-done((bf16[16,8,1024]{2,1,0:T(8,128)(2,1)S(1)}, bf16[16,8,1024]{2,1,0:T(8,128)(2,1)S(1)}, u32[]{:S(2)}, u32[]{:S(2)}) %collective-permute-start.17) | collective-permute-done | bytes 262176 | tf_op jit(solution)/shard_map/ppermute | solution.py:301
  273.3 5.6 %all-to-all-start.2 = ((bf16[16,16,1024]{2,1,0:T(8,128)(2,1)}), bf16[16,16,1024]{2,1,0:T(8,128)(2,1)S(1)}, u32[]{:S(2)}, u32[]{:S(2)}) async-start(bf16[16,16,1024]{2,1,0:T(8,128)(2,1)} %pad_maximum_fusion.1), calls=%async_computation.2 | async-start | bytes 1048576 | tf_op jit(solution)/shard_map/all_to_all | solution.py:468
  283.7 5.3 %all-to-all-done.2 = bf16[16,16,1024]{2,1,0:T(8,128)(2,1)S(1)} async-done(((bf16[16,16,1024]{2,1,0:T(8,128)(2,1)}), bf16[16,16,1024]{2,1,0:T(8,128)(2,1)S(1)}, u32[]{:S(2)}, u32[]{:S(2)}) %all-to-all-start.2) | async-done | bytes 524320 | tf_op jit(solution)/shard_map/all_to_all | solution.py:468
  (154 shorter events, 31.3 us)
Async XLA Ops:
  0.6 80.4 %copy-start = (f32[8,768]{1,0:T(8,128)S(1)}, f32[8,768]{1,0:T(8,128)}, u32[]{:S(2)}) copy-start(f32[8,768]{1,0:T(8,128)} %param.11) | copy-start | bytes 73732
  5.3 30.8 %collective-permute-start = (bf16[2432,256]{1,0:T(8,128)(2,1)}, bf16[2432,256]{1,0:T(8,128)(2,1)}, u32[]{:S(2)}, u32[]{:S(2)}) collective-permute-start(bf16[2432,256]{1,0:T(8,128)(2,1)} %packed.2.refs_2_), channel_id=1, source_target_pairs={{0,1},{1,2},{2,3},{3,0},{4,5},{5,6},{6,7},{7,4},{8,9},{9,10},{10,1... | collective-permute-start | bytes 3735560 | tf_op jit(solution)/shard_map/ppermute | solution.py:26
  7.0 29.1 %collective-permute-start.1 = (bf16[2432,256]{1,0:T(8,128)(2,1)}, bf16[2432,256]{1,0:T(8,128)(2,1)S(1)}, u32[]{:S(2)}, u32[]{:S(2)}) collective-permute-start(bf16[2432,256]{1,0:T(8,128)(2,1)} %packed.2.refs_2_), channel_id=1, source_target_pairs={{0,3},{1,0},{2,1},{3,2},{4,7},{5,4},{6,5},{7,6},{8,11},{9,8},{10,9... | collective-permute-start | bytes 3735560 | tf_op jit(solution)/shard_map/ppermute | solution.py:26
  8.5 2.0 copy-start.30
  8.5 2.2 copy-start.32
  8.5 2.3 copy-start.36
  20.2 3.3 %copy-start.2 = (f32[1024,2048]{1,0:T(8,128)}, f32[1024,2048]{1,0:T(8,128)S(1)}, u32[]{:S(2)}) copy-start(f32[1024,2048]{1,0:T(8,128)S(1)} %get-tuple-element.77.refs_5_) | copy-start | bytes 25165828
  23.5 2.0 copy-start.6
  25.5 1.9 copy-start.12
  27.5 2.1 copy-start.18
  38.9 5.0 %collective-permute-start.5 = (bf16[2432,256]{1,0:T(8,128)(2,1)}, bf16[2432,256]{1,0:T(8,128)(2,1)}, u32[]{:S(2)}, u32[]{:S(2)}) collective-permute-start(bf16[2432,256]{1,0:T(8,128)(2,1)} %collective-permute-done.refs_2_), channel_id=1, source_target_pairs={{0,4},{4,0},{1,5},{5,1},{2,6},{6,2},{3,7},{7,3},{8,12},{12,8},{9,1... | collective-permute-start | bytes 3735560 | tf_op jit(solution)/shard_map/ppermute | solution.py:26
  38.9 23.8 %collective-permute-start.4 = (bf16[2432,256]{1,0:T(8,128)(2,1)S(1)}, bf16[2432,256]{1,0:T(8,128)(2,1)}, u32[]{:S(2)}, u32[]{:S(2)}) collective-permute-start(bf16[2432,256]{1,0:T(8,128)(2,1)S(1)} %collective-permute-done.1.refs_2_), channel_id=1, source_target_pairs={{0,4},{4,0},{1,5},{5,1},{2,6},{6,2},{3,7},{7,3},{8,12},{12,8},{9,1... | collective-permute-start | bytes 3735560 | tf_op jit(solution)/shard_map/ppermute | solution.py:26
  39.4 40.9 %collective-permute-start.2 = (bf16[1216,256]{1,0:T(8,128)(2,1)}, bf16[1216,256]{1,0:T(8,128)(2,1)S(1)}, u32[]{:S(2)}, u32[]{:S(2)}) collective-permute-start(bf16[1216,256]{1,0:T(8,128)(2,1)} %slice.39), channel_id=1, source_target_pairs={{0,1},{1,2},{2,3},{3,0},{4,5},{5,6},{6,7},{7,4},{8,9},{9,10},{10,1... | collective-permute-start | bytes 1867784 | tf_op jit(solution)/shard_map/ppermute | solution.py:26
  40.9 39.4 %collective-permute-start.3 = (bf16[1216,256]{1,0:T(8,128)(2,1)}, bf16[1216,256]{1,0:T(8,128)(2,1)S(1)}, u32[]{:S(2)}, u32[]{:S(2)}) collective-permute-start(bf16[1216,256]{1,0:T(8,128)(2,1)} %slice.40), channel_id=1, source_target_pairs={{0,3},{1,0},{2,1},{3,2},{4,7},{5,4},{6,5},{7,6},{8,11},{9,8},{10,9... | collective-permute-start | bytes 1867784 | tf_op jit(solution)/shard_map/ppermute | solution.py:26
  43.9 3.4 %copy-start.3 = (f32[1024,2048]{1,0:T(8,128)S(1)}, f32[1024,2048]{1,0:T(8,128)}, u32[]{:S(2)}) copy-start(f32[1024,2048]{1,0:T(8,128)} %copy-done.2) | copy-start | bytes 25165828
  47.3 2.2 copy-start.7
  49.5 2.2 copy-start.13
  51.7 2.2 copy-start.19
  53.9 1.4 copy-start.23
  69.8 3.3 %copy-start.4 = (f32[1024,2048]{1,0:T(8,128)}, f32[1024,2048]{1,0:T(8,128)S(1)}, u32[]{:S(2)}) copy-start(f32[1024,2048]{1,0:T(8,128)S(1)} %get-tuple-element.94.refs_5_) | copy-start | bytes 25165828
  73.2 2.0 copy-start.8
  75.1 1.9 copy-start.14
  77.1 2.1 copy-start.20
  80.5 3.2 %collective-permute-start.6 = (bf16[2432,256]{1,0:T(8,128)(2,1)S(1)}, bf16[2432,256]{1,0:T(8,128)(2,1)}, u32[]{:S(2)}, u32[]{:S(2)}) collective-permute-start(bf16[2432,256]{1,0:T(8,128)(2,1)S(1)} %constant_dynamic-update-slice_fusion.refs_2_), channel_id=1, source_target_pairs={{0,4},{4,0},{1,5},{5,1},{2,6},{6,2},{3,7},{7,3},{8,12},{12,8},{9,1... | collective-permute-start | bytes 3735560 | tf_op jit(solution)/shard_map/ppermute | solution.py:26
  83.6 2.2 copy-start.9
  85.8 2.2 copy-start.15
  88.0 2.2 copy-start.21
  100.1 1.9 copy-start.16
  103.2 30.5 %copy-start.10 = (bf16[2048,1024]{1,0:T(8,128)(2,1)}, bf16[2048,1024]{1,0:T(8,128)(2,1)S(1)}, u32[]{:S(2)}) copy-start(bf16[2048,1024]{1,0:T(8,128)(2,1)S(1)} %get-tuple-element.106.second) | copy-start | bytes 12582916
  103.2 30.6 %copy-start.39 = (bf16[1024,1024]{1,0:T(8,128)(2,1)}, bf16[1024,1024]{1,0:T(8,128)(2,1)S(1)}, u32[]{:S(2)}) copy-start(bf16[1024,1024]{1,0:T(8,128)(2,1)S(1)} %get-tuple-element.103.residual) | copy-start | bytes 6291460
  135.0 3.0 %copy-start.51 = (s32[8]{0:T(128)S(1)}, s32[8]{0:T(128)}, u32[]{:S(2)}) copy-start(s32[8]{0:T(128)} %param.13) | copy-start | bytes 100
  135.0 3.6 %copy-start.47 = (bf16[32,32,768]{2,1,0:T(8,128)(2,1)S(1)}, bf16[32,32,768]{2,1,0:T(8,128)(2,1)}, u32[]{:S(2)}) copy-start(bf16[32,32,768]{2,1,0:T(8,128)(2,1)} %copy-done.46) | copy-start | bytes 4718596
  143.4 27.8 %all-to-all-start.1 = ((bf16[32,32,768]{2,1,0:T(8,128)(2,1)}), bf16[32,32,768]{2,1,0:T(8,128)(2,1)}, u32[]{:S(2)}, u32[]{:S(2)}) async-start(bf16[32,32,768]{2,1,0:T(8,128)(2,1)} %bitcast.105), calls=%async_computation.1 | async-start | bytes 3145728 | tf_op jit(solution)/shard_map/all_to_all | solution.py:425
  171.2 3.8 %copy-start.17 = (bf16[1024,2048]{1,0:T(8,128)(2,1)S(1)}, bf16[1024,2048]{1,0:T(8,128)(2,1)}, u32[]{:S(2)}) copy-start(bf16[1024,2048]{1,0:T(8,128)(2,1)} %copy-done.16) | copy-start | bytes 12582916
  171.2 3.9 %copy-start.40 = (bf16[1024,1024]{1,0:T(8,128)(2,1)S(1)}, bf16[1024,1024]{1,0:T(8,128)(2,1)}, u32[]{:S(2)}) copy-start(bf16[1024,1024]{1,0:T(8,128)(2,1)} %copy-done.39) | copy-start | bytes 6291460
  175.0 11.1 %copy-start.26 = (bf16[1024,1024]{1,0:T(8,128)(2,1)}, bf16[1024,1024]{1,0:T(8,128)(2,1)S(1)}, u32[]{:S(2)}) copy-start(bf16[1024,1024]{1,0:T(8,128)(2,1)S(1)} %convolution_convert_fusion.resid_grad) | copy-start | bytes 6291460
  186.2 1.7 copy-start.33
  187.8 14.0 %collective-permute-start.7 = (bf16[4,384,1024]{2,1,0:T(8,128)(2,1)}, bf16[4,384,1024]{2,1,0:T(8,128)(2,1)}, u32[]{:S(2)}, u32[]{:S(2)}) collective-permute-start(bf16[4,384,1024]{2,1,0:T(8,128)(2,1)} %get-tuple-element.104), channel_id=1, source_target_pairs={{0,4},{4,0},{1,5},{5,1},{2,6},{6,2},{3,7},{7,3},{8,12},{12,8},{9,1... | collective-permute-start | bytes 9437192 | tf_op jit(solution)/shard_map/ppermute | solution.py:26
  187.8 3.4 %copy-start.5 = (f32[1024,2048]{1,0:T(8,128)S(1)}, f32[1024,2048]{1,0:T(8,128)}, u32[]{:S(2)}) copy-start(f32[1024,2048]{1,0:T(8,128)} %get-tuple-element.107.slope) | copy-start | bytes 25165828
  191.2 2.2 copy-start.11
  193.4 1.6 copy-start.27
  195.0 6.9 %copy-start.34 = (bf16[4,384,1024]{2,1,0:T(8,128)(2,1)S(1)}, bf16[4,384,1024]{2,1,0:T(8,128)(2,1)}, u32[]{:S(2)}) copy-start(bf16[4,384,1024]{2,1,0:T(8,128)(2,1)} %copy-done.33) | copy-start | bytes 9437188
  201.0 5.2 %collective-permute-start.8 = (bf16[1,512,1024]{2,1,0:T(8,128)(2,1)S(1)}, bf16[1,512,1024]{2,1,0:T(8,128)(2,1)S(1)}, u32[]{:S(2)}, u32[]{:S(2)}) collective-permute-start(bf16[1,512,1024]{2,1,0:T(8,128)(2,1)S(1)} %get-tuple-element.110), channel_id=1, source_target_pairs={{0,4},{4,0},{1,5},{5,1},{2,6},{6,2},{3,7},{7,3},{8,12},{12,8},{9,1... | collective-permute-start | bytes 3145736 | tf_op jit(solution)/shard_map/ppermute | solution.py:26
  204.8 4.6 %slice-start = ((s8[8388608]{0:T(1024)(128)(4,1)}), s8[4194304]{0:T(1024)(128)(4,1)S(1)}, s32[]{:S(2)}) async-start(s8[8388608]{0:T(1024)(128)(4,1)} %bitcast.92), calls=%async_computation.4 | async-start | bytes 8388608
  205.2 1.5 copy-start.42
  205.2 1.6 copy-start.44
  205.3 20.9 %collective-permute-start.12 = (bf16[2,192,1024]{2,1,0:T(8,128)(2,1)S(1)}, bf16[2,192,1024]{2,1,0:T(8,128)(2,1)}, u32[]{:S(2)}, u32[]{:S(2)}) collective-permute-start(bf16[2,192,1024]{2,1,0:T(8,128)(2,1)S(1)} %dynamic-slice_bitcast_fusion), channel_id=1, source_target_pairs={{0,96},{96,0},{32,64},{64,32},{1,97},{97,1},{33,65},{65,33},{2,98}... | collective-permute-start | bytes 2359304 | tf_op jit(solution)/shard_map/ppermute | solution.py:301
  206.1 3.5 %slice-start.1 = ((s8[8388608]{0:T(1024)(128)(4,1)}), s8[4194304]{0:T(1024)(128)(4,1)S(1)}, s32[]{:S(2)}) async-start(s8[8388608]{0:T(1024)(128)(4,1)} %bitcast.92), calls=%async_computation.5 | async-start | bytes 8388608
  206.1 20.0 %collective-permute-start.11 = (bf16[2,192,1024]{2,1,0:T(8,128)(2,1)S(1)}, bf16[2,192,1024]{2,1,0:T(8,128)(2,1)}, u32[]{:S(2)}, u32[]{:S(2)}) collective-permute-start(bf16[2,192,1024]{2,1,0:T(8,128)(2,1)S(1)} %dynamic-slice_bitcast_fusion.1), channel_id=1, source_target_pairs={{0,32},{32,0},{64,96},{96,64},{1,33},{33,1},{65,97},{97,65},{2,34}... | collective-permute-start | bytes 2359304 | tf_op jit(solution)/shard_map/ppermute | solution.py:301
  206.8 3.6 %copy-start.28 = (bf16[1024,1024]{1,0:T(8,128)(2,1)S(1)}, bf16[1024,1024]{1,0:T(8,128)(2,1)}, u32[]{:S(2)}) copy-start(bf16[1024,1024]{1,0:T(8,128)(2,1)} %copy-done.26) | copy-start | bytes 6291460
  207.7 13.9 %collective-permute-start.9 = (bf16[2,16,8,1024]{3,2,1,0:T(8,128)(2,1)S(1)}, bf16[2,16,8,1024]{3,2,1,0:T(8,128)(2,1)S(1)}, u32[]{:S(2)}, u32[]{:S(2)}) collective-permute-start(bf16[2,16,8,1024]{3,2,1,0:T(8,128)(2,1)S(1)} %bitcast.112), channel_id=1, source_target_pairs={{0,1},{1,0},{2,3},{3,2},{4,5},{5,4},{6,7},{7,6},{8,9},{9,8},{10,11... | collective-permute-start | bytes 1572872 | tf_op jit(solution)/shard_map/ppermute | solution.py:301
  221.7 4.5 %copy-start.49 = (bf16[2,16,8,1024]{3,2,1,0:T(8,128)(2,1)}, bf16[2,16,8,1024]{3,2,1,0:T(8,128)(2,1)S(1)}, u32[]{:S(2)}) copy-start(bf16[2,16,8,1024]{3,2,1,0:T(8,128)(2,1)S(1)} %collective-permute-done.9) | copy-start | bytes 1572868
  226.2 3.0 %collective-permute-start.13 = (bf16[1,512,1024]{2,1,0:T(8,128)(2,1)}, bf16[1,512,1024]{2,1,0:T(8,128)(2,1)}, u32[]{:S(2)}, u32[]{:S(2)}) collective-permute-start(bf16[1,512,1024]{2,1,0:T(8,128)(2,1)} %get-tuple-element.117), channel_id=1, source_target_pairs={{0,4},{4,0},{1,5},{5,1},{2,6},{6,2},{3,7},{7,3},{8,12},{12,8},{9,1... | collective-permute-start | bytes 3145736 | tf_op jit(solution)/shard_map/ppermute | solution.py:26
  228.3 6.2 %copy-start.45 = (bf16[2,2,1,192,1024]{4,3,2,1,0:T(8,128)(2,1)S(1)}, bf16[2,2,1,192,1024]{4,3,2,1,0:T(8,128)(2,1)}, u32[]{:S(2)}) copy-start(bf16[2,2,1,192,1024]{4,3,2,1,0:T(8,128)(2,1)} %copy-done.44) | copy-start | bytes 4718596
  230.8 6.6 %copy-start.48 = (bf16[1,512,1024]{2,1,0:T(8,128)(2,1)}, bf16[1,512,1024]{2,1,0:T(8,128)(2,1)S(1)}, u32[]{:S(2)}) copy-start(bf16[1,512,1024]{2,1,0:T(8,128)(2,1)S(1)} %add_convert_fusion.1) | copy-start | bytes 3145732
  230.8 5.1 %copy-start.43 = (bf16[2,2,1,192,1024]{4,3,2,1,0:T(8,128)(2,1)S(1)}, bf16[2,2,1,192,1024]{4,3,2,1,0:T(8,128)(2,1)}, u32[]{:S(2)}) copy-start(bf16[2,2,1,192,1024]{4,3,2,1,0:T(8,128)(2,1)} %copy-done.42) | copy-start | bytes 4718596
  231.7 16.2 %collective-permute-start.15 = (bf16[2,16,8,1024]{3,2,0,1:T(8,128)(2,1)}, bf16[2,16,8,1024]{3,2,0,1:T(8,128)(2,1)S(1)}, u32[]{:S(2)}, u32[]{:S(2)}) collective-permute-start(bf16[2,16,8,1024]{3,2,0,1:T(8,128)(2,1)} %dynamic-slice_bitcast_fusion.2), channel_id=1, source_target_pairs={{0,3},{3,0},{1,2},{2,1},{4,7},{7,4},{5,6},{6,5},{8,11},{11,8},{9,1... | collective-permute-start | bytes 1572872 | tf_op jit(solution)/shard_map/ppermute | solution.py:301
  238.3 12.4 %collective-permute-start.14 = (bf16[192,1024]{1,0:T(8,128)(2,1)}, bf16[192,1024]{1,0:T(8,128)(2,1)}, u32[]{:S(2)}, u32[]{:S(2)}) collective-permute-start(bf16[192,1024]{1,0:T(8,128)(2,1)} %get-tuple-element.147), channel_id=1, source_target_pairs={{0,96},{96,0},{32,64},{64,32},{1,97},{97,1},{33,65},{65,33},{2,98}... | collective-permute-start | bytes 1179656 | tf_op jit(solution)/shard_map/ppermute | solution.py:301
  240.2 18.7 %collective-permute-start.10 = (bf16[16,8,1024]{2,1,0:T(8,128)(2,1)}, bf16[16,8,1024]{2,1,0:T(8,128)(2,1)}, u32[]{:S(2)}, u32[]{:S(2)}) collective-permute-start(bf16[16,8,1024]{2,1,0:T(8,128)(2,1)} %dynamic-slice_bitcast_fusion.6), channel_id=1, source_target_pairs={{0,3},{3,0},{1,2},{2,1},{4,7},{7,4},{5,6},{6,5},{8,11},{11,8},{9,1... | collective-permute-start | bytes 786440 | tf_op jit(solution)/shard_map/ppermute | solution.py:301
  240.6 11.3 %collective-permute-start.16 = (bf16[192,1024]{1,0:T(8,128)(2,1)}, bf16[192,1024]{1,0:T(8,128)(2,1)S(1)}, u32[]{:S(2)}, u32[]{:S(2)}) collective-permute-start(bf16[192,1024]{1,0:T(8,128)(2,1)} %get-tuple-element.146), channel_id=1, source_target_pairs={{0,32},{32,0},{64,96},{96,64},{1,33},{33,1},{65,97},{97,65},{2,34}... | collective-permute-start | bytes 1179656 | tf_op jit(solution)/shard_map/ppermute | solution.py:301
  253.0 20.3 %all-to-all-start.3 = ((bf16[16,24,1024]{2,1,0:T(8,128)(2,1)}), bf16[16,24,1024]{2,1,0:T(8,128)(2,1)S(1)}, u32[]{:S(2)}, u32[]{:S(2)}) async-start(bf16[16,24,1024]{2,1,0:T(8,128)(2,1)} %bitcast.45), calls=%async_computation.3 | async-start | bytes 1572864 | tf_op jit(solution)/shard_map/all_to_all | solution.py:467
  257.0 15.3 %collective-permute-start.17 = (bf16[16,8,1024]{2,1,0:T(8,128)(2,1)S(1)}, bf16[16,8,1024]{2,1,0:T(8,128)(2,1)S(1)}, u32[]{:S(2)}, u32[]{:S(2)}) collective-permute-start(bf16[16,8,1024]{2,1,0:T(8,128)(2,1)S(1)} %dynamic-slice_bitcast_fusion.5), channel_id=1, source_target_pairs={{0,1},{1,0},{2,3},{3,2},{4,5},{5,4},{6,7},{7,6},{8,9},{9,8},{10,11... | collective-permute-start | bytes 786440 | tf_op jit(solution)/shard_map/ppermute | solution.py:301
  272.3 17.4 %copy-start.1 = (f32[8,768]{1,0:T(8,128)S(1)}, f32[8,768]{1,0:T(8,128)}, u32[]{:S(2)}) copy-start(f32[8,768]{1,0:T(8,128)} %param.11) | copy-start | bytes 73732
  273.3 15.7 %all-to-all-start.2 = ((bf16[16,16,1024]{2,1,0:T(8,128)(2,1)}), bf16[16,16,1024]{2,1,0:T(8,128)(2,1)S(1)}, u32[]{:S(2)}, u32[]{:S(2)}) async-start(bf16[16,16,1024]{2,1,0:T(8,128)(2,1)} %pad_maximum_fusion.1), calls=%async_computation.2 | async-start | bytes 1048576 | tf_op jit(solution)/shard_map/all_to_all | solution.py:468
  (11 other events, 12.6 us)

commit v4 on v3

--- a/solution.py
+++ b/solution.py
@@ -28,6 +28,10 @@
 
 def dot(a, b, contract=((1,), (0,))):
     return lax.dot_general(a, b, (contract, ((), ())), preferred_element_type=F32)
+
+
+def in_hbm(x):
+    return pltpu.with_memory_space_constraint(x, pltpu.HBM)
 
 
 def params(mib):
@@ -102,13 +106,14 @@
         shape, lambda i, s: (0,) * len(shape), pipeline_mode=pl.Buffered(1)
     )
     by_rows = lambda cols: pl.BlockSpec((block_rows, cols), lambda i, s: (i, 0))
-    in_place = pl.BlockSpec(memory_space=pl.ANY)
+    in_place = pl.BlockSpec(memory_space=pltpu.HBM)
     in_specs = [by_rows(width), whole(mine.shape), whole(theirs.shape)]
     args = [tokens, mine, theirs]
     aliases = {}
     if not first_call:
         slope, hidden, second, head, total = carried
-        args += [total, slope, hidden, second, head]
+        args += [total, in_hbm(slope), in_hbm(hidden), in_hbm(second)]
+        args += [head if last_call else in_hbm(head)]
         in_specs += [by_rows(width), in_place, in_place, in_place]
         in_specs += [whole((out_width, width)) if last_call else in_place]
         aliases = {5: 0, 6: 1, 7: 2}
@@ -187,26 +192,18 @@
         term = score.astype(BF16).astype(F32)
         out = jnp.where(line == i, term, out)
         score = score - term
-    return jnp.where(lane == 2 * place[2] + place[1], out, 0.0)
-
-
-def early_kernel(place, hidden, resid_grad, residual, grad_rows, scalars, keep, send):
+    return jnp.where(lane == 2 * place[0] + place[1], out, 0.0)
+
+
+def early_kernel(place, hidden, resid_grad, keep, send):
     second = dot(hidden[...], resid_grad[...], ((0,), (0,)))
-    head = dot(residual[...], grad_rows[...], ((0,), (0,)))
-    width, out_width = second.shape[1], head.shape[1]
-    second = second.reshape(RING, 2, RING, -1, width)
-    head = head.reshape(RING, 2, RING, -1, out_width)
-    blank = riders(place, scalars, (head.shape[3], width - out_width))
-    blank = jnp.broadcast_to(blank, (*head.shape[:3], *blank.shape))
-    both = jnp.concatenate([second, jnp.concatenate([head, blank], 4)], 3)
-    both = both.reshape(RING, 2, -1, width)
-    store_halves(place[1], both, keep, send)
-
-
-def early_grads(place, hidden, resid_grad, residual, grad_rows, scalars):
+    store_halves(place[1], second.reshape(RING, 2, -1, second.shape[1]), keep, send)
+
+
+def early_grads(place, hidden, resid_grad):
     rows, hid = hidden.shape
-    width, out_width = residual.shape[1], grad_rows.shape[1]
-    lines = (hid + width) // RING // 2
+    width = resid_grad.shape[1]
+    lines = hid // RING // 2
     gray = lambda i: 2 * ((i // 2 + i) % 2) + i // 2
     out = pl.BlockSpec((1, lines, width), lambda i, s: (gray(i), 0, 0))
     return pl.pallas_call(
@@ -217,38 +214,58 @@
             in_specs=[
                 pl.BlockSpec((rows, hid // RING), lambda i, s: (0, i)),
                 once((rows, width)),
-                pl.BlockSpec((rows, width // RING), lambda i, s: (0, i)),
-                once((rows, out_width)),
-                pl.BlockSpec(memory_space=pltpu.SMEM),
             ],
             out_specs=[out, out],
         ),
         out_shape=[jax.ShapeDtypeStruct((RING, lines, width), BF16)] * 2,
-        compiler_params=params(32),
+        compiler_params=params(28),
         cost_estimate=pl.CostEstimate(
-            flops=2 * rows * width * (hid + out_width), bytes_accessed=18 * MIB, transcendentals=0
+            flops=2 * rows * width * hid, bytes_accessed=12 * MIB, transcendentals=0
         ),
         name="early_grads",
-    )(place, hidden, resid_grad, residual, grad_rows, scalars)
-
-
-def late_kernel(place, resid_grad, second, slope, tokens, keep, send):
+    )(place, in_hbm(hidden), resid_grad)
+
+
+def late_kernel(steps, place, resid_grad, second, slope, tokens, *refs):
+    keep, send = refs[-2:]
     hidden_grad = dot(resid_grad[...], second[...], ((1,), (1,)))
     preact_grad = (slope[...] * hidden_grad).astype(BF16)
     first = dot(tokens[...], preact_grad, ((0,), (0,)))
     cols = first.shape[1]
-    parts = first.reshape(16, 2, RING, -1, cols)
-    parts = jnp.stack([parts[:, :, i] for i in (0, 3, 1, 2)], 2)
-    store_halves(place[1], parts.reshape(16, 2, -1, cols), keep, send)
-
-
-def late_grads(place, part, resid_grad, second, slope, tokens):
+
+    def store(*grads):
+        parts = jnp.concatenate([g.reshape(16, 2, RING, -1, cols) for g in grads], 3)
+        parts = jnp.stack([parts[:, :, i] for i in (0, 3, 1, 2)], 2)
+        store_halves(place[1], parts.reshape(16, 2, -1, cols), keep, send)
+
+    if len(refs) == 2:
+        store(first)
+        return
+    residual, grad_rows, scalars = refs[:3]
+    width, out_width = residual.shape[1], grad_rows.shape[1]
+    for j in range(steps):
+
+        @pl.when(pl.program_id(0) == j)
+        def _(j=j):
+            head = dot(residual[...], grad_rows[:, j * cols : (j + 1) * cols], ((0,), (0,)))
+            if j == steps - 1:
+                blank = riders(place, scalars, (8, width - out_width))
+                blank = jnp.broadcast_to(blank, (width // 8, *blank.shape))
+                head = jnp.concatenate([head, blank.reshape(width, -1)], 1)
+            store(first, head)
+
+
+def late_grads(place, part, resid_grad, second, slope, tokens, *head):
     rows, width = resid_grad.shape
     tile = 2 * LANES
     steps = width // tile
-    out = pl.BlockSpec((1, width // 2, tile), lambda j, s: (0, 0, j))
+    lines = width if head else width // 2
+    out = pl.BlockSpec((1, lines, tile), lambda j, s: (0, 0, j))
+    specs = []
+    if head:
+        specs = [once(head[0].shape), once(head[1].shape), pl.BlockSpec(memory_space=pltpu.SMEM)]
     return pl.pallas_call(
-        late_kernel,
+        functools.partial(late_kernel, steps),
         grid_spec=pltpu.PrefetchScalarGridSpec(
             num_scalar_prefetch=1,
             grid=(steps,),
@@ -257,16 +274,17 @@
                 pl.BlockSpec((tile, width), lambda j, s: (part * steps + j, 0)),
                 pl.BlockSpec((rows, tile), lambda j, s: (0, part * steps + j)),
                 once((rows, width)),
+                *specs,
             ],
             out_specs=[out, out],
         ),
-        out_shape=[jax.ShapeDtypeStruct((1, width // 2, width), BF16)] * 2,
-        compiler_params=params(28),
+        out_shape=[jax.ShapeDtypeStruct((1, lines, width), BF16)] * 2,
+        compiler_params=params(36 if head else 28),
         cost_estimate=pl.CostEstimate(
             flops=4 * rows * width * width, bytes_accessed=12 * MIB, transcendentals=0
         ),
         name="late_grads",
-    )(place, resid_grad, second, slope, tokens)
+    )(place, resid_grad, in_hbm(second), in_hbm(slope), tokens, *head)
 
 
 def add(a, b):
@@ -429,9 +447,19 @@
     at = place(0)
     scalars = jnp.stack([score_part, count_part])
     resid_grad = dot(grad_rows, head).astype(BF16)
-    early = early_grads(at, hidden, resid_grad, residual, grad_rows, scalars)
+    early = early_grads(at, hidden, resid_grad)
     early_in = shift(early[1], "c", 1)
-    late = late_grads(at, 0, after(resid_grad, early[1]), second, slope, tokens)
+    late = late_grads(
+        at,
+        0,
+        after(resid_grad, early[1]),
+        second,
+        slope,
+        tokens,
+        residual,
+        grad_rows,
+        scalars,
+    )
     a_in = shift(late[1], "c", 1)
     x_steps = [ring_chain("x", True), ring_chain("x", False)]
     y_steps = [ring_chain("y", True), ring_chain("y", False)]
@@ -443,41 +471,38 @@
     a_sent = outgoing(a, y_steps[0][0])
     a_in = sent_along(a_sent, y_steps[0][0])
     late = late_grads(at, 1, after(resid_grad, a_sent), second, slope, tokens)
-    b_in = shift(after(late[1], a_in, *early_in), "c", 1)
-    a = kept_plus(a, a_in, y_steps[0][0])
-    a_sent = outgoing(a, y_steps[0][1])
-    a_in = sent_along(a_sent, y_steps[0][1])
-    b = by_ring(add(after(late[0], a_sent), b_in))
+    b_in = shift(after(late[1], *early_in), "c", 1)
+    early = [kept_plus(x, v, steps[0]) for x, v, steps in zip(early, early_in, x_steps)]
+    early_sent = [outgoing(x, steps[1]) for x, steps in zip(early, x_steps)]
+    early_in = [sent_along(x, steps[1]) for x, steps in zip(early_sent, x_steps)]
+    b = by_ring(add(after(late[0], *early_sent), b_in))
     b_sent = outgoing(b, y_steps[1][0])
     b_in = sent_along(b_sent, y_steps[1][0])
-    early = [
-        kept_plus(x, after(v, b_sent), steps[0]) for x, v, steps in zip(early, early_in, x_steps)
-    ]
-    early_sent = [outgoing(x, steps[1]) for x, steps in zip(early, x_steps)]
-    early_in = [sent_along(x, steps[1]) for x, steps in zip(early_sent, x_steps)]
-    b = kept_plus(b, after(b_in, *early_sent), y_steps[1][0])
-    b_sent = outgoing(b, y_steps[1][1])
-    b_in = sent_along(b_sent, y_steps[1][1])
     early = [
         kept_plus(x, after(v, b_sent), steps[1]) for x, v, steps in zip(early, early_in, x_steps)
     ]
     early = jnp.concatenate(early).reshape(16, -1, width)
-    a = kept_plus(a, after(a_in, early), y_steps[0][1])
+    a = kept_plus(a, after(a_in, b_sent), y_steps[0][0])
+    a_sent = outgoing(a, y_steps[0][1])
+    a_in = sent_along(a_sent, y_steps[0][1])
+    b = kept_plus(b, after(b_in, a_sent), y_steps[1][0])
+    b_sent = outgoing(b, y_steps[1][1])
+    b_in = sent_along(b_sent, y_steps[1][1])
+    a = kept_plus(a, after(a_in, b_sent), y_steps[0][1])
     b = kept_plus(b, b_in, y_steps[1][1])
     early = lax.all_to_all(early, ("z", "y"), 0, 0, tiled=True)
     late = lax.all_to_all(jnp.concatenate([a, b], 1), ("x", "z"), 0, 0, tiled=True)
     early = jnp.sum(early.astype(F32), 0)
     late = jnp.sum(late.astype(F32), 0)
-    n_second = shard * RING // 128
-    ride = jnp.sum(early[n_second : n_second + 8, out_width:], 1)
+    n = width // 128
+    ride = jnp.sum(late[n : 2 * n, out_width:], 1)
     score_total = ride[0] + ride[1] + ride[2]
     valid_total = jnp.maximum(ride[3], 1.0)
     scale = 1.0 / valid_total
-    n_first = late.shape[0] // 2
     return (
-        jnp.concatenate([late[:n_first], late[n_first:]], 1) * scale,
-        early[:n_second] * scale,
-        early[n_second:, :out_width] * scale,
+        jnp.concatenate([late[:n], late[2 * n :]], 1) * scale,
+        early * scale,
+        late[n : 2 * n, :out_width] * scale,
         score_total / valid_total,
     )
 

time: 292 us -> 266 us (0.911)
  local copies, waits for them, and re-layouts: 72.5 us -> 39.1 us
  blocking collectives: 30.3 us -> 56.8 us
  waiting for transfers between devices: 66.4 us -> 46.3 us
  Pallas kernels: 55.2 us -> 62.3 us
  starting transfers between devices: 31.9 us -> 28.2 us
    unnamed x110 -> x75, local copies, waits for them, and re-layouts: 60.2 us -> 29.4 us
    all_to_all x0 -> x1, blocking collectives: none -> 26.4 us  [per_device(): lax.all_to_all(grad_raw.reshape(32, members * own, out_width), group, 0,...]
    all_to_all x1 -> x0, waiting for transfers between devices: 21.7 us -> none  [per_device(): lax.all_to_all(grad_raw.reshape(32, members * own, out_width), group, 0,...]
    all_to_all x1, waiting for transfers between devices: 5.33 us -> 12.3 us  [per_device(): lax.all_to_all(jnp.concatenate([a, b], 1), ('x', 'z'), 0, 0, tiled=True)]
    pallas_call x2, Pallas kernels: 12.9 us -> 19.5 us  [late_grads(): pl.pallas_call(functools.partial(late_kernel, steps), grid_spec=pltpu.Pre...]
    all_to_all x1 -> x0, starting transfers between devices: 4.7 us -> none  [per_device(): lax.all_to_all(grad_raw.reshape(32, members * own, out_width), group, 0,...]
    ppermute x8, waiting for transfers between devices: 30.2 us -> 25.5 us  [sent_along(): return lax.ppermute(x, step[1], step[0])]
  transfers between devices with their start and end apart: 21 -> 20, of which waited for: 11 -> 6; matrix products, arithmetic and copies ran while one was open for 8% -> 8% of each run, Pallas kernels for 12% -> 16%
where the time goes in v4:
time: 266 us; the launch traced here: 265 us
  Pallas kernels  62.3 us (23%)
  blocking collectives  56.8 us (21%)
  waiting for transfers between devices  46.3 us (17%)
  local copies, waits for them, and re-layouts  39.1 us (15%)
  starting transfers between devices  28.2 us (11%)
  other arithmetic  19.3 us (7%)
  matrix products  7.58 us (3%)
  between operations  4.92 us (2%)
    pallas_call x4, Pallas kernels, forward_part(): pl.pallas_call(functools.partial(forward_kernel, first_call, last_call, b...  32.3 us
    all_to_all x1, blocking collectives, per_device(): gathered = lax.all_to_all(forecast, group, 0, 0, tiled=True)  30.3 us
    unnamed x75, local copies, waits for them, and re-layouts  29.4 us
    all_to_all x1, blocking collectives, per_device(): lax.all_to_all(grad_raw.reshape(32, members * own, out_width), group, 0,...  26.4 us
    ppermute x8, waiting for transfers between devices, sent_along(): return lax.ppermute(x, step[1], step[0])  25.5 us
    pallas_call x2, Pallas kernels, late_grads(): pl.pallas_call(functools.partial(late_kernel, steps), grid_spec=pltpu.Pre...  19.5 us
    all_to_all x1, waiting for transfers between devices, per_device(): lax.all_to_all(jnp.concatenate([a, b], 1), ('x', 'z'), 0, 0, tiled=True)  12.3 us
    convert_element_type x11, other arithmetic, add(): return (a.astype(F32) + b.astype(F32)).astype(BF16)  12.2 us
  transfers between devices with their start and end apart: 20, of which 6 were waited for; matrix products, arithmetic and copies ran while one was open for 8% of the time, Pallas kernels for 16%

profile of v4, /device:TPU:0, one launch (start us, length us, event | category | flops | bytes accessed | tf_op | source)
XLA Modules:
  0.0 264.5 jit_solution(15358892037623566527)
XLA Ops:
  0.7 1.2 copy-done.13
  1.9 1.2 copy-done.15
  3.1 1.0 copy-done.22
  4.1 1.2 packed.2.refs_2_
  5.3 1.7 collective-permute-start
  7.0 1.6 collective-permute-start.1
  8.6 1.9 copy.29
  10.9 1.0 copy-done.24
  12.0 1.3 copy-done.25
  13.3 6.9 %forward_part.4 = (f32[1024,2048]{1,0:T(8,128)S(1)}, bf16[1024,2048]{1,0:T(8,128)(2,1)S(1)}, bf16[2048,1024]{1,0:T(8,128)(2,1)S(1)}, bf16[768,1024]{1,0:T(8,128)(2,1)S(1)}, f32[1024,1024]{1,0:T(8,128)S(1)}) custom-call(s32[3]{0:T(128)S(1)} %add_add_fusion.refs_0_.place, bf16[1024,1024]{1,0:T(8,128)(2,1)S(1)} %bitcast.93, bf16[2432,256]{1,0:T(8,128)(2,1)} %packed.2.refs_2_, ...), custom_call_target="tpu_custom_call" | custom-call | flops 2147483648 | bytes 12582912 | tf_op jit(solution)/shard_map/forward_part/pallas_call | solution.py:146
  20.3 3.3 %copy-done.2 = f32[1024,2048]{1,0:T(8,128)} copy-done((f32[1024,2048]{1,0:T(8,128)}, f32[1024,2048]{1,0:T(8,128)S(1)}, u32[]{:S(2)}) %copy-start.2) | copy-done | bytes 8388632
  23.5 1.9 copy-done.3
  25.5 2.0 copy-done.4
  27.5 2.0 copy-done.5
  29.4 1.2 copy-done.9
  30.6 5.5 %collective-permute-done.refs_2_ = bf16[2432,256]{1,0:T(8,128)(2,1)} collective-permute-done((bf16[2432,256]{1,0:T(8,128)(2,1)}, bf16[2432,256]{1,0:T(8,128)(2,1)}, u32[]{:S(2)}, u32[]{:S(2)}) %collective-permute-start) | collective-permute-done | bytes 1245216 | tf_op jit(solution)/shard_map/ppermute | solution.py:26
  36.1 2.0 slice.36
  38.1 0.9 slice.37
  39.5 1.5 collective-permute-start.2
  41.0 1.7 collective-permute-start.3
  42.9 1.1 collective-permute-done.5.refs_3_
  44.0 2.2 copy-done.6
  46.2 8.5 %forward_part.5 = (f32[1024,2048]{1,0:T(8,128)}, bf16[1024,2048]{1,0:T(8,128)(2,1)}, bf16[2048,1024]{1,0:T(8,128)(2,1)}, bf16[768,1024]{1,0:T(8,128)(2,1)}, f32[1024,1024]{1,0:T(8,128)S(1)}) custom-call(s32[3]{0:T(128)S(1)} %add_add_fusion.3.refs_0_, ...), custom_call_target="tpu_custom_call", output_to_operand_aliasing={{0}: (5, {}), {1}: (6, {}), {2}: (7, {}), {3}: (8, {}), {4}... | custom-call | flops 2147483648 | bytes 12582912 | tf_op jit(solution)/shard_map/forward_part/pallas_call | solution.py:146
  54.7 8.0 %forward_part.6 = (f32[1024,2048]{1,0:T(8,128)}, bf16[1024,2048]{1,0:T(8,128)(2,1)}, bf16[2048,1024]{1,0:T(8,128)(2,1)}, bf16[768,1024]{1,0:T(8,128)(2,1)}, f32[1024,1024]{1,0:T(8,128)S(1)}) custom-call(s32[3]{0:T(128)S(1)} %add_add_fusion.2.refs_0_, ...), custom_call_target="tpu_custom_call", output_to_operand_aliasing={{0}: (5, {}), {1}: (6, {}), {2}: (7, {}), {3}: (8, {}), {4}... | custom-call | flops 2147483648 | bytes 12582912 | tf_op jit(solution)/shard_map/forward_part/pallas_call | solution.py:146
  62.7 2.0 copy-done.7
  66.1 1.9 collective-permute-done.6.refs_3_
  67.9 2.2 copy-done.8
  70.1 1.4 copy-done.10
  71.5 8.9 %forward_part.7 = (f32[1024,2048]{1,0:T(8,128)}, bf16[1024,2048]{1,0:T(8,128)(2,1)}, bf16[2048,1024]{1,0:T(8,128)(2,1)}, bf16[768,1024]{1,0:T(8,128)(2,1)S(1)}, ...) custom-call(s32[3]{0:T(128)S(1)} %add_add_fusion.1.refs_0_, ...), custom_call_target="tpu_custom_call", output_to_operand_aliasing={{0}: (5, {}), {1}: (6, {}), {2}: (7, {})} | custom-call | flops 2147483648 | bytes 12582912 | tf_op jit(solution)/shard_map/forward_part/pallas_call | solution.py:146
  80.4 30.3 %all_to_all.20 = bf16[32,32,768]{2,1,0:T(8,128)(2,1)S(1)} all-to-all(bf16[32,32,768]{2,1,0:T(8,128)(2,1)S(1)} %bitcast.101), channel_id=1, replica_groups=mesh['x'=4,'z'=4,'c'=2,'y'=4] {'x','z','c'}, dimensions={0} | all-to-all | bytes 3145728 | tf_op jit(solution)/shard_map/all_to_all | solution.py:440
  112.3 3.0 %fusion.34 = (f32[8]{0:T(128)S(1)}, f32[8,128]{1,0:T(8,128)S(1)}, f32[8,128,128]{1,2,0:T(8,128)S(1)}) fusion(bf16[128,8,768]{2,1,0:T(8,128)(2,1)} %bitcast.109, f32[8,128]{1,0:T(8,128)S(1)} %copy.33), kind=kOutput, calls=%fused_computation.76 | convolution fusion | flops 202243072 | bytes 2105376 | tf_op jit(solution)/shard_map/mpo,npo->pmn/dot_general | solution.py:376
  115.9 2.8 %fusion.8 = bf16[128,8,768]{2,0,1:T(8,128)(2,1)S(1)} fusion(f32[128,8]{0,1:T(8,128)S(1)} %bitcast.115, f32[128,8]{0,1:T(8,128)S(1)} %copy.32, f32[8,768]{1,0:T(8,128)S(1)} %broadcast_select_fusion, f32[8]{0:T(128)S(1)} %get-tuple-element.140, bf16[128,8,768]{2,1,0:T(8,128)(2,1)S(1)} %bitcast.110, f32[8,128,128]{1,2,0:T(8,128)S(1)} %get-tuple-element.141), kind=kOutput, calls=%fused_computation.15 | convolution fusion | flops 1215168512 | bytes 3702816 | tf_op jit(solution)/shard_map/pmn,npo->mpo/dot_general | solution.py:382
  118.7 0.9 copy.39
  119.6 26.4 %all_to_all.21 = bf16[32,32,768]{2,1,0:T(8,128)(2,1)S(1)} all-to-all(bf16[32,32,768]{2,1,0:T(8,128)(2,1)S(1)} %bitcast.108), channel_id=1, replica_groups=mesh['x'=4,'z'=4,'c'=2,'y'=4] {'x','z','c'}, dimensions={0} | all-to-all | bytes 3145728 | tf_op jit(solution)/shard_map/all_to_all | solution.py:443
  146.0 1.8 convolution_convert_fusion.resid_grad
  147.8 9.2 %early_grads.1 = (bf16[4,256,1024]{2,1,0:T(8,128)(2,1)S(1)}, bf16[4,256,1024]{2,1,0:T(8,128)(2,1)}) custom-call(s32[3]{0:T(128)S(1)} %add_add_fusion.refs_0_.place, bf16[1024,2048]{1,0:T(8,128)(2,1)} %get-tuple-element.101.hidden, bf16[1024,1024]{1,0:T(8,128)(2,1)S(1)} %convolution_convert_fusion.resid_grad), custom_call_target="tpu_custom_call" | custom-call | flops 4294967296 | bytes 12582912 | tf_op jit(solution)/shard_map/early_grads/pallas_call | solution.py:209
  157.0 1.3 copy-done.19
  158.3 0.7 collective-permute-start.7
  159.1 1.4 pad_maximum_fusion.2.refs_2_
  160.5 11.1 %late_grads.2 = (bf16[1,1024,1024]{2,1,0:T(8,128)(2,1)S(1)}, bf16[1,1024,1024]{2,1,0:T(8,128)(2,1)}) custom-call(s32[3]{0:T(128)S(1)} %add_add_fusion.refs_0_.place, bf16[1024,1024]{1,0:T(8,128)(2,1)S(1)} %convolution_convert_fusion.resid_grad, bf16[2048,1024]{1,0:T(8,128)(2,1)} %get-tuple-element.104.second, f32[1024,2048]{1,0:T(8,128)} %get-tuple-element.105.slope, ...), custom_call_target="tpu_custom_call" | custom-call | flops 4294967296 | bytes 12582912 | tf_op jit(solution)/shard_map/late_grads/pallas_call | solution.py:267
  171.5 1.3 copy-done.17
  172.9 3.2 %add_convert_fusion.1 = bf16[4,256,1024]{2,1,0:T(8,128)(2,1)S(1)} fusion(bf16[4,256,1024]{2,1,0:T(8,128)(2,1)} %collective-permute-done.7, bf16[4,256,1024]{2,1,0:T(8,128)(2,1)} %copy-done.19), kind=kLoop, calls=%fused_computation.2 | loop fusion | flops 4194304 | bytes 6291456 | tf_op jit(solution)/shard_map/convert_element_type | solution.py:291
  176.4 1.0 collective-permute-start.11
  178.7 2.6 add_convert_fusion
  181.3 1.3 copy-done.28
  182.6 1.1 dynamic-slice_bitcast_fusion
  183.7 8.5 %late_grads.3 = (bf16[1,512,1024]{2,1,0:T(8,128)(2,1)S(1)}, bf16[1,512,1024]{2,1,0:T(8,128)(2,1)}) custom-call(s32[3]{0:T(128)S(1)} %add_add_fusion.refs_0_.place, bf16[1024,1024]{1,0:T(8,128)(2,1)S(1)} %copy-done.12, bf16[2048,1024]{1,0:T(8,128)(2,1)} %get-tuple-element.104.second, f32[1024,2048]{1,0:T(8,128)} %get-tuple-element.105.slope, ...), custom_call_target="tpu_custom_call" | custom-call | flops 4294967296 | bytes 12582912 | tf_op jit(solution)/shard_map/late_grads/pallas_call | solution.py:267
  192.7 1.4 collective-permute-start.9
  194.1 1.4 fusion.28
  195.5 1.3 collective-permute-start.16
  196.8 1.2 fusion.27
  198.1 1.1 collective-permute-start.17
  199.1 1.8 add_convert_fusion.2
  201.0 2.0 collective-permute-start.14
  203.0 15.1 %collective-permute-done.9 = bf16[2,16,16,1024]{3,2,0,1:T(8,128)(2,1)S(1)} collective-permute-done((bf16[2,16,16,1024]{3,2,0,1:T(8,128)(2,1)}, bf16[2,16,16,1024]{3,2,0,1:T(8,128)(2,1)S(1)}, u32[]{:S(2)}, u32[]{:S(2)}) %collective-permute-start.9) | collective-permute-done | bytes 1048608 | tf_op jit(solution)/shard_map/ppermute | solution.py:319
  218.6 0.9 dynamic-slice_bitcast_fusion.1
  219.4 2.7 %collective-permute-start.13 = (bf16[16,16,1024]{2,1,0:T(8,128)(2,1)}, bf16[16,16,1024]{2,1,0:T(8,128)(2,1)S(1)}, u32[]{:S(2)}, u32[]{:S(2)}) collective-permute-start(bf16[16,16,1024]{2,1,0:T(8,128)(2,1)} %dynamic-slice_bitcast_fusion.1), channel_id=1, source_target_pairs={{0,3},{3,0},{1,2},{2,1},{4,7},{7,4},{5,6},{6,5},{8,11},{11,8},{9,1... | collective-permute-start | bytes 1572872 | tf_op jit(solution)/shard_map/ppermute | solution.py:319
  222.6 0.8 pad_maximum_fusion.1
  223.5 4.3 %all-to-all-start.3 = ((bf16[16,16,1024]{2,1,0:T(8,128)(2,1)}), bf16[16,16,1024]{2,1,0:T(8,128)(2,1)S(1)}, u32[]{:S(2)}, u32[]{:S(2)}) async-start(bf16[16,16,1024]{2,1,0:T(8,128)(2,1)} %bitcast.47), calls=%async_computation.3 | async-start | bytes 1048576 | tf_op jit(solution)/shard_map/all_to_all | solution.py:493
  227.8 10.4 %collective-permute-done.13 = bf16[16,16,1024]{2,1,0:T(8,128)(2,1)S(1)} collective-permute-done((bf16[16,16,1024]{2,1,0:T(8,128)(2,1)}, bf16[16,16,1024]{2,1,0:T(8,128)(2,1)S(1)}, u32[]{:S(2)}, u32[]{:S(2)}) %collective-permute-start.13) | collective-permute-done | bytes 524320 | tf_op jit(solution)/shard_map/ppermute | solution.py:319
  238.4 1.0 fusion.31
  239.5 1.0 pad_maximum_fusion
  240.4 5.2 %all-to-all-start.2 = ((bf16[16,24,1024]{2,1,0:T(8,128)(2,1)}), bf16[16,24,1024]{2,1,0:T(8,128)(2,1)S(1)}, u32[]{:S(2)}, u32[]{:S(2)}) async-start(bf16[16,24,1024]{2,1,0:T(8,128)(2,1)} %pad_maximum_fusion), calls=%async_computation.2 | async-start | bytes 1572864 | tf_op jit(solution)/shard_map/all_to_all | solution.py:494
  245.7 12.3 %all-to-all-done.2 = bf16[16,24,1024]{2,1,0:T(8,128)(2,1)S(1)} async-done(((bf16[16,24,1024]{2,1,0:T(8,128)(2,1)}), bf16[16,24,1024]{2,1,0:T(8,128)(2,1)S(1)}, u32[]{:S(2)}, u32[]{:S(2)}) %all-to-all-start.2) | async-done | bytes 786464 | tf_op jit(solution)/shard_map/all_to_all | solution.py:494
  (118 shorter events, 10.7 us)
Async XLA Ops:
  0.6 64.7 %copy-start = (f32[8,768]{1,0:T(8,128)S(1)}, f32[8,768]{1,0:T(8,128)}, u32[]{:S(2)}) copy-start(f32[8,768]{1,0:T(8,128)} %param.11) | copy-start | bytes 73732
  0.7 1.2 copy-start.13
  1.9 1.2 copy-start.15
  3.1 1.0 copy-start.22
  5.3 30.8 %collective-permute-start = (bf16[2432,256]{1,0:T(8,128)(2,1)}, bf16[2432,256]{1,0:T(8,128)(2,1)}, u32[]{:S(2)}, u32[]{:S(2)}) collective-permute-start(bf16[2432,256]{1,0:T(8,128)(2,1)} %packed.2.refs_2_), channel_id=1, source_target_pairs={{0,1},{1,2},{2,3},{3,0},{4,5},{5,6},{6,7},{7,4},{8,9},{9,10},{10,1... | collective-permute-start | bytes 3735560 | tf_op jit(solution)/shard_map/ppermute | solution.py:26
  7.0 29.1 %collective-permute-start.1 = (bf16[2432,256]{1,0:T(8,128)(2,1)}, bf16[2432,256]{1,0:T(8,128)(2,1)S(1)}, u32[]{:S(2)}, u32[]{:S(2)}) collective-permute-start(bf16[2432,256]{1,0:T(8,128)(2,1)} %packed.2.refs_2_), channel_id=1, source_target_pairs={{0,3},{1,0},{2,1},{3,2},{4,7},{5,4},{6,5},{7,6},{8,11},{9,8},{10,9... | collective-permute-start | bytes 3735560 | tf_op jit(solution)/shard_map/ppermute | solution.py:26
  8.6 2.0 copy-start.14
  8.6 2.2 copy-start.16
  8.6 2.3 copy-start.23
  10.9 1.1 copy-start.24
  12.0 1.3 copy-start.25
  20.2 3.3 %copy-start.2 = (f32[1024,2048]{1,0:T(8,128)}, f32[1024,2048]{1,0:T(8,128)S(1)}, u32[]{:S(2)}) copy-start(f32[1024,2048]{1,0:T(8,128)S(1)} %get-tuple-element.76.refs_5_) | copy-start | bytes 25165828
  23.5 1.9 copy-start.3
  25.5 2.0 copy-start.4
  27.5 2.0 copy-start.5
  29.4 1.2 copy-start.9
  39.0 5.0 %collective-permute-start.5 = (bf16[2432,256]{1,0:T(8,128)(2,1)}, bf16[2432,256]{1,0:T(8,128)(2,1)}, u32[]{:S(2)}, u32[]{:S(2)}) collective-permute-start(bf16[2432,256]{1,0:T(8,128)(2,1)} %collective-permute-done.refs_2_), channel_id=1, source_target_pairs={{0,4},{4,0},{1,5},{5,1},{2,6},{6,2},{3,7},{7,3},{8,12},{12,8},{9,1... | collective-permute-start | bytes 3735560 | tf_op jit(solution)/shard_map/ppermute | solution.py:26
  39.0 15.7 %collective-permute-start.4 = (bf16[2432,256]{1,0:T(8,128)(2,1)S(1)}, bf16[2432,256]{1,0:T(8,128)(2,1)}, u32[]{:S(2)}, u32[]{:S(2)}) collective-permute-start(bf16[2432,256]{1,0:T(8,128)(2,1)S(1)} %collective-permute-done.1.refs_2_), channel_id=1, source_target_pairs={{0,4},{4,0},{1,5},{5,1},{2,6},{6,2},{3,7},{7,3},{8,12},{12,8},{9,1... | collective-permute-start | bytes 3735560 | tf_op jit(solution)/shard_map/ppermute | solution.py:26
  39.5 25.2 %collective-permute-start.2 = (bf16[1216,256]{1,0:T(8,128)(2,1)}, bf16[1216,256]{1,0:T(8,128)(2,1)S(1)}, u32[]{:S(2)}, u32[]{:S(2)}) collective-permute-start(bf16[1216,256]{1,0:T(8,128)(2,1)} %slice.36), channel_id=1, source_target_pairs={{0,1},{1,2},{2,3},{3,0},{4,5},{5,6},{6,7},{7,4},{8,9},{9,10},{10,1... | collective-permute-start | bytes 1867784 | tf_op jit(solution)/shard_map/ppermute | solution.py:26
  41.0 23.7 %collective-permute-start.3 = (bf16[1216,256]{1,0:T(8,128)(2,1)}, bf16[1216,256]{1,0:T(8,128)(2,1)S(1)}, u32[]{:S(2)}, u32[]{:S(2)}) collective-permute-start(bf16[1216,256]{1,0:T(8,128)(2,1)} %slice.37), channel_id=1, source_target_pairs={{0,3},{1,0},{2,1},{3,2},{4,7},{5,4},{6,5},{7,6},{8,11},{9,8},{10,9... | collective-permute-start | bytes 1867784 | tf_op jit(solution)/shard_map/ppermute | solution.py:26
  44.0 2.2 copy-start.6
  62.7 2.0 copy-start.7
  64.7 0.7 copy-start.35
  64.8 3.2 %collective-permute-start.6 = (bf16[2432,256]{1,0:T(8,128)(2,1)S(1)}, bf16[2432,256]{1,0:T(8,128)(2,1)}, u32[]{:S(2)}, u32[]{:S(2)}) collective-permute-start(bf16[2432,256]{1,0:T(8,128)(2,1)S(1)} %constant_dynamic-update-slice_fusion.refs_2_), channel_id=1, source_target_pairs={{0,4},{4,0},{1,5},{5,1},{2,6},{6,2},{3,7},{7,3},{8,12},{12,8},{9,1... | collective-permute-start | bytes 3735560 | tf_op jit(solution)/shard_map/ppermute | solution.py:26
  67.9 2.2 copy-start.8
  70.1 1.4 copy-start.10
  80.4 30.6 %copy-start.20 = (bf16[1024,1024]{1,0:T(8,128)(2,1)}, bf16[1024,1024]{1,0:T(8,128)(2,1)S(1)}, u32[]{:S(2)}) copy-start(bf16[1024,1024]{1,0:T(8,128)(2,1)S(1)} %get-tuple-element.106.refs_0_) | copy-start | bytes 6291460
  80.4 30.6 %copy-start.26 = (bf16[768,1024]{1,0:T(8,128)(2,1)}, bf16[768,1024]{1,0:T(8,128)(2,1)S(1)}, u32[]{:S(2)}) copy-start(bf16[768,1024]{1,0:T(8,128)(2,1)S(1)} %get-tuple-element.100) | copy-start | bytes 4718596
  110.8 1.2 copy-start.30
  112.3 3.0 %copy-start.36 = (s32[8]{0:T(128)S(1)}, s32[8]{0:T(128)}, u32[]{:S(2)}) copy-start(s32[8]{0:T(128)} %param.13) | copy-start | bytes 100
  112.3 3.6 %copy-start.31 = (bf16[32,32,768]{2,1,0:T(8,128)(2,1)S(1)}, bf16[32,32,768]{2,1,0:T(8,128)(2,1)}, u32[]{:S(2)}) copy-start(bf16[32,32,768]{2,1,0:T(8,128)(2,1)} %copy-done.30) | copy-start | bytes 4718596
  119.6 26.4 %copy-start.27 = (bf16[768,1024]{1,0:T(8,128)(2,1)S(1)}, bf16[768,1024]{1,0:T(8,128)(2,1)}, u32[]{:S(2)}) copy-start(bf16[768,1024]{1,0:T(8,128)(2,1)} %copy-done.26) | copy-start | bytes 4718596
  147.8 12.7 %copy-start.11 = (bf16[1024,1024]{1,0:T(8,128)(2,1)}, bf16[1024,1024]{1,0:T(8,128)(2,1)S(1)}, u32[]{:S(2)}) copy-start(bf16[1024,1024]{1,0:T(8,128)(2,1)S(1)} %convolution_convert_fusion.resid_grad) | copy-start | bytes 6291460
  147.8 12.6 %copy-start.21 = (bf16[1024,1024]{1,0:T(8,128)(2,1)S(1)}, bf16[1024,1024]{1,0:T(8,128)(2,1)}, u32[]{:S(2)}) copy-start(bf16[1024,1024]{1,0:T(8,128)(2,1)} %copy-done.20) | copy-start | bytes 6291460
  157.0 1.3 copy-start.19
  158.3 14.5 %collective-permute-start.7 = (bf16[4,256,1024]{2,1,0:T(8,128)(2,1)}, bf16[4,256,1024]{2,1,0:T(8,128)(2,1)}, u32[]{:S(2)}, u32[]{:S(2)}) collective-permute-start(bf16[4,256,1024]{2,1,0:T(8,128)(2,1)} %get-tuple-element.102), channel_id=1, source_target_pairs={{0,4},{4,0},{1,5},{5,1},{2,6},{6,2},{3,7},{7,3},{8,12},{12,8},{9,1... | collective-permute-start | bytes 6291464 | tf_op jit(solution)/shard_map/ppermute | solution.py:26
  171.5 1.3 copy-start.17
  172.8 5.2 %collective-permute-start.8 = (bf16[1,1024,1024]{2,1,0:T(8,128)(2,1)}, bf16[1,1024,1024]{2,1,0:T(8,128)(2,1)}, u32[]{:S(2)}, u32[]{:S(2)}) collective-permute-start(bf16[1,1024,1024]{2,1,0:T(8,128)(2,1)} %get-tuple-element.109), channel_id=1, source_target_pairs={{0,4},{4,0},{1,5},{5,1},{2,6},{6,2},{3,7},{7,3},{8,12},{12,8},{9,1... | collective-permute-start | bytes 6291464 | tf_op jit(solution)/shard_map/ppermute | solution.py:26
  176.3 1.7 copy-start.32
  176.3 1.7 copy-start.33
  176.3 2.3 copy-start.18
  176.4 15.8 %collective-permute-start.11 = (bf16[2,128,1024]{2,1,0:T(8,128)(2,1)S(1)}, bf16[2,128,1024]{2,1,0:T(8,128)(2,1)}, u32[]{:S(2)}, u32[]{:S(2)}) collective-permute-start(bf16[2,128,1024]{2,1,0:T(8,128)(2,1)S(1)} %dynamic-slice_bitcast_fusion.3), channel_id=1, source_target_pairs={{0,96},{96,0},{32,64},{64,32},{1,97},{97,1},{33,65},{65,33},{2,98}... | collective-permute-start | bytes 1572872 | tf_op jit(solution)/shard_map/ppermute | solution.py:319
  177.4 14.7 %collective-permute-start.10 = (bf16[2,128,1024]{2,1,0:T(8,128)(2,1)S(1)}, bf16[2,128,1024]{2,1,0:T(8,128)(2,1)}, u32[]{:S(2)}, u32[]{:S(2)}) collective-permute-start(bf16[2,128,1024]{2,1,0:T(8,128)(2,1)S(1)} %dynamic-slice_bitcast_fusion.4), channel_id=1, source_target_pairs={{0,32},{32,0},{64,96},{96,64},{1,33},{33,1},{65,97},{97,65},{2,34}... | collective-permute-start | bytes 1572872 | tf_op jit(solution)/shard_map/ppermute | solution.py:319
  181.3 1.3 copy-start.28
  181.3 2.4 copy-start.12
  192.1 4.7 %copy-start.34 = (bf16[2,2,1,128,1024]{4,3,2,1,0:T(8,128)(2,1)S(1)}, bf16[2,2,1,128,1024]{4,3,2,1,0:T(8,128)(2,1)}, u32[]{:S(2)}) copy-start(bf16[2,2,1,128,1024]{4,3,2,1,0:T(8,128)(2,1)} %copy-done.33) | copy-start | bytes 3145732
  192.1 7.0 %collective-permute-start.12 = (bf16[1,512,1024]{2,1,0:T(8,128)(2,1)}, bf16[1,512,1024]{2,1,0:T(8,128)(2,1)}, u32[]{:S(2)}, u32[]{:S(2)}) collective-permute-start(bf16[1,512,1024]{2,1,0:T(8,128)(2,1)} %get-tuple-element.116), channel_id=1, source_target_pairs={{0,4},{4,0},{1,5},{5,1},{2,6},{6,2},{3,7},{7,3},{8,12},{12,8},{9,1... | collective-permute-start | bytes 3145736 | tf_op jit(solution)/shard_map/ppermute | solution.py:26
  192.7 25.4 %collective-permute-start.9 = (bf16[2,16,16,1024]{3,2,0,1:T(8,128)(2,1)}, bf16[2,16,16,1024]{3,2,0,1:T(8,128)(2,1)S(1)}, u32[]{:S(2)}, u32[]{:S(2)}) collective-permute-start(bf16[2,16,16,1024]{3,2,0,1:T(8,128)(2,1)} %dynamic-slice_bitcast_fusion), channel_id=1, source_target_pairs={{0,1},{1,0},{2,3},{3,2},{4,5},{5,4},{6,7},{7,6},{8,9},{9,8},{10,11... | collective-permute-start | bytes 3145736 | tf_op jit(solution)/shard_map/ppermute | solution.py:319
  195.5 26.6 %collective-permute-start.16 = (bf16[128,1024]{1,0:T(8,128)(2,1)S(1)}, bf16[128,1024]{1,0:T(8,128)(2,1)S(1)}, u32[]{:S(2)}, u32[]{:S(2)}) collective-permute-start(bf16[128,1024]{1,0:T(8,128)(2,1)S(1)} %dynamic-slice_bitcast_fusion.7), channel_id=1, source_target_pairs={{0,96},{96,0},{32,64},{64,32},{1,97},{97,1},{33,65},{65,33},{2,98}... | collective-permute-start | bytes 786440 | tf_op jit(solution)/shard_map/ppermute | solution.py:319
  198.1 24.1 %collective-permute-start.17 = (bf16[128,1024]{1,0:T(8,128)(2,1)S(1)}, bf16[128,1024]{1,0:T(8,128)(2,1)S(1)}, u32[]{:S(2)}, u32[]{:S(2)}) collective-permute-start(bf16[128,1024]{1,0:T(8,128)(2,1)S(1)} %dynamic-slice_bitcast_fusion.6), channel_id=1, source_target_pairs={{0,32},{32,0},{64,96},{96,64},{1,33},{33,1},{65,97},{97,65},{2,34}... | collective-permute-start | bytes 786440 | tf_op jit(solution)/shard_map/ppermute | solution.py:319
  199.1 19.0 %copy-start.29 = (bf16[1,1024,1024]{2,1,0:T(8,128)(2,1)S(1)}, bf16[1,1024,1024]{2,1,0:T(8,128)(2,1)}, u32[]{:S(2)}) copy-start(bf16[1,1024,1024]{2,1,0:T(8,128)(2,1)} %copy-done.28) | copy-start | bytes 6291460
  201.0 21.3 %collective-permute-start.14 = (bf16[2,16,8,1024]{3,2,0,1:T(8,128)(2,1)S(1)}, bf16[2,16,8,1024]{3,2,0,1:T(8,128)(2,1)S(1)}, u32[]{:S(2)}, u32[]{:S(2)}) collective-permute-start(bf16[2,16,8,1024]{3,2,0,1:T(8,128)(2,1)S(1)} %dynamic-slice_bitcast_fusion.2), channel_id=1, source_target_pairs={{0,3},{3,0},{1,2},{2,1},{4,7},{7,4},{5,6},{6,5},{8,11},{11,8},{9,1... | collective-permute-start | bytes 1572872 | tf_op jit(solution)/shard_map/ppermute | solution.py:319
  219.4 18.8 %collective-permute-start.13 = (bf16[16,16,1024]{2,1,0:T(8,128)(2,1)}, bf16[16,16,1024]{2,1,0:T(8,128)(2,1)S(1)}, u32[]{:S(2)}, u32[]{:S(2)}) collective-permute-start(bf16[16,16,1024]{2,1,0:T(8,128)(2,1)} %dynamic-slice_bitcast_fusion.1), channel_id=1, source_target_pairs={{0,3},{3,0},{1,2},{2,1},{4,7},{7,4},{5,6},{6,5},{8,11},{11,8},{9,1... | collective-permute-start | bytes 1572872 | tf_op jit(solution)/shard_map/ppermute | solution.py:319
  222.5 15.9 %collective-permute-start.15 = (bf16[16,8,1024]{2,1,0:T(8,128)(2,1)S(1)}, bf16[16,8,1024]{2,1,0:T(8,128)(2,1)}, u32[]{:S(2)}, u32[]{:S(2)}) collective-permute-start(bf16[16,8,1024]{2,1,0:T(8,128)(2,1)S(1)} %dynamic-slice_bitcast_fusion.5), channel_id=1, source_target_pairs={{0,1},{1,0},{2,3},{3,2},{4,5},{5,4},{6,7},{7,6},{8,9},{9,8},{10,11... | collective-permute-start | bytes 786440 | tf_op jit(solution)/shard_map/ppermute | solution.py:319
  223.5 17.0 %all-to-all-start.3 = ((bf16[16,16,1024]{2,1,0:T(8,128)(2,1)}), bf16[16,16,1024]{2,1,0:T(8,128)(2,1)S(1)}, u32[]{:S(2)}, u32[]{:S(2)}) async-start(bf16[16,16,1024]{2,1,0:T(8,128)(2,1)} %bitcast.47), calls=%async_computation.3 | async-start | bytes 1048576 | tf_op jit(solution)/shard_map/all_to_all | solution.py:493
  239.5 23.9 %copy-start.1 = (f32[8,768]{1,0:T(8,128)S(1)}, f32[8,768]{1,0:T(8,128)}, u32[]{:S(2)}) copy-start(f32[8,768]{1,0:T(8,128)} %param.11) | copy-start | bytes 73732
  240.4 17.5 %all-to-all-start.2 = ((bf16[16,24,1024]{2,1,0:T(8,128)(2,1)}), bf16[16,24,1024]{2,1,0:T(8,128)(2,1)S(1)}, u32[]{:S(2)}, u32[]{:S(2)}) async-start(bf16[16,24,1024]{2,1,0:T(8,128)(2,1)} %pad_maximum_fusion), calls=%async_computation.2 | async-start | bytes 1572864 | tf_op jit(solution)/shard_map/all_to_all | solution.py:494

commit v5 on v4

--- a/solution.py
+++ b/solution.py
@@ -40,8 +40,9 @@
 
 def forward_kernel(first_call, last_call, block_rows, sizes, *refs):
     width, half, head_rows = sizes
-    place, tokens, mine, theirs = refs[:4]
-    refs = refs[4:]
+    place, tokens = refs[:2]
+    packs = (refs[2:4], refs[4:6])
+    refs = refs[6:]
     if first_call:
         total_in = None
         slope, hidden, second, head, total = refs
@@ -51,41 +52,38 @@
         total_in, _, _, _, _, slope, hidden, second, head, total = refs
     block, core = place[0], place[1]
     chunks = width // LANES
-    start = width
-    head_start = start + chunks * half
+    sides = (core, 1 - core)
 
     @pl.when(pl.program_id(0) == 0)
     def _():
         if last_call:
             head[...] = head_in[...]
-        for pack, side in ((mine, core), (theirs, 1 - core)):
+        for pair, side in zip(packs, sides):
             below = pl.multiple_of(side * half, half)
             for q in range(chunks):
-                second[pl.ds(below, half), q * LANES : (q + 1) * LANES] = pack[
-                    start + q * half : start + (q + 1) * half, :
+                second[pl.ds(below, half), q * LANES : (q + 1) * LANES] = pair[1][
+                    q * half : (q + 1) * half, :
                 ]
+            row = pl.multiple_of(block * head_rows, 64) if last_call else 0
             for e in range(2):
-                piece = pack[head_start + e * head_rows : head_start + (e + 1) * head_rows, :]
                 lane = pl.multiple_of(side * (width // 2) + e * LANES, LANES)
-                row = pl.multiple_of(block * head_rows, 64) if last_call else 0
-                head[pl.ds(row, head_rows), pl.ds(lane, LANES)] = piece
+                head[pl.ds(row, head_rows), pl.ds(lane, LANES)] = pair[e][width:, :]
 
     rows = tokens[...]
     base = rows.astype(F32) if first_call else total_in[...]
     sums = [base[:, q * LANES : (q + 1) * LANES] for q in range(chunks)]
-    for pack, side in ((mine, core), (theirs, 1 - core)):
-        x = dot(rows, pack[:width, :])
+    for pair, side in zip(packs, sides):
+        x = dot(rows, pair[0][:width, :])
         sq = x * x
         t = jnp.tanh(ROOT_2_PI * (x + CUBIC * x * sq))
         up = 0.5 * (1.0 + t)
         active = (x * up).astype(BF16)
         lane = pl.multiple_of(side * half, half)
-        slope[:, pl.ds(lane, half)] = up + (0.5 * ROOT_2_PI) * x * (1.0 - t * t) * (
-            1.0 + (3.0 * CUBIC) * sq
-        )
+        turn = up + (0.5 * ROOT_2_PI) * x * (1.0 - t * t) * (1.0 + (3.0 * CUBIC) * sq)
+        slope[:, pl.ds(lane, half)] = turn.astype(BF16)
         hidden[:, pl.ds(lane, half)] = active
         for q in range(chunks):
-            sums[q] = sums[q] + dot(active, pack[start + q * half : start + (q + 1) * half, :])
+            sums[q] = sums[q] + dot(active, pair[1][q * half : (q + 1) * half, :])
     full = jnp.concatenate(sums, 1)
     if last_call:
         rounded = full.astype(BF16)
@@ -95,7 +93,7 @@
         total[...] = full
 
 
-def forward_part(place, tokens, mine, theirs, carried, out_width, last_call):
+def forward_part(place, tokens, packs, carried, out_width, last_call):
     rows, width = tokens.shape
     half = LANES
     hid = 2 * half * RING
@@ -107,18 +105,17 @@
     )
     by_rows = lambda cols: pl.BlockSpec((block_rows, cols), lambda i, s: (i, 0))
     in_place = pl.BlockSpec(memory_space=pltpu.HBM)
-    in_specs = [by_rows(width), whole(mine.shape), whole(theirs.shape)]
-    args = [tokens, mine, theirs]
+    in_specs = [by_rows(width), *[whole(p.shape) for p in packs]]
+    args = [tokens, *packs]
     aliases = {}
     if not first_call:
         slope, hidden, second, head, total = carried
-        args += [total, in_hbm(slope), in_hbm(hidden), in_hbm(second)]
-        args += [head if last_call else in_hbm(head)]
+        args += [in_hbm(v) for v in (total, slope, hidden, second, head)]
         in_specs += [by_rows(width), in_place, in_place, in_place]
         in_specs += [whole((out_width, width)) if last_call else in_place]
-        aliases = {5: 0, 6: 1, 7: 2}
+        aliases = {7: 0, 8: 1, 9: 2}
         if not last_call:
-            aliases = {**aliases, 8: 3, 4: 4}
+            aliases = {**aliases, 10: 3, 6: 4}
     column = pl.BlockSpec((block_rows, 2 * half), lambda i, s: (i, s[0]))
     out_specs = [
         column,
@@ -129,7 +126,7 @@
         else pl.BlockSpec((head_rows, width), lambda i, s: (s[0], 0)),
     ]
     out_shape = [
-        jax.ShapeDtypeStruct((rows, hid), F32),
+        jax.ShapeDtypeStruct((rows, hid), BF16),
         jax.ShapeDtypeStruct((rows, hid), BF16),
         jax.ShapeDtypeStruct((hid, width), BF16),
         jax.ShapeDtypeStruct((out_width, width), BF16),
@@ -204,8 +201,7 @@
     rows, hid = hidden.shape
     width = resid_grad.shape[1]
     lines = hid // RING // 2
-    gray = lambda i: 2 * ((i // 2 + i) % 2) + i // 2
-    out = pl.BlockSpec((1, lines, width), lambda i, s: (gray(i), 0, 0))
+    out = pl.BlockSpec((1, lines, width), lambda i, s: (i, 0, 0))
     return pl.pallas_call(
         early_kernel,
         grid_spec=pltpu.PrefetchScalarGridSpec(
@@ -229,7 +225,7 @@
 def late_kernel(steps, place, resid_grad, second, slope, tokens, *refs):
     keep, send = refs[-2:]
     hidden_grad = dot(resid_grad[...], second[...], ((1,), (1,)))
-    preact_grad = (slope[...] * hidden_grad).astype(BF16)
+    preact_grad = (slope[...].astype(F32) * hidden_grad).astype(BF16)
     first = dot(tokens[...], preact_grad, ((0,), (0,)))
     cols = first.shape[1]
 
@@ -336,22 +332,21 @@
     return lax.optimization_barrier((x, *others))[0]
 
 
-def pack_kernel(side, first, second, head, out):
-    width, half = first.shape
-    out[:width, :] = first[...]
-    at = width
-    for q in range(second.shape[1] // LANES):
-        out[at : at + half, :] = second[:, q * LANES : (q + 1) * LANES]
-        at += half
-    for e in range(head.shape[1] // LANES):
-        out[at : at + head.shape[0], :] = head[:, e * LANES : (e + 1) * LANES]
-        at += head.shape[0]
+def pack_kernel(side, first, second, head, a, b):
+    width = first.shape[0]
+    half = second.shape[0]
+    a[:width, :] = first[...]
+    for q in range(width // LANES):
+        b[q * half : (q + 1) * half, :] = second[:, q * LANES : (q + 1) * LANES]
+    a[width:, :] = head[:, :LANES]
+    b[width:, :] = head[:, LANES:]
 
 
 def packed(side, first, second, head):
     width, shard = first.shape
     half = shard // 2
-    lines = width + half * width // LANES + head.shape[0] * width // 2 // LANES
+    lines = width + head.shape[0]
+    out = pl.BlockSpec((lines, LANES), lambda i, s: (0, 0))
     return pl.pallas_call(
         pack_kernel,
         grid_spec=pltpu.PrefetchScalarGridSpec(
@@ -362,9 +357,9 @@
                 pl.BlockSpec((half, width), lambda i, s: (s[0], 0)),
                 pl.BlockSpec((head.shape[0], width // 2), lambda i, s: (0, s[0])),
             ],
-            out_specs=pl.BlockSpec((lines, LANES), lambda i, s: (0, 0)),
-        ),
-        out_shape=jax.ShapeDtypeStruct((lines, LANES), BF16),
+            out_specs=[out, out],
+        ),
+        out_shape=[jax.ShapeDtypeStruct((lines, LANES), BF16)] * 2,
         compiler_params=params(8),
         name="packed",
     )(side, first, second, head)
@@ -407,30 +402,34 @@
 
     side = jnp.reshape(core, (1,)).astype(jnp.int32)
     turned = readout_matrix.T
-    mine = packed(side, w_first, w_second, turned)
-    right = shift(mine, "y", 1)
-    left = shift(mine, "y", -1)
-    lines = mine.shape[0] // 2
-    latents, other_side, mine = tie(latents, 1 - side, mine)
+    own_a, own_b = packed(side, w_first, w_second, turned)
+    right_a = shift(own_a, "y", 1)
+    left_b = shift(own_b, "y", -1)
+    latents, other_side, own_a, own_b = tie(latents, 1 - side, own_a, own_b)
     tokens = (
         latents.reshape(members, 32, own, width).transpose(1, 0, 2, 3).reshape(rows, width)
     )
-    theirs = packed(other_side, w_first, w_second, turned)
-    place = lambda off: jnp.stack([(here + off) % RING, core, lax.axis_index("x")]).astype(jnp.int32)
+    place = lambda off: jnp.stack([(here + off) % RING, core]).astype(jnp.int32)
     run = functools.partial(forward_part, out_width=out_width)
-    carried = run(place(0), tokens, mine, theirs, carried=None, last_call=False)
-    right, left, *carried = tie(right, left, *carried)
-    far = [right[:lines], left[lines:]]
-    right_other = shift(after(right, *far), "c", 1)
-    left_other = shift(after(left, *far), "c", 1)
-    far = [shift(far[0], "y", 1), shift(far[1], "y", -1)]
-    carried = run(place(3), tokens, right, right_other, carried=carried, last_call=False)
-    carried = run(place(1), tokens, left, left_other, carried=carried, last_call=False)
-    near, past, *carried = tie(*far, *carried)
-    far = jnp.concatenate([near, past], 0)
-    far_other = shift(far, "c", 1)
+    swap = lambda x: shift(x, "c", 1)
+    packs = (own_a, own_b, *packed(other_side, w_first, w_second, turned))
+    carried = run(place(0), tokens, packs, carried=None, last_call=False)
+    right_a, left_b, *carried = tie(right_a, left_b, *carried)
+    left_a = shift(after(own_a, right_a, left_b), "y", -1)
+    right_b = shift(after(own_b, right_a, left_b), "y", 1)
+    right_a_other, left_b_other = swap(right_a), swap(left_b)
+    left_a, right_b, right_a_other, left_b_other = tie(
+        left_a, right_b, right_a_other, left_b_other
+    )
+    far_a = shift(after(right_a, left_a, right_b), "y", 1)
+    far_b = shift(after(left_b, left_a, right_b), "y", -1)
+    packs = (right_a, right_b, right_a_other, swap(right_b))
+    carried = run(place(3), tokens, packs, carried=carried, last_call=False)
+    packs = (left_a, left_b, swap(left_a), left_b_other)
+    carried = run(place(1), tokens, packs, carried=carried, last_call=False)
+    far_a, far_b, *carried = tie(far_a, far_b, *carried)
     slope, hidden, second, head, residual, forecast = run(
-        place(2), tokens, far, far_other, carried=carried, last_call=True
+        place(2), tokens, (far_a, far_b, swap(far_a), swap(far_b)), carried=carried, last_call=True
     )
 
     group = ("x", "z", "c")
@@ -461,36 +460,27 @@
         scalars,
     )
     a_in = shift(late[1], "c", 1)
-    x_steps = [ring_chain("x", True), ring_chain("x", False)]
     y_steps = [ring_chain("y", True), ring_chain("y", False)]
-    early = add(after(early[0], late[1]), early_in).reshape(2, 2, 2, -1, width)
-    early = [early[:, :, 0], early[:, :, 1]]
-    early_sent = [outgoing(x, steps[0]) for x, steps in zip(early, x_steps)]
-    early_in = [sent_along(x, steps[0]) for x, steps in zip(early_sent, x_steps)]
-    a = by_ring(add(after(late[0], *early_sent), a_in))
+    early = add(after(early[0], late[1]), early_in).reshape(-1, width)
+    early_sum = lax.psum_scatter(early, "x", scatter_dimension=0, tiled=True)
+    a = by_ring(add(after(late[0], early), a_in))
     a_sent = outgoing(a, y_steps[0][0])
     a_in = sent_along(a_sent, y_steps[0][0])
     late = late_grads(at, 1, after(resid_grad, a_sent), second, slope, tokens)
-    b_in = shift(after(late[1], *early_in), "c", 1)
-    early = [kept_plus(x, v, steps[0]) for x, v, steps in zip(early, early_in, x_steps)]
-    early_sent = [outgoing(x, steps[1]) for x, steps in zip(early, x_steps)]
-    early_in = [sent_along(x, steps[1]) for x, steps in zip(early_sent, x_steps)]
-    b = by_ring(add(after(late[0], *early_sent), b_in))
+    b_in = shift(late[1], "c", 1)
+    b = by_ring(add(late[0], b_in))
     b_sent = outgoing(b, y_steps[1][0])
     b_in = sent_along(b_sent, y_steps[1][0])
-    early = [
-        kept_plus(x, after(v, b_sent), steps[1]) for x, v, steps in zip(early, early_in, x_steps)
-    ]
-    early = jnp.concatenate(early).reshape(16, -1, width)
     a = kept_plus(a, after(a_in, b_sent), y_steps[0][0])
     a_sent = outgoing(a, y_steps[0][1])
     a_in = sent_along(a_sent, y_steps[0][1])
     b = kept_plus(b, after(b_in, a_sent), y_steps[1][0])
     b_sent = outgoing(b, y_steps[1][1])
     b_in = sent_along(b_sent, y_steps[1][1])
-    a = kept_plus(a, after(a_in, b_sent), y_steps[0][1])
-    b = kept_plus(b, b_in, y_steps[1][1])
+    early = early_sum.reshape(16, -1, width)
     early = lax.all_to_all(early, ("z", "y"), 0, 0, tiled=True)
+    a = kept_plus(a, after(a_in, b_sent, early_sum), y_steps[0][1])
+    b = kept_plus(b, after(b_in, early_sum), y_steps[1][1])
     late = lax.all_to_all(jnp.concatenate([a, b], 1), ("x", "z"), 0, 0, tiled=True)
     early = jnp.sum(early.astype(F32), 0)
     late = jnp.sum(late.astype(F32), 0)

time: 266 us -> 282 us (1.060)
  waiting for transfers between devices: 46.3 us -> 64.8 us
  between operations: 4.92 us -> 18.3 us
  local copies, waits for them, and re-layouts: 39.1 us -> 29.8 us
  starting transfers between devices: 28.2 us -> 25.3 us
    ppermute x10 -> x15, waiting for transfers between devices: 8.51 us -> 19.9 us  [shift(): return lax.ppermute(x, axis, [(i, (i + by) % size) for i in range(size)])]
    all_to_all x1, waiting for transfers between devices: 0.01 us -> 9.01 us  [per_device(): early = lax.all_to_all(early, ('z', 'y'), 0, 0, tiled=True)]
    unnamed x75 -> x72, local copies, waits for them, and re-layouts: 29.4 us -> 22.5 us
    ppermute x8 -> x4, starting transfers between devices: 10.2 us -> 6.08 us  [sent_along(): return lax.ppermute(x, step[1], step[0])]
    ppermute x10 -> x15, starting transfers between devices: 8.55 us -> 12 us  [shift(): return lax.ppermute(x, axis, [(i, (i + by) % size) for i in range(size)])]
    slice x3 -> x0, local copies, waits for them, and re-layouts: 3.03 us -> none  [the longest x2 2.85 us: per_device(): far = [right[:lines], left[lines:]]]
    convert_element_type x11 -> x7, other arithmetic: 12.2 us -> 10.4 us  [add(): return (a.astype(F32) + b.astype(F32)).astype(BF16)]
    ppermute x8 -> x4, waiting for transfers between devices: 25.5 us -> 23.8 us  [sent_along(): return lax.ppermute(x, step[1], step[0])]
  transfers between devices with their start and end apart: 20 -> 22, of which waited for: 6 -> 9; matrix products, arithmetic and copies ran while one was open for 8% -> 7% of each run, Pallas kernels for 16% -> 15%
where the time goes in v5:
time: 282 us; the launch traced here: 281 us
  waiting for transfers between devices  64.8 us (23%)
  Pallas kernels  62.3 us (22%)
  blocking collectives  56.8 us (20%)
  local copies, waits for them, and re-layouts  29.8 us (11%)
  starting transfers between devices  25.3 us (9%)
  between operations  18.3 us (6%)
  other arithmetic  16.7 us (6%)
  matrix products  7.57 us (3%)
    pallas_call x4, Pallas kernels, forward_part(): pl.pallas_call(functools.partial(forward_kernel, first_call, last_call, b...  34.3 us
    all_to_all x1, blocking collectives, per_device(): gathered = lax.all_to_all(forecast, group, 0, 0, tiled=True)  30.3 us
    all_to_all x1, blocking collectives, per_device(): lax.all_to_all(grad_raw.reshape(32, members * own, out_width), group, 0,...  26.4 us
    ppermute x4, waiting for transfers between devices, sent_along(): return lax.ppermute(x, step[1], step[0])  23.8 us
    unnamed x72, local copies, waits for them, and re-layouts  22.5 us
    ppermute x15, waiting for transfers between devices, shift(): return lax.ppermute(x, axis, [(i, (i + by) % size) for i in range(size)])  19.9 us
    pallas_call x2, Pallas kernels, late_grads(): pl.pallas_call(functools.partial(late_kernel, steps), grid_spec=pltpu.Pre...  18.7 us
    all_to_all x1, waiting for transfers between devices, per_device(): lax.all_to_all(jnp.concatenate([a, b], 1), ('x', 'z'), 0, 0, tiled=True)  12 us
  transfers between devices with their start and end apart: 22, of which 9 were waited for; matrix products, arithmetic and copies ran while one was open for 7% of the time, Pallas kernels for 15%

profile of v5, /device:TPU:0, one launch (start us, length us, event | category | flops | bytes accessed | tf_op | source)
XLA Modules:
  0.0 281.5 jit_solution(13112965006580287971)
XLA Ops:
  7.2 1.2 copy-done.7
  8.5 1.2 copy-done.9
  9.7 1.0 copy-done.16
  10.7 1.1 packed.2
  11.8 1.7 collective-permute-start
  13.5 1.6 collective-permute-start.1
  15.0 2.0 copy.28
  17.4 0.8 copy-done.24
  18.2 0.8 copy-done.26
  19.1 1.1 copy-done.25
  20.2 1.1 copy-done.27
  21.3 6.9 %forward_part.4 = (bf16[1024,2048]{1,0:T(8,128)(2,1)S(1)}, bf16[1024,2048]{1,0:T(8,128)(2,1)S(1)}, bf16[2048,1024]{1,0:T(8,128)(2,1)S(1)}, bf16[768,1024]{1,0:T(8,128)(2,1)S(1)}, f32[1024,1024]{1,0:T(8,128)S(1)}) custom-call(s32[2]{0:T(128)S(1)} %pad_add_fusion.refs_0_.place, bf16[1024,1024]{1,0:T(8,128)(2,1)S(1)} %bitcast.67, ...), custom_call_target="tpu_custom_call" | custom-call | flops 2147483648 | bytes 12582912 | tf_op jit(solution)/shard_map/forward_part/pallas_call | solution.py:143
  28.2 2.0 copy-done.2
  30.2 1.9 copy-done.3
  32.1 2.0 copy-done.4
  34.1 2.0 copy-done.5
  36.1 1.2 copy-done.6
  37.7 2.8 collective-permute-start.2
  41.0 13.1 %collective-permute-done.3.refs_3_ = bf16[1216,256]{1,0:T(8,128)(2,1)} collective-permute-done((bf16[1216,256]{1,0:T(8,128)(2,1)}, bf16[1216,256]{1,0:T(8,128)(2,1)}, u32[]{:S(2)}, u32[]{:S(2)}) %collective-permute-start.3) | collective-permute-done | bytes 622624 | tf_op jit(solution)/shard_map/ppermute | solution.py:26
  54.2 0.8 copy-done.20
  55.0 0.9 copy-done.18
  56.4 3.0 %collective-permute-start.7 = (bf16[1216,256]{1,0:T(8,128)(2,1)S(1)}, bf16[1216,256]{1,0:T(8,128)(2,1)}, u32[]{:S(2)}, u32[]{:S(2)}) collective-permute-start(bf16[1216,256]{1,0:T(8,128)(2,1)S(1)} %collective-permute-done.1.refs_3_), channel_id=1, source_target_pairs={{0,3},{1,0},{2,1},{3,2},{4,7},{5,4},{6,5},{7,6},{8,11},{9,8},{10,9... | collective-permute-start | bytes 1867784 | tf_op jit(solution)/shard_map/ppermute | solution.py:26
  59.5 1.1 copy-done.21
  60.6 8.8 %forward_part.5 = (bf16[1024,2048]{1,0:T(8,128)(2,1)}, bf16[1024,2048]{1,0:T(8,128)(2,1)}, bf16[2048,1024]{1,0:T(8,128)(2,1)}, bf16[768,1024]{1,0:T(8,128)(2,1)}, f32[1024,1024]{1,0:T(8,128)}) custom-call(s32[2]{0:T(128)S(1)} %pad_add_fusion.3.refs_0_, ...), custom_call_target="tpu_custom_call", output_to_operand_aliasing={{0}: (7, {}), {1}: (8, {}), {2}: (9, {}), {3}: (10, {}), {4... | custom-call | flops 2147483648 | bytes 12582912 | tf_op jit(solution)/shard_map/forward_part/pallas_call | solution.py:143
  69.5 8.9 %forward_part.6 = (bf16[1024,2048]{1,0:T(8,128)(2,1)}, bf16[1024,2048]{1,0:T(8,128)(2,1)}, bf16[2048,1024]{1,0:T(8,128)(2,1)}, bf16[768,1024]{1,0:T(8,128)(2,1)}, f32[1024,1024]{1,0:T(8,128)}) custom-call(s32[2]{0:T(128)S(1)} %pad_add_fusion.2.refs_0_, ...), custom_call_target="tpu_custom_call", output_to_operand_aliasing={{0}: (7, {}), {1}: (8, {}), {2}: (9, {}), {3}: (10, {}), {4... | custom-call | flops 2147483648 | bytes 12582912 | tf_op jit(solution)/shard_map/forward_part/pallas_call | solution.py:143
  79.7 1.0 collective-permute-done.10.refs_4_
  80.7 0.9 collective-permute-done.11.refs_5_
  81.6 9.7 %forward_part.7 = (bf16[1024,2048]{1,0:T(8,128)(2,1)}, bf16[1024,2048]{1,0:T(8,128)(2,1)}, bf16[2048,1024]{1,0:T(8,128)(2,1)}, bf16[768,1024]{1,0:T(8,128)(2,1)S...) custom-call(s32[2]{0:T(128)S(1)} %pad_add_fusion.1.refs_0_, ...), custom_call_target="tpu_custom_call", output_to_operand_aliasing={{0}: (7, {}), {1}: (8, {}), {2}: (9, {})} | custom-call | flops 2147483648 | bytes 12582912 | tf_op jit(solution)/shard_map/forward_part/pallas_call | solution.py:143
  91.4 30.3 %all_to_all.20 = bf16[32,32,768]{2,1,0:T(8,128)(2,1)S(1)} all-to-all(bf16[32,32,768]{2,1,0:T(8,128)(2,1)S(1)} %bitcast.75), channel_id=1, replica_groups=mesh['x'=4,'z'=4,'c'=2,'y'=4] {'x','z','c'}, dimensions={0} | all-to-all | bytes 3145728 | tf_op jit(solution)/shard_map/all_to_all | solution.py:439
  121.9 0.7 fusion.6
  123.2 3.0 %fusion.30 = (f32[8]{0:T(128)S(1)}, f32[8,128]{1,0:T(8,128)S(1)}, f32[8,128,128]{1,2,0:T(8,128)S(1)}) fusion(bf16[128,8,768]{2,1,0:T(8,128)(2,1)} %bitcast.83, f32[8,128]{1,0:T(8,128)S(1)} %copy.32), kind=kOutput, calls=%fused_computation.61 | convolution fusion | flops 202243072 | bytes 2105376 | tf_op jit(solution)/shard_map/mpo,npo->pmn/dot_general | solution.py:371
  126.8 2.8 fusion.8
  129.6 0.9 copy.38
  130.5 26.4 %all_to_all.21 = bf16[32,32,768]{2,1,0:T(8,128)(2,1)S(1)} all-to-all(bf16[32,32,768]{2,1,0:T(8,128)(2,1)S(1)} %bitcast.82), channel_id=1, replica_groups=mesh['x'=4,'z'=4,'c'=2,'y'=4] {'x','z','c'}, dimensions={0} | all-to-all | bytes 3145728 | tf_op jit(solution)/shard_map/all_to_all | solution.py:442
  156.9 1.8 convolution_convert_fusion.resid_grad
  158.7 8.2 %early_grads.1 = (bf16[4,256,1024]{2,1,0:T(8,128)(2,1)S(1)}, bf16[4,256,1024]{2,1,0:T(8,128)(2,1)S(1)}) custom-call(s32[2]{0:T(128)S(1)} %pad_add_fusion.refs_0_.place, bf16[1024,2048]{1,0:T(8,128)(2,1)} %get-tuple-element.120.hidden, bf16[1024,1024]{1,0:T(8,128)(2,1)S(1)} %convolution_convert_fusion.resid_grad), custom_call_target="tpu_custom_call" | custom-call | flops 4294967296 | bytes 12582912 | tf_op jit(solution)/shard_map/early_grads/pallas_call | solution.py:205
  166.9 0.8 collective-permute-start.12
  167.7 1.4 pad_maximum_fusion.1.refs_2_
  169.1 10.6 %late_grads.2 = (bf16[1,1024,1024]{2,1,0:T(8,128)(2,1)S(1)}, bf16[1,1024,1024]{2,1,0:T(8,128)(2,1)}) custom-call(s32[2]{0:T(128)S(1)} %pad_add_fusion.refs_0_.place, bf16[1024,1024]{1,0:T(8,128)(2,1)S(1)} %convolution_convert_fusion.resid_grad, bf16[2048,1024]{1,0:T(8,128)(2,1)} %get-tuple-element.123.second, bf16[1024,2048]{1,0:T(8,128)(2,1)} %get-tuple-element.124.slope, ...), custom_call_target="tpu_custom_call" | custom-call | flops 4294967296 | bytes 12582912 | tf_op jit(solution)/shard_map/late_grads/pallas_call | solution.py:263
  179.7 2.4 add_convert_fusion.1
  182.2 2.0 collective-permute-done.13
  184.2 3.2 %add_convert_fusion = bf16[1,1024,1024]{2,1,0:T(8,128)(2,1)S(1)} fusion(bf16[1,1024,1024]{2,1,0:T(8,128)(2,1)} %collective-permute-done.13, bf16[1,1024,1024]{2,1,0:T(8,128)(2,1)} %copy-done.11), kind=kLoop, calls=%fused_computation.1 | loop fusion | flops 4194304 | bytes 6291456 | tf_op jit(solution)/shard_map/convert_element_type | solution.py:287
  187.4 1.3 copy-done.28
  188.7 1.1 dynamic-slice_bitcast_fusion
  190.3 8.0 %late_grads.3 = (bf16[1,512,1024]{2,1,0:T(8,128)(2,1)S(1)}, bf16[1,512,1024]{2,1,0:T(8,128)(2,1)}) custom-call(s32[2]{0:T(128)S(1)} %pad_add_fusion.refs_0_.place, bf16[1024,1024]{1,0:T(8,128)(2,1)S(1)} %copy-done.13, bf16[2048,1024]{1,0:T(8,128)(2,1)} %get-tuple-element.123.second, bf16[1024,2048]{1,0:T(8,128)(2,1)} %get-tuple-element.124.slope, ...), custom_call_target="tpu_custom_call" | custom-call | flops 4294967296 | bytes 12582912 | tf_op jit(solution)/shard_map/late_grads/pallas_call | solution.py:263
  198.5 2.9 %collective-permute-done.15 = bf16[1,512,1024]{2,1,0:T(8,128)(2,1)} collective-permute-done((bf16[1,512,1024]{2,1,0:T(8,128)(2,1)}, bf16[1,512,1024]{2,1,0:T(8,128)(2,1)}, u32[]{:S(2)}, u32[]{:S(2)}) %collective-permute-start.15) | collective-permute-done | bytes 1048608 | tf_op jit(solution)/shard_map/ppermute | solution.py:26
  201.3 1.7 add_convert_fusion.2
  203.0 1.0 copy-done.32
  204.0 0.8 dynamic-slice_bitcast_fusion.2
  204.9 3.0 %collective-permute-start.17 = (bf16[2,16,8,1024]{3,2,0,1:T(8,128)(2,1)}, bf16[2,16,8,1024]{3,2,0,1:T(8,128)(2,1)}, u32[]{:S(2)}, u32[]{:S(2)}) collective-permute-start(bf16[2,16,8,1024]{3,2,0,1:T(8,128)(2,1)} %dynamic-slice_bitcast_fusion.2), channel_id=1, source_target_pairs={{0,3},{3,0},{1,2},{2,1},{4,7},{7,4},{5,6},{6,5},{8,11},{11,8},{9,1... | collective-permute-start | bytes 1572872 | tf_op jit(solution)/shard_map/ppermute | solution.py:315
  207.8 16.4 %collective-permute-done.14 = bf16[2,16,16,1024]{3,2,0,1:T(8,128)(2,1)} collective-permute-done((bf16[2,16,16,1024]{3,2,0,1:T(8,128)(2,1)}, bf16[2,16,16,1024]{3,2,0,1:T(8,128)(2,1)}, u32[]{:S(2)}, u32[]{:S(2)}) %collective-permute-start.14) | collective-permute-done | bytes 1048608 | tf_op jit(solution)/shard_map/ppermute | solution.py:315
  224.2 1.6 fusion.9
  225.9 0.8 dynamic-slice_bitcast_fusion.1
  226.7 3.0 %collective-permute-start.16 = (bf16[16,16,1024]{2,1,0:T(8,128)(2,1)}, bf16[16,16,1024]{2,1,0:T(8,128)(2,1)S(1)}, u32[]{:S(2)}, u32[]{:S(2)}) collective-permute-start(bf16[16,16,1024]{2,1,0:T(8,128)(2,1)} %dynamic-slice_bitcast_fusion.1), channel_id=1, source_target_pairs={{0,3},{3,0},{1,2},{2,1},{4,7},{7,4},{5,6},{6,5},{8,11},{11,8},{9,1... | collective-permute-start | bytes 1572872 | tf_op jit(solution)/shard_map/ppermute | solution.py:315
  229.7 1.2 fusion.25
  231.0 7.4 %collective-permute-done.18 = bf16[16,8,1024]{2,1,0:T(8,128)(2,1)S(1)} collective-permute-done((bf16[16,8,1024]{2,1,0:T(8,128)(2,1)S(1)}, bf16[16,8,1024]{2,1,0:T(8,128)(2,1)S(1)}, u32[]{:S(2)}, u32[]{:S(2)}) %collective-permute-start.18) | collective-permute-done | bytes 262176 | tf_op jit(solution)/shard_map/ppermute | solution.py:315
  238.5 3.6 %all-to-all-start.3 = ((bf16[16,16,1024]{2,1,0:T(8,128)(2,1)}), bf16[16,16,1024]{2,1,0:T(8,128)(2,1)S(1)}, u32[]{:S(2)}, u32[]{:S(2)}) async-start(bf16[16,16,1024]{2,1,0:T(8,128)(2,1)} %bitcast.88), calls=%async_computation.4 | async-start | bytes 1048576 | tf_op jit(solution)/shard_map/all_to_all | solution.py:481
  242.4 1.0 pad_maximum_fusion
  243.3 9.0 %all-to-all-done.3 = bf16[16,16,1024]{2,1,0:T(8,128)(2,1)S(1)} async-done(((bf16[16,16,1024]{2,1,0:T(8,128)(2,1)}), bf16[16,16,1024]{2,1,0:T(8,128)(2,1)S(1)}, u32[]{:S(2)}, u32[]{:S(2)}) %all-to-all-start.3) | async-done | bytes 524320 | tf_op jit(solution)/shard_map/all_to_all | solution.py:481
  252.3 3.6 %all-to-all-start.2 = ((bf16[16,24,1024]{2,1,0:T(8,128)(2,1)}), bf16[16,24,1024]{2,1,0:T(8,128)(2,1)S(1)}, u32[]{:S(2)}, u32[]{:S(2)}) async-start(bf16[16,24,1024]{2,1,0:T(8,128)(2,1)} %pad_maximum_fusion), calls=%async_computation.3 | async-start | bytes 1572864 | tf_op jit(solution)/shard_map/all_to_all | solution.py:484
  256.0 12.0 %all-to-all-done.2 = bf16[16,24,1024]{2,1,0:T(8,128)(2,1)S(1)} async-done(((bf16[16,24,1024]{2,1,0:T(8,128)(2,1)}), bf16[16,24,1024]{2,1,0:T(8,128)(2,1)S(1)}, u32[]{:S(2)}, u32[]{:S(2)}) %all-to-all-start.2) | async-done | bytes 786464 | tf_op jit(solution)/shard_map/all_to_all | solution.py:484
  271.6 0.6 slice_multiply_fusion
  272.2 0.6 broadcast_multiply_fusion
  272.8 0.6 maximum_multiply_fusion
  (107 shorter events, 6.8 us)
Async XLA Ops:
  7.2 71.8 %copy-start = (f32[8,768]{1,0:T(8,128)S(1)}, f32[8,768]{1,0:T(8,128)}, u32[]{:S(2)}) copy-start(f32[8,768]{1,0:T(8,128)} %param.11) | copy-start | bytes 73732
  7.2 231.3 %reduce-scatter.2.cloned.1.call-start = ((), (), s32[]{:S(2)}) async-start(), calls=%async_computation.5 | async-start | bytes 2621440 | tf_op jit(solution)/shard_map/reduce_scatter | solution.py:465
  7.2 1.2 copy-start.7
  8.5 1.2 copy-start.9
  9.7 1.0 copy-start.16
  11.8 25.5 %collective-permute-start = (bf16[1216,256]{1,0:T(8,128)(2,1)}, bf16[1216,256]{1,0:T(8,128)(2,1)S(1)}, u32[]{:S(2)}, u32[]{:S(2)}) collective-permute-start(bf16[1216,256]{1,0:T(8,128)(2,1)} %get-tuple-element.86.refs_2_), channel_id=1, source_target_pairs={{0,1},{1,2},{2,3},{3,0},{4,5},{5,6},{6,7},{7,4},{8,9},{9,10},{10,1... | collective-permute-start | bytes 1867784 | tf_op jit(solution)/shard_map/ppermute | solution.py:26
  13.5 23.8 %collective-permute-start.1 = (bf16[1216,256]{1,0:T(8,128)(2,1)}, bf16[1216,256]{1,0:T(8,128)(2,1)S(1)}, u32[]{:S(2)}, u32[]{:S(2)}) collective-permute-start(bf16[1216,256]{1,0:T(8,128)(2,1)} %get-tuple-element.87.refs_3_), channel_id=1, source_target_pairs={{0,3},{1,0},{2,1},{3,2},{4,7},{5,4},{6,5},{7,6},{8,11},{9,8},{10,9... | collective-permute-start | bytes 1867784 | tf_op jit(solution)/shard_map/ppermute | solution.py:26
  15.0 2.0 copy-start.8
  15.0 2.2 copy-start.10
  15.0 2.3 copy-start.17
  17.4 0.8 copy-start.24
  18.2 0.8 copy-start.26
  19.1 1.1 copy-start.25
  20.2 1.1 copy-start.27
  28.1 2.0 copy-start.2
  30.2 1.9 copy-start.3
  32.1 2.0 copy-start.4
  34.1 2.0 copy-start.5
  36.1 1.2 copy-start.6
  37.3 16.9 %collective-permute-start.3 = (bf16[1216,256]{1,0:T(8,128)(2,1)}, bf16[1216,256]{1,0:T(8,128)(2,1)}, u32[]{:S(2)}, u32[]{:S(2)}) collective-permute-start(bf16[1216,256]{1,0:T(8,128)(2,1)} %get-tuple-element.87.refs_3_), channel_id=1, source_target_pairs={{0,1},{1,2},{2,3},{3,0},{4,5},{5,6},{6,7},{7,4},{8,9},{9,10},{10,1... | collective-permute-start | bytes 1867784 | tf_op jit(solution)/shard_map/ppermute | solution.py:26
  37.7 16.4 %collective-permute-start.2 = (bf16[1216,256]{1,0:T(8,128)(2,1)}, bf16[1216,256]{1,0:T(8,128)(2,1)}, u32[]{:S(2)}, u32[]{:S(2)}) collective-permute-start(bf16[1216,256]{1,0:T(8,128)(2,1)} %get-tuple-element.86.refs_2_), channel_id=1, source_target_pairs={{0,3},{1,0},{2,1},{3,2},{4,7},{5,4},{6,5},{7,6},{8,11},{9,8},{10,9... | collective-permute-start | bytes 1867784 | tf_op jit(solution)/shard_map/ppermute | solution.py:26
  40.5 13.7 %collective-permute-start.4 = (bf16[1216,256]{1,0:T(8,128)(2,1)S(1)}, bf16[1216,256]{1,0:T(8,128)(2,1)S(1)}, u32[]{:S(2)}, u32[]{:S(2)}) collective-permute-start(bf16[1216,256]{1,0:T(8,128)(2,1)S(1)} %collective-permute-done.refs_2_), channel_id=1, source_target_pairs={{0,4},{4,0},{1,5},{5,1},{2,6},{6,2},{3,7},{7,3},{8,12},{12,8},{9,1... | collective-permute-start | bytes 1867784 | tf_op jit(solution)/shard_map/ppermute | solution.py:26
  40.5 14.5 %collective-permute-start.5 = (bf16[1216,256]{1,0:T(8,128)(2,1)S(1)}, bf16[1216,256]{1,0:T(8,128)(2,1)S(1)}, u32[]{:S(2)}, u32[]{:S(2)}) collective-permute-start(bf16[1216,256]{1,0:T(8,128)(2,1)S(1)} %collective-permute-done.1.refs_3_), channel_id=1, source_target_pairs={{0,4},{4,0},{1,5},{5,1},{2,6},{6,2},{3,7},{7,3},{8,12},{12,8},{9,1... | collective-permute-start | bytes 1867784 | tf_op jit(solution)/shard_map/ppermute | solution.py:26
  54.2 0.8 copy-start.20
  55.0 0.9 copy-start.18
  55.9 3.6 %collective-permute-start.9 = (bf16[1216,256]{1,0:T(8,128)(2,1)}, bf16[1216,256]{1,0:T(8,128)(2,1)}, u32[]{:S(2)}, u32[]{:S(2)}) collective-permute-start(bf16[1216,256]{1,0:T(8,128)(2,1)} %collective-permute-done.3.refs_3_), channel_id=1, source_target_pairs={{0,4},{4,0},{1,5},{5,1},{2,6},{6,2},{3,7},{7,3},{8,12},{12,8},{9,1... | collective-permute-start | bytes 1867784 | tf_op jit(solution)/shard_map/ppermute | solution.py:26
  55.9 13.6 %collective-permute-start.8 = (bf16[1216,256]{1,0:T(8,128)(2,1)}, bf16[1216,256]{1,0:T(8,128)(2,1)}, u32[]{:S(2)}, u32[]{:S(2)}) collective-permute-start(bf16[1216,256]{1,0:T(8,128)(2,1)} %collective-permute-done.2.refs_2_), channel_id=1, source_target_pairs={{0,4},{4,0},{1,5},{5,1},{2,6},{6,2},{3,7},{7,3},{8,12},{12,8},{9,1... | collective-permute-start | bytes 1867784 | tf_op jit(solution)/shard_map/ppermute | solution.py:26
  56.4 22.0 %collective-permute-start.7 = (bf16[1216,256]{1,0:T(8,128)(2,1)S(1)}, bf16[1216,256]{1,0:T(8,128)(2,1)}, u32[]{:S(2)}, u32[]{:S(2)}) collective-permute-start(bf16[1216,256]{1,0:T(8,128)(2,1)S(1)} %collective-permute-done.1.refs_3_), channel_id=1, source_target_pairs={{0,3},{1,0},{2,1},{3,2},{4,7},{5,4},{6,5},{7,6},{8,11},{9,8},{10,9... | collective-permute-start | bytes 1867784 | tf_op jit(solution)/shard_map/ppermute | solution.py:26
  59.3 19.0 %collective-permute-start.6 = (bf16[1216,256]{1,0:T(8,128)(2,1)S(1)}, bf16[1216,256]{1,0:T(8,128)(2,1)}, u32[]{:S(2)}, u32[]{:S(2)}) collective-permute-start(bf16[1216,256]{1,0:T(8,128)(2,1)S(1)} %collective-permute-done.refs_2_), channel_id=1, source_target_pairs={{0,1},{1,2},{2,3},{3,0},{4,5},{5,6},{6,7},{7,4},{8,9},{9,10},{10,1... | collective-permute-start | bytes 1867784 | tf_op jit(solution)/shard_map/ppermute | solution.py:26
  59.5 10.0 %copy-start.19 = (bf16[1216,256]{1,0:T(8,128)(2,1)S(1)}, bf16[1216,256]{1,0:T(8,128)(2,1)}, u32[]{:S(2)}) copy-start(bf16[1216,256]{1,0:T(8,128)(2,1)} %copy-done.18) | copy-start | bytes 1867780
  59.5 1.1 copy-start.21
  69.5 9.5 %copy-start.34 = (s32[8]{0:T(128)S(1)}, s32[8]{0:T(128)}, u32[]{:S(2)}) copy-start(s32[8]{0:T(128)} %param.12) | copy-start | bytes 100
  78.4 2.3 collective-permute-start.10
  78.5 3.1 %collective-permute-start.11 = (bf16[1216,256]{1,0:T(8,128)(2,1)}, bf16[1216,256]{1,0:T(8,128)(2,1)S(1)}, u32[]{:S(2)}, u32[]{:S(2)}) collective-permute-start(bf16[1216,256]{1,0:T(8,128)(2,1)} %collective-permute-done.7.refs_3_), channel_id=1, source_target_pairs={{0,4},{4,0},{1,5},{5,1},{2,6},{6,2},{3,7},{7,3},{8,12},{12,8},{9,1... | collective-permute-start | bytes 1867784 | tf_op jit(solution)/shard_map/ppermute | solution.py:26
  91.3 30.6 %copy-start.14 = (bf16[1024,1024]{1,0:T(8,128)(2,1)}, bf16[1024,1024]{1,0:T(8,128)(2,1)S(1)}, u32[]{:S(2)}) copy-start(bf16[1024,1024]{1,0:T(8,128)(2,1)S(1)} %get-tuple-element.125.refs_0_) | copy-start | bytes 6291460
  91.3 30.6 %copy-start.22 = (bf16[768,1024]{1,0:T(8,128)(2,1)}, bf16[768,1024]{1,0:T(8,128)(2,1)S(1)}, u32[]{:S(2)}) copy-start(bf16[768,1024]{1,0:T(8,128)(2,1)S(1)} %get-tuple-element.119) | copy-start | bytes 4718596
  121.7 1.2 copy-start.30
  123.2 3.0 %copy-start.35 = (s32[8]{0:T(128)S(1)}, s32[8]{0:T(128)}, u32[]{:S(2)}) copy-start(s32[8]{0:T(128)} %param.13) | copy-start | bytes 100
  123.2 3.6 %copy-start.31 = (bf16[32,32,768]{2,1,0:T(8,128)(2,1)S(1)}, bf16[32,32,768]{2,1,0:T(8,128)(2,1)}, u32[]{:S(2)}) copy-start(bf16[32,32,768]{2,1,0:T(8,128)(2,1)} %copy-done.30) | copy-start | bytes 4718596
  130.5 26.4 %copy-start.23 = (bf16[768,1024]{1,0:T(8,128)(2,1)S(1)}, bf16[768,1024]{1,0:T(8,128)(2,1)}, u32[]{:S(2)}) copy-start(bf16[768,1024]{1,0:T(8,128)(2,1)} %copy-done.22) | copy-start | bytes 4718596
  158.7 10.4 %copy-start.12 = (bf16[1024,1024]{1,0:T(8,128)(2,1)}, bf16[1024,1024]{1,0:T(8,128)(2,1)S(1)}, u32[]{:S(2)}) copy-start(bf16[1024,1024]{1,0:T(8,128)(2,1)S(1)} %convolution_convert_fusion.resid_grad) | copy-start | bytes 6291460
  158.7 10.4 %copy-start.15 = (bf16[1024,1024]{1,0:T(8,128)(2,1)S(1)}, bf16[1024,1024]{1,0:T(8,128)(2,1)}, u32[]{:S(2)}) copy-start(bf16[1024,1024]{1,0:T(8,128)(2,1)} %copy-done.14) | copy-start | bytes 6291460
  166.9 12.9 %collective-permute-start.12 = (bf16[4,256,1024]{2,1,0:T(8,128)(2,1)S(1)}, bf16[4,256,1024]{2,1,0:T(8,128)(2,1)S(1)}, u32[]{:S(2)}, u32[]{:S(2)}) collective-permute-start(bf16[4,256,1024]{2,1,0:T(8,128)(2,1)S(1)} %get-tuple-element.121), channel_id=1, source_target_pairs={{0,4},{4,0},{1,5},{5,1},{2,6},{6,2},{3,7},{7,3},{8,12},{12,8},{9,1... | collective-permute-start | bytes 6291464 | tf_op jit(solution)/shard_map/ppermute | solution.py:26
  179.7 2.4 copy-start.11
  179.7 4.5 %collective-permute-start.13 = (bf16[1,1024,1024]{2,1,0:T(8,128)(2,1)}, bf16[1,1024,1024]{2,1,0:T(8,128)(2,1)}, u32[]{:S(2)}, u32[]{:S(2)}) collective-permute-start(bf16[1,1024,1024]{2,1,0:T(8,128)(2,1)} %get-tuple-element.128), channel_id=1, source_target_pairs={{0,4},{4,0},{1,5},{5,1},{2,6},{6,2},{3,7},{7,3},{8,12},{12,8},{9,1... | collective-permute-start | bytes 6291464 | tf_op jit(solution)/shard_map/ppermute | solution.py:26
  187.4 1.3 copy-start.28
  187.4 2.9 %copy-start.13 = (bf16[1024,1024]{1,0:T(8,128)(2,1)S(1)}, bf16[1024,1024]{1,0:T(8,128)(2,1)}, u32[]{:S(2)}) copy-start(bf16[1024,1024]{1,0:T(8,128)(2,1)} %copy-done.12) | copy-start | bytes 6291460
  198.3 3.0 %collective-permute-start.15 = (bf16[1,512,1024]{2,1,0:T(8,128)(2,1)}, bf16[1,512,1024]{2,1,0:T(8,128)(2,1)}, u32[]{:S(2)}, u32[]{:S(2)}) collective-permute-start(bf16[1,512,1024]{2,1,0:T(8,128)(2,1)} %get-tuple-element.133), channel_id=1, source_target_pairs={{0,4},{4,0},{1,5},{5,1},{2,6},{6,2},{3,7},{7,3},{8,12},{12,8},{9,1... | collective-permute-start | bytes 3145736 | tf_op jit(solution)/shard_map/ppermute | solution.py:26
  198.5 25.8 %collective-permute-start.14 = (bf16[2,16,16,1024]{3,2,0,1:T(8,128)(2,1)}, bf16[2,16,16,1024]{3,2,0,1:T(8,128)(2,1)}, u32[]{:S(2)}, u32[]{:S(2)}) collective-permute-start(bf16[2,16,16,1024]{3,2,0,1:T(8,128)(2,1)} %dynamic-slice_bitcast_fusion), channel_id=1, source_target_pairs={{0,1},{1,0},{2,3},{3,2},{4,5},{5,4},{6,7},{7,6},{8,9},{9,8},{10,11... | collective-permute-start | bytes 3145736 | tf_op jit(solution)/shard_map/ppermute | solution.py:315
  201.3 22.9 %copy-start.29 = (bf16[1,1024,1024]{2,1,0:T(8,128)(2,1)S(1)}, bf16[1,1024,1024]{2,1,0:T(8,128)(2,1)}, u32[]{:S(2)}) copy-start(bf16[1,1024,1024]{2,1,0:T(8,128)(2,1)} %copy-done.28) | copy-start | bytes 6291460
  203.0 1.0 copy-start.32
  204.9 24.9 %collective-permute-start.17 = (bf16[2,16,8,1024]{3,2,0,1:T(8,128)(2,1)}, bf16[2,16,8,1024]{3,2,0,1:T(8,128)(2,1)}, u32[]{:S(2)}, u32[]{:S(2)}) collective-permute-start(bf16[2,16,8,1024]{3,2,0,1:T(8,128)(2,1)} %dynamic-slice_bitcast_fusion.2), channel_id=1, source_target_pairs={{0,3},{3,0},{1,2},{2,1},{4,7},{7,4},{5,6},{6,5},{8,11},{11,8},{9,1... | collective-permute-start | bytes 1572872 | tf_op jit(solution)/shard_map/ppermute | solution.py:315
  207.8 21.9 %copy-start.33 = (bf16[1,512,1024]{2,1,0:T(8,128)(2,1)S(1)}, bf16[1,512,1024]{2,1,0:T(8,128)(2,1)}, u32[]{:S(2)}) copy-start(bf16[1,512,1024]{2,1,0:T(8,128)(2,1)} %copy-done.32) | copy-start | bytes 3145732
  226.7 15.4 %collective-permute-start.16 = (bf16[16,16,1024]{2,1,0:T(8,128)(2,1)}, bf16[16,16,1024]{2,1,0:T(8,128)(2,1)S(1)}, u32[]{:S(2)}, u32[]{:S(2)}) collective-permute-start(bf16[16,16,1024]{2,1,0:T(8,128)(2,1)} %dynamic-slice_bitcast_fusion.1), channel_id=1, source_target_pairs={{0,3},{3,0},{1,2},{2,1},{4,7},{7,4},{5,6},{6,5},{8,11},{11,8},{9,1... | collective-permute-start | bytes 1572872 | tf_op jit(solution)/shard_map/ppermute | solution.py:315
  231.0 7.5 %collective-permute-start.18 = (bf16[16,8,1024]{2,1,0:T(8,128)(2,1)S(1)}, bf16[16,8,1024]{2,1,0:T(8,128)(2,1)S(1)}, u32[]{:S(2)}, u32[]{:S(2)}) collective-permute-start(bf16[16,8,1024]{2,1,0:T(8,128)(2,1)S(1)} %dynamic-slice_bitcast_fusion.3), channel_id=1, source_target_pairs={{0,1},{1,0},{2,3},{3,2},{4,5},{5,4},{6,7},{7,6},{8,9},{9,8},{10,11... | collective-permute-start | bytes 786440 | tf_op jit(solution)/shard_map/ppermute | solution.py:315
  238.5 13.9 %all-to-all-start.3 = ((bf16[16,16,1024]{2,1,0:T(8,128)(2,1)}), bf16[16,16,1024]{2,1,0:T(8,128)(2,1)S(1)}, u32[]{:S(2)}, u32[]{:S(2)}) async-start(bf16[16,16,1024]{2,1,0:T(8,128)(2,1)} %bitcast.88), calls=%async_computation.4 | async-start | bytes 1048576 | tf_op jit(solution)/shard_map/all_to_all | solution.py:481
  242.4 31.1 %copy-start.1 = (f32[8,768]{1,0:T(8,128)S(1)}, f32[8,768]{1,0:T(8,128)}, u32[]{:S(2)}) copy-start(f32[8,768]{1,0:T(8,128)} %param.11) | copy-start | bytes 73732
  252.3 15.7 %all-to-all-start.2 = ((bf16[16,24,1024]{2,1,0:T(8,128)(2,1)}), bf16[16,24,1024]{2,1,0:T(8,128)(2,1)S(1)}, u32[]{:S(2)}, u32[]{:S(2)}) async-start(bf16[16,24,1024]{2,1,0:T(8,128)(2,1)} %pad_maximum_fusion), calls=%async_computation.3 | async-start | bytes 1572864 | tf_op jit(solution)/shard_map/all_to_all | solution.py:484
Sparse Core Ops, SparseCore 0:
  182.3 27.7 reduce-scatter.1

commit v6 on v5

--- a/solution.py
+++ b/solution.py
@@ -28,10 +28,6 @@
 
 def dot(a, b, contract=((1,), (0,))):
     return lax.dot_general(a, b, (contract, ((), ())), preferred_element_type=F32)
-
-
-def in_hbm(x):
-    return pltpu.with_memory_space_constraint(x, pltpu.HBM)
 
 
 def params(mib):
@@ -104,13 +100,13 @@
         shape, lambda i, s: (0,) * len(shape), pipeline_mode=pl.Buffered(1)
     )
     by_rows = lambda cols: pl.BlockSpec((block_rows, cols), lambda i, s: (i, 0))
-    in_place = pl.BlockSpec(memory_space=pltpu.HBM)
+    in_place = pl.BlockSpec(memory_space=pl.ANY)
     in_specs = [by_rows(width), *[whole(p.shape) for p in packs]]
     args = [tokens, *packs]
     aliases = {}
     if not first_call:
         slope, hidden, second, head, total = carried
-        args += [in_hbm(v) for v in (total, slope, hidden, second, head)]
+        args += [total, slope, hidden, second, head]
         in_specs += [by_rows(width), in_place, in_place, in_place]
         in_specs += [whole((out_width, width)) if last_call else in_place]
         aliases = {7: 0, 8: 1, 9: 2}
@@ -152,7 +148,7 @@
         ),
         out_shape=out_shape,
         input_output_aliases=aliases,
-        compiler_params=params(24),
+        compiler_params=params(56),
         cost_estimate=pl.CostEstimate(
             flops=8 * rows * width * half, bytes_accessed=12 * MIB, transcendentals=rows * 2 * half
         ),
@@ -201,7 +197,8 @@
     rows, hid = hidden.shape
     width = resid_grad.shape[1]
     lines = hid // RING // 2
-    out = pl.BlockSpec((1, lines, width), lambda i, s: (i, 0, 0))
+    gray = lambda i: 2 * ((i // 2 + i) % 2) + i // 2
+    out = pl.BlockSpec((1, lines, width), lambda i, s: (gray(i), 0, 0))
     return pl.pallas_call(
         early_kernel,
         grid_spec=pltpu.PrefetchScalarGridSpec(
@@ -214,12 +211,12 @@
             out_specs=[out, out],
         ),
         out_shape=[jax.ShapeDtypeStruct((RING, lines, width), BF16)] * 2,
-        compiler_params=params(28),
+        compiler_params=params(56),
         cost_estimate=pl.CostEstimate(
             flops=2 * rows * width * hid, bytes_accessed=12 * MIB, transcendentals=0
         ),
         name="early_grads",
-    )(place, in_hbm(hidden), resid_grad)
+    )(place, hidden, resid_grad)
 
 
 def late_kernel(steps, place, resid_grad, second, slope, tokens, *refs):
@@ -275,12 +272,12 @@
             out_specs=[out, out],
         ),
         out_shape=[jax.ShapeDtypeStruct((1, lines, width), BF16)] * 2,
-        compiler_params=params(36 if head else 28),
+        compiler_params=params(56),
         cost_estimate=pl.CostEstimate(
             flops=4 * rows * width * width, bytes_accessed=12 * MIB, transcendentals=0
         ),
         name="late_grads",
-    )(place, resid_grad, in_hbm(second), in_hbm(slope), tokens, *head)
+    )(place, resid_grad, second, slope, tokens, *head)
 
 
 def add(a, b):
@@ -414,7 +411,7 @@
     swap = lambda x: shift(x, "c", 1)
     packs = (own_a, own_b, *packed(other_side, w_first, w_second, turned))
     carried = run(place(0), tokens, packs, carried=None, last_call=False)
-    right_a, left_b, *carried = tie(right_a, left_b, *carried)
+    right_a, left_b, *_ = tie(right_a, left_b, carried[-1])
     left_a = shift(after(own_a, right_a, left_b), "y", -1)
     right_b = shift(after(own_b, right_a, left_b), "y", 1)
     right_a_other, left_b_other = swap(right_a), swap(left_b)
@@ -461,26 +458,38 @@
     )
     a_in = shift(late[1], "c", 1)
     y_steps = [ring_chain("y", True), ring_chain("y", False)]
-    early = add(after(early[0], late[1]), early_in).reshape(-1, width)
-    early_sum = lax.psum_scatter(early, "x", scatter_dimension=0, tiled=True)
-    a = by_ring(add(after(late[0], early), a_in))
+    x_steps = [ring_chain("x", True), ring_chain("x", False)]
+    early = add(after(early[0], late[1]), early_in).reshape(2, 2, 2, -1, width)
+    early = [early[:, :, 0], early[:, :, 1]]
+    early_sent = [outgoing(x, steps[0]) for x, steps in zip(early, x_steps)]
+    early_in = [sent_along(x, steps[0]) for x, steps in zip(early_sent, x_steps)]
+    a = by_ring(add(after(late[0], *early_sent), a_in))
     a_sent = outgoing(a, y_steps[0][0])
     a_in = sent_along(a_sent, y_steps[0][0])
     late = late_grads(at, 1, after(resid_grad, a_sent), second, slope, tokens)
     b_in = shift(late[1], "c", 1)
-    b = by_ring(add(late[0], b_in))
+    early = [
+        kept_plus(x, after(v, late[1]), steps[0]) for x, v, steps in zip(early, early_in, x_steps)
+    ]
+    early_sent = [outgoing(x, steps[1]) for x, steps in zip(early, x_steps)]
+    early_in = [sent_along(x, steps[1]) for x, steps in zip(early_sent, x_steps)]
+    a = kept_plus(a, after(a_in, *early_sent), y_steps[0][0])
+    a_sent = outgoing(a, y_steps[0][1])
+    a_in = sent_along(a_sent, y_steps[0][1])
+    b = by_ring(add(after(late[0], a_sent), b_in))
     b_sent = outgoing(b, y_steps[1][0])
     b_in = sent_along(b_sent, y_steps[1][0])
-    a = kept_plus(a, after(a_in, b_sent), y_steps[0][0])
-    a_sent = outgoing(a, y_steps[0][1])
-    a_in = sent_along(a_sent, y_steps[0][1])
-    b = kept_plus(b, after(b_in, a_sent), y_steps[1][0])
+    early = [
+        kept_plus(x, after(v, b_sent), steps[1]) for x, v, steps in zip(early, early_in, x_steps)
+    ]
+    early = jnp.concatenate(early).reshape(16, -1, width)
+    early_all = lax.all_to_all(early, ("z", "y"), 0, 0, tiled=True)
+    b = kept_plus(b, after(b_in, early), y_steps[1][0])
     b_sent = outgoing(b, y_steps[1][1])
     b_in = sent_along(b_sent, y_steps[1][1])
-    early = early_sum.reshape(16, -1, width)
-    early = lax.all_to_all(early, ("z", "y"), 0, 0, tiled=True)
-    a = kept_plus(a, after(a_in, b_sent, early_sum), y_steps[0][1])
-    b = kept_plus(b, after(b_in, early_sum), y_steps[1][1])
+    a = kept_plus(a, after(a_in, b_sent), y_steps[0][1])
+    b = kept_plus(b, b_in, y_steps[1][1])
+    early = early_all
     late = lax.all_to_all(jnp.concatenate([a, b], 1), ("x", "z"), 0, 0, tiled=True)
     early = jnp.sum(early.astype(F32), 0)
     late = jnp.sum(late.astype(F32), 0)

time: 282 us -> 270 us (0.957)
  local copies, waits for them, and re-layouts: 29.8 us -> 13 us
  between operations: 18.3 us -> 5.03 us
  Pallas kernels: 62.3 us -> 72.4 us
  starting transfers between devices: 25.3 us -> 31 us
    unnamed x72 -> x56, local copies, waits for them, and re-layouts: 22.5 us -> 7.57 us
    ppermute x4 -> x8, waiting for transfers between devices: 23.8 us -> 33 us  [sent_along(): return lax.ppermute(x, step[1], step[0])]
    pallas_call x4, Pallas kernels: 34.3 us -> 39.9 us  [forward_part(): pl.pallas_call(functools.partial(forward_kernel, first_call, last_call, b...]
    ppermute x15, waiting for transfers between devices: 19.9 us -> 14.4 us  [shift(): return lax.ppermute(x, axis, [(i, (i + by) % size) for i in range(size)])]
    pallas_call x2, Pallas kernels: 18.7 us -> 22.8 us  [late_grads(): pl.pallas_call(functools.partial(late_kernel, steps), grid_spec=pltpu.Pre...]
    all_to_all x1, starting transfers between devices: 3.57 us -> 6.96 us  [per_device(): early_all = lax.all_to_all(early, ('z', 'y'), 0, 0, tiled=True)]
    convert_element_type x7 -> x11, other arithmetic: 10.4 us -> 7.05 us  [add(): return (a.astype(F32) + b.astype(F32)).astype(BF16)]
    ppermute x4 -> x8, starting transfers between devices: 6.08 us -> 7.49 us  [sent_along(): return lax.ppermute(x, step[1], step[0])]
  transfers between devices with their start and end apart: 22 -> 25, of which waited for: 9 -> 10; matrix products, arithmetic and copies ran while one was open for 7% -> 6% of each run, Pallas kernels for 15% -> 19%
where the time goes in v6:
time: 270 us; the launch traced here: 269 us
  Pallas kernels  72.4 us (27%)
  waiting for transfers between devices  66.7 us (25%)
  blocking collectives  57 us (21%)
  starting transfers between devices  31 us (11%)
  other arithmetic  16.9 us (6%)
  local copies, waits for them, and re-layouts  13 us (5%)
  matrix products  6.83 us (3%)
  between operations  5.03 us (2%)
    pallas_call x4, Pallas kernels, forward_part(): pl.pallas_call(functools.partial(forward_kernel, first_call, last_call, b...  39.9 us
    ppermute x8, waiting for transfers between devices, sent_along(): return lax.ppermute(x, step[1], step[0])  33 us
    all_to_all x1, blocking collectives, per_device(): gathered = lax.all_to_all(forecast, group, 0, 0, tiled=True)  30.5 us
    all_to_all x1, blocking collectives, per_device(): lax.all_to_all(grad_raw.reshape(32, members * own, out_width), group, 0,...  26.4 us
    pallas_call x2, Pallas kernels, late_grads(): pl.pallas_call(functools.partial(late_kernel, steps), grid_spec=pltpu.Pre...  22.8 us
    ppermute x15, waiting for transfers between devices, shift(): return lax.ppermute(x, axis, [(i, (i + by) % size) for i in range(size)])  14.4 us
    ppermute x15, starting transfers between devices, shift(): return lax.ppermute(x, axis, [(i, (i + by) % size) for i in range(size)])  11.9 us
    all_to_all x1, waiting for transfers between devices, per_device(): lax.all_to_all(jnp.concatenate([a, b], 1), ('x', 'z'), 0, 0, tiled=True)  11.4 us
  transfers between devices with their start and end apart: 25, of which 10 were waited for; matrix products, arithmetic and copies ran while one was open for 6% of the time, Pallas kernels for 19%

profile of v6, /device:TPU:0, one launch (start us, length us, event | category | flops | bytes accessed | tf_op | source)
XLA Modules:
  0.0 268.7 jit_solution(14406606672345870354)
XLA Ops:
  0.7 1.2 copy-done.2
  1.9 1.2 copy-done.4
  3.1 1.0 copy-done.6
  4.2 1.7 collective-permute-start
  5.9 1.6 collective-permute-start.1
  7.5 1.6 copy.29
  9.1 0.7 copy-done.5
  10.0 0.8 copy-done.12
  10.8 0.8 copy-done.13
  11.6 0.6 pad_add_fusion.refs_0_.place
  12.2 9.1 %forward_part.4 = (bf16[1024,2048]{1,0:T(8,128)(2,1)}, bf16[1024,2048]{1,0:T(8,128)(2,1)}, bf16[2048,1024]{1,0:T(8,128)(2,1)}, bf16[768,1024]{1,0:T(8,128)(2,1)}, f32[1024,1024]{1,0:T(8,128)}) custom-call(s32[2]{0:T(128)} %pad_add_fusion.refs_0_.place, bf16[1024,1024]{1,0:T(8,128)(2,1)} %bitcast.94, bf16[1216,256]{1,0:T(8,128)(2,1)} %copy-done.8, ...), custom_call_target="tpu_custom_call" | custom-call | flops 2147483648 | bytes 12582912 | tf_op jit(solution)/shard_map/forward_part/pallas_call | solution.py:139
  21.5 1.6 collective-permute-start.3
  23.1 1.7 collective-permute-start.2
  24.8 0.5 collective-permute-start.5
  25.3 12.8 %collective-permute-done.3.refs_3_ = bf16[1216,256]{1,0:T(8,128)(2,1)S(1)} collective-permute-done((bf16[1216,256]{1,0:T(8,128)(2,1)S(1)}, bf16[1216,256]{1,0:T(8,128)(2,1)S(1)}, u32[]{:S(2)}, u32[]{:S(2)}) %collective-permute-start.3) | collective-permute-done | bytes 622624 | tf_op jit(solution)/shard_map/ppermute | solution.py:26
  38.2 0.5 collective-permute-start.8
  38.7 2.9 %collective-permute-start.7 = (bf16[1216,256]{1,0:T(8,128)(2,1)}, bf16[1216,256]{1,0:T(8,128)(2,1)}, u32[]{:S(2)}, u32[]{:S(2)}) collective-permute-start(bf16[1216,256]{1,0:T(8,128)(2,1)} %collective-permute-done.1.refs_3_), channel_id=1, source_target_pairs={{0,3},{1,0},{2,1},{3,2},{4,7},{5,4},{6,5},{7,6},{8,11},{9,8},{10,9... | collective-permute-start | bytes 1867784 | tf_op jit(solution)/shard_map/ppermute | solution.py:26
  41.7 0.6 pad_add_fusion.3.refs_0_
  42.3 0.6 pad_add_fusion.2.refs_0_
  42.9 9.8 %forward_part.5 = (bf16[1024,2048]{1,0:T(8,128)(2,1)}, bf16[1024,2048]{1,0:T(8,128)(2,1)}, bf16[2048,1024]{1,0:T(8,128)(2,1)}, bf16[768,1024]{1,0:T(8,128)(2,1)}, f32[1024,1024]{1,0:T(8,128)}) custom-call(s32[2]{0:T(128)} %pad_add_fusion.3.refs_0_, ...), custom_call_target="tpu_custom_call", output_to_operand_aliasing={{0}: (7, {}), {1}: (8, {}), {2}: (9, {}), {3}: (10, {}), {4... | custom-call | flops 2147483648 | bytes 12582912 | tf_op jit(solution)/shard_map/forward_part/pallas_call | solution.py:139
  52.8 0.8 copy-done.22
  53.6 9.8 %forward_part.6 = (bf16[1024,2048]{1,0:T(8,128)(2,1)}, bf16[1024,2048]{1,0:T(8,128)(2,1)}, bf16[2048,1024]{1,0:T(8,128)(2,1)}, bf16[768,1024]{1,0:T(8,128)(2,1)}, f32[1024,1024]{1,0:T(8,128)}) custom-call(s32[2]{0:T(128)} %pad_add_fusion.2.refs_0_, ...), custom_call_target="tpu_custom_call", output_to_operand_aliasing={{0}: (7, {}), {1}: (8, {}), {2}: (9, {}), {3}: (10, {}), {4... | custom-call | flops 2147483648 | bytes 12582912 | tf_op jit(solution)/shard_map/forward_part/pallas_call | solution.py:139
  63.5 0.5 collective-permute-start.11
  64.0 0.6 gather_fusion
  64.6 0.6 pad_add_fusion.1.refs_0_
  65.3 0.5 collective-permute-done.10.refs_4_
  65.8 0.9 collective-permute-done.11.refs_5_
  66.7 0.8 copy-done.24
  67.5 11.2 %forward_part.7 = (bf16[1024,2048]{1,0:T(8,128)(2,1)}, bf16[1024,2048]{1,0:T(8,128)(2,1)}, bf16[2048,1024]{1,0:T(8,128)(2,1)}, bf16[768,1024]{1,0:T(8,128)(2,1)}...) custom-call(s32[2]{0:T(128)} %pad_add_fusion.1.refs_0_, ...), custom_call_target="tpu_custom_call", output_to_operand_aliasing={{0}: (7, {}), {1}: (8, {}), {2}: (9, {})} | custom-call | flops 2147483648 | bytes 12582912 | tf_op jit(solution)/shard_map/forward_part/pallas_call | solution.py:139
  78.7 30.5 %all_to_all.20 = bf16[32,32,768]{2,1,0:T(8,128)(2,1)S(1)} all-to-all(bf16[32,32,768]{2,1,0:T(8,128)(2,1)} %bitcast.112), channel_id=1, replica_groups=mesh['x'=4,'z'=4,'c'=2,'y'=4] {'x','z','c'}, dimensions={0} | all-to-all | bytes 3145728 | tf_op jit(solution)/shard_map/all_to_all | solution.py:436
  109.4 0.8 fusion.6
  110.5 0.9 fusion.34
  111.5 0.6 multiply_reduce_fusion
  112.1 2.8 %fusion.8 = bf16[128,8,768]{2,0,1:T(8,128)(2,1)S(1)} fusion(f32[128,8]{0,1:T(8,128)S(1)} %bitcast.114, f32[128,8]{0,1:T(8,128)S(1)} %copy.32, f32[8,768]{1,0:T(8,128)S(1)} %broadcast_select_fusion, f32[8]{0:T(128)S(1)} %get-tuple-element.154, bf16[128,8,768]{2,1,0:T(8,128)(2,1)S(1)} %bitcast.108, f32[8,128,128]{1,2,0:T(8,128)S(1)} %get-tuple-element.155), kind=kOutput, calls=%fused_computation.15 | convolution fusion | flops 1215168512 | bytes 3702816 | tf_op jit(solution)/shard_map/pmn,npo->mpo/dot_general | solution.py:374
  114.9 0.9 copy.39
  115.8 26.4 %all_to_all.21 = bf16[32,32,768]{2,1,0:T(8,128)(2,1)S(1)} all-to-all(bf16[32,32,768]{2,1,0:T(8,128)(2,1)S(1)} %bitcast.106), channel_id=1, replica_groups=mesh['x'=4,'z'=4,'c'=2,'y'=4] {'x','z','c'}, dimensions={0} | all-to-all | bytes 3145728 | tf_op jit(solution)/shard_map/all_to_all | solution.py:439
  142.2 3.1 %convolution_convert_fusion.resid_grad = bf16[1024,1024]{1,0:T(8,128)(2,1)} fusion(bf16[1024,768]{1,0:T(8,128)(2,1)S(1)} %bitcast.104, bf16[768,1024]{1,0:T(8,128)(2,1)S(1)} %copy-done.27), kind=kOutput, calls=%fused_computation.19 | convolution fusion | flops 1611661312 | bytes 5242880 | tf_op jit(solution)/shard_map/dot_general | solution.py:30
  145.3 9.5 %early_grads.1 = (bf16[4,256,1024]{2,1,0:T(8,128)(2,1)}, bf16[4,256,1024]{2,1,0:T(8,128)(2,1)}) custom-call(s32[2]{0:T(128)} %pad_add_fusion.refs_0_.place, bf16[1024,2048]{1,0:T(8,128)(2,1)} %get-tuple-element.114.hidden, bf16[1024,1024]{1,0:T(8,128)(2,1)} %convolution_convert_fusion.resid_grad), custom_call_target="tpu_custom_call" | custom-call | flops 4294967296 | bytes 12582912 | tf_op jit(solution)/shard_map/early_grads/pallas_call | solution.py:202
  154.8 0.7 collective-permute-start.12
  155.5 1.9 pad_maximum_fusion.2.refs_2_
  157.4 13.3 %late_grads.2 = (bf16[1,1024,1024]{2,1,0:T(8,128)(2,1)}, bf16[1,1024,1024]{2,1,0:T(8,128)(2,1)}) custom-call(s32[2]{0:T(128)} %pad_add_fusion.refs_0_.place, bf16[1024,1024]{1,0:T(8,128)(2,1)} %convolution_convert_fusion.resid_grad, bf16[2048,1024]{1,0:T(8,128)(2,1)} %get-tuple-element.117.second, bf16[1024,2048]{1,0:T(8,128)(2,1)} %get-tuple-element.118.slope, ...), custom_call_target="tpu_custom_call" | custom-call | flops 4294967296 | bytes 12582912 | tf_op jit(solution)/shard_map/late_grads/pallas_call | solution.py:260
  170.8 3.2 %add_convert_fusion.1 = bf16[4,256,1024]{2,1,0:T(8,128)(2,1)S(1)} fusion(bf16[4,256,1024]{2,1,0:T(8,128)(2,1)} %collective-permute-done.12, bf16[4,256,1024]{2,1,0:T(8,128)(2,1)} %get-tuple-element.123), kind=kLoop, calls=%fused_computation.2 | loop fusion | flops 4194304 | bytes 6291456 | tf_op jit(solution)/shard_map/convert_element_type | solution.py:284
  174.2 1.0 collective-permute-start.16
  175.2 0.8 dynamic-slice_bitcast_fusion.4
  176.1 0.4 collective-permute-start.15
  176.5 1.0 add_convert_fusion
  177.8 9.5 %late_grads.3 = (bf16[1,512,1024]{2,1,0:T(8,128)(2,1)}, bf16[1,512,1024]{2,1,0:T(8,128)(2,1)}) custom-call(s32[2]{0:T(128)} %pad_add_fusion.refs_0_.place, bf16[1024,1024]{1,0:T(8,128)(2,1)} %convolution_convert_fusion.resid_grad, bf16[2048,1024]{1,0:T(8,128)(2,1)} %get-tuple-element.117.second, bf16[1024,2048]{1,0:T(8,128)(2,1)} %get-tuple-element.118.slope, ...), custom_call_target="tpu_custom_call" | custom-call | flops 4294967296 | bytes 12582912 | tf_op jit(solution)/shard_map/late_grads/pallas_call | solution.py:260
  187.3 2.5 collective-permute-done.16
  189.8 0.5 collective-permute-done.15
  190.5 2.4 collective-permute-start.20
  193.3 9.4 %collective-permute-done.14 = bf16[2,16,16,1024]{3,2,0,1:T(8,128)(2,1)S(1)} collective-permute-done((bf16[2,16,16,1024]{3,2,0,1:T(8,128)(2,1)S(1)}, bf16[2,16,16,1024]{3,2,0,1:T(8,128)(2,1)S(1)}, u32[]{:S(2)}, u32[]{:S(2)}) %collective-permute-start.14) | collective-permute-done | bytes 1048608 | tf_op jit(solution)/shard_map/ppermute | solution.py:312
  203.2 3.2 %collective-permute-start.17 = (bf16[16,16,1024]{2,1,0:T(8,128)(2,1)S(1)}, bf16[16,16,1024]{2,1,0:T(8,128)(2,1)S(1)}, u32[]{:S(2)}, u32[]{:S(2)}) collective-permute-start(bf16[16,16,1024]{2,1,0:T(8,128)(2,1)S(1)} %dynamic-slice_bitcast_fusion.2), channel_id=1, source_target_pairs={{0,3},{3,0},{1,2},{2,1},{4,7},{7,4},{5,6},{6,5},{8,11},{11,8},{9,1... | collective-permute-start | bytes 1572872 | tf_op jit(solution)/shard_map/ppermute | solution.py:312
  207.2 0.9 pad_maximum_fusion.1
  208.0 20.6 %collective-permute-done.19 = bf16[2,16,8,1024]{3,2,0,1:T(8,128)(2,1)S(1)} collective-permute-done((bf16[2,16,8,1024]{3,2,0,1:T(8,128)(2,1)S(1)}, bf16[2,16,8,1024]{3,2,0,1:T(8,128)(2,1)S(1)}, u32[]{:S(2)}, u32[]{:S(2)}) %collective-permute-start.19) | collective-permute-done | bytes 524320 | tf_op jit(solution)/shard_map/ppermute | solution.py:312
  229.0 7.0 %all-to-all-start.3 = ((bf16[16,16,1024]{2,1,0:T(8,128)(2,1)}), bf16[16,16,1024]{2,1,0:T(8,128)(2,1)S(1)}, u32[]{:S(2)}, u32[]{:S(2)}) async-start(bf16[16,16,1024]{2,1,0:T(8,128)(2,1)} %bitcast.43), calls=%async_computation.3 | async-start | bytes 1048576 | tf_op jit(solution)/shard_map/all_to_all | solution.py:486
  236.2 1.0 fusion.29
  237.2 1.0 pad_maximum_fusion
  238.2 7.9 %all-to-all-done.3 = bf16[16,16,1024]{2,1,0:T(8,128)(2,1)S(1)} async-done(((bf16[16,16,1024]{2,1,0:T(8,128)(2,1)}), bf16[16,16,1024]{2,1,0:T(8,128)(2,1)S(1)}, u32[]{:S(2)}, u32[]{:S(2)}) %all-to-all-start.3) | async-done | bytes 524320 | tf_op jit(solution)/shard_map/all_to_all | solution.py:486
  246.1 4.6 %all-to-all-start.2 = ((bf16[16,24,1024]{2,1,0:T(8,128)(2,1)}), bf16[16,24,1024]{2,1,0:T(8,128)(2,1)S(1)}, u32[]{:S(2)}, u32[]{:S(2)}) async-start(bf16[16,24,1024]{2,1,0:T(8,128)(2,1)} %pad_maximum_fusion), calls=%async_computation.2 | async-start | bytes 1572864 | tf_op jit(solution)/shard_map/all_to_all | solution.py:493
  250.8 11.4 %all-to-all-done.2 = bf16[16,24,1024]{2,1,0:T(8,128)(2,1)S(1)} async-done(((bf16[16,24,1024]{2,1,0:T(8,128)(2,1)}), bf16[16,24,1024]{2,1,0:T(8,128)(2,1)S(1)}, u32[]{:S(2)}, u32[]{:S(2)}) %all-to-all-start.2) | async-done | bytes 786464 | tf_op jit(solution)/shard_map/all_to_all | solution.py:493
  262.5 0.6 fusion.38
  265.7 0.6 slice_multiply_fusion
  266.3 0.6 broadcast_multiply_fusion
  267.0 0.6 maximum_multiply_fusion
  (106 shorter events, 4.5 us)
Async XLA Ops:
  0.6 63.4 %copy-start = (f32[8,768]{1,0:T(8,128)S(1)}, f32[8,768]{1,0:T(8,128)}, u32[]{:S(2)}) copy-start(f32[8,768]{1,0:T(8,128)} %param.11) | copy-start | bytes 73732
  0.7 1.2 copy-start.2
  1.9 1.2 copy-start.4
  3.1 1.0 copy-start.6
  4.1 3.4 %copy-start.16 = (bf16[4,256,1024]{2,1,0:T(8,128)(2,1)S(1)}, bf16[4,256,1024]{2,1,0:T(8,128)(2,1)}, u32[]{:S(2)}) copy-start(bf16[4,256,1024]{2,1,0:T(8,128)(2,1)} %param.7) | copy-start | bytes 6291460
  4.2 4.9 %copy-start.8 = (bf16[1216,256]{1,0:T(8,128)(2,1)}, bf16[1216,256]{1,0:T(8,128)(2,1)S(1)}, u32[]{:S(2)}) copy-start(bf16[1216,256]{1,0:T(8,128)(2,1)S(1)} %get-tuple-element.81.refs_2_) | copy-start | bytes 1867780
  4.2 4.9 %copy-start.10 = (bf16[1216,256]{1,0:T(8,128)(2,1)}, bf16[1216,256]{1,0:T(8,128)(2,1)S(1)}, u32[]{:S(2)}) copy-start(bf16[1216,256]{1,0:T(8,128)(2,1)S(1)} %get-tuple-element.82.refs_3_) | copy-start | bytes 1867780
  4.2 17.3 %collective-permute-start = (bf16[1216,256]{1,0:T(8,128)(2,1)S(1)}, bf16[1216,256]{1,0:T(8,128)(2,1)}, u32[]{:S(2)}, u32[]{:S(2)}) collective-permute-start(bf16[1216,256]{1,0:T(8,128)(2,1)S(1)} %get-tuple-element.81.refs_2_), channel_id=1, source_target_pairs={{0,1},{1,2},{2,3},{3,0},{4,5},{5,6},{6,7},{7,4},{8,9},{9,10},{10,1... | collective-permute-start | bytes 1867784 | tf_op jit(solution)/shard_map/ppermute | solution.py:26
  5.9 15.6 %collective-permute-start.1 = (bf16[1216,256]{1,0:T(8,128)(2,1)S(1)}, bf16[1216,256]{1,0:T(8,128)(2,1)}, u32[]{:S(2)}, u32[]{:S(2)}) collective-permute-start(bf16[1216,256]{1,0:T(8,128)(2,1)S(1)} %get-tuple-element.82.refs_3_), channel_id=1, source_target_pairs={{0,3},{1,0},{2,1},{3,2},{4,7},{5,4},{6,5},{7,6},{8,11},{9,8},{10,9... | collective-permute-start | bytes 1867784 | tf_op jit(solution)/shard_map/ppermute | solution.py:26
  7.5 1.6 copy-start.3
  7.5 2.3 copy-start.5
  7.5 2.4 copy-start.7
  10.0 0.8 copy-start.12
  10.8 0.8 copy-start.13
  12.2 9.3 %copy-start.11 = (bf16[1216,256]{1,0:T(8,128)(2,1)S(1)}, bf16[1216,256]{1,0:T(8,128)(2,1)}, u32[]{:S(2)}) copy-start(bf16[1216,256]{1,0:T(8,128)(2,1)} %copy-done.10) | copy-start | bytes 1867780
  12.2 10.9 %copy-start.9 = (bf16[1216,256]{1,0:T(8,128)(2,1)S(1)}, bf16[1216,256]{1,0:T(8,128)(2,1)}, u32[]{:S(2)}) copy-start(bf16[1216,256]{1,0:T(8,128)(2,1)} %copy-done.8) | copy-start | bytes 1867780
  21.5 16.6 %collective-permute-start.3 = (bf16[1216,256]{1,0:T(8,128)(2,1)S(1)}, bf16[1216,256]{1,0:T(8,128)(2,1)S(1)}, u32[]{:S(2)}, u32[]{:S(2)}) collective-permute-start(bf16[1216,256]{1,0:T(8,128)(2,1)S(1)} %copy-done.11), channel_id=1, source_target_pairs={{0,1},{1,2},{2,3},{3,0},{4,5},{5,6},{6,7},{7,4},{8,9},{9,10},{10,1... | collective-permute-start | bytes 1867784 | tf_op jit(solution)/shard_map/ppermute | solution.py:26
  23.1 15.0 %collective-permute-start.2 = (bf16[1216,256]{1,0:T(8,128)(2,1)S(1)}, bf16[1216,256]{1,0:T(8,128)(2,1)S(1)}, u32[]{:S(2)}, u32[]{:S(2)}) collective-permute-start(bf16[1216,256]{1,0:T(8,128)(2,1)S(1)} %copy-done.9), channel_id=1, source_target_pairs={{0,3},{1,0},{2,1},{3,2},{4,7},{5,4},{6,5},{7,6},{8,11},{9,8},{10,9... | collective-permute-start | bytes 1867784 | tf_op jit(solution)/shard_map/ppermute | solution.py:26
  24.8 13.3 %collective-permute-start.4 = (bf16[1216,256]{1,0:T(8,128)(2,1)}, bf16[1216,256]{1,0:T(8,128)(2,1)S(1)}, u32[]{:S(2)}, u32[]{:S(2)}) collective-permute-start(bf16[1216,256]{1,0:T(8,128)(2,1)} %collective-permute-done.refs_2_), channel_id=1, source_target_pairs={{0,4},{4,0},{1,5},{5,1},{2,6},{6,2},{3,7},{7,3},{8,12},{12,8},{9,1... | collective-permute-start | bytes 1867784 | tf_op jit(solution)/shard_map/ppermute | solution.py:26
  24.8 13.3 %collective-permute-start.5 = (bf16[1216,256]{1,0:T(8,128)(2,1)}, bf16[1216,256]{1,0:T(8,128)(2,1)S(1)}, u32[]{:S(2)}, u32[]{:S(2)}) collective-permute-start(bf16[1216,256]{1,0:T(8,128)(2,1)} %collective-permute-done.1.refs_3_), channel_id=1, source_target_pairs={{0,4},{4,0},{1,5},{5,1},{2,6},{6,2},{3,7},{7,3},{8,12},{12,8},{9,1... | collective-permute-start | bytes 1867784 | tf_op jit(solution)/shard_map/ppermute | solution.py:26
  38.1 4.8 %copy-start.20 = (bf16[1216,256]{1,0:T(8,128)(2,1)}, bf16[1216,256]{1,0:T(8,128)(2,1)S(1)}, u32[]{:S(2)}) copy-start(bf16[1216,256]{1,0:T(8,128)(2,1)S(1)} %collective-permute-done.3.refs_3_) | copy-start | bytes 1867780
  38.1 14.6 %copy-start.18 = (bf16[1216,256]{1,0:T(8,128)(2,1)}, bf16[1216,256]{1,0:T(8,128)(2,1)S(1)}, u32[]{:S(2)}) copy-start(bf16[1216,256]{1,0:T(8,128)(2,1)S(1)} %collective-permute-done.2.refs_2_) | copy-start | bytes 1867780
  38.1 4.8 %copy-start.21 = (bf16[1216,256]{1,0:T(8,128)(2,1)}, bf16[1216,256]{1,0:T(8,128)(2,1)S(1)}, u32[]{:S(2)}) copy-start(bf16[1216,256]{1,0:T(8,128)(2,1)S(1)} %collective-permute-done.4.refs_4_) | copy-start | bytes 1867780
  38.1 14.6 %copy-start.19 = (bf16[1216,256]{1,0:T(8,128)(2,1)}, bf16[1216,256]{1,0:T(8,128)(2,1)S(1)}, u32[]{:S(2)}) copy-start(bf16[1216,256]{1,0:T(8,128)(2,1)S(1)} %collective-permute-done.5.refs_5_) | copy-start | bytes 1867780
  38.1 4.8 %collective-permute-start.9 = (bf16[1216,256]{1,0:T(8,128)(2,1)S(1)}, bf16[1216,256]{1,0:T(8,128)(2,1)}, u32[]{:S(2)}, u32[]{:S(2)}) collective-permute-start(bf16[1216,256]{1,0:T(8,128)(2,1)S(1)} %collective-permute-done.3.refs_3_), channel_id=1, source_target_pairs={{0,4},{4,0},{1,5},{5,1},{2,6},{6,2},{3,7},{7,3},{8,12},{12,8},{9,1... | collective-permute-start | bytes 1867784 | tf_op jit(solution)/shard_map/ppermute | solution.py:26
  38.2 14.5 %collective-permute-start.8 = (bf16[1216,256]{1,0:T(8,128)(2,1)S(1)}, bf16[1216,256]{1,0:T(8,128)(2,1)S(1)}, u32[]{:S(2)}, u32[]{:S(2)}) collective-permute-start(bf16[1216,256]{1,0:T(8,128)(2,1)S(1)} %collective-permute-done.2.refs_2_), channel_id=1, source_target_pairs={{0,4},{4,0},{1,5},{5,1},{2,6},{6,2},{3,7},{7,3},{8,12},{12,8},{9,1... | collective-permute-start | bytes 1867784 | tf_op jit(solution)/shard_map/ppermute | solution.py:26
  38.7 24.7 %collective-permute-start.7 = (bf16[1216,256]{1,0:T(8,128)(2,1)}, bf16[1216,256]{1,0:T(8,128)(2,1)}, u32[]{:S(2)}, u32[]{:S(2)}) collective-permute-start(bf16[1216,256]{1,0:T(8,128)(2,1)} %collective-permute-done.1.refs_3_), channel_id=1, source_target_pairs={{0,3},{1,0},{2,1},{3,2},{4,7},{5,4},{6,5},{7,6},{8,11},{9,8},{10,9... | collective-permute-start | bytes 1867784 | tf_op jit(solution)/shard_map/ppermute | solution.py:26
  41.7 21.7 %collective-permute-start.6 = (bf16[1216,256]{1,0:T(8,128)(2,1)}, bf16[1216,256]{1,0:T(8,128)(2,1)}, u32[]{:S(2)}, u32[]{:S(2)}) collective-permute-start(bf16[1216,256]{1,0:T(8,128)(2,1)} %collective-permute-done.refs_2_), channel_id=1, source_target_pairs={{0,1},{1,2},{2,3},{3,0},{4,5},{5,6},{6,7},{7,4},{8,9},{9,10},{10,1... | collective-permute-start | bytes 1867784 | tf_op jit(solution)/shard_map/ppermute | solution.py:26
  52.8 0.8 copy-start.22
  53.6 10.4 %copy-start.25 = (s32[8]{0:T(128)S(1)}, s32[8]{0:T(128)}, u32[]{:S(2)}) copy-start(s32[8]{0:T(128)} %param.12) | copy-start | bytes 100
  63.4 2.3 collective-permute-start.10
  63.5 3.1 %collective-permute-start.11 = (bf16[1216,256]{1,0:T(8,128)(2,1)}, bf16[1216,256]{1,0:T(8,128)(2,1)S(1)}, u32[]{:S(2)}, u32[]{:S(2)}) collective-permute-start(bf16[1216,256]{1,0:T(8,128)(2,1)} %collective-permute-done.7.refs_3_), channel_id=1, source_target_pairs={{0,4},{4,0},{1,5},{5,1},{2,6},{6,2},{3,7},{7,3},{8,12},{12,8},{9,1... | collective-permute-start | bytes 1867784 | tf_op jit(solution)/shard_map/ppermute | solution.py:26
  65.8 0.9 copy-start.23
  66.7 0.8 copy-start.24
  110.5 1.0 copy-start.26
  115.7 26.4 %copy-start.27 = (bf16[768,1024]{1,0:T(8,128)(2,1)S(1)}, bf16[768,1024]{1,0:T(8,128)(2,1)}, u32[]{:S(2)}) copy-start(bf16[768,1024]{1,0:T(8,128)(2,1)} %get-tuple-element.113) | copy-start | bytes 4718596
  142.2 3.1 %copy-start.14 = (bf16[32,32,768]{2,1,0:T(8,128)(2,1)}, bf16[32,32,768]{2,1,0:T(8,128)(2,1)S(1)}, u32[]{:S(2)}) copy-start(bf16[32,32,768]{2,1,0:T(8,128)(2,1)S(1)} %all_to_all.21) | copy-start | bytes 4718596
  154.8 16.0 %collective-permute-start.12 = (bf16[4,256,1024]{2,1,0:T(8,128)(2,1)}, bf16[4,256,1024]{2,1,0:T(8,128)(2,1)}, u32[]{:S(2)}, u32[]{:S(2)}) collective-permute-start(bf16[4,256,1024]{2,1,0:T(8,128)(2,1)} %get-tuple-element.115), channel_id=1, source_target_pairs={{0,4},{4,0},{1,5},{5,1},{2,6},{6,2},{3,7},{7,3},{8,12},{12,8},{9,1... | collective-permute-start | bytes 6291464 | tf_op jit(solution)/shard_map/ppermute | solution.py:26
  170.7 5.8 %collective-permute-start.13 = (bf16[1,1024,1024]{2,1,0:T(8,128)(2,1)}, bf16[1,1024,1024]{2,1,0:T(8,128)(2,1)S(1)}, u32[]{:S(2)}, u32[]{:S(2)}) collective-permute-start(bf16[1,1024,1024]{2,1,0:T(8,128)(2,1)} %get-tuple-element.122), channel_id=1, source_target_pairs={{0,4},{4,0},{1,5},{5,1},{2,6},{6,2},{3,7},{7,3},{8,12},{12,8},{9,1... | collective-permute-start | bytes 6291464 | tf_op jit(solution)/shard_map/ppermute | solution.py:26
  174.2 2.3 copy-start.15
  174.2 15.5 %collective-permute-start.16 = (bf16[2,128,1024]{2,1,0:T(8,128)(2,1)S(1)}, bf16[2,128,1024]{2,1,0:T(8,128)(2,1)S(1)}, u32[]{:S(2)}, u32[]{:S(2)}) collective-permute-start(bf16[2,128,1024]{2,1,0:T(8,128)(2,1)S(1)} %dynamic-slice_bitcast_fusion.3), channel_id=1, source_target_pairs={{0,96},{96,0},{32,64},{64,32},{1,97},{97,1},{33,65},{65,33},{2,98}... | collective-permute-start | bytes 1572872 | tf_op jit(solution)/shard_map/ppermute | solution.py:312
  176.1 14.2 %collective-permute-start.15 = (bf16[2,128,1024]{2,1,0:T(8,128)(2,1)}, bf16[2,128,1024]{2,1,0:T(8,128)(2,1)S(1)}, u32[]{:S(2)}, u32[]{:S(2)}) collective-permute-start(bf16[2,128,1024]{2,1,0:T(8,128)(2,1)} %dynamic-slice_bitcast_fusion.4), channel_id=1, source_target_pairs={{0,32},{32,0},{64,96},{96,64},{1,33},{33,1},{65,97},{97,65},{2,34}... | collective-permute-start | bytes 1572872 | tf_op jit(solution)/shard_map/ppermute | solution.py:312
  177.7 25.0 %collective-permute-start.14 = (bf16[2,16,16,1024]{3,2,0,1:T(8,128)(2,1)S(1)}, bf16[2,16,16,1024]{3,2,0,1:T(8,128)(2,1)S(1)}, u32[]{:S(2)}, u32[]{:S(2)}) collective-permute-start(bf16[2,16,16,1024]{3,2,0,1:T(8,128)(2,1)S(1)} %dynamic-slice_bitcast_fusion), channel_id=1, source_target_pairs={{0,1},{1,0},{2,3},{3,2},{4,5},{5,4},{6,7},{7,6},{8,9},{9,8},{10,11... | collective-permute-start | bytes 3145736 | tf_op jit(solution)/shard_map/ppermute | solution.py:312
  187.3 19.0 %collective-permute-start.18 = (bf16[1,512,1024]{2,1,0:T(8,128)(2,1)}, bf16[1,512,1024]{2,1,0:T(8,128)(2,1)S(1)}, u32[]{:S(2)}, u32[]{:S(2)}) collective-permute-start(bf16[1,512,1024]{2,1,0:T(8,128)(2,1)} %get-tuple-element.126), channel_id=1, source_target_pairs={{0,4},{4,0},{1,5},{5,1},{2,6},{6,2},{3,7},{7,3},{8,12},{12,8},{9,1... | collective-permute-start | bytes 3145736 | tf_op jit(solution)/shard_map/ppermute | solution.py:26
  190.5 16.5 %collective-permute-start.20 = (bf16[128,1024]{1,0:T(8,128)(2,1)S(1)}, bf16[128,1024]{1,0:T(8,128)(2,1)S(1)}, u32[]{:S(2)}, u32[]{:S(2)}) collective-permute-start(bf16[128,1024]{1,0:T(8,128)(2,1)S(1)} %dynamic-slice_bitcast_fusion.7), channel_id=1, source_target_pairs={{0,96},{96,0},{32,64},{64,32},{1,97},{97,1},{33,65},{65,33},{2,98}... | collective-permute-start | bytes 786440 | tf_op jit(solution)/shard_map/ppermute | solution.py:312
  193.1 13.2 %copy-start.17 = (bf16[1,512,1024]{2,1,0:T(8,128)(2,1)S(1)}, bf16[1,512,1024]{2,1,0:T(8,128)(2,1)}, u32[]{:S(2)}) copy-start(bf16[1,512,1024]{2,1,0:T(8,128)(2,1)} %get-tuple-element.131) | copy-start | bytes 3145732
  193.2 13.9 %collective-permute-start.21 = (bf16[128,1024]{1,0:T(8,128)(2,1)S(1)}, bf16[128,1024]{1,0:T(8,128)(2,1)S(1)}, u32[]{:S(2)}, u32[]{:S(2)}) collective-permute-start(bf16[128,1024]{1,0:T(8,128)(2,1)S(1)} %dynamic-slice_bitcast_fusion.6), channel_id=1, source_target_pairs={{0,32},{32,0},{64,96},{96,64},{1,33},{33,1},{65,97},{97,65},{2,34}... | collective-permute-start | bytes 786440 | tf_op jit(solution)/shard_map/ppermute | solution.py:312
  203.2 32.8 %collective-permute-start.17 = (bf16[16,16,1024]{2,1,0:T(8,128)(2,1)S(1)}, bf16[16,16,1024]{2,1,0:T(8,128)(2,1)S(1)}, u32[]{:S(2)}, u32[]{:S(2)}) collective-permute-start(bf16[16,16,1024]{2,1,0:T(8,128)(2,1)S(1)} %dynamic-slice_bitcast_fusion.2), channel_id=1, source_target_pairs={{0,3},{3,0},{1,2},{2,1},{4,7},{7,4},{5,6},{6,5},{8,11},{11,8},{9,1... | collective-permute-start | bytes 1572872 | tf_op jit(solution)/shard_map/ppermute | solution.py:312
  206.8 21.9 %collective-permute-start.19 = (bf16[2,16,8,1024]{3,2,0,1:T(8,128)(2,1)S(1)}, bf16[2,16,8,1024]{3,2,0,1:T(8,128)(2,1)S(1)}, u32[]{:S(2)}, u32[]{:S(2)}) collective-permute-start(bf16[2,16,8,1024]{3,2,0,1:T(8,128)(2,1)S(1)} %dynamic-slice_bitcast_fusion.1), channel_id=1, source_target_pairs={{0,3},{3,0},{1,2},{2,1},{4,7},{7,4},{5,6},{6,5},{8,11},{11,8},{9,1... | collective-permute-start | bytes 1572872 | tf_op jit(solution)/shard_map/ppermute | solution.py:312
  228.9 7.3 %collective-permute-start.22 = (bf16[16,8,1024]{2,1,0:T(8,128)(2,1)S(1)}, bf16[16,8,1024]{2,1,0:T(8,128)(2,1)}, u32[]{:S(2)}, u32[]{:S(2)}) collective-permute-start(bf16[16,8,1024]{2,1,0:T(8,128)(2,1)S(1)} %dynamic-slice_bitcast_fusion.5), channel_id=1, source_target_pairs={{0,1},{1,0},{2,3},{3,2},{4,5},{5,4},{6,7},{7,6},{8,9},{9,8},{10,11... | collective-permute-start | bytes 786440 | tf_op jit(solution)/shard_map/ppermute | solution.py:312
  229.0 17.1 %all-to-all-start.3 = ((bf16[16,16,1024]{2,1,0:T(8,128)(2,1)}), bf16[16,16,1024]{2,1,0:T(8,128)(2,1)S(1)}, u32[]{:S(2)}, u32[]{:S(2)}) async-start(bf16[16,16,1024]{2,1,0:T(8,128)(2,1)} %bitcast.43), calls=%async_computation.3 | async-start | bytes 1048576 | tf_op jit(solution)/shard_map/all_to_all | solution.py:486
  237.2 30.4 %copy-start.1 = (f32[8,768]{1,0:T(8,128)S(1)}, f32[8,768]{1,0:T(8,128)}, u32[]{:S(2)}) copy-start(f32[8,768]{1,0:T(8,128)} %param.11) | copy-start | bytes 73732
  246.1 16.1 %all-to-all-start.2 = ((bf16[16,24,1024]{2,1,0:T(8,128)(2,1)}), bf16[16,24,1024]{2,1,0:T(8,128)(2,1)S(1)}, u32[]{:S(2)}, u32[]{:S(2)}) async-start(bf16[16,24,1024]{2,1,0:T(8,128)(2,1)} %pad_maximum_fusion), calls=%async_computation.2 | async-start | bytes 1572864 | tf_op jit(solution)/shard_map/all_to_all | solution.py:493

commit v7 on v3

--- a/solution.py
+++ b/solution.py
@@ -34,97 +34,122 @@
     return pltpu.CompilerParams(dimension_semantics=("arbitrary",), vmem_limit_bytes=mib * MIB)
 
 
-def forward_kernel(first_call, last_call, block_rows, sizes, *refs):
+def forward_kernel(groups, first_call, last_call, sizes, *refs):
     width, half, head_rows = sizes
-    place, tokens, mine, theirs = refs[:4]
-    refs = refs[4:]
+    place, tokens = refs[:2]
+    packs = [(refs[2 + 4 * g : 4 + 4 * g], refs[4 + 4 * g : 6 + 4 * g]) for g in range(groups)]
+    refs = refs[2 + 4 * groups :]
     if first_call:
-        total_in = None
         slope, hidden, second, head, total = refs
     elif last_call:
         total_in, _, _, _, head_in, slope, hidden, second, head, residual, forecast = refs
+    elif groups > 1:
+        total_in, _, _, _, _, slope, hidden, second, head, total, kept = refs
     else:
         total_in, _, _, _, _, slope, hidden, second, head, total = refs
-    block, core = place[0], place[1]
+    group, step = pl.program_id(0), pl.program_id(1)
+    core = place[1]
     chunks = width // LANES
-    start = width
-    head_start = start + chunks * half
-
-    @pl.when(pl.program_id(0) == 0)
-    def _():
+    sides = (core, 1 - core)
+
+    def run(g):
+        @pl.when(step == 0)
+        def _():
+            if last_call:
+                head[...] = head_in[...]
+            for pair, side in zip(packs[g], sides):
+                below = pl.multiple_of(side * half, half)
+                for q in range(chunks):
+                    second[pl.ds(below, half), q * LANES : (q + 1) * LANES] = pair[1][
+                        q * half : (q + 1) * half, :
+                    ]
+                row = pl.multiple_of(place[3] * head_rows, 64) if last_call else 0
+                for e in range(2):
+                    lane = pl.multiple_of(side * (width // 2) + e * LANES, LANES)
+                    head[pl.ds(row, head_rows), pl.ds(lane, LANES)] = pair[e][width:, :]
+
+        rows = tokens[...]
+        count = rows.shape[0]
+        line = pl.multiple_of(step * count, count)
+        if first_call:
+            base = rows.astype(F32)
+        elif g == 0:
+            base = total_in[...]
+        else:
+            base = kept[pl.ds(line, count), :]
+        sums = [base[:, q * LANES : (q + 1) * LANES] for q in range(chunks)]
+        for pair, side in zip(packs[g], sides):
+            x = dot(rows, pair[0][:width, :])
+            sq = x * x
+            t = jnp.tanh(ROOT_2_PI * (x + CUBIC * x * sq))
+            up = 0.5 * (1.0 + t)
+            active = (x * up).astype(BF16)
+            lane = pl.multiple_of(side * half, half)
+            turn = up + (0.5 * ROOT_2_PI) * x * (1.0 - t * t) * (1.0 + (3.0 * CUBIC) * sq)
+            slope[:, pl.ds(lane, half)] = turn.astype(BF16)
+            hidden[:, pl.ds(lane, half)] = active
+            for q in range(chunks):
+                sums[q] = sums[q] + dot(active, pair[1][q * half : (q + 1) * half, :])
+        full = jnp.concatenate(sums, 1)
         if last_call:
-            head[...] = head_in[...]
-        for pack, side in ((mine, core), (theirs, 1 - core)):
-            below = pl.multiple_of(side * half, half)
-            for q in range(chunks):
-                second[pl.ds(below, half), q * LANES : (q + 1) * LANES] = pack[
-                    start + q * half : start + (q + 1) * half, :
-                ]
-            for e in range(2):
-                piece = pack[head_start + e * head_rows : head_start + (e + 1) * head_rows, :]
-                lane = pl.multiple_of(side * (width // 2) + e * LANES, LANES)
-                row = pl.multiple_of(block * head_rows, 64) if last_call else 0
-                head[pl.ds(row, head_rows), pl.ds(lane, LANES)] = piece
-
-    rows = tokens[...]
-    base = rows.astype(F32) if first_call else total_in[...]
-    sums = [base[:, q * LANES : (q + 1) * LANES] for q in range(chunks)]
-    for pack, side in ((mine, core), (theirs, 1 - core)):
-        x = dot(rows, pack[:width, :])
-        sq = x * x
-        t = jnp.tanh(ROOT_2_PI * (x + CUBIC * x * sq))
-        up = 0.5 * (1.0 + t)
-        active = (x * up).astype(BF16)
-        lane = pl.multiple_of(side * half, half)
-        slope[:, pl.ds(lane, half)] = up + (0.5 * ROOT_2_PI) * x * (1.0 - t * t) * (
-            1.0 + (3.0 * CUBIC) * sq
-        )
-        hidden[:, pl.ds(lane, half)] = active
-        for q in range(chunks):
-            sums[q] = sums[q] + dot(active, pack[start + q * half : start + (q + 1) * half, :])
-    full = jnp.concatenate(sums, 1)
-    if last_call:
-        rounded = full.astype(BF16)
-        residual[...] = rounded
-        forecast[...] = dot(rounded, head[...], ((1,), (1,))).astype(BF16)
-    else:
-        total[...] = full
-
-
-def forward_part(place, tokens, mine, theirs, carried, out_width, last_call):
+            rounded = full.astype(BF16)
+            residual[...] = rounded
+            forecast[...] = dot(rounded, head[...], ((1,), (1,))).astype(BF16)
+        elif g + 1 < groups:
+            kept[pl.ds(line, count), :] = full
+        else:
+            total[...] = full
+
+    for g in range(groups):
+        if groups == 1:
+            run(g)
+        else:
+            pl.when(group == g)(functools.partial(run, g))
+
+
+def forward_part(place, tokens, packs, carried, out_width, last_call):
     rows, width = tokens.shape
+    groups = len(packs) // 4
     half = LANES
     hid = 2 * half * RING
     head_rows = out_width // RING
     first_call = carried is None
     block_rows = min(rows, 256)
     whole = lambda shape: pl.BlockSpec(
-        shape, lambda i, s: (0,) * len(shape), pipeline_mode=pl.Buffered(1)
-    )
-    by_rows = lambda cols: pl.BlockSpec((block_rows, cols), lambda i, s: (i, 0))
+        shape, lambda g, i, s: (0,) * len(shape), pipeline_mode=pl.Buffered(1)
+    )
+    by_rows = lambda cols: pl.BlockSpec((block_rows, cols), lambda g, i, s: (i, 0))
+    last_of = rows // block_rows - 1
+    entering = pl.BlockSpec(
+        (block_rows, width), lambda g, i, s: (jnp.where(g == 0, i, last_of), 0)
+    )
+    leaving = pl.BlockSpec(
+        (block_rows, width), lambda g, i, s: (jnp.where(g == groups - 1, i, 0), 0)
+    )
     in_place = pl.BlockSpec(memory_space=pl.ANY)
-    in_specs = [by_rows(width), whole(mine.shape), whole(theirs.shape)]
-    args = [tokens, mine, theirs]
+    in_specs = [by_rows(width), *[whole(p.shape) for p in packs]]
+    args = [tokens, *packs]
     aliases = {}
     if not first_call:
         slope, hidden, second, head, total = carried
+        at = 1 + len(args)
         args += [total, slope, hidden, second, head]
-        in_specs += [by_rows(width), in_place, in_place, in_place]
+        in_specs += [entering, in_place, in_place, in_place]
         in_specs += [whole((out_width, width)) if last_call else in_place]
-        aliases = {5: 0, 6: 1, 7: 2}
+        aliases = {at + 1: 0, at + 2: 1, at + 3: 2}
         if not last_call:
-            aliases = {**aliases, 8: 3, 4: 4}
-    column = pl.BlockSpec((block_rows, 2 * half), lambda i, s: (i, s[0]))
+            aliases = {**aliases, at + 4: 3}
+    column = pl.BlockSpec((block_rows, 2 * half), lambda g, i, s: (i, s[3 + g]))
     out_specs = [
         column,
         column,
-        pl.BlockSpec((2 * half, width), lambda i, s: (s[0], 0)),
+        pl.BlockSpec((2 * half, width), lambda g, i, s: (s[3 + g], 0)),
         whole((out_width, width))
         if last_call
-        else pl.BlockSpec((head_rows, width), lambda i, s: (s[0], 0)),
+        else pl.BlockSpec((head_rows, width), lambda g, i, s: (s[3 + g], 0)),
     ]
     out_shape = [
-        jax.ShapeDtypeStruct((rows, hid), F32),
+        jax.ShapeDtypeStruct((rows, hid), BF16),
         jax.ShapeDtypeStruct((rows, hid), BF16),
         jax.ShapeDtypeStruct((hid, width), BF16),
         jax.ShapeDtypeStruct((out_width, width), BF16),
@@ -136,23 +161,28 @@
             jax.ShapeDtypeStruct((rows, out_width), BF16),
         ]
     else:
-        out_specs += [by_rows(width)]
+        out_specs += [leaving]
         out_shape += [jax.ShapeDtypeStruct((rows, width), F32)]
     return pl.pallas_call(
         functools.partial(
-            forward_kernel, first_call, last_call, block_rows, (width, half, head_rows)
+            forward_kernel, groups, first_call, last_call, (width, half, head_rows)
         ),
         grid_spec=pltpu.PrefetchScalarGridSpec(
             num_scalar_prefetch=1,
-            grid=(rows // block_rows,),
+            grid=(groups, rows // block_rows),
             in_specs=in_specs,
             out_specs=out_specs,
+            scratch_shapes=[pltpu.VMEM((rows, width), F32)] if groups > 1 else [],
         ),
         out_shape=out_shape,
         input_output_aliases=aliases,
-        compiler_params=params(24),
+        compiler_params=pltpu.CompilerParams(
+            dimension_semantics=("arbitrary",) * 2, vmem_limit_bytes=56 * MIB
+        ),
         cost_estimate=pl.CostEstimate(
-            flops=8 * rows * width * half, bytes_accessed=12 * MIB, transcendentals=rows * 2 * half
+            flops=8 * groups * rows * width * half,
+            bytes_accessed=12 * MIB,
+            transcendentals=groups * rows * 2 * half,
         ),
         name="forward_part",
     )(place, *args)
@@ -224,7 +254,7 @@
             out_specs=[out, out],
         ),
         out_shape=[jax.ShapeDtypeStruct((RING, lines, width), BF16)] * 2,
-        compiler_params=params(32),
+        compiler_params=params(56),
         cost_estimate=pl.CostEstimate(
             flops=2 * rows * width * (hid + out_width), bytes_accessed=18 * MIB, transcendentals=0
         ),
@@ -234,7 +264,7 @@
 
 def late_kernel(place, resid_grad, second, slope, tokens, keep, send):
     hidden_grad = dot(resid_grad[...], second[...], ((1,), (1,)))
-    preact_grad = (slope[...] * hidden_grad).astype(BF16)
+    preact_grad = (slope[...].astype(F32) * hidden_grad).astype(BF16)
     first = dot(tokens[...], preact_grad, ((0,), (0,)))
     cols = first.shape[1]
     parts = first.reshape(16, 2, RING, -1, cols)
@@ -261,7 +291,7 @@
             out_specs=[out, out],
         ),
         out_shape=[jax.ShapeDtypeStruct((1, width // 2, width), BF16)] * 2,
-        compiler_params=params(28),
+        compiler_params=params(56),
         cost_estimate=pl.CostEstimate(
             flops=4 * rows * width * width, bytes_accessed=12 * MIB, transcendentals=0
         ),
@@ -292,20 +322,18 @@
     return [(pairs, axis, bit, dim) for pairs, bit, dim in steps]
 
 
-def outgoing(x, step):
-    _, _, bit, dim = step
-    return take(x, 1 - bit, dim)
+def outgoing(parts, step):
+    return add(*[take(x, 1 - step[2], step[3]) for x in parts])
+
+
+def staying(parts, step):
+    return add(*[take(x, step[2], step[3]) for x in parts])
 
 
 def sent_along(x, step):
     return lax.ppermute(x, step[1], step[0])
 
 
-def kept_plus(x, arrived, step):
-    _, _, bit, dim = step
-    return add(take(x, bit, dim), arrived)
-
-
 def by_ring(x):
     return x.reshape(16, 2, 2, -1, x.shape[-1]).transpose(1, 2, 0, 3, 4)
 
@@ -318,22 +346,21 @@
     return lax.optimization_barrier((x, *others))[0]
 
 
-def pack_kernel(side, first, second, head, out):
-    width, half = first.shape
-    out[:width, :] = first[...]
-    at = width
-    for q in range(second.shape[1] // LANES):
-        out[at : at + half, :] = second[:, q * LANES : (q + 1) * LANES]
-        at += half
-    for e in range(head.shape[1] // LANES):
-        out[at : at + head.shape[0], :] = head[:, e * LANES : (e + 1) * LANES]
-        at += head.shape[0]
+def pack_kernel(side, first, second, head, a, b):
+    width = first.shape[0]
+    half = second.shape[0]
+    a[:width, :] = first[...]
+    for q in range(width // LANES):
+        b[q * half : (q + 1) * half, :] = second[:, q * LANES : (q + 1) * LANES]
+    a[width:, :] = head[:, :LANES]
+    b[width:, :] = head[:, LANES:]
 
 
 def packed(side, first, second, head):
     width, shard = first.shape
     half = shard // 2
-    lines = width + half * width // LANES + head.shape[0] * width // 2 // LANES
+    lines = width + head.shape[0]
+    out = pl.BlockSpec((lines, LANES), lambda i, s: (0, 0))
     return pl.pallas_call(
         pack_kernel,
         grid_spec=pltpu.PrefetchScalarGridSpec(
@@ -344,9 +371,9 @@
                 pl.BlockSpec((half, width), lambda i, s: (s[0], 0)),
                 pl.BlockSpec((head.shape[0], width // 2), lambda i, s: (0, s[0])),
             ],
-            out_specs=pl.BlockSpec((lines, LANES), lambda i, s: (0, 0)),
-        ),
-        out_shape=jax.ShapeDtypeStruct((lines, LANES), BF16),
+            out_specs=[out, out],
+        ),
+        out_shape=[jax.ShapeDtypeStruct((lines, LANES), BF16)] * 2,
         compiler_params=params(8),
         name="packed",
     )(side, first, second, head)
@@ -389,30 +416,35 @@
 
     side = jnp.reshape(core, (1,)).astype(jnp.int32)
     turned = readout_matrix.T
-    mine = packed(side, w_first, w_second, turned)
-    right = shift(mine, "y", 1)
-    left = shift(mine, "y", -1)
-    lines = mine.shape[0] // 2
-    latents, other_side, mine = tie(latents, 1 - side, mine)
+    own_a, own_b = packed(side, w_first, w_second, turned)
+    right_a = shift(own_a, "y", 1)
+    left_b = shift(own_b, "y", -1)
+    latents, other_side, own_a, own_b = tie(latents, 1 - side, own_a, own_b)
     tokens = (
         latents.reshape(members, 32, own, width).transpose(1, 0, 2, 3).reshape(rows, width)
     )
-    theirs = packed(other_side, w_first, w_second, turned)
-    place = lambda off: jnp.stack([(here + off) % RING, core, lax.axis_index("x")]).astype(jnp.int32)
+    place = lambda *offs: jnp.stack(
+        [here, core, lax.axis_index("x"), *[(here + off) % RING for off in offs]]
+    ).astype(jnp.int32)
     run = functools.partial(forward_part, out_width=out_width)
-    carried = run(place(0), tokens, mine, theirs, carried=None, last_call=False)
-    right, left, *carried = tie(right, left, *carried)
-    far = [right[:lines], left[lines:]]
-    right_other = shift(after(right, *far), "c", 1)
-    left_other = shift(after(left, *far), "c", 1)
-    far = [shift(far[0], "y", 1), shift(far[1], "y", -1)]
-    carried = run(place(3), tokens, right, right_other, carried=carried, last_call=False)
-    carried = run(place(1), tokens, left, left_other, carried=carried, last_call=False)
-    near, past, *carried = tie(*far, *carried)
-    far = jnp.concatenate([near, past], 0)
-    far_other = shift(far, "c", 1)
+    swap = lambda x: shift(x, "c", 1)
+    packs = (own_a, own_b, *packed(other_side, w_first, w_second, turned))
+    carried = run(place(0), tokens, packs, carried=None, last_call=False)
+    right_a, left_b, *_ = tie(right_a, left_b, carried[-1])
+    left_a = shift(after(own_a, right_a, left_b), "y", -1)
+    right_b = shift(after(own_b, right_a, left_b), "y", 1)
+    right_a_other, left_b_other = swap(right_a), swap(left_b)
+    left_a, right_b, right_a_other, left_b_other = tie(
+        left_a, right_b, right_a_other, left_b_other
+    )
+    far_a = shift(after(right_a, left_a, right_b), "y", 1)
+    far_b = shift(after(left_b, left_a, right_b), "y", -1)
+    packs = (right_a, right_b, right_a_other, swap(right_b))
+    packs = (*packs, left_a, left_b, swap(left_a), left_b_other)
+    carried = run(place(3, 1), tokens, packs, carried=carried, last_call=False)
+    far_a, far_b, *carried = tie(far_a, far_b, *carried)
     slope, hidden, second, head, residual, forecast = run(
-        place(2), tokens, far, far_other, carried=carried, last_call=True
+        place(2), tokens, (far_a, far_b, swap(far_a), swap(far_b)), carried=carried, last_call=True
     )
 
     group = ("x", "z", "c")
@@ -435,37 +467,37 @@
     a_in = shift(late[1], "c", 1)
     x_steps = [ring_chain("x", True), ring_chain("x", False)]
     y_steps = [ring_chain("y", True), ring_chain("y", False)]
-    early = add(after(early[0], late[1]), early_in).reshape(2, 2, 2, -1, width)
-    early = [early[:, :, 0], early[:, :, 1]]
+    early = [v.reshape(2, 2, 2, -1, width) for v in (after(early[0], late[1]), early_in)]
+    early = [[v[:, :, i] for v in early] for i in range(2)]
     early_sent = [outgoing(x, steps[0]) for x, steps in zip(early, x_steps)]
     early_in = [sent_along(x, steps[0]) for x, steps in zip(early_sent, x_steps)]
-    a = by_ring(add(after(late[0], *early_sent), a_in))
+    a = [by_ring(after(late[0], *early_sent)), by_ring(a_in)]
     a_sent = outgoing(a, y_steps[0][0])
     a_in = sent_along(a_sent, y_steps[0][0])
+    early = [staying(x, steps[0]) for x, steps in zip(early, x_steps)]
+    a = staying(a, y_steps[0][0])
     late = late_grads(at, 1, after(resid_grad, a_sent), second, slope, tokens)
     b_in = shift(after(late[1], a_in, *early_in), "c", 1)
-    a = kept_plus(a, a_in, y_steps[0][0])
+    a = [a, a_in]
     a_sent = outgoing(a, y_steps[0][1])
     a_in = sent_along(a_sent, y_steps[0][1])
-    b = by_ring(add(after(late[0], a_sent), b_in))
+    b = [by_ring(after(late[0], a_sent)), by_ring(b_in)]
     b_sent = outgoing(b, y_steps[1][0])
     b_in = sent_along(b_sent, y_steps[1][0])
-    early = [
-        kept_plus(x, after(v, b_sent), steps[0]) for x, v, steps in zip(early, early_in, x_steps)
-    ]
+    early = [[x, after(v, b_sent)] for x, v in zip(early, early_in)]
     early_sent = [outgoing(x, steps[1]) for x, steps in zip(early, x_steps)]
     early_in = [sent_along(x, steps[1]) for x, steps in zip(early_sent, x_steps)]
-    b = kept_plus(b, after(b_in, *early_sent), y_steps[1][0])
+    early = [staying(x, steps[1]) for x, steps in zip(early, x_steps)]
+    a = staying(a, y_steps[0][1])
+    b = [staying(b, y_steps[1][0]), after(b_in, *early_sent)]
     b_sent = outgoing(b, y_steps[1][1])
     b_in = sent_along(b_sent, y_steps[1][1])
-    early = [
-        kept_plus(x, after(v, b_sent), steps[1]) for x, v, steps in zip(early, early_in, x_steps)
-    ]
+    b = staying(b, y_steps[1][1])
+    early = [add(x, after(v, b_sent)) for x, v in zip(early, early_in)]
     early = jnp.concatenate(early).reshape(16, -1, width)
-    a = kept_plus(a, after(a_in, early), y_steps[0][1])
-    b = kept_plus(b, b_in, y_steps[1][1])
     early = lax.all_to_all(early, ("z", "y"), 0, 0, tiled=True)
-    late = lax.all_to_all(jnp.concatenate([a, b], 1), ("x", "z"), 0, 0, tiled=True)
+    late = jnp.concatenate([add(a, a_in), add(b, b_in)], 1)
+    late = lax.all_to_all(late, ("x", "z"), 0, 0, tiled=True)
     early = jnp.sum(early.astype(F32), 0)
     late = jnp.sum(late.astype(F32), 0)
     n_second = shard * RING // 128

time: 292 us -> 261 us (0.89)
  local copies, waits for them, and re-layouts: 72.5 us -> 20.8 us
  Pallas kernels: 55.2 us -> 68.1 us
  waiting for transfers between devices: 66.4 us -> 72.6 us
    unnamed x110 -> x78, local copies, waits for them, and re-layouts: 60.2 us -> 10.1 us
    ppermute x10 -> x15, waiting for transfers between devices: 9.19 us -> 16.2 us  [shift(): return lax.ppermute(x, axis, [(i, (i + by) % size) for i in range(size)])]
    pallas_call x4 -> x3, Pallas kernels: 29.9 us -> 36.5 us  [forward_part(): pl.pallas_call(functools.partial(forward_kernel, groups, first_call, last...]
    pallas_call x2, Pallas kernels: 12.9 us -> 19.3 us  [late_grads(): pl.pallas_call(late_kernel, grid_spec=pltpu.PrefetchScalarGridSpec(num_sc...]
    ppermute x10 -> x15, starting transfers between devices: 8.01 us -> 11.7 us  [shift(): return lax.ppermute(x, axis, [(i, (i + by) % size) for i in range(size)])]
    convert_element_type x11 -> x13, other arithmetic: 12.7 us -> 12.6 us  [add(): return (a.astype(F32) + b.astype(F32)).astype(BF16)]
  transfers between devices with their start and end apart: 21 -> 26, of which waited for: 11 -> 11; matrix products, arithmetic and copies ran while one was open for 8% -> 9% of each run, Pallas kernels for 12% -> 17%
where the time goes in v7:
time: 261 us; the launch traced here: 260 us
  waiting for transfers between devices  72.6 us (28%)
  Pallas kernels  68.1 us (26%)
  starting transfers between devices  34.7 us (13%)
  blocking collectives  30.5 us (12%)
  other arithmetic  21.2 us (8%)
  local copies, waits for them, and re-layouts  20.8 us (8%)
  matrix products  6.83 us (3%)
  between operations  4.91 us (2%)
    pallas_call x3, Pallas kernels, forward_part(): pl.pallas_call(functools.partial(forward_kernel, groups, first_call, last...  36.5 us
    all_to_all x1, blocking collectives, per_device(): gathered = lax.all_to_all(forecast, group, 0, 0, tiled=True)  30.5 us
    ppermute x8, waiting for transfers between devices, sent_along(): return lax.ppermute(x, step[1], step[0])  29.8 us
    all_to_all x1, waiting for transfers between devices, per_device(): lax.all_to_all(grad_raw.reshape(32, members * own, out_width), group, 0,...  21.3 us
    pallas_call x2, Pallas kernels, late_grads(): pl.pallas_call(late_kernel, grid_spec=pltpu.PrefetchScalarGridSpec(num_sc...  19.3 us
    ppermute x15, waiting for transfers between devices, shift(): return lax.ppermute(x, axis, [(i, (i + by) % size) for i in range(size)])  16.2 us
    convert_element_type x13, other arithmetic, add(): return (a.astype(F32) + b.astype(F32)).astype(BF16)  12.6 us
    pallas_call x1, Pallas kernels, early_grads(): pl.pallas_call(early_kernel, grid_spec=pltpu.PrefetchScalarGridSpec(num_s...  12.2 us
  transfers between devices with their start and end apart: 26, of which 11 were waited for; matrix products, arithmetic and copies ran while one was open for 9% of the time, Pallas kernels for 17%

profile of v7, /device:TPU:0, one launch (start us, length us, event | category | flops | bytes accessed | tf_op | source)
XLA Modules:
  0.0 259.7 jit_solution(1276578036279617327)
XLA Ops:
  0.7 1.2 copy-done.2
  1.9 1.2 copy-done.4
  3.1 1.0 copy-done.6
  4.2 1.7 collective-permute-start
  5.9 1.6 collective-permute-start.1
  7.5 1.6 copy.28
  9.1 0.7 copy-done.5
  10.0 0.8 copy-done.12
  10.8 0.8 copy-done.13
  11.7 0.6 pad_add_fusion.2
  12.9 9.1 %forward_part.3 = (bf16[1024,2048]{1,0:T(8,128)(2,1)}, bf16[1024,2048]{1,0:T(8,128)(2,1)}, bf16[2048,1024]{1,0:T(8,128)(2,1)}, bf16[768,1024]{1,0:T(8,128)(2,1)}, f32[1024,1024]{1,0:T(8,128)}) custom-call(s32[4]{0:T(128)} %pad_add_fusion.refs_0_.place, bf16[1024,1024]{1,0:T(8,128)(2,1)} %bitcast.107, bf16[1216,256]{1,0:T(8,128)(2,1)} %copy-done.8, ...), custom_call_target="tpu_custom_call" | custom-call | flops 2147483648 | bytes 12582912 | tf_op jit(solution)/shard_map/forward_part/pallas_call | solution.py:166
  22.0 1.1 collective-permute-start.3
  23.1 2.2 collective-permute-start.2
  25.8 12.9 %collective-permute-done.3.refs_3_ = bf16[1216,256]{1,0:T(8,128)(2,1)S(1)} collective-permute-done((bf16[1216,256]{1,0:T(8,128)(2,1)S(1)}, bf16[1216,256]{1,0:T(8,128)(2,1)S(1)}, u32[]{:S(2)}, u32[]{:S(2)}) %collective-permute-start.3) | collective-permute-done | bytes 622624 | tf_op jit(solution)/shard_map/ppermute | solution.py:26
  39.6 2.9 %collective-permute-start.7 = (bf16[1216,256]{1,0:T(8,128)(2,1)}, bf16[1216,256]{1,0:T(8,128)(2,1)S(1)}, u32[]{:S(2)}, u32[]{:S(2)}) collective-permute-start(bf16[1216,256]{1,0:T(8,128)(2,1)} %collective-permute-done.1.refs_7_), channel_id=1, source_target_pairs={{0,3},{1,0},{2,1},{3,2},{4,7},{5,4},{6,5},{7,6},{8,11},{9,8},{10,9... | collective-permute-start | bytes 1867784 | tf_op jit(solution)/shard_map/ppermute | solution.py:26
  42.6 0.7 stack.59.refs_0_
  43.3 16.2 %forward_part.4 = (bf16[1024,2048]{1,0:T(8,128)(2,1)}, bf16[1024,2048]{1,0:T(8,128)(2,1)}, bf16[2048,1024]{1,0:T(8,128)(2,1)}, bf16[768,1024]{1,0:T(8,128)(2,1)}, f32[1024,1024]{1,0:T(8,128)}) custom-call(s32[5]{0:T(128)} %stack.59.refs_0_, ...), custom_call_target="tpu_custom_call", output_to_operand_aliasing={{0}: (11, {}), {1}: (12, {}), {2}: (13, {}), {3}: (14, {})} | custom-call | flops 4294967296 | bytes 12582912 | tf_op jit(solution)/shard_map/forward_part/pallas_call | solution.py:166
  60.8 0.9 collective-permute-done.10.refs_4_
  61.7 0.9 collective-permute-done.11.refs_5_
  62.6 0.8 copy-done.31
  63.4 11.1 %forward_part.5 = (bf16[1024,2048]{1,0:T(8,128)(2,1)}, bf16[1024,2048]{1,0:T(8,128)(2,1)}, bf16[2048,1024]{1,0:T(8,128)(2,1)}, bf16[768,1024]{1,0:T(8,128)(2,1)}...) custom-call(s32[4]{0:T(128)} %get-tuple-element.132.refs_0_, ...), custom_call_target="tpu_custom_call", output_to_operand_aliasing={{0}: (7, {}), {1}: (8, {}), {2}: (9, {})} | custom-call | flops 2147483648 | bytes 12582912 | tf_op jit(solution)/shard_map/forward_part/pallas_call | solution.py:166
  74.6 30.5 %all_to_all.20 = bf16[32,32,768]{2,1,0:T(8,128)(2,1)S(1)} all-to-all(bf16[32,32,768]{2,1,0:T(8,128)(2,1)} %bitcast.120), channel_id=1, replica_groups=mesh['x'=4,'z'=4,'c'=2,'y'=4] {'x','z','c'}, dimensions={0} | all-to-all | bytes 3145728 | tf_op jit(solution)/shard_map/all_to_all | solution.py:454
  105.3 0.8 fusion.6
  106.4 0.9 fusion.50
  108.0 2.8 %fusion.8 = bf16[128,8,768]{2,0,1:T(8,128)(2,1)S(1)} fusion(f32[128,8]{0,1:T(8,128)S(1)} %bitcast.125, f32[128,8]{0,1:T(8,128)S(1)} %copy.31, f32[8,768]{1,0:T(8,128)S(1)} %broadcast_select_fusion, f32[8]{0:T(128)S(1)} %get-tuple-element.154, bf16[128,8,768]{2,1,0:T(8,128)(2,1)S(1)} %bitcast.114, f32[8,128,128]{1,2,0:T(8,128)S(1)} %get-tuple-element.155), kind=kOutput, calls=%fused_computation.13 | convolution fusion | flops 1215168512 | bytes 3702816 | tf_op jit(solution)/shard_map/pmn,npo->mpo/dot_general | solution.py:391
  110.8 2.0 copy.38
  112.8 4.2 %all-to-all-start.1 = ((bf16[32,32,768]{2,1,0:T(8,128)(2,1)}), bf16[32,32,768]{2,1,0:T(8,128)(2,1)S(1)}, u32[]{:S(2)}, u32[]{:S(2)}) async-start(bf16[32,32,768]{2,1,0:T(8,128)(2,1)} %bitcast.18), calls=%async_computation.1 | async-start | bytes 3145728 | tf_op jit(solution)/shard_map/all_to_all | solution.py:457
  117.1 1.9 pad_maximum_fusion.2.scalars
  118.9 21.3 %all-to-all-done.1 = bf16[32,32,768]{2,1,0:T(8,128)(2,1)S(1)} async-done(((bf16[32,32,768]{2,1,0:T(8,128)(2,1)}), bf16[32,32,768]{2,1,0:T(8,128)(2,1)S(1)}, u32[]{:S(2)}, u32[]{:S(2)}) %all-to-all-start.1) | async-done | bytes 1572896 | tf_op jit(solution)/shard_map/all_to_all | solution.py:457
  140.2 3.1 %convolution_convert_fusion.resid_grad = bf16[1024,1024]{1,0:T(8,128)(2,1)} fusion(bf16[1024,768]{1,0:T(8,128)(2,1)S(1)} %bitcast.118, bf16[768,1024]{1,0:T(8,128)(2,1)S(1)} %copy-done.38), kind=kOutput, calls=%fused_computation.14 | convolution fusion | flops 1611661312 | bytes 5242880 | tf_op jit(solution)/shard_map/dot_general | solution.py:30
  143.3 12.2 %early_grads.1 = (bf16[4,384,1024]{2,1,0:T(8,128)(2,1)}, bf16[4,384,1024]{2,1,0:T(8,128)(2,1)}) custom-call(s32[4]{0:T(128)} %pad_add_fusion.refs_0_.place, bf16[1024,2048]{1,0:T(8,128)(2,1)} %get-tuple-element.103.hidden, bf16[1024,1024]{1,0:T(8,128)(2,1)} %convolution_convert_fusion.resid_grad, bf16[1024,1024]{1,0:T(8,128)(2,1)} %get-tuple-element.104.residual, ...), custom_call_target="tpu_custom_call" | custom-call | flops 5905580032 | bytes 18874368 | tf_op jit(solution)/shard_map/early_grads/pallas_call | solution.py:242
  155.5 9.6 %late_grads.2 = (bf16[1,512,1024]{2,1,0:T(8,128)(2,1)}, bf16[1,512,1024]{2,1,0:T(8,128)(2,1)}) custom-call(s32[4]{0:T(128)} %pad_add_fusion.refs_0_.place, bf16[1024,1024]{1,0:T(8,128)(2,1)} %convolution_convert_fusion.resid_grad, bf16[2048,1024]{1,0:T(8,128)(2,1)} %get-tuple-element.107.second, bf16[1024,2048]{1,0:T(8,128)(2,1)} %get-tuple-element.108.slope, ...), custom_call_target="tpu_custom_call" | custom-call | flops 4294967296 | bytes 12582912 | tf_op jit(solution)/shard_map/late_grads/pallas_call | solution.py:280
  165.5 2.2 fusion.51
  168.2 2.1 constant_dynamic-slice_fusion.4
  170.7 0.7 add_convert_fusion
  171.4 1.1 collective-permute-start.17
  172.5 0.7 add_convert_fusion.1
  174.1 9.7 %late_grads.3 = (bf16[1,512,1024]{2,1,0:T(8,128)(2,1)}, bf16[1,512,1024]{2,1,0:T(8,128)(2,1)}) custom-call(s32[4]{0:T(128)} %pad_add_fusion.refs_0_.place, bf16[1024,1024]{1,0:T(8,128)(2,1)} %convolution_convert_fusion.resid_grad, bf16[2048,1024]{1,0:T(8,128)(2,1)} %get-tuple-element.107.second, bf16[1024,2048]{1,0:T(8,128)(2,1)} %get-tuple-element.108.slope, ...), custom_call_target="tpu_custom_call" | custom-call | flops 4294967296 | bytes 12582912 | tf_op jit(solution)/shard_map/late_grads/pallas_call | solution.py:280
  183.8 4.2 %collective-permute-done.14 = bf16[2,16,8,1024]{3,2,1,0:T(8,128)(2,1)S(1)} collective-permute-done((bf16[2,16,8,1024]{3,2,1,0:T(8,128)(2,1)S(1)}, bf16[2,16,8,1024]{3,2,1,0:T(8,128)(2,1)S(1)}, u32[]{:S(2)}, u32[]{:S(2)}) %collective-permute-start.14) | collective-permute-done | bytes 524320 | tf_op jit(solution)/shard_map/ppermute | solution.py:334
  188.0 4.7 %collective-permute-done.17 = bf16[2,192,1024]{2,1,0:T(8,128)(2,1)S(1)} collective-permute-done((bf16[2,192,1024]{2,1,0:T(8,128)(2,1)S(1)}, bf16[2,192,1024]{2,1,0:T(8,128)(2,1)S(1)}, u32[]{:S(2)}, u32[]{:S(2)}) %collective-permute-start.17) | collective-permute-done | bytes 786464 | tf_op jit(solution)/shard_map/ppermute | solution.py:334
  192.8 0.9 copy-done.19
  193.7 0.9 copy-done.21
  194.8 0.9 copy-done.33
  195.7 0.8 fusion.45
  196.5 1.1 collective-permute-done.18
  197.6 2.0 fusion.33
  199.6 3.3 %collective-permute-start.19 = (bf16[2,16,8,1024]{3,2,0,1:T(8,128)(2,1)}, bf16[2,16,8,1024]{3,2,0,1:T(8,128)(2,1)}, u32[]{:S(2)}, u32[]{:S(2)}) collective-permute-start(bf16[2,16,8,1024]{3,2,0,1:T(8,128)(2,1)} %fusion.33), channel_id=1, source_target_pairs={{0,3},{3,0},{1,2},{2,1},{4,7},{7,4},{5,6},{6,5},{8,11},{11,8},{9,1... | collective-permute-start | bytes 1572872 | tf_op jit(solution)/shard_map/ppermute | solution.py:334
  202.9 1.2 fusion.40
  204.1 1.6 collective-permute-start.21
  205.8 1.5 add_convert_fusion.5
  207.2 8.7 %collective-permute-done.19 = bf16[2,16,8,1024]{3,2,0,1:T(8,128)(2,1)} collective-permute-done((bf16[2,16,8,1024]{3,2,0,1:T(8,128)(2,1)}, bf16[2,16,8,1024]{3,2,0,1:T(8,128)(2,1)}, u32[]{:S(2)}, u32[]{:S(2)}) %collective-permute-start.19) | collective-permute-done | bytes 524320 | tf_op jit(solution)/shard_map/ppermute | solution.py:334
  215.9 1.8 fusion.47
  217.7 1.2 fusion.28
  219.1 0.9 pad_maximum_fusion
  220.1 5.2 %all-to-all-start.3 = ((bf16[16,24,1024]{2,1,0:T(8,128)(2,1)}), bf16[16,24,1024]{2,1,0:T(8,128)(2,1)S(1)}, u32[]{:S(2)}, u32[]{:S(2)}) async-start(bf16[16,24,1024]{2,1,0:T(8,128)(2,1)} %bitcast.53), calls=%async_computation.3 | async-start | bytes 1572864 | tf_op jit(solution)/shard_map/all_to_all | solution.py:498
  225.3 2.0 collective-permute-start.20
  227.3 1.1 fusion.38
  228.4 12.1 %collective-permute-done.20 = bf16[16,8,1024]{2,1,0:T(8,128)(2,1)S(1)} collective-permute-done((bf16[16,8,1024]{2,1,0:T(8,128)(2,1)S(1)}, bf16[16,8,1024]{2,1,0:T(8,128)(2,1)S(1)}, u32[]{:S(2)}, u32[]{:S(2)}) %collective-permute-start.20) | collective-permute-done | bytes 262176 | tf_op jit(solution)/shard_map/ppermute | solution.py:334
  240.5 1.1 fusion.35
  241.5 0.9 pad_maximum_fusion.1
  242.4 5.3 %all-to-all-start.2 = ((bf16[16,16,1024]{2,1,0:T(8,128)(2,1)}), bf16[16,16,1024]{2,1,0:T(8,128)(2,1)S(1)}, u32[]{:S(2)}, u32[]{:S(2)}) async-start(bf16[16,16,1024]{2,1,0:T(8,128)(2,1)} %pad_maximum_fusion.1), calls=%async_computation.2 | async-start | bytes 1048576 | tf_op jit(solution)/shard_map/all_to_all | solution.py:500
  251.9 0.6 slice_multiply_fusion
  252.5 5.3 %all-to-all-done.2 = bf16[16,16,1024]{2,1,0:T(8,128)(2,1)S(1)} async-done(((bf16[16,16,1024]{2,1,0:T(8,128)(2,1)}), bf16[16,16,1024]{2,1,0:T(8,128)(2,1)S(1)}, u32[]{:S(2)}, u32[]{:S(2)}) %all-to-all-start.2) | async-done | bytes 524320 | tf_op jit(solution)/shard_map/all_to_all | solution.py:500
  257.9 0.6 maximum_multiply_fusion
  (124 shorter events, 9.0 us)
Async XLA Ops:
  0.6 59.6 %copy-start = (f32[8,768]{1,0:T(8,128)S(1)}, f32[8,768]{1,0:T(8,128)}, u32[]{:S(2)}) copy-start(f32[8,768]{1,0:T(8,128)} %param.11) | copy-start | bytes 73732
  0.7 1.2 copy-start.2
  1.9 1.2 copy-start.4
  3.1 1.0 copy-start.6
  4.1 3.4 %copy-start.14 = (bf16[4,256,1024]{2,1,0:T(8,128)(2,1)S(1)}, bf16[4,256,1024]{2,1,0:T(8,128)(2,1)}, u32[]{:S(2)}) copy-start(bf16[4,256,1024]{2,1,0:T(8,128)(2,1)} %param.7) | copy-start | bytes 6291460
  4.2 4.9 %copy-start.8 = (bf16[1216,256]{1,0:T(8,128)(2,1)}, bf16[1216,256]{1,0:T(8,128)(2,1)S(1)}, u32[]{:S(2)}) copy-start(bf16[1216,256]{1,0:T(8,128)(2,1)S(1)} %get-tuple-element.75.refs_2_) | copy-start | bytes 1867780
  4.2 4.9 %copy-start.10 = (bf16[1216,256]{1,0:T(8,128)(2,1)}, bf16[1216,256]{1,0:T(8,128)(2,1)S(1)}, u32[]{:S(2)}) copy-start(bf16[1216,256]{1,0:T(8,128)(2,1)S(1)} %get-tuple-element.76.refs_3_) | copy-start | bytes 1867780
  4.2 17.8 %collective-permute-start = (bf16[1216,256]{1,0:T(8,128)(2,1)S(1)}, bf16[1216,256]{1,0:T(8,128)(2,1)}, u32[]{:S(2)}, u32[]{:S(2)}) collective-permute-start(bf16[1216,256]{1,0:T(8,128)(2,1)S(1)} %get-tuple-element.75.refs_2_), channel_id=1, source_target_pairs={{0,1},{1,2},{2,3},{3,0},{4,5},{5,6},{6,7},{7,4},{8,9},{9,10},{10,1... | collective-permute-start | bytes 1867784 | tf_op jit(solution)/shard_map/ppermute | solution.py:26
  5.9 16.0 %collective-permute-start.1 = (bf16[1216,256]{1,0:T(8,128)(2,1)S(1)}, bf16[1216,256]{1,0:T(8,128)(2,1)}, u32[]{:S(2)}, u32[]{:S(2)}) collective-permute-start(bf16[1216,256]{1,0:T(8,128)(2,1)S(1)} %get-tuple-element.76.refs_3_), channel_id=1, source_target_pairs={{0,3},{1,0},{2,1},{3,2},{4,7},{5,4},{6,5},{7,6},{8,11},{9,8},{10,9... | collective-permute-start | bytes 1867784 | tf_op jit(solution)/shard_map/ppermute | solution.py:26
  7.5 1.6 copy-start.3
  7.5 2.3 copy-start.5
  7.5 2.4 copy-start.7
  10.0 0.8 copy-start.12
  10.8 0.8 copy-start.13
  12.9 9.1 %copy-start.11 = (bf16[1216,256]{1,0:T(8,128)(2,1)S(1)}, bf16[1216,256]{1,0:T(8,128)(2,1)}, u32[]{:S(2)}) copy-start(bf16[1216,256]{1,0:T(8,128)(2,1)} %copy-done.10) | copy-start | bytes 1867780
  12.9 10.2 %copy-start.9 = (bf16[1216,256]{1,0:T(8,128)(2,1)S(1)}, bf16[1216,256]{1,0:T(8,128)(2,1)}, u32[]{:S(2)}) copy-start(bf16[1216,256]{1,0:T(8,128)(2,1)} %copy-done.8) | copy-start | bytes 1867780
  22.0 16.7 %collective-permute-start.3 = (bf16[1216,256]{1,0:T(8,128)(2,1)S(1)}, bf16[1216,256]{1,0:T(8,128)(2,1)S(1)}, u32[]{:S(2)}, u32[]{:S(2)}) collective-permute-start(bf16[1216,256]{1,0:T(8,128)(2,1)S(1)} %copy-done.11), channel_id=1, source_target_pairs={{0,1},{1,2},{2,3},{3,0},{4,5},{5,6},{6,7},{7,4},{8,9},{9,10},{10,1... | collective-permute-start | bytes 1867784 | tf_op jit(solution)/shard_map/ppermute | solution.py:26
  23.1 15.6 %collective-permute-start.2 = (bf16[1216,256]{1,0:T(8,128)(2,1)S(1)}, bf16[1216,256]{1,0:T(8,128)(2,1)S(1)}, u32[]{:S(2)}, u32[]{:S(2)}) collective-permute-start(bf16[1216,256]{1,0:T(8,128)(2,1)S(1)} %copy-done.9), channel_id=1, source_target_pairs={{0,3},{1,0},{2,1},{3,2},{4,7},{5,4},{6,5},{7,6},{8,11},{9,8},{10,9... | collective-permute-start | bytes 1867784 | tf_op jit(solution)/shard_map/ppermute | solution.py:26
  25.3 13.4 %collective-permute-start.4 = (bf16[1216,256]{1,0:T(8,128)(2,1)}, bf16[1216,256]{1,0:T(8,128)(2,1)S(1)}, u32[]{:S(2)}, u32[]{:S(2)}) collective-permute-start(bf16[1216,256]{1,0:T(8,128)(2,1)} %collective-permute-done.refs_2_), channel_id=1, source_target_pairs={{0,4},{4,0},{1,5},{5,1},{2,6},{6,2},{3,7},{7,3},{8,12},{12,8},{9,1... | collective-permute-start | bytes 1867784 | tf_op jit(solution)/shard_map/ppermute | solution.py:26
  25.3 13.4 %collective-permute-start.5 = (bf16[1216,256]{1,0:T(8,128)(2,1)}, bf16[1216,256]{1,0:T(8,128)(2,1)S(1)}, u32[]{:S(2)}, u32[]{:S(2)}) collective-permute-start(bf16[1216,256]{1,0:T(8,128)(2,1)} %collective-permute-done.1.refs_7_), channel_id=1, source_target_pairs={{0,4},{4,0},{1,5},{5,1},{2,6},{6,2},{3,7},{7,3},{8,12},{12,8},{9,1... | collective-permute-start | bytes 1867784 | tf_op jit(solution)/shard_map/ppermute | solution.py:26
  38.7 4.6 %copy-start.26 = (bf16[1216,256]{1,0:T(8,128)(2,1)}, bf16[1216,256]{1,0:T(8,128)(2,1)S(1)}, u32[]{:S(2)}) copy-start(bf16[1216,256]{1,0:T(8,128)(2,1)S(1)} %collective-permute-done.3.refs_3_) | copy-start | bytes 1867780
  38.7 4.6 %copy-start.27 = (bf16[1216,256]{1,0:T(8,128)(2,1)}, bf16[1216,256]{1,0:T(8,128)(2,1)S(1)}, u32[]{:S(2)}) copy-start(bf16[1216,256]{1,0:T(8,128)(2,1)S(1)} %collective-permute-done.2.refs_6_) | copy-start | bytes 1867780
  38.7 4.6 %copy-start.28 = (bf16[1216,256]{1,0:T(8,128)(2,1)}, bf16[1216,256]{1,0:T(8,128)(2,1)S(1)}, u32[]{:S(2)}) copy-start(bf16[1216,256]{1,0:T(8,128)(2,1)S(1)} %collective-permute-done.4.refs_4_) | copy-start | bytes 1867780
  38.7 0.9 copy-start.29
  38.7 4.5 %collective-permute-start.8 = (bf16[1216,256]{1,0:T(8,128)(2,1)S(1)}, bf16[1216,256]{1,0:T(8,128)(2,1)}, u32[]{:S(2)}, u32[]{:S(2)}) collective-permute-start(bf16[1216,256]{1,0:T(8,128)(2,1)S(1)} %collective-permute-done.3.refs_3_), channel_id=1, source_target_pairs={{0,4},{4,0},{1,5},{5,1},{2,6},{6,2},{3,7},{7,3},{8,12},{12,8},{9,1... | collective-permute-start | bytes 1867784 | tf_op jit(solution)/shard_map/ppermute | solution.py:26
  38.8 4.4 %collective-permute-start.9 = (bf16[1216,256]{1,0:T(8,128)(2,1)S(1)}, bf16[1216,256]{1,0:T(8,128)(2,1)}, u32[]{:S(2)}, u32[]{:S(2)}) collective-permute-start(bf16[1216,256]{1,0:T(8,128)(2,1)S(1)} %collective-permute-done.2.refs_6_), channel_id=1, source_target_pairs={{0,4},{4,0},{1,5},{5,1},{2,6},{6,2},{3,7},{7,3},{8,12},{12,8},{9,1... | collective-permute-start | bytes 1867784 | tf_op jit(solution)/shard_map/ppermute | solution.py:26
  39.6 19.9 %collective-permute-start.7 = (bf16[1216,256]{1,0:T(8,128)(2,1)}, bf16[1216,256]{1,0:T(8,128)(2,1)S(1)}, u32[]{:S(2)}, u32[]{:S(2)}) collective-permute-start(bf16[1216,256]{1,0:T(8,128)(2,1)} %collective-permute-done.1.refs_7_), channel_id=1, source_target_pairs={{0,3},{1,0},{2,1},{3,2},{4,7},{5,4},{6,5},{7,6},{8,11},{9,8},{10,9... | collective-permute-start | bytes 1867784 | tf_op jit(solution)/shard_map/ppermute | solution.py:26
  42.6 17.0 %collective-permute-start.6 = (bf16[1216,256]{1,0:T(8,128)(2,1)}, bf16[1216,256]{1,0:T(8,128)(2,1)S(1)}, u32[]{:S(2)}, u32[]{:S(2)}) collective-permute-start(bf16[1216,256]{1,0:T(8,128)(2,1)} %collective-permute-done.refs_2_), channel_id=1, source_target_pairs={{0,1},{1,2},{2,3},{3,0},{4,5},{5,6},{6,7},{7,4},{8,9},{9,10},{10,1... | collective-permute-start | bytes 1867784 | tf_op jit(solution)/shard_map/ppermute | solution.py:26
  43.3 16.9 %copy-start.36 = (s32[8]{0:T(128)S(1)}, s32[8]{0:T(128)}, u32[]{:S(2)}) copy-start(s32[8]{0:T(128)} %param.12) | copy-start | bytes 100
  59.5 3.1 %copy-start.24 = (bf16[1216,256]{1,0:T(8,128)(2,1)}, bf16[1216,256]{1,0:T(8,128)(2,1)S(1)}, u32[]{:S(2)}) copy-start(bf16[1216,256]{1,0:T(8,128)(2,1)S(1)} %collective-permute-done.7.refs_3_) | copy-start | bytes 1867780
  59.6 3.0 %copy-start.25 = (bf16[1216,256]{1,0:T(8,128)(2,1)}, bf16[1216,256]{1,0:T(8,128)(2,1)S(1)}, u32[]{:S(2)}) copy-start(bf16[1216,256]{1,0:T(8,128)(2,1)S(1)} %collective-permute-done.6.refs_2_) | copy-start | bytes 1867780
  59.6 2.1 collective-permute-start.10
  59.7 2.9 %collective-permute-start.11 = (bf16[1216,256]{1,0:T(8,128)(2,1)S(1)}, bf16[1216,256]{1,0:T(8,128)(2,1)S(1)}, u32[]{:S(2)}, u32[]{:S(2)}) collective-permute-start(bf16[1216,256]{1,0:T(8,128)(2,1)S(1)} %collective-permute-done.7.refs_3_), channel_id=1, source_target_pairs={{0,4},{4,0},{1,5},{5,1},{2,6},{6,2},{3,7},{7,3},{8,12},{12,8},{9,1... | collective-permute-start | bytes 1867784 | tf_op jit(solution)/shard_map/ppermute | solution.py:26
  61.7 0.9 copy-start.30
  106.4 1.0 copy-start.37
  112.8 27.4 %copy-start.38 = (bf16[768,1024]{1,0:T(8,128)(2,1)S(1)}, bf16[768,1024]{1,0:T(8,128)(2,1)}, u32[]{:S(2)}) copy-start(bf16[768,1024]{1,0:T(8,128)(2,1)} %get-tuple-element.102) | copy-start | bytes 4718596
  112.8 27.4 %all-to-all-start.1 = ((bf16[32,32,768]{2,1,0:T(8,128)(2,1)}), bf16[32,32,768]{2,1,0:T(8,128)(2,1)S(1)}, u32[]{:S(2)}, u32[]{:S(2)}) async-start(bf16[32,32,768]{2,1,0:T(8,128)(2,1)} %bitcast.18), calls=%async_computation.1 | async-start | bytes 3145728 | tf_op jit(solution)/shard_map/all_to_all | solution.py:457
  140.2 3.1 %copy-start.16 = (bf16[32,32,768]{2,1,0:T(8,128)(2,1)}, bf16[32,32,768]{2,1,0:T(8,128)(2,1)S(1)}, u32[]{:S(2)}) copy-start(bf16[32,32,768]{2,1,0:T(8,128)(2,1)S(1)} %all-to-all-done.1) | copy-start | bytes 4718596
  155.5 14.8 %collective-permute-start.12 = (bf16[4,384,1024]{2,1,0:T(8,128)(2,1)}, bf16[4,384,1024]{2,1,0:T(8,128)(2,1)S(1)}, u32[]{:S(2)}, u32[]{:S(2)}) collective-permute-start(bf16[4,384,1024]{2,1,0:T(8,128)(2,1)} %get-tuple-element.105), channel_id=1, source_target_pairs={{0,4},{4,0},{1,5},{5,1},{2,6},{6,2},{3,7},{7,3},{8,12},{12,8},{9,1... | collective-permute-start | bytes 9437192 | tf_op jit(solution)/shard_map/ppermute | solution.py:26
  165.0 3.1 %collective-permute-start.13 = (bf16[1,512,1024]{2,1,0:T(8,128)(2,1)}, bf16[1,512,1024]{2,1,0:T(8,128)(2,1)}, u32[]{:S(2)}, u32[]{:S(2)}) collective-permute-start(bf16[1,512,1024]{2,1,0:T(8,128)(2,1)} %get-tuple-element.111), channel_id=1, source_target_pairs={{0,4},{4,0},{1,5},{5,1},{2,6},{6,2},{3,7},{7,3},{8,12},{12,8},{9,1... | collective-permute-start | bytes 3145736 | tf_op jit(solution)/shard_map/ppermute | solution.py:26
  171.4 21.3 %collective-permute-start.17 = (bf16[2,192,1024]{2,1,0:T(8,128)(2,1)S(1)}, bf16[2,192,1024]{2,1,0:T(8,128)(2,1)S(1)}, u32[]{:S(2)}, u32[]{:S(2)}) collective-permute-start(bf16[2,192,1024]{2,1,0:T(8,128)(2,1)S(1)} %get-tuple-element.135), channel_id=1, source_target_pairs={{0,96},{96,0},{32,64},{64,32},{1,97},{97,1},{33,65},{65,33},{2,98}... | collective-permute-start | bytes 2359304 | tf_op jit(solution)/shard_map/ppermute | solution.py:334
  172.5 1.2 copy-start.17
  173.2 19.6 %collective-permute-start.16 = (bf16[2,192,1024]{2,1,0:T(8,128)(2,1)S(1)}, bf16[2,192,1024]{2,1,0:T(8,128)(2,1)S(1)}, u32[]{:S(2)}, u32[]{:S(2)}) collective-permute-start(bf16[2,192,1024]{2,1,0:T(8,128)(2,1)S(1)} %get-tuple-element.137), channel_id=1, source_target_pairs={{0,32},{32,0},{64,96},{96,64},{1,33},{33,1},{65,97},{97,65},{2,34}... | collective-permute-start | bytes 2359304 | tf_op jit(solution)/shard_map/ppermute | solution.py:334
  174.0 20.6 %copy-start.15 = (bf16[16,1,2,8,1024]{4,3,2,1,0:T(8,128)(2,1)S(1)}, bf16[16,1,2,8,1024]{4,3,2,1,0:T(8,128)(2,1)}, u32[]{:S(2)}) copy-start(bf16[16,1,2,8,1024]{4,3,2,1,0:T(8,128)(2,1)} %get-tuple-element.144) | copy-start | bytes 1572868
  174.0 14.0 %collective-permute-start.14 = (bf16[2,16,8,1024]{3,2,1,0:T(8,128)(2,1)S(1)}, bf16[2,16,8,1024]{3,2,1,0:T(8,128)(2,1)S(1)}, u32[]{:S(2)}, u32[]{:S(2)}) collective-permute-start(bf16[2,16,8,1024]{3,2,1,0:T(8,128)(2,1)S(1)} %fusion.32), channel_id=1, source_target_pairs={{0,1},{1,0},{2,3},{3,2},{4,5},{5,4},{6,7},{7,6},{8,9},{9,8},{10,11... | collective-permute-start | bytes 1572872 | tf_op jit(solution)/shard_map/ppermute | solution.py:334
  188.0 6.6 %copy-start.32 = (bf16[2,16,8,1024]{3,2,1,0:T(8,128)(2,1)}, bf16[2,16,8,1024]{3,2,1,0:T(8,128)(2,1)S(1)}, u32[]{:S(2)}) copy-start(bf16[2,16,8,1024]{3,2,1,0:T(8,128)(2,1)S(1)} %collective-permute-done.14) | copy-start | bytes 1572868
  192.8 0.9 copy-start.19
  193.7 0.9 copy-start.21
  194.6 3.0 %collective-permute-start.18 = (bf16[1,512,1024]{2,1,0:T(8,128)(2,1)}, bf16[1,512,1024]{2,1,0:T(8,128)(2,1)}, u32[]{:S(2)}, u32[]{:S(2)}) collective-permute-start(bf16[1,512,1024]{2,1,0:T(8,128)(2,1)} %get-tuple-element.118), channel_id=1, source_target_pairs={{0,4},{4,0},{1,5},{5,1},{2,6},{6,2},{3,7},{7,3},{8,12},{12,8},{9,1... | collective-permute-start | bytes 3145736 | tf_op jit(solution)/shard_map/ppermute | solution.py:26
  194.6 3.0 %copy-start.18 = (bf16[1,512,1024]{2,1,0:T(8,128)(2,1)S(1)}, bf16[1,512,1024]{2,1,0:T(8,128)(2,1)}, u32[]{:S(2)}) copy-start(bf16[1,512,1024]{2,1,0:T(8,128)(2,1)} %get-tuple-element.116) | copy-start | bytes 3145732
  194.6 1.1 copy-start.33
  195.7 7.2 %copy-start.20 = (bf16[2,192,1024]{2,1,0:T(8,128)(2,1)S(1)}, bf16[2,192,1024]{2,1,0:T(8,128)(2,1)}, u32[]{:S(2)}) copy-start(bf16[2,192,1024]{2,1,0:T(8,128)(2,1)} %copy-done.19) | copy-start | bytes 2359300
  195.7 7.2 %copy-start.22 = (bf16[2,192,1024]{2,1,0:T(8,128)(2,1)S(1)}, bf16[2,192,1024]{2,1,0:T(8,128)(2,1)}, u32[]{:S(2)}) copy-start(bf16[2,192,1024]{2,1,0:T(8,128)(2,1)} %copy-done.21) | copy-start | bytes 2359300
  199.6 16.3 %collective-permute-start.19 = (bf16[2,16,8,1024]{3,2,0,1:T(8,128)(2,1)}, bf16[2,16,8,1024]{3,2,0,1:T(8,128)(2,1)}, u32[]{:S(2)}, u32[]{:S(2)}) collective-permute-start(bf16[2,16,8,1024]{3,2,0,1:T(8,128)(2,1)} %fusion.33), channel_id=1, source_target_pairs={{0,3},{3,0},{1,2},{2,1},{4,7},{7,4},{5,6},{6,5},{8,11},{11,8},{9,1... | collective-permute-start | bytes 1572872 | tf_op jit(solution)/shard_map/ppermute | solution.py:334
  204.1 13.5 %collective-permute-start.21 = (bf16[192,1024]{1,0:T(8,128)(2,1)}, bf16[192,1024]{1,0:T(8,128)(2,1)}, u32[]{:S(2)}, u32[]{:S(2)}) collective-permute-start(bf16[192,1024]{1,0:T(8,128)(2,1)} %get-tuple-element.156), channel_id=1, source_target_pairs={{0,96},{96,0},{32,64},{64,32},{1,97},{97,1},{33,65},{65,33},{2,98}... | collective-permute-start | bytes 1179656 | tf_op jit(solution)/shard_map/ppermute | solution.py:334
  205.7 11.9 %copy-start.23 = (bf16[2,192,1024]{2,1,0:T(8,128)(2,1)S(1)}, bf16[2,192,1024]{2,1,0:T(8,128)(2,1)}, u32[]{:S(2)}) copy-start(bf16[2,192,1024]{2,1,0:T(8,128)(2,1)} %copy-done.21) | copy-start | bytes 2359300
  205.7 21.5 %collective-permute-start.15 = (bf16[16,8,1024]{2,1,0:T(8,128)(2,1)}, bf16[16,8,1024]{2,1,0:T(8,128)(2,1)}, u32[]{:S(2)}, u32[]{:S(2)}) collective-permute-start(bf16[16,8,1024]{2,1,0:T(8,128)(2,1)} %fusion.45), channel_id=1, source_target_pairs={{0,3},{3,0},{1,2},{2,1},{4,7},{7,4},{5,6},{6,5},{8,11},{11,8},{9,1... | collective-permute-start | bytes 786440 | tf_op jit(solution)/shard_map/ppermute | solution.py:334
  205.8 13.1 %collective-permute-start.22 = (bf16[192,1024]{1,0:T(8,128)(2,1)}, bf16[192,1024]{1,0:T(8,128)(2,1)S(1)}, u32[]{:S(2)}, u32[]{:S(2)}) collective-permute-start(bf16[192,1024]{1,0:T(8,128)(2,1)} %get-tuple-element.157), channel_id=1, source_target_pairs={{0,32},{32,0},{64,96},{96,64},{1,33},{33,1},{65,97},{97,65},{2,34}... | collective-permute-start | bytes 1179656 | tf_op jit(solution)/shard_map/ppermute | solution.py:334
  219.1 6.2 %copy-start.35 = (bf16[16,8,1024]{2,1,0:T(8,128)(2,1)S(1)}, bf16[16,8,1024]{2,1,0:T(8,128)(2,1)}, u32[]{:S(2)}) copy-start(bf16[16,8,1024]{2,1,0:T(8,128)(2,1)} %fusion.47) | copy-start | bytes 786436
  219.1 8.2 %copy-start.34 = (bf16[2,16,8,1024]{3,2,1,0:T(8,128)(2,1)S(1)}, bf16[2,16,8,1024]{3,2,1,0:T(8,128)(2,1)}, u32[]{:S(2)}) copy-start(bf16[2,16,8,1024]{3,2,1,0:T(8,128)(2,1)} %copy-done.32) | copy-start | bytes 1572868
  220.1 22.3 %all-to-all-start.3 = ((bf16[16,24,1024]{2,1,0:T(8,128)(2,1)}), bf16[16,24,1024]{2,1,0:T(8,128)(2,1)S(1)}, u32[]{:S(2)}, u32[]{:S(2)}) async-start(bf16[16,24,1024]{2,1,0:T(8,128)(2,1)} %bitcast.53), calls=%async_computation.3 | async-start | bytes 1572864 | tf_op jit(solution)/shard_map/all_to_all | solution.py:498
  225.3 15.2 %collective-permute-start.20 = (bf16[16,8,1024]{2,1,0:T(8,128)(2,1)S(1)}, bf16[16,8,1024]{2,1,0:T(8,128)(2,1)S(1)}, u32[]{:S(2)}, u32[]{:S(2)}) collective-permute-start(bf16[16,8,1024]{2,1,0:T(8,128)(2,1)S(1)} %copy-done.35), channel_id=1, source_target_pairs={{0,1},{1,0},{2,3},{3,2},{4,5},{5,4},{6,7},{7,6},{8,9},{9,8},{10,11... | collective-permute-start | bytes 786440 | tf_op jit(solution)/shard_map/ppermute | solution.py:334
  241.5 17.1 %copy-start.1 = (f32[8,768]{1,0:T(8,128)S(1)}, f32[8,768]{1,0:T(8,128)}, u32[]{:S(2)}) copy-start(f32[8,768]{1,0:T(8,128)} %param.11) | copy-start | bytes 73732
  242.4 15.4 %all-to-all-start.2 = ((bf16[16,16,1024]{2,1,0:T(8,128)(2,1)}), bf16[16,16,1024]{2,1,0:T(8,128)(2,1)S(1)}, u32[]{:S(2)}, u32[]{:S(2)}) async-start(bf16[16,16,1024]{2,1,0:T(8,128)(2,1)} %pad_maximum_fusion.1), calls=%async_computation.2 | async-start | bytes 1048576 | tf_op jit(solution)/shard_map/all_to_all | solution.py:500
  (1 other events, 0.8 us)

commit v8 on v7

--- a/solution.py
+++ b/solution.py
@@ -217,7 +217,7 @@
         term = score.astype(BF16).astype(F32)
         out = jnp.where(line == i, term, out)
         score = score - term
-    return jnp.where(lane == 2 * place[2] + place[1], out, 0.0)
+    return jnp.where(lane == 2 * place[0] + place[1], out, 0.0)
 
 
 def early_kernel(place, hidden, resid_grad, residual, grad_rows, scalars, keep, send):
@@ -229,16 +229,15 @@
     blank = riders(place, scalars, (head.shape[3], width - out_width))
     blank = jnp.broadcast_to(blank, (*head.shape[:3], *blank.shape))
     both = jnp.concatenate([second, jnp.concatenate([head, blank], 4)], 3)
-    both = both.reshape(RING, 2, -1, width)
-    store_halves(place[1], both, keep, send)
+    both = jnp.stack([both[:, :, i] for i in (0, 3, 1, 2)], 2)
+    store_halves(place[1], both.reshape(RING, 2, -1, width), keep, send)
 
 
 def early_grads(place, hidden, resid_grad, residual, grad_rows, scalars):
     rows, hid = hidden.shape
     width, out_width = residual.shape[1], grad_rows.shape[1]
     lines = (hid + width) // RING // 2
-    gray = lambda i: 2 * ((i // 2 + i) % 2) + i // 2
-    out = pl.BlockSpec((1, lines, width), lambda i, s: (gray(i), 0, 0))
+    out = pl.BlockSpec((1, lines, width), lambda i, s: (i, 0, 0))
     return pl.pallas_call(
         early_kernel,
         grid_spec=pltpu.PrefetchScalarGridSpec(
@@ -267,9 +266,7 @@
     preact_grad = (slope[...].astype(F32) * hidden_grad).astype(BF16)
     first = dot(tokens[...], preact_grad, ((0,), (0,)))
     cols = first.shape[1]
-    parts = first.reshape(16, 2, RING, -1, cols)
-    parts = jnp.stack([parts[:, :, i] for i in (0, 3, 1, 2)], 2)
-    store_halves(place[1], parts.reshape(16, 2, -1, cols), keep, send)
+    store_halves(place[1], first.reshape(16, 2, -1, cols), keep, send)
 
 
 def late_grads(place, part, resid_grad, second, slope, tokens):
@@ -322,20 +319,28 @@
     return [(pairs, axis, bit, dim) for pairs, bit, dim in steps]
 
 
-def outgoing(parts, step):
-    return add(*[take(x, 1 - step[2], step[3]) for x in parts])
-
-
-def staying(parts, step):
-    return add(*[take(x, step[2], step[3]) for x in parts])
+def outgoing(x, step):
+    return take(x, 1 - step[2], step[3])
 
 
 def sent_along(x, step):
     return lax.ppermute(x, step[1], step[0])
 
 
-def by_ring(x):
-    return x.reshape(16, 2, 2, -1, x.shape[-1]).transpose(1, 2, 0, 3, 4)
+def kept_plus(x, arrived, step):
+    return add(take(x, step[2], step[3]), arrived)
+
+
+def by_ring(x, lines):
+    return x.reshape(-1, 2, 2, lines, x.shape[-1]).transpose(1, 2, 0, 3, 4)
+
+
+def summed_over_y(x):
+    here = lax.axis_index("y")
+    total = take(x, here, 1)
+    for by in range(1, RING):
+        total = total + shift(take(x, (here + by) % RING, 1), "y", by)
+    return total
 
 
 def tie(*arrays):
@@ -465,49 +470,37 @@
     early_in = shift(early[1], "c", 1)
     late = late_grads(at, 0, after(resid_grad, early[1]), second, slope, tokens)
     a_in = shift(late[1], "c", 1)
-    x_steps = [ring_chain("x", True), ring_chain("x", False)]
-    y_steps = [ring_chain("y", True), ring_chain("y", False)]
-    early = [v.reshape(2, 2, 2, -1, width) for v in (after(early[0], late[1]), early_in)]
-    early = [[v[:, :, i] for v in early] for i in range(2)]
-    early_sent = [outgoing(x, steps[0]) for x, steps in zip(early, x_steps)]
-    early_in = [sent_along(x, steps[0]) for x, steps in zip(early_sent, x_steps)]
-    a = [by_ring(after(late[0], *early_sent)), by_ring(a_in)]
-    a_sent = outgoing(a, y_steps[0][0])
-    a_in = sent_along(a_sent, y_steps[0][0])
-    early = [staying(x, steps[0]) for x, steps in zip(early, x_steps)]
-    a = staying(a, y_steps[0][0])
-    late = late_grads(at, 1, after(resid_grad, a_sent), second, slope, tokens)
-    b_in = shift(after(late[1], a_in, *early_in), "c", 1)
-    a = [a, a_in]
-    a_sent = outgoing(a, y_steps[0][1])
-    a_in = sent_along(a_sent, y_steps[0][1])
-    b = [by_ring(after(late[0], a_sent)), by_ring(b_in)]
-    b_sent = outgoing(b, y_steps[1][0])
-    b_in = sent_along(b_sent, y_steps[1][0])
-    early = [[x, after(v, b_sent)] for x, v in zip(early, early_in)]
-    early_sent = [outgoing(x, steps[1]) for x, steps in zip(early, x_steps)]
-    early_in = [sent_along(x, steps[1]) for x, steps in zip(early_sent, x_steps)]
-    early = [staying(x, steps[1]) for x, steps in zip(early, x_steps)]
-    a = staying(a, y_steps[0][1])
-    b = [staying(b, y_steps[1][0]), after(b_in, *early_sent)]
-    b_sent = outgoing(b, y_steps[1][1])
-    b_in = sent_along(b_sent, y_steps[1][1])
-    b = staying(b, y_steps[1][1])
-    early = [add(x, after(v, b_sent)) for x, v in zip(early, early_in)]
-    early = jnp.concatenate(early).reshape(16, -1, width)
-    early = lax.all_to_all(early, ("z", "y"), 0, 0, tiled=True)
-    late = jnp.concatenate([add(a, a_in), add(b, b_in)], 1)
-    late = lax.all_to_all(late, ("x", "z"), 0, 0, tiled=True)
+    steps = [ring_chain("y", True), ring_chain("y", False)]
+    group = ("x", "z")
+    n = width // 128
+    early = add(after(early[0], late[1]), early_in)
+    lines = early.shape[1] // 16
+    early = [by_ring(v, lines) for v in (early[:2], early[2:])]
+    early_sent = [outgoing(x, s[0]) for x, s in zip(early, steps)]
+    early_in = [sent_along(x, s[0]) for x, s in zip(early_sent, steps)]
+    a = add(after(late[0], *early_sent), a_in).reshape(16, RING * n, width)
+    a_all = lax.all_to_all(a, group, 0, 0, tiled=True)
+    late = late_grads(at, 1, after(resid_grad, a), second, slope, tokens)
+    b_in = shift(after(late[1], a_all, *early_in), "c", 1)
+    early = [kept_plus(x, v, s[0]) for x, v, s in zip(early, early_in, steps)]
+    early_sent = [outgoing(x, s[1]) for x, s in zip(early, steps)]
+    early_in = [sent_along(x, s[1]) for x, s in zip(early_sent, steps)]
+    b = add(after(late[0], *early_sent), b_in).reshape(16, RING * n, width)
+    b_all = lax.all_to_all(b, group, 0, 0, tiled=True)
+    a = jnp.sum(after(a_all, b).astype(F32), 0)
+    early = [kept_plus(x, after(v, b), s[1]) for x, v, s in zip(early, early_in, steps)]
+    early = jnp.concatenate(early)
+    b = jnp.sum(b_all.astype(F32), 0)
+    early = lax.all_to_all(after(early, b_all), group, 0, 0, tiled=True)
+    first = summed_over_y(jnp.stack([a, b]).reshape(2, RING, n, width))
     early = jnp.sum(early.astype(F32), 0)
-    late = jnp.sum(late.astype(F32), 0)
     n_second = shard * RING // 128
-    ride = jnp.sum(early[n_second : n_second + 8, out_width:], 1)
+    ride = jnp.sum(early[n_second:, out_width:], 1)
     score_total = ride[0] + ride[1] + ride[2]
     valid_total = jnp.maximum(ride[3], 1.0)
     scale = 1.0 / valid_total
-    n_first = late.shape[0] // 2
     return (
-        jnp.concatenate([late[:n_first], late[n_first:]], 1) * scale,
+        jnp.concatenate([first[0], first[1]], 1) * scale,
         early[:n_second] * scale,
         early[n_second:, :out_width] * scale,
         score_total / valid_total,

time: 261 us -> 255 us (0.977)
  starting transfers between devices: 34.7 us -> 40.4 us
  waiting for transfers between devices: 72.6 us -> 67.7 us
  local copies, waits for them, and re-layouts: 20.8 us -> 17 us
  other arithmetic: 21.2 us -> 17.8 us
    ppermute x8 -> x4, waiting for transfers between devices: 29.8 us -> 11 us  [sent_along(): return lax.ppermute(x, step[1], step[0])]
    all_to_all x2 -> x3, waiting for transfers between devices: 5.33 us -> 18 us  [the longest x1 12.6 us: per_device(): b_all = lax.all_to_all(b, group, 0, 0, tiled=True)]
    ppermute x15 -> x18, starting transfers between devices: 11.7 us -> 16.4 us  [shift(): return lax.ppermute(x, axis, [(i, (i + by) % size) for i in range(size)])]
    all_to_all x2 -> x3, starting transfers between devices: 10.5 us -> 14.1 us  [the longest x1 6.8 us: per_device(): b_all = lax.all_to_all(b, group, 0, 0, tiled=True)]
    convert_element_type x13 -> x7, other arithmetic: 12.6 us -> 9.68 us  [add(): return (a.astype(F32) + b.astype(F32)).astype(BF16)]
    ppermute x8 -> x4, starting transfers between devices: 8.27 us -> 5.71 us  [sent_along(): return lax.ppermute(x, step[1], step[0])]
    ppermute x15 -> x18, waiting for transfers between devices: 16.2 us -> 17.4 us  [shift(): return lax.ppermute(x, axis, [(i, (i + by) % size) for i in range(size)])]
    unnamed x78 -> x67, local copies, waits for them, and re-layouts: 10.1 us -> 8.97 us
  transfers between devices with their start and end apart: 26 -> 26, of which waited for: 11 -> 12; matrix products, arithmetic and copies ran while one was open for 9% -> 7% of each run, Pallas kernels for 17% -> 18%
where the time goes in v8:
time: 255 us; the launch traced here: 253 us
  Pallas kernels  68 us (27%)
  waiting for transfers between devices  67.7 us (27%)
  starting transfers between devices  40.4 us (16%)
  blocking collectives  30.5 us (12%)
  other arithmetic  17.8 us (7%)
  local copies, waits for them, and re-layouts  17 us (7%)
  matrix products  6.82 us (3%)
  between operations  4.98 us (2%)
    pallas_call x3, Pallas kernels, forward_part(): pl.pallas_call(functools.partial(forward_kernel, groups, first_call, last...  36.5 us
    all_to_all x1, blocking collectives, per_device(): gathered = lax.all_to_all(forecast, group, 0, 0, tiled=True)  30.5 us
    all_to_all x1, waiting for transfers between devices, per_device(): lax.all_to_all(grad_raw.reshape(32, members * own, out_width), group, 0,...  21.3 us
    pallas_call x2, Pallas kernels, late_grads(): pl.pallas_call(late_kernel, grid_spec=pltpu.PrefetchScalarGridSpec(num_sc...  19.4 us
    ppermute x18, waiting for transfers between devices, shift(): return lax.ppermute(x, axis, [(i, (i + by) % size) for i in range(size)])  17.4 us
    ppermute x18, starting transfers between devices, shift(): return lax.ppermute(x, axis, [(i, (i + by) % size) for i in range(size)])  16.4 us
    all_to_all x1, waiting for transfers between devices, per_device(): b_all = lax.all_to_all(b, group, 0, 0, tiled=True)  12.6 us
    pallas_call x1, Pallas kernels, early_grads(): pl.pallas_call(early_kernel, grid_spec=pltpu.PrefetchScalarGridSpec(num_s...  12 us
  transfers between devices with their start and end apart: 26, of which 12 were waited for; matrix products, arithmetic and copies ran while one was open for 7% of the time, Pallas kernels for 18%

profile of v8, /device:TPU:0, one launch (start us, length us, event | category | flops | bytes accessed | tf_op | source)
XLA Modules:
  0.0 253.5 jit_solution(7085322031481760435)
XLA Ops:
  0.7 1.2 copy-done.2
  1.9 1.2 copy-done.4
  3.1 1.0 copy-done.6
  4.2 1.7 collective-permute-start
  5.9 1.6 collective-permute-start.1
  7.5 1.6 copy.23
  9.1 0.7 copy-done.5
  10.0 0.8 copy-done.12
  10.8 0.8 copy-done.13
  12.3 0.7 pad_add_fusion.refs_0_.place
  12.9 9.1 %forward_part.3 = (bf16[1024,2048]{1,0:T(8,128)(2,1)}, bf16[1024,2048]{1,0:T(8,128)(2,1)}, bf16[2048,1024]{1,0:T(8,128)(2,1)}, bf16[768,1024]{1,0:T(8,128)(2,1)}, f32[1024,1024]{1,0:T(8,128)}) custom-call(s32[4]{0:T(128)} %pad_add_fusion.refs_0_.place, bf16[1024,1024]{1,0:T(8,128)(2,1)} %bitcast.90, bf16[1216,256]{1,0:T(8,128)(2,1)} %copy-done.8, ...), custom_call_target="tpu_custom_call" | custom-call | flops 2147483648 | bytes 12582912 | tf_op jit(solution)/shard_map/forward_part/pallas_call | solution.py:166
  22.1 1.1 collective-permute-start.3
  23.1 2.3 collective-permute-start.2
  25.9 12.9 %collective-permute-done.3.refs_3_ = bf16[1216,256]{1,0:T(8,128)(2,1)S(1)} collective-permute-done((bf16[1216,256]{1,0:T(8,128)(2,1)S(1)}, bf16[1216,256]{1,0:T(8,128)(2,1)S(1)}, u32[]{:S(2)}, u32[]{:S(2)}) %collective-permute-start.3) | collective-permute-done | bytes 622624 | tf_op jit(solution)/shard_map/ppermute | solution.py:26
  39.7 2.9 %collective-permute-start.7 = (bf16[1216,256]{1,0:T(8,128)(2,1)}, bf16[1216,256]{1,0:T(8,128)(2,1)S(1)}, u32[]{:S(2)}, u32[]{:S(2)}) collective-permute-start(bf16[1216,256]{1,0:T(8,128)(2,1)} %collective-permute-done.1.refs_7_), channel_id=1, source_target_pairs={{0,3},{1,0},{2,1},{3,2},{4,7},{5,4},{6,5},{7,6},{8,11},{9,8},{10,9... | collective-permute-start | bytes 1867784 | tf_op jit(solution)/shard_map/ppermute | solution.py:26
  42.7 0.6 stack.68.refs_0_
  43.3 16.2 %forward_part.4 = (bf16[1024,2048]{1,0:T(8,128)(2,1)}, bf16[1024,2048]{1,0:T(8,128)(2,1)}, bf16[2048,1024]{1,0:T(8,128)(2,1)}, bf16[768,1024]{1,0:T(8,128)(2,1)}, f32[1024,1024]{1,0:T(8,128)}) custom-call(s32[5]{0:T(128)} %stack.68.refs_0_, bf16[1024,1024]{1,0:T(8,128)(2,1)} %bitcast.91, ...), custom_call_target="tpu_custom_call", output_to_operand_aliasing={{0}: (11, {}), {1}: (12, {}), {2}: (13, {}), {3}: (14, {})} | custom-call | flops 4294967296 | bytes 12582912 | tf_op jit(solution)/shard_map/forward_part/pallas_call | solution.py:166
  60.9 0.9 collective-permute-done.10.refs_4_
  61.7 0.9 collective-permute-done.11.refs_5_
  62.6 0.8 copy-done.29
  63.5 11.1 %forward_part.5 = (bf16[1024,2048]{1,0:T(8,128)(2,1)}, bf16[1024,2048]{1,0:T(8,128)(2,1)}, bf16[2048,1024]{1,0:T(8,128)(2,1)}, bf16[768,1024]{1,0:T(8,128)(2,1)}...) custom-call(s32[4]{0:T(128)} %get-tuple-element.130.refs_0_, ...), custom_call_target="tpu_custom_call", output_to_operand_aliasing={{0}: (7, {}), {1}: (8, {}), {2}: (9, {})} | custom-call | flops 2147483648 | bytes 12582912 | tf_op jit(solution)/shard_map/forward_part/pallas_call | solution.py:166
  74.6 30.5 %all_to_all.25 = bf16[32,32,768]{2,1,0:T(8,128)(2,1)S(1)} all-to-all(bf16[32,32,768]{2,1,0:T(8,128)(2,1)} %bitcast.104), channel_id=1, replica_groups=mesh['x'=4,'z'=4,'c'=2,'y'=4] {'x','z','c'}, dimensions={0} | all-to-all | bytes 3145728 | tf_op jit(solution)/shard_map/all_to_all | solution.py:459
  105.3 0.8 fusion.6
  106.4 0.9 fusion.41
  107.4 0.6 multiply_reduce_fusion
  108.0 2.8 %fusion.8 = bf16[128,8,768]{2,0,1:T(8,128)(2,1)S(1)} fusion(f32[128,8]{0,1:T(8,128)S(1)} %bitcast.111, f32[128,8]{0,1:T(8,128)S(1)} %copy.26, f32[8,768]{1,0:T(8,128)S(1)} %broadcast_select_fusion, f32[8]{0:T(128)S(1)} %get-tuple-element.147, bf16[128,8,768]{2,1,0:T(8,128)(2,1)S(1)} %bitcast.99, f32[8,128,128]{1,2,0:T(8,128)S(1)} %get-tuple-element.148), kind=kOutput, calls=%fused_computation.14 | convolution fusion | flops 1215168512 | bytes 3702816 | tf_op jit(solution)/shard_map/pmn,npo->mpo/dot_general | solution.py:396
  110.8 2.0 copy.33
  112.8 4.2 %all-to-all-start.1 = ((bf16[32,32,768]{2,1,0:T(8,128)(2,1)}), bf16[32,32,768]{2,1,0:T(8,128)(2,1)S(1)}, u32[]{:S(2)}, u32[]{:S(2)}) async-start(bf16[32,32,768]{2,1,0:T(8,128)(2,1)} %bitcast.18), calls=%async_computation.1 | async-start | bytes 3145728 | tf_op jit(solution)/shard_map/all_to_all | solution.py:462
  117.0 1.8 pad_maximum_fusion.1.scalars
  118.9 21.3 %all-to-all-done.1 = bf16[32,32,768]{2,1,0:T(8,128)(2,1)S(1)} async-done(((bf16[32,32,768]{2,1,0:T(8,128)(2,1)}), bf16[32,32,768]{2,1,0:T(8,128)(2,1)S(1)}, u32[]{:S(2)}, u32[]{:S(2)}) %all-to-all-start.1) | async-done | bytes 1572896 | tf_op jit(solution)/shard_map/all_to_all | solution.py:462
  140.2 3.1 %convolution_convert_fusion.resid_grad = bf16[1024,1024]{1,0:T(8,128)(2,1)} fusion(bf16[1024,768]{1,0:T(8,128)(2,1)S(1)} %bitcast.102, bf16[768,1024]{1,0:T(8,128)(2,1)S(1)} %copy-done.32), kind=kOutput, calls=%fused_computation.19 | convolution fusion | flops 1611661312 | bytes 5242880 | tf_op jit(solution)/shard_map/dot_general | solution.py:30
  143.3 12.0 %early_grads.1 = (bf16[4,384,1024]{2,1,0:T(8,128)(2,1)}, bf16[4,384,1024]{2,1,0:T(8,128)(2,1)}) custom-call(s32[4]{0:T(128)} %pad_add_fusion.refs_0_.place, bf16[1024,2048]{1,0:T(8,128)(2,1)} %get-tuple-element.102.hidden, bf16[1024,1024]{1,0:T(8,128)(2,1)} %convolution_convert_fusion.resid_grad, bf16[1024,1024]{1,0:T(8,128)(2,1)} %get-tuple-element.103.residual, ...), custom_call_target="tpu_custom_call" | custom-call | flops 5905580032 | bytes 18874368 | tf_op jit(solution)/shard_map/early_grads/pallas_call | solution.py:241
  155.4 9.8 %late_grads.2 = (bf16[1,512,1024]{2,1,0:T(8,128)(2,1)}, bf16[1,512,1024]{2,1,0:T(8,128)(2,1)}) custom-call(s32[4]{0:T(128)} %pad_add_fusion.refs_0_.place, bf16[1024,1024]{1,0:T(8,128)(2,1)} %convolution_convert_fusion.resid_grad, bf16[2048,1024]{1,0:T(8,128)(2,1)} %get-tuple-element.106.second, bf16[1024,2048]{1,0:T(8,128)(2,1)} %get-tuple-element.107.slope, ...), custom_call_target="tpu_custom_call" | custom-call | flops 4294967296 | bytes 12582912 | tf_op jit(solution)/shard_map/late_grads/pallas_call | solution.py:277
  165.6 1.6 add_convert_fusion
  167.7 0.9 copy.58
  168.6 1.0 dynamic-slice_bitcast_fusion
  169.6 1.4 add_convert_fusion.2
  171.0 3.7 %all-to-all-start.2 = ((bf16[16,32,1024]{2,1,0:T(8,128)(2,1)}), bf16[16,32,1024]{2,1,0:T(8,128)(2,1)S(1)}, u32[]{:S(2)}, u32[]{:S(2)}) async-start(bf16[16,32,1024]{2,1,0:T(8,128)(2,1)} %bitcast.28), calls=%async_computation.2 | async-start | bytes 2097152 | tf_op jit(solution)/shard_map/all_to_all | solution.py:482
  174.7 3.3 %collective-permute-start.15 = (bf16[2,8,24,1024]{3,2,0,1:T(8,128)(2,1)}, bf16[2,8,24,1024]{3,2,0,1:T(8,128)(2,1)S(1)}, u32[]{:S(2)}, u32[]{:S(2)}) collective-permute-start(bf16[2,8,24,1024]{3,2,0,1:T(8,128)(2,1)} %dynamic-slice_bitcast_fusion), channel_id=1, source_target_pairs={{0,3},{3,0},{1,2},{2,1},{4,7},{7,4},{5,6},{6,5},{8,11},{11,8},{9,1... | collective-permute-start | bytes 2359304 | tf_op jit(solution)/shard_map/ppermute | solution.py:327
  178.0 9.6 %late_grads.3 = (bf16[1,512,1024]{2,1,0:T(8,128)(2,1)}, bf16[1,512,1024]{2,1,0:T(8,128)(2,1)}) custom-call(s32[4]{0:T(128)} %pad_add_fusion.refs_0_.place, bf16[1024,1024]{1,0:T(8,128)(2,1)} %convolution_convert_fusion.resid_grad, bf16[2048,1024]{1,0:T(8,128)(2,1)} %get-tuple-element.106.second, bf16[1024,2048]{1,0:T(8,128)(2,1)} %get-tuple-element.107.slope, ...), custom_call_target="tpu_custom_call" | custom-call | flops 4294967296 | bytes 12582912 | tf_op jit(solution)/shard_map/late_grads/pallas_call | solution.py:277
  187.5 8.4 %collective-permute-done.15 = bf16[2,8,24,1024]{3,2,0,1:T(8,128)(2,1)S(1)} collective-permute-done((bf16[2,8,24,1024]{3,2,0,1:T(8,128)(2,1)}, bf16[2,8,24,1024]{3,2,0,1:T(8,128)(2,1)S(1)}, u32[]{:S(2)}, u32[]{:S(2)}) %collective-permute-start.15) | collective-permute-done | bytes 786464 | tf_op jit(solution)/shard_map/ppermute | solution.py:327
  195.9 0.9 copy-done.20
  196.9 0.7 collective-permute-done.14
  197.5 1.5 fusion.10
  199.1 0.8 dynamic-slice_bitcast_fusion.2
  199.8 2.3 collective-permute-start.20
  202.6 2.5 add_convert_fusion.1
  205.1 6.8 %all-to-all-start.3 = ((bf16[16,32,1024]{2,1,0:T(8,128)(2,1)}), bf16[16,32,1024]{2,1,0:T(8,128)(2,1)S(1)}, u32[]{:S(2)}, u32[]{:S(2)}) async-start(bf16[16,32,1024]{2,1,0:T(8,128)(2,1)} %bitcast.37), calls=%async_computation.3 | async-start | bytes 2097152 | tf_op jit(solution)/shard_map/all_to_all | solution.py:489
  212.0 0.9 collective-permute-done.20
  212.9 1.0 collective-permute-done.21
  213.9 1.2 fusion.27
  215.2 1.1 fusion.26
  216.3 1.0 pad_maximum_fusion
  217.5 12.6 %all-to-all-done.3 = bf16[16,32,1024]{2,1,0:T(8,128)(2,1)S(1)} async-done(((bf16[16,32,1024]{2,1,0:T(8,128)(2,1)}), bf16[16,32,1024]{2,1,0:T(8,128)(2,1)S(1)}, u32[]{:S(2)}, u32[]{:S(2)}) %all-to-all-start.3) | async-done | bytes 1048608 | tf_op jit(solution)/shard_map/all_to_all | solution.py:489
  230.1 3.6 %all-to-all-start.4 = ((bf16[16,24,1024]{2,1,0:T(8,128)(2,1)}), bf16[16,24,1024]{2,1,0:T(8,128)(2,1)S(1)}, u32[]{:S(2)}, u32[]{:S(2)}) async-start(bf16[16,24,1024]{2,1,0:T(8,128)(2,1)} %pad_maximum_fusion), calls=%async_computation.4 | async-start | bytes 1572864 | tf_op jit(solution)/shard_map/all_to_all | solution.py:494
  234.0 1.7 collective-permute-start.17
  235.7 0.7 collective-permute-start.18
  236.5 2.3 collective-permute-start.19
  238.7 0.8 collective-permute-done.17
  239.5 2.0 collective-permute-done.18
  241.5 5.4 %all-to-all-done.4 = bf16[16,24,1024]{2,1,0:T(8,128)(2,1)S(1)} async-done(((bf16[16,24,1024]{2,1,0:T(8,128)(2,1)}), bf16[16,24,1024]{2,1,0:T(8,128)(2,1)S(1)}, u32[]{:S(2)}, u32[]{:S(2)}) %all-to-all-start.4) | async-done | bytes 786464 | tf_op jit(solution)/shard_map/all_to_all | solution.py:494
  247.2 0.6 fusion.44
  249.1 0.6 slice_multiply_fusion
  251.7 0.6 maximum_multiply_fusion
  (110 shorter events, 6.8 us)
Async XLA Ops:
  0.6 59.6 %copy-start = (f32[8,768]{1,0:T(8,128)S(1)}, f32[8,768]{1,0:T(8,128)}, u32[]{:S(2)}) copy-start(f32[8,768]{1,0:T(8,128)} %param.11) | copy-start | bytes 73732
  0.7 1.2 copy-start.2
  1.9 1.2 copy-start.4
  3.1 1.0 copy-start.6
  4.1 3.4 %copy-start.16 = (bf16[4,256,1024]{2,1,0:T(8,128)(2,1)S(1)}, bf16[4,256,1024]{2,1,0:T(8,128)(2,1)}, u32[]{:S(2)}) copy-start(bf16[4,256,1024]{2,1,0:T(8,128)(2,1)} %param.7) | copy-start | bytes 6291460
  4.2 4.9 %copy-start.8 = (bf16[1216,256]{1,0:T(8,128)(2,1)}, bf16[1216,256]{1,0:T(8,128)(2,1)S(1)}, u32[]{:S(2)}) copy-start(bf16[1216,256]{1,0:T(8,128)(2,1)S(1)} %get-tuple-element.74.refs_2_) | copy-start | bytes 1867780
  4.2 4.9 %copy-start.10 = (bf16[1216,256]{1,0:T(8,128)(2,1)}, bf16[1216,256]{1,0:T(8,128)(2,1)S(1)}, u32[]{:S(2)}) copy-start(bf16[1216,256]{1,0:T(8,128)(2,1)S(1)} %get-tuple-element.75.refs_3_) | copy-start | bytes 1867780
  4.2 17.8 %collective-permute-start = (bf16[1216,256]{1,0:T(8,128)(2,1)S(1)}, bf16[1216,256]{1,0:T(8,128)(2,1)}, u32[]{:S(2)}, u32[]{:S(2)}) collective-permute-start(bf16[1216,256]{1,0:T(8,128)(2,1)S(1)} %get-tuple-element.74.refs_2_), channel_id=1, source_target_pairs={{0,1},{1,2},{2,3},{3,0},{4,5},{5,6},{6,7},{7,4},{8,9},{9,10},{10,1... | collective-permute-start | bytes 1867784 | tf_op jit(solution)/shard_map/ppermute | solution.py:26
  5.9 16.1 %collective-permute-start.1 = (bf16[1216,256]{1,0:T(8,128)(2,1)S(1)}, bf16[1216,256]{1,0:T(8,128)(2,1)}, u32[]{:S(2)}, u32[]{:S(2)}) collective-permute-start(bf16[1216,256]{1,0:T(8,128)(2,1)S(1)} %get-tuple-element.75.refs_3_), channel_id=1, source_target_pairs={{0,3},{1,0},{2,1},{3,2},{4,7},{5,4},{6,5},{7,6},{8,11},{9,8},{10,9... | collective-permute-start | bytes 1867784 | tf_op jit(solution)/shard_map/ppermute | solution.py:26
  7.5 1.6 copy-start.3
  7.5 2.3 copy-start.5
  7.5 2.4 copy-start.7
  10.0 0.8 copy-start.12
  10.8 0.8 copy-start.13
  12.9 9.1 %copy-start.11 = (bf16[1216,256]{1,0:T(8,128)(2,1)S(1)}, bf16[1216,256]{1,0:T(8,128)(2,1)}, u32[]{:S(2)}) copy-start(bf16[1216,256]{1,0:T(8,128)(2,1)} %copy-done.10) | copy-start | bytes 1867780
  12.9 10.2 %copy-start.9 = (bf16[1216,256]{1,0:T(8,128)(2,1)S(1)}, bf16[1216,256]{1,0:T(8,128)(2,1)}, u32[]{:S(2)}) copy-start(bf16[1216,256]{1,0:T(8,128)(2,1)} %copy-done.8) | copy-start | bytes 1867780
  22.1 16.7 %collective-permute-start.3 = (bf16[1216,256]{1,0:T(8,128)(2,1)S(1)}, bf16[1216,256]{1,0:T(8,128)(2,1)S(1)}, u32[]{:S(2)}, u32[]{:S(2)}) collective-permute-start(bf16[1216,256]{1,0:T(8,128)(2,1)S(1)} %copy-done.11), channel_id=1, source_target_pairs={{0,1},{1,2},{2,3},{3,0},{4,5},{5,6},{6,7},{7,4},{8,9},{9,10},{10,1... | collective-permute-start | bytes 1867784 | tf_op jit(solution)/shard_map/ppermute | solution.py:26
  23.1 15.7 %collective-permute-start.2 = (bf16[1216,256]{1,0:T(8,128)(2,1)S(1)}, bf16[1216,256]{1,0:T(8,128)(2,1)S(1)}, u32[]{:S(2)}, u32[]{:S(2)}) collective-permute-start(bf16[1216,256]{1,0:T(8,128)(2,1)S(1)} %copy-done.9), channel_id=1, source_target_pairs={{0,3},{1,0},{2,1},{3,2},{4,7},{5,4},{6,5},{7,6},{8,11},{9,8},{10,9... | collective-permute-start | bytes 1867784 | tf_op jit(solution)/shard_map/ppermute | solution.py:26
  25.4 13.4 %collective-permute-start.4 = (bf16[1216,256]{1,0:T(8,128)(2,1)}, bf16[1216,256]{1,0:T(8,128)(2,1)S(1)}, u32[]{:S(2)}, u32[]{:S(2)}) collective-permute-start(bf16[1216,256]{1,0:T(8,128)(2,1)} %collective-permute-done.refs_2_), channel_id=1, source_target_pairs={{0,4},{4,0},{1,5},{5,1},{2,6},{6,2},{3,7},{7,3},{8,12},{12,8},{9,1... | collective-permute-start | bytes 1867784 | tf_op jit(solution)/shard_map/ppermute | solution.py:26
  25.4 13.4 %collective-permute-start.5 = (bf16[1216,256]{1,0:T(8,128)(2,1)}, bf16[1216,256]{1,0:T(8,128)(2,1)S(1)}, u32[]{:S(2)}, u32[]{:S(2)}) collective-permute-start(bf16[1216,256]{1,0:T(8,128)(2,1)} %collective-permute-done.1.refs_7_), channel_id=1, source_target_pairs={{0,4},{4,0},{1,5},{5,1},{2,6},{6,2},{3,7},{7,3},{8,12},{12,8},{9,1... | collective-permute-start | bytes 1867784 | tf_op jit(solution)/shard_map/ppermute | solution.py:26
  38.8 4.5 %copy-start.24 = (bf16[1216,256]{1,0:T(8,128)(2,1)}, bf16[1216,256]{1,0:T(8,128)(2,1)S(1)}, u32[]{:S(2)}) copy-start(bf16[1216,256]{1,0:T(8,128)(2,1)S(1)} %collective-permute-done.3.refs_3_) | copy-start | bytes 1867780
  38.8 4.5 %copy-start.25 = (bf16[1216,256]{1,0:T(8,128)(2,1)}, bf16[1216,256]{1,0:T(8,128)(2,1)S(1)}, u32[]{:S(2)}) copy-start(bf16[1216,256]{1,0:T(8,128)(2,1)S(1)} %collective-permute-done.2.refs_6_) | copy-start | bytes 1867780
  38.8 4.5 %copy-start.26 = (bf16[1216,256]{1,0:T(8,128)(2,1)}, bf16[1216,256]{1,0:T(8,128)(2,1)S(1)}, u32[]{:S(2)}) copy-start(bf16[1216,256]{1,0:T(8,128)(2,1)S(1)} %collective-permute-done.4.refs_4_) | copy-start | bytes 1867780
  38.8 0.9 copy-start.27
  38.8 4.5 %collective-permute-start.8 = (bf16[1216,256]{1,0:T(8,128)(2,1)S(1)}, bf16[1216,256]{1,0:T(8,128)(2,1)}, u32[]{:S(2)}, u32[]{:S(2)}) collective-permute-start(bf16[1216,256]{1,0:T(8,128)(2,1)S(1)} %collective-permute-done.3.refs_3_), channel_id=1, source_target_pairs={{0,4},{4,0},{1,5},{5,1},{2,6},{6,2},{3,7},{7,3},{8,12},{12,8},{9,1... | collective-permute-start | bytes 1867784 | tf_op jit(solution)/shard_map/ppermute | solution.py:26
  38.9 4.4 %collective-permute-start.9 = (bf16[1216,256]{1,0:T(8,128)(2,1)S(1)}, bf16[1216,256]{1,0:T(8,128)(2,1)}, u32[]{:S(2)}, u32[]{:S(2)}) collective-permute-start(bf16[1216,256]{1,0:T(8,128)(2,1)S(1)} %collective-permute-done.2.refs_6_), channel_id=1, source_target_pairs={{0,4},{4,0},{1,5},{5,1},{2,6},{6,2},{3,7},{7,3},{8,12},{12,8},{9,1... | collective-permute-start | bytes 1867784 | tf_op jit(solution)/shard_map/ppermute | solution.py:26
  39.7 19.8 %collective-permute-start.7 = (bf16[1216,256]{1,0:T(8,128)(2,1)}, bf16[1216,256]{1,0:T(8,128)(2,1)S(1)}, u32[]{:S(2)}, u32[]{:S(2)}) collective-permute-start(bf16[1216,256]{1,0:T(8,128)(2,1)} %collective-permute-done.1.refs_7_), channel_id=1, source_target_pairs={{0,3},{1,0},{2,1},{3,2},{4,7},{5,4},{6,5},{7,6},{8,11},{9,8},{10,9... | collective-permute-start | bytes 1867784 | tf_op jit(solution)/shard_map/ppermute | solution.py:26
  42.7 16.9 %collective-permute-start.6 = (bf16[1216,256]{1,0:T(8,128)(2,1)}, bf16[1216,256]{1,0:T(8,128)(2,1)S(1)}, u32[]{:S(2)}, u32[]{:S(2)}) collective-permute-start(bf16[1216,256]{1,0:T(8,128)(2,1)} %collective-permute-done.refs_2_), channel_id=1, source_target_pairs={{0,1},{1,2},{2,3},{3,0},{4,5},{5,6},{6,7},{7,4},{8,9},{9,10},{10,1... | collective-permute-start | bytes 1867784 | tf_op jit(solution)/shard_map/ppermute | solution.py:26
  43.3 16.9 %copy-start.30 = (s32[8]{0:T(128)S(1)}, s32[8]{0:T(128)}, u32[]{:S(2)}) copy-start(s32[8]{0:T(128)} %param.12) | copy-start | bytes 100
  59.6 3.1 %copy-start.22 = (bf16[1216,256]{1,0:T(8,128)(2,1)}, bf16[1216,256]{1,0:T(8,128)(2,1)S(1)}, u32[]{:S(2)}) copy-start(bf16[1216,256]{1,0:T(8,128)(2,1)S(1)} %collective-permute-done.7.refs_3_) | copy-start | bytes 1867780
  59.6 3.0 %copy-start.23 = (bf16[1216,256]{1,0:T(8,128)(2,1)}, bf16[1216,256]{1,0:T(8,128)(2,1)S(1)}, u32[]{:S(2)}) copy-start(bf16[1216,256]{1,0:T(8,128)(2,1)S(1)} %collective-permute-done.6.refs_2_) | copy-start | bytes 1867780
  59.6 2.1 collective-permute-start.10
  59.7 2.9 %collective-permute-start.11 = (bf16[1216,256]{1,0:T(8,128)(2,1)S(1)}, bf16[1216,256]{1,0:T(8,128)(2,1)S(1)}, u32[]{:S(2)}, u32[]{:S(2)}) collective-permute-start(bf16[1216,256]{1,0:T(8,128)(2,1)S(1)} %collective-permute-done.7.refs_3_), channel_id=1, source_target_pairs={{0,4},{4,0},{1,5},{5,1},{2,6},{6,2},{3,7},{7,3},{8,12},{12,8},{9,1... | collective-permute-start | bytes 1867784 | tf_op jit(solution)/shard_map/ppermute | solution.py:26
  61.7 0.9 copy-start.28
  62.6 0.8 copy-start.29
  106.4 0.9 copy-start.31
  112.8 27.4 %copy-start.32 = (bf16[768,1024]{1,0:T(8,128)(2,1)S(1)}, bf16[768,1024]{1,0:T(8,128)(2,1)}, u32[]{:S(2)}) copy-start(bf16[768,1024]{1,0:T(8,128)(2,1)} %get-tuple-element.101) | copy-start | bytes 4718596
  112.8 27.4 %all-to-all-start.1 = ((bf16[32,32,768]{2,1,0:T(8,128)(2,1)}), bf16[32,32,768]{2,1,0:T(8,128)(2,1)S(1)}, u32[]{:S(2)}, u32[]{:S(2)}) async-start(bf16[32,32,768]{2,1,0:T(8,128)(2,1)} %bitcast.18), calls=%async_computation.1 | async-start | bytes 3145728 | tf_op jit(solution)/shard_map/all_to_all | solution.py:462
  140.2 3.1 %copy-start.17 = (bf16[32,32,768]{2,1,0:T(8,128)(2,1)}, bf16[32,32,768]{2,1,0:T(8,128)(2,1)S(1)}, u32[]{:S(2)}) copy-start(bf16[32,32,768]{2,1,0:T(8,128)(2,1)S(1)} %all-to-all-done.1) | copy-start | bytes 4718596
  155.3 10.3 %collective-permute-start.12 = (bf16[4,384,1024]{2,1,0:T(8,128)(2,1)}, bf16[4,384,1024]{2,1,0:T(8,128)(2,1)S(1)}, u32[]{:S(2)}, u32[]{:S(2)}) collective-permute-start(bf16[4,384,1024]{2,1,0:T(8,128)(2,1)} %get-tuple-element.104), channel_id=1, source_target_pairs={{0,4},{4,0},{1,5},{5,1},{2,6},{6,2},{3,7},{7,3},{8,12},{12,8},{9,1... | collective-permute-start | bytes 9437192 | tf_op jit(solution)/shard_map/ppermute | solution.py:26
  155.3 10.3 %copy-start.14 = (bf16[4,384,1024]{2,1,0:T(8,128)(2,1)S(1)}, bf16[4,384,1024]{2,1,0:T(8,128)(2,1)}, u32[]{:S(2)}) copy-start(bf16[4,384,1024]{2,1,0:T(8,128)(2,1)} %get-tuple-element.111) | copy-start | bytes 9437188
  165.2 4.4 %collective-permute-start.13 = (bf16[1,512,1024]{2,1,0:T(8,128)(2,1)}, bf16[1,512,1024]{2,1,0:T(8,128)(2,1)S(1)}, u32[]{:S(2)}, u32[]{:S(2)}) collective-permute-start(bf16[1,512,1024]{2,1,0:T(8,128)(2,1)} %get-tuple-element.110), channel_id=1, source_target_pairs={{0,4},{4,0},{1,5},{5,1},{2,6},{6,2},{3,7},{7,3},{8,12},{12,8},{9,1... | collective-permute-start | bytes 3145736 | tf_op jit(solution)/shard_map/ppermute | solution.py:26
  167.7 1.9 copy-start.19
  171.0 26.5 %all-to-all-start.2 = ((bf16[16,32,1024]{2,1,0:T(8,128)(2,1)}), bf16[16,32,1024]{2,1,0:T(8,128)(2,1)S(1)}, u32[]{:S(2)}, u32[]{:S(2)}) async-start(bf16[16,32,1024]{2,1,0:T(8,128)(2,1)} %bitcast.28), calls=%async_computation.2 | async-start | bytes 2097152 | tf_op jit(solution)/shard_map/all_to_all | solution.py:482
  174.7 21.3 %collective-permute-start.15 = (bf16[2,8,24,1024]{3,2,0,1:T(8,128)(2,1)}, bf16[2,8,24,1024]{3,2,0,1:T(8,128)(2,1)S(1)}, u32[]{:S(2)}, u32[]{:S(2)}) collective-permute-start(bf16[2,8,24,1024]{3,2,0,1:T(8,128)(2,1)} %dynamic-slice_bitcast_fusion), channel_id=1, source_target_pairs={{0,3},{3,0},{1,2},{2,1},{4,7},{7,4},{5,6},{6,5},{8,11},{11,8},{9,1... | collective-permute-start | bytes 2359304 | tf_op jit(solution)/shard_map/ppermute | solution.py:327
  178.0 19.5 %collective-permute-start.14 = (bf16[2,8,24,1024]{3,2,1,0:T(8,128)(2,1)}, bf16[2,8,24,1024]{3,2,1,0:T(8,128)(2,1)}, u32[]{:S(2)}, u32[]{:S(2)}) collective-permute-start(bf16[2,8,24,1024]{3,2,1,0:T(8,128)(2,1)} %bitcast.109), channel_id=1, source_target_pairs={{0,1},{1,0},{2,3},{3,2},{4,5},{5,4},{6,7},{7,6},{8,9},{9,8},{10,11... | collective-permute-start | bytes 2359304 | tf_op jit(solution)/shard_map/ppermute | solution.py:327
  195.9 0.9 copy-start.20
  197.5 5.1 %collective-permute-start.16 = (bf16[1,512,1024]{2,1,0:T(8,128)(2,1)}, bf16[1,512,1024]{2,1,0:T(8,128)(2,1)}, u32[]{:S(2)}, u32[]{:S(2)}) collective-permute-start(bf16[1,512,1024]{2,1,0:T(8,128)(2,1)} %get-tuple-element.117), channel_id=1, source_target_pairs={{0,4},{4,0},{1,5},{5,1},{2,6},{6,2},{3,7},{7,3},{8,12},{12,8},{9,1... | collective-permute-start | bytes 3145736 | tf_op jit(solution)/shard_map/ppermute | solution.py:26
  197.5 4.7 %copy-start.21 = (bf16[2,8,24,1024]{3,2,0,1:T(8,128)(2,1)S(1)}, bf16[2,8,24,1024]{3,2,0,1:T(8,128)(2,1)}, u32[]{:S(2)}) copy-start(bf16[2,8,24,1024]{3,2,0,1:T(8,128)(2,1)} %copy-done.20) | copy-start | bytes 2359300
  199.0 3.5 %copy-start.15 = (bf16[2,8,24,1024]{3,2,1,0:T(8,128)(2,1)}, bf16[2,8,24,1024]{3,2,1,0:T(8,128)(2,1)S(1)}, u32[]{:S(2)}) copy-start(bf16[2,8,24,1024]{3,2,1,0:T(8,128)(2,1)S(1)} %fusion.10) | copy-start | bytes 2359300
  199.0 3.6 %copy-start.18 = (bf16[1,512,1024]{2,1,0:T(8,128)(2,1)S(1)}, bf16[1,512,1024]{2,1,0:T(8,128)(2,1)}, u32[]{:S(2)}) copy-start(bf16[1,512,1024]{2,1,0:T(8,128)(2,1)} %get-tuple-element.115) | copy-start | bytes 3145732
  199.8 13.1 %collective-permute-start.20 = (bf16[8,24,1024]{2,1,0:T(8,128)(2,1)}, bf16[8,24,1024]{2,1,0:T(8,128)(2,1)}, u32[]{:S(2)}, u32[]{:S(2)}) collective-permute-start(bf16[8,24,1024]{2,1,0:T(8,128)(2,1)} %dynamic-slice_bitcast_fusion.2), channel_id=1, source_target_pairs={{0,3},{3,0},{1,2},{2,1},{4,7},{7,4},{5,6},{6,5},{8,11},{11,8},{9,1... | collective-permute-start | bytes 1179656 | tf_op jit(solution)/shard_map/ppermute | solution.py:327
  202.5 11.4 %collective-permute-start.21 = (bf16[8,24,1024]{2,1,0:T(8,128)(2,1)S(1)}, bf16[8,24,1024]{2,1,0:T(8,128)(2,1)}, u32[]{:S(2)}, u32[]{:S(2)}) collective-permute-start(bf16[8,24,1024]{2,1,0:T(8,128)(2,1)S(1)} %dynamic-slice_bitcast_fusion.1), channel_id=1, source_target_pairs={{0,1},{1,0},{2,3},{3,2},{4,5},{5,4},{6,7},{7,6},{8,9},{9,8},{10,11... | collective-permute-start | bytes 1179656 | tf_op jit(solution)/shard_map/ppermute | solution.py:327
  205.1 25.0 %all-to-all-start.3 = ((bf16[16,32,1024]{2,1,0:T(8,128)(2,1)}), bf16[16,32,1024]{2,1,0:T(8,128)(2,1)S(1)}, u32[]{:S(2)}, u32[]{:S(2)}) async-start(bf16[16,32,1024]{2,1,0:T(8,128)(2,1)} %bitcast.37), calls=%async_computation.3 | async-start | bytes 2097152 | tf_op jit(solution)/shard_map/all_to_all | solution.py:489
  230.1 16.8 %all-to-all-start.4 = ((bf16[16,24,1024]{2,1,0:T(8,128)(2,1)}), bf16[16,24,1024]{2,1,0:T(8,128)(2,1)S(1)}, u32[]{:S(2)}, u32[]{:S(2)}) async-start(bf16[16,24,1024]{2,1,0:T(8,128)(2,1)} %pad_maximum_fusion), calls=%async_computation.4 | async-start | bytes 1572864 | tf_op jit(solution)/shard_map/all_to_all | solution.py:494
  233.7 18.6 %copy-start.1 = (f32[8,768]{1,0:T(8,128)S(1)}, f32[8,768]{1,0:T(8,128)}, u32[]{:S(2)}) copy-start(f32[8,768]{1,0:T(8,128)} %param.11) | copy-start | bytes 73732
  234.0 5.5 %collective-permute-start.17 = (f32[2,8,1024]{2,1,0:T(8,128)S(1)}, f32[2,8,1024]{2,1,0:T(8,128)S(1)}, u32[]{:S(2)}, u32[]{:S(2)}) collective-permute-start(f32[2,8,1024]{2,1,0:T(8,128)S(1)} %get-tuple-element.136), channel_id=1, source_target_pairs={{0,1},{1,2},{2,3},{3,0},{4,5},{5,6},{6,7},{7,4},{8,9},{9,10},{10,1... | collective-permute-start | bytes 196616 | tf_op jit(solution)/shard_map/ppermute | solution.py:26
  235.7 5.8 %collective-permute-start.18 = (f32[2,8,1024]{2,1,0:T(8,128)S(1)}, f32[2,8,1024]{2,1,0:T(8,128)S(1)}, u32[]{:S(2)}, u32[]{:S(2)}) collective-permute-start(f32[2,8,1024]{2,1,0:T(8,128)S(1)} %get-tuple-element.137), channel_id=1, source_target_pairs={{0,2},{1,3},{2,0},{3,1},{4,6},{5,7},{6,4},{7,5},{8,10},{9,11},{10,... | collective-permute-start | bytes 196616 | tf_op jit(solution)/shard_map/ppermute | solution.py:26
  236.5 5.0 %collective-permute-start.19 = (f32[2,8,1024]{2,1,0:T(8,128)S(1)}, f32[2,8,1024]{2,1,0:T(8,128)S(1)}, u32[]{:S(2)}, u32[]{:S(2)}) collective-permute-start(f32[2,8,1024]{2,1,0:T(8,128)S(1)} %get-tuple-element.138), channel_id=1, source_target_pairs={{0,3},{1,0},{2,1},{3,2},{4,7},{5,4},{6,5},{7,6},{8,11},{9,8},{10,9... | collective-permute-start | bytes 196616 | tf_op jit(solution)/shard_map/ppermute | solution.py:26

commit v9 on v8

--- a/solution.py
+++ b/solution.py
@@ -481,14 +481,14 @@
     a = add(after(late[0], *early_sent), a_in).reshape(16, RING * n, width)
     a_all = lax.all_to_all(a, group, 0, 0, tiled=True)
     late = late_grads(at, 1, after(resid_grad, a), second, slope, tokens)
-    b_in = shift(after(late[1], a_all, *early_in), "c", 1)
-    early = [kept_plus(x, v, s[0]) for x, v, s in zip(early, early_in, steps)]
+    b_in = shift(after(late[1], a_all), "c", 1)
+    b = add(late[0], b_in).reshape(16, RING * n, width)
+    b_all = lax.all_to_all(b, group, 0, 0, tiled=True)
+    early = [kept_plus(x, after(v, b), s[0]) for x, v, s in zip(early, early_in, steps)]
     early_sent = [outgoing(x, s[1]) for x, s in zip(early, steps)]
     early_in = [sent_along(x, s[1]) for x, s in zip(early_sent, steps)]
-    b = add(after(late[0], *early_sent), b_in).reshape(16, RING * n, width)
-    b_all = lax.all_to_all(b, group, 0, 0, tiled=True)
-    a = jnp.sum(after(a_all, b).astype(F32), 0)
-    early = [kept_plus(x, after(v, b), s[1]) for x, v, s in zip(early, early_in, steps)]
+    a = jnp.sum(after(a_all, *early_sent).astype(F32), 0)
+    early = [kept_plus(x, v, s[1]) for x, v, s in zip(early, early_in, steps)]
     early = jnp.concatenate(early)
     b = jnp.sum(b_all.astype(F32), 0)
     early = lax.all_to_all(after(early, b_all), group, 0, 0, tiled=True)

time: 255 us -> 256 us (level)
  waiting for transfers between devices: 67.7 us -> 73 us
  starting transfers between devices: 40.4 us -> 37.3 us
    all_to_all x1, waiting for transfers between devices: 12.6 us -> 0.01 us  [per_device(): b_all = lax.all_to_all(b, group, 0, 0, tiled=True)]
    ppermute x4, waiting for transfers between devices: 11 us -> 20 us  [sent_along(): return lax.ppermute(x, step[1], step[0])]
    all_to_all x1, waiting for transfers between devices: 0.01 us -> 8.69 us  [per_device(): a_all = lax.all_to_all(a, group, 0, 0, tiled=True)]
    unnamed x67 -> x59, local copies, waits for them, and re-layouts: 8.97 us -> 8.08 us
  transfers between devices with their start and end apart: 26 -> 26, of which waited for: 12 -> 11; matrix products, arithmetic and copies ran while one was open for 7% -> 7% of each run, Pallas kernels for 18% -> 18%
where the time goes in v9:
time: 256 us; the launch traced here: 254 us
  waiting for transfers between devices  73 us (29%)
  Pallas kernels  67.9 us (27%)
  starting transfers between devices  37.3 us (15%)
  blocking collectives  30.5 us (12%)
  other arithmetic  18.4 us (7%)
  local copies, waits for them, and re-layouts  15.4 us (6%)
  matrix products  6.82 us (3%)
  between operations  4.96 us (2%)
    pallas_call x3, Pallas kernels, forward_part(): pl.pallas_call(functools.partial(forward_kernel, groups, first_call, last...  36.4 us
    all_to_all x1, blocking collectives, per_device(): gathered = lax.all_to_all(forecast, group, 0, 0, tiled=True)  30.5 us
    all_to_all x1, waiting for transfers between devices, per_device(): lax.all_to_all(grad_raw.reshape(32, members * own, out_width), group, 0,...  21.3 us
    ppermute x4, waiting for transfers between devices, sent_along(): return lax.ppermute(x, step[1], step[0])  20 us
    pallas_call x2, Pallas kernels, late_grads(): pl.pallas_call(late_kernel, grid_spec=pltpu.PrefetchScalarGridSpec(num_sc...  19.3 us
    ppermute x18, waiting for transfers between devices, shift(): return lax.ppermute(x, axis, [(i, (i + by) % size) for i in range(size)])  18.5 us
    ppermute x18, starting transfers between devices, shift(): return lax.ppermute(x, axis, [(i, (i + by) % size) for i in range(size)])  15 us
    pallas_call x1, Pallas kernels, early_grads(): pl.pallas_call(early_kernel, grid_spec=pltpu.PrefetchScalarGridSpec(num_s...  12 us
  transfers between devices with their start and end apart: 26, of which 11 were waited for; matrix products, arithmetic and copies ran while one was open for 7% of the time, Pallas kernels for 18%

profile of v9, /device:TPU:0, one launch (start us, length us, event | category | flops | bytes accessed | tf_op | source)
XLA Modules:
  0.0 254.5 jit_solution(16107749764329255109)
XLA Ops:
  0.7 1.2 copy-done.2
  1.9 1.2 copy-done.4
  3.1 1.0 copy-done.6
  4.2 1.7 collective-permute-start
  5.9 1.6 collective-permute-start.1
  7.5 1.6 copy.23
  9.1 0.7 copy-done.5
  10.0 0.8 copy-done.12
  10.8 0.8 copy-done.13
  11.7 0.6 pad_add_fusion.2
  12.2 0.6 pad_add_fusion.refs_0_.place
  12.9 9.1 %forward_part.3 = (bf16[1024,2048]{1,0:T(8,128)(2,1)}, bf16[1024,2048]{1,0:T(8,128)(2,1)}, bf16[2048,1024]{1,0:T(8,128)(2,1)}, bf16[768,1024]{1,0:T(8,128)(2,1)}, f32[1024,1024]{1,0:T(8,128)}) custom-call(s32[4]{0:T(128)} %pad_add_fusion.refs_0_.place, bf16[1024,1024]{1,0:T(8,128)(2,1)} %bitcast.90, bf16[1216,256]{1,0:T(8,128)(2,1)} %copy-done.8, ...), custom_call_target="tpu_custom_call" | custom-call | flops 2147483648 | bytes 12582912 | tf_op jit(solution)/shard_map/forward_part/pallas_call | solution.py:166
  22.0 1.1 collective-permute-start.3
  23.1 2.2 collective-permute-start.2
  25.3 0.5 collective-permute-start.5
  25.9 12.9 %collective-permute-done.3.refs_3_ = bf16[1216,256]{1,0:T(8,128)(2,1)S(1)} collective-permute-done((bf16[1216,256]{1,0:T(8,128)(2,1)S(1)}, bf16[1216,256]{1,0:T(8,128)(2,1)S(1)}, u32[]{:S(2)}, u32[]{:S(2)}) %collective-permute-start.3) | collective-permute-done | bytes 622624 | tf_op jit(solution)/shard_map/ppermute | solution.py:26
  39.7 2.9 %collective-permute-start.7 = (bf16[1216,256]{1,0:T(8,128)(2,1)}, bf16[1216,256]{1,0:T(8,128)(2,1)S(1)}, u32[]{:S(2)}, u32[]{:S(2)}) collective-permute-start(bf16[1216,256]{1,0:T(8,128)(2,1)} %collective-permute-done.1.refs_7_), channel_id=1, source_target_pairs={{0,3},{1,0},{2,1},{3,2},{4,7},{5,4},{6,5},{7,6},{8,11},{9,8},{10,9... | collective-permute-start | bytes 1867784 | tf_op jit(solution)/shard_map/ppermute | solution.py:26
  42.6 0.6 stack.68.refs_0_
  43.3 16.2 %forward_part.4 = (bf16[1024,2048]{1,0:T(8,128)(2,1)}, bf16[1024,2048]{1,0:T(8,128)(2,1)}, bf16[2048,1024]{1,0:T(8,128)(2,1)}, bf16[768,1024]{1,0:T(8,128)(2,1)}, f32[1024,1024]{1,0:T(8,128)}) custom-call(s32[5]{0:T(128)} %stack.68.refs_0_, bf16[1024,1024]{1,0:T(8,128)(2,1)} %bitcast.91, ...), custom_call_target="tpu_custom_call", output_to_operand_aliasing={{0}: (11, {}), {1}: (12, {}), {2}: (13, {}), {3}: (14, {})} | custom-call | flops 4294967296 | bytes 12582912 | tf_op jit(solution)/shard_map/forward_part/pallas_call | solution.py:166
  60.2 0.6 gather_fusion
  60.8 0.9 collective-permute-done.10.refs_4_
  61.7 0.9 collective-permute-done.11.refs_5_
  62.6 0.8 copy-done.25
  63.4 11.1 %forward_part.5 = (bf16[1024,2048]{1,0:T(8,128)(2,1)}, bf16[1024,2048]{1,0:T(8,128)(2,1)}, bf16[2048,1024]{1,0:T(8,128)(2,1)}, bf16[768,1024]{1,0:T(8,128)(2,1)}...) custom-call(s32[4]{0:T(128)} %get-tuple-element.128.refs_0_, ...), custom_call_target="tpu_custom_call", output_to_operand_aliasing={{0}: (7, {}), {1}: (8, {}), {2}: (9, {})} | custom-call | flops 2147483648 | bytes 12582912 | tf_op jit(solution)/shard_map/forward_part/pallas_call | solution.py:166
  74.5 30.5 %all_to_all.25 = bf16[32,32,768]{2,1,0:T(8,128)(2,1)S(1)} all-to-all(bf16[32,32,768]{2,1,0:T(8,128)(2,1)} %bitcast.104), channel_id=1, replica_groups=mesh['x'=4,'z'=4,'c'=2,'y'=4] {'x','z','c'}, dimensions={0} | all-to-all | bytes 3145728 | tf_op jit(solution)/shard_map/all_to_all | solution.py:459
  105.3 0.8 fusion.6
  106.4 0.9 fusion.41
  107.3 0.6 multiply_reduce_fusion
  107.9 2.8 %fusion.8 = bf16[128,8,768]{2,0,1:T(8,128)(2,1)S(1)} fusion(f32[128,8]{0,1:T(8,128)S(1)} %bitcast.111, f32[128,8]{0,1:T(8,128)S(1)} %copy.26, f32[8,768]{1,0:T(8,128)S(1)} %broadcast_select_fusion, f32[8]{0:T(128)S(1)} %get-tuple-element.145, bf16[128,8,768]{2,1,0:T(8,128)(2,1)S(1)} %bitcast.99, f32[8,128,128]{1,2,0:T(8,128)S(1)} %get-tuple-element.146), kind=kOutput, calls=%fused_computation.14 | convolution fusion | flops 1215168512 | bytes 3702816 | tf_op jit(solution)/shard_map/pmn,npo->mpo/dot_general | solution.py:396
  110.7 2.0 copy.33
  112.8 4.2 %all-to-all-start.1 = ((bf16[32,32,768]{2,1,0:T(8,128)(2,1)}), bf16[32,32,768]{2,1,0:T(8,128)(2,1)S(1)}, u32[]{:S(2)}, u32[]{:S(2)}) async-start(bf16[32,32,768]{2,1,0:T(8,128)(2,1)} %bitcast.18), calls=%async_computation.1 | async-start | bytes 3145728 | tf_op jit(solution)/shard_map/all_to_all | solution.py:462
  117.0 1.8 pad_maximum_fusion.1.scalars
  118.8 21.3 %all-to-all-done.1 = bf16[32,32,768]{2,1,0:T(8,128)(2,1)S(1)} async-done(((bf16[32,32,768]{2,1,0:T(8,128)(2,1)}), bf16[32,32,768]{2,1,0:T(8,128)(2,1)S(1)}, u32[]{:S(2)}, u32[]{:S(2)}) %all-to-all-start.1) | async-done | bytes 1572896 | tf_op jit(solution)/shard_map/all_to_all | solution.py:462
  140.1 3.1 %convolution_convert_fusion.resid_grad = bf16[1024,1024]{1,0:T(8,128)(2,1)} fusion(bf16[1024,768]{1,0:T(8,128)(2,1)S(1)} %bitcast.102, bf16[768,1024]{1,0:T(8,128)(2,1)S(1)} %copy-done.28), kind=kOutput, calls=%fused_computation.19 | convolution fusion | flops 1611661312 | bytes 5242880 | tf_op jit(solution)/shard_map/dot_general | solution.py:30
  143.2 12.0 %early_grads.1 = (bf16[4,384,1024]{2,1,0:T(8,128)(2,1)}, bf16[4,384,1024]{2,1,0:T(8,128)(2,1)}) custom-call(s32[4]{0:T(128)} %pad_add_fusion.refs_0_.place, bf16[1024,2048]{1,0:T(8,128)(2,1)} %get-tuple-element.101.hidden, bf16[1024,1024]{1,0:T(8,128)(2,1)} %convolution_convert_fusion.resid_grad, bf16[1024,1024]{1,0:T(8,128)(2,1)} %get-tuple-element.102.residual, ...), custom_call_target="tpu_custom_call" | custom-call | flops 5905580032 | bytes 18874368 | tf_op jit(solution)/shard_map/early_grads/pallas_call | solution.py:241
  155.3 9.8 %late_grads.2 = (bf16[1,512,1024]{2,1,0:T(8,128)(2,1)}, bf16[1,512,1024]{2,1,0:T(8,128)(2,1)}) custom-call(s32[4]{0:T(128)} %pad_add_fusion.refs_0_.place, bf16[1024,1024]{1,0:T(8,128)(2,1)} %convolution_convert_fusion.resid_grad, bf16[2048,1024]{1,0:T(8,128)(2,1)} %get-tuple-element.105.second, bf16[1024,2048]{1,0:T(8,128)(2,1)} %get-tuple-element.106.slope, ...), custom_call_target="tpu_custom_call" | custom-call | flops 4294967296 | bytes 12582912 | tf_op jit(solution)/shard_map/late_grads/pallas_call | solution.py:277
  165.5 1.6 add_convert_fusion
  167.6 0.9 copy.58
  168.6 1.0 dynamic-slice_bitcast_fusion
  169.5 1.4 add_convert_fusion.2
  170.9 3.7 %all-to-all-start.2 = ((bf16[16,32,1024]{2,1,0:T(8,128)(2,1)}), bf16[16,32,1024]{2,1,0:T(8,128)(2,1)S(1)}, u32[]{:S(2)}, u32[]{:S(2)}) async-start(bf16[16,32,1024]{2,1,0:T(8,128)(2,1)} %bitcast.28), calls=%async_computation.2 | async-start | bytes 2097152 | tf_op jit(solution)/shard_map/all_to_all | solution.py:482
  174.6 9.5 %late_grads.3 = (bf16[1,512,1024]{2,1,0:T(8,128)(2,1)}, bf16[1,512,1024]{2,1,0:T(8,128)(2,1)}) custom-call(s32[4]{0:T(128)} %pad_add_fusion.refs_0_.place, bf16[1024,1024]{1,0:T(8,128)(2,1)} %convolution_convert_fusion.resid_grad, bf16[2048,1024]{1,0:T(8,128)(2,1)} %get-tuple-element.105.second, bf16[1024,2048]{1,0:T(8,128)(2,1)} %get-tuple-element.106.slope, ...), custom_call_target="tpu_custom_call" | custom-call | flops 4294967296 | bytes 12582912 | tf_op jit(solution)/shard_map/late_grads/pallas_call | solution.py:277
  184.2 8.7 %all-to-all-done.2 = bf16[16,32,1024]{2,1,0:T(8,128)(2,1)S(1)} async-done(((bf16[16,32,1024]{2,1,0:T(8,128)(2,1)}), bf16[16,32,1024]{2,1,0:T(8,128)(2,1)S(1)}, u32[]{:S(2)}, u32[]{:S(2)}) %all-to-all-start.2) | async-done | bytes 1048608 | tf_op jit(solution)/shard_map/all_to_all | solution.py:482
  192.8 3.2 %collective-permute-start.16 = (bf16[2,8,24,1024]{3,2,0,1:T(8,128)(2,1)}, bf16[2,8,24,1024]{3,2,0,1:T(8,128)(2,1)}, u32[]{:S(2)}, u32[]{:S(2)}) collective-permute-start(bf16[2,8,24,1024]{3,2,0,1:T(8,128)(2,1)} %dynamic-slice_bitcast_fusion), channel_id=1, source_target_pairs={{0,3},{3,0},{1,2},{2,1},{4,7},{7,4},{5,6},{6,5},{8,11},{11,8},{9,1... | collective-permute-start | bytes 2359304 | tf_op jit(solution)/shard_map/ppermute | solution.py:327
  196.0 2.9 %add_convert_fusion.1 = bf16[1,512,1024]{2,1,0:T(8,128)(2,1)} fusion(bf16[1,512,1024]{2,1,0:T(8,128)(2,1)} %collective-permute-done.15, bf16[1,512,1024]{2,1,0:T(8,128)(2,1)} %get-tuple-element.113), kind=kLoop, calls=%fused_computation.17 | loop fusion | flops 2097152 | bytes 3145728 | tf_op jit(solution)/shard_map/convert_element_type | solution.py:300
  198.9 4.3 %all-to-all-start.3 = ((bf16[16,32,1024]{2,1,0:T(8,128)(2,1)}), bf16[16,32,1024]{2,1,0:T(8,128)(2,1)}, u32[]{:S(2)}, u32[]{:S(2)}) async-start(bf16[16,32,1024]{2,1,0:T(8,128)(2,1)} %bitcast.32), calls=%async_computation.3 | async-start | bytes 2097152 | tf_op jit(solution)/shard_map/all_to_all | solution.py:486
  203.3 9.8 %collective-permute-done.14 = bf16[2,8,24,1024]{3,2,1,0:T(8,128)(2,1)} collective-permute-done((bf16[2,8,24,1024]{3,2,1,0:T(8,128)(2,1)}, bf16[2,8,24,1024]{3,2,1,0:T(8,128)(2,1)}, u32[]{:S(2)}, u32[]{:S(2)}) %collective-permute-start.14) | collective-permute-done | bytes 786464 | tf_op jit(solution)/shard_map/ppermute | solution.py:327
  213.1 1.4 fusion.10
  214.6 3.2 %collective-permute-start.20 = (bf16[8,24,1024]{2,1,0:T(8,128)(2,1)S(1)}, bf16[8,24,1024]{2,1,0:T(8,128)(2,1)S(1)}, u32[]{:S(2)}, u32[]{:S(2)}) collective-permute-start(bf16[8,24,1024]{2,1,0:T(8,128)(2,1)S(1)} %dynamic-slice_bitcast_fusion.2), channel_id=1, source_target_pairs={{0,3},{3,0},{1,2},{2,1},{4,7},{7,4},{5,6},{6,5},{8,11},{11,8},{9,1... | collective-permute-start | bytes 1179656 | tf_op jit(solution)/shard_map/ppermute | solution.py:327
  217.8 1.4 fusion.9
  219.6 7.2 %collective-permute-done.20 = bf16[8,24,1024]{2,1,0:T(8,128)(2,1)S(1)} collective-permute-done((bf16[8,24,1024]{2,1,0:T(8,128)(2,1)S(1)}, bf16[8,24,1024]{2,1,0:T(8,128)(2,1)S(1)}, u32[]{:S(2)}, u32[]{:S(2)}) %collective-permute-start.20) | collective-permute-done | bytes 393248 | tf_op jit(solution)/shard_map/ppermute | solution.py:327
  227.0 2.9 %collective-permute-done.21 = bf16[8,24,1024]{2,1,0:T(8,128)(2,1)S(1)} collective-permute-done((bf16[8,24,1024]{2,1,0:T(8,128)(2,1)S(1)}, bf16[8,24,1024]{2,1,0:T(8,128)(2,1)S(1)}, u32[]{:S(2)}, u32[]{:S(2)}) %collective-permute-start.21) | collective-permute-done | bytes 393248 | tf_op jit(solution)/shard_map/ppermute | solution.py:327
  230.0 1.0 pad_maximum_fusion
  231.0 3.6 %all-to-all-start.4 = ((bf16[16,24,1024]{2,1,0:T(8,128)(2,1)}), bf16[16,24,1024]{2,1,0:T(8,128)(2,1)S(1)}, u32[]{:S(2)}, u32[]{:S(2)}) async-start(bf16[16,24,1024]{2,1,0:T(8,128)(2,1)} %pad_maximum_fusion), calls=%async_computation.4 | async-start | bytes 1572864 | tf_op jit(solution)/shard_map/all_to_all | solution.py:494
  234.6 1.4 convert_reduce_fusion
  236.4 1.5 collective-permute-start.18
  237.9 1.5 collective-permute-start.19
  239.4 2.9 %collective-permute-done.17 = f32[2,8,1024]{2,1,0:T(8,128)S(1)} collective-permute-done((f32[2,8,1024]{2,1,0:T(8,128)S(1)}, f32[2,8,1024]{2,1,0:T(8,128)S(1)}, u32[]{:S(2)}, u32[]{:S(2)}) %collective-permute-start.17) | collective-permute-done | bytes 65568 | tf_op jit(solution)/shard_map/ppermute | solution.py:26
  242.3 0.9 collective-permute-done.19
  243.2 4.6 %all-to-all-done.4 = bf16[16,24,1024]{2,1,0:T(8,128)(2,1)S(1)} async-done(((bf16[16,24,1024]{2,1,0:T(8,128)(2,1)}), bf16[16,24,1024]{2,1,0:T(8,128)(2,1)S(1)}, u32[]{:S(2)}, u32[]{:S(2)}) %all-to-all-start.4) | async-done | bytes 786464 | tf_op jit(solution)/shard_map/all_to_all | solution.py:494
  248.1 0.7 fusion.44
  249.4 0.6 slice_multiply_fusion.1
  250.0 0.6 slice_multiply_fusion
  252.7 0.6 maximum_multiply_fusion
  (102 shorter events, 4.7 us)
Async XLA Ops:
  0.6 59.5 %copy-start = (f32[8,768]{1,0:T(8,128)S(1)}, f32[8,768]{1,0:T(8,128)}, u32[]{:S(2)}) copy-start(f32[8,768]{1,0:T(8,128)} %param.11) | copy-start | bytes 73732
  0.7 1.2 copy-start.2
  1.9 1.2 copy-start.4
  3.1 1.0 copy-start.6
  4.1 3.4 %copy-start.15 = (bf16[4,256,1024]{2,1,0:T(8,128)(2,1)S(1)}, bf16[4,256,1024]{2,1,0:T(8,128)(2,1)}, u32[]{:S(2)}) copy-start(bf16[4,256,1024]{2,1,0:T(8,128)(2,1)} %param.7) | copy-start | bytes 6291460
  4.2 4.9 %copy-start.8 = (bf16[1216,256]{1,0:T(8,128)(2,1)}, bf16[1216,256]{1,0:T(8,128)(2,1)S(1)}, u32[]{:S(2)}) copy-start(bf16[1216,256]{1,0:T(8,128)(2,1)S(1)} %get-tuple-element.73.refs_2_) | copy-start | bytes 1867780
  4.2 4.9 %copy-start.10 = (bf16[1216,256]{1,0:T(8,128)(2,1)}, bf16[1216,256]{1,0:T(8,128)(2,1)S(1)}, u32[]{:S(2)}) copy-start(bf16[1216,256]{1,0:T(8,128)(2,1)S(1)} %get-tuple-element.74.refs_3_) | copy-start | bytes 1867780
  4.2 17.8 %collective-permute-start = (bf16[1216,256]{1,0:T(8,128)(2,1)S(1)}, bf16[1216,256]{1,0:T(8,128)(2,1)}, u32[]{:S(2)}, u32[]{:S(2)}) collective-permute-start(bf16[1216,256]{1,0:T(8,128)(2,1)S(1)} %get-tuple-element.73.refs_2_), channel_id=1, source_target_pairs={{0,1},{1,2},{2,3},{3,0},{4,5},{5,6},{6,7},{7,4},{8,9},{9,10},{10,1... | collective-permute-start | bytes 1867784 | tf_op jit(solution)/shard_map/ppermute | solution.py:26
  5.9 16.1 %collective-permute-start.1 = (bf16[1216,256]{1,0:T(8,128)(2,1)S(1)}, bf16[1216,256]{1,0:T(8,128)(2,1)}, u32[]{:S(2)}, u32[]{:S(2)}) collective-permute-start(bf16[1216,256]{1,0:T(8,128)(2,1)S(1)} %get-tuple-element.74.refs_3_), channel_id=1, source_target_pairs={{0,3},{1,0},{2,1},{3,2},{4,7},{5,4},{6,5},{7,6},{8,11},{9,8},{10,9... | collective-permute-start | bytes 1867784 | tf_op jit(solution)/shard_map/ppermute | solution.py:26
  7.5 1.6 copy-start.3
  7.5 2.3 copy-start.5
  7.5 2.4 copy-start.7
  10.0 0.8 copy-start.12
  10.8 0.8 copy-start.13
  12.9 9.1 %copy-start.11 = (bf16[1216,256]{1,0:T(8,128)(2,1)S(1)}, bf16[1216,256]{1,0:T(8,128)(2,1)}, u32[]{:S(2)}) copy-start(bf16[1216,256]{1,0:T(8,128)(2,1)} %copy-done.10) | copy-start | bytes 1867780
  12.9 10.2 %copy-start.9 = (bf16[1216,256]{1,0:T(8,128)(2,1)S(1)}, bf16[1216,256]{1,0:T(8,128)(2,1)}, u32[]{:S(2)}) copy-start(bf16[1216,256]{1,0:T(8,128)(2,1)} %copy-done.8) | copy-start | bytes 1867780
  22.0 16.7 %collective-permute-start.3 = (bf16[1216,256]{1,0:T(8,128)(2,1)S(1)}, bf16[1216,256]{1,0:T(8,128)(2,1)S(1)}, u32[]{:S(2)}, u32[]{:S(2)}) collective-permute-start(bf16[1216,256]{1,0:T(8,128)(2,1)S(1)} %copy-done.11), channel_id=1, source_target_pairs={{0,1},{1,2},{2,3},{3,0},{4,5},{5,6},{6,7},{7,4},{8,9},{9,10},{10,1... | collective-permute-start | bytes 1867784 | tf_op jit(solution)/shard_map/ppermute | solution.py:26
  23.1 15.6 %collective-permute-start.2 = (bf16[1216,256]{1,0:T(8,128)(2,1)S(1)}, bf16[1216,256]{1,0:T(8,128)(2,1)S(1)}, u32[]{:S(2)}, u32[]{:S(2)}) collective-permute-start(bf16[1216,256]{1,0:T(8,128)(2,1)S(1)} %copy-done.9), channel_id=1, source_target_pairs={{0,3},{1,0},{2,1},{3,2},{4,7},{5,4},{6,5},{7,6},{8,11},{9,8},{10,9... | collective-permute-start | bytes 1867784 | tf_op jit(solution)/shard_map/ppermute | solution.py:26
  25.3 13.4 %collective-permute-start.4 = (bf16[1216,256]{1,0:T(8,128)(2,1)}, bf16[1216,256]{1,0:T(8,128)(2,1)S(1)}, u32[]{:S(2)}, u32[]{:S(2)}) collective-permute-start(bf16[1216,256]{1,0:T(8,128)(2,1)} %collective-permute-done.refs_2_), channel_id=1, source_target_pairs={{0,4},{4,0},{1,5},{5,1},{2,6},{6,2},{3,7},{7,3},{8,12},{12,8},{9,1... | collective-permute-start | bytes 1867784 | tf_op jit(solution)/shard_map/ppermute | solution.py:26
  25.3 13.4 %collective-permute-start.5 = (bf16[1216,256]{1,0:T(8,128)(2,1)}, bf16[1216,256]{1,0:T(8,128)(2,1)S(1)}, u32[]{:S(2)}, u32[]{:S(2)}) collective-permute-start(bf16[1216,256]{1,0:T(8,128)(2,1)} %collective-permute-done.1.refs_7_), channel_id=1, source_target_pairs={{0,4},{4,0},{1,5},{5,1},{2,6},{6,2},{3,7},{7,3},{8,12},{12,8},{9,1... | collective-permute-start | bytes 1867784 | tf_op jit(solution)/shard_map/ppermute | solution.py:26
  38.8 4.5 %copy-start.20 = (bf16[1216,256]{1,0:T(8,128)(2,1)}, bf16[1216,256]{1,0:T(8,128)(2,1)S(1)}, u32[]{:S(2)}) copy-start(bf16[1216,256]{1,0:T(8,128)(2,1)S(1)} %collective-permute-done.3.refs_3_) | copy-start | bytes 1867780
  38.8 4.5 %copy-start.21 = (bf16[1216,256]{1,0:T(8,128)(2,1)}, bf16[1216,256]{1,0:T(8,128)(2,1)S(1)}, u32[]{:S(2)}) copy-start(bf16[1216,256]{1,0:T(8,128)(2,1)S(1)} %collective-permute-done.2.refs_6_) | copy-start | bytes 1867780
  38.8 4.5 %copy-start.22 = (bf16[1216,256]{1,0:T(8,128)(2,1)}, bf16[1216,256]{1,0:T(8,128)(2,1)S(1)}, u32[]{:S(2)}) copy-start(bf16[1216,256]{1,0:T(8,128)(2,1)S(1)} %collective-permute-done.4.refs_4_) | copy-start | bytes 1867780
  38.8 1.0 copy-start.23
  38.8 4.5 %collective-permute-start.8 = (bf16[1216,256]{1,0:T(8,128)(2,1)S(1)}, bf16[1216,256]{1,0:T(8,128)(2,1)}, u32[]{:S(2)}, u32[]{:S(2)}) collective-permute-start(bf16[1216,256]{1,0:T(8,128)(2,1)S(1)} %collective-permute-done.3.refs_3_), channel_id=1, source_target_pairs={{0,4},{4,0},{1,5},{5,1},{2,6},{6,2},{3,7},{7,3},{8,12},{12,8},{9,1... | collective-permute-start | bytes 1867784 | tf_op jit(solution)/shard_map/ppermute | solution.py:26
  38.9 4.4 %collective-permute-start.9 = (bf16[1216,256]{1,0:T(8,128)(2,1)S(1)}, bf16[1216,256]{1,0:T(8,128)(2,1)}, u32[]{:S(2)}, u32[]{:S(2)}) collective-permute-start(bf16[1216,256]{1,0:T(8,128)(2,1)S(1)} %collective-permute-done.2.refs_6_), channel_id=1, source_target_pairs={{0,4},{4,0},{1,5},{5,1},{2,6},{6,2},{3,7},{7,3},{8,12},{12,8},{9,1... | collective-permute-start | bytes 1867784 | tf_op jit(solution)/shard_map/ppermute | solution.py:26
  39.7 19.8 %collective-permute-start.7 = (bf16[1216,256]{1,0:T(8,128)(2,1)}, bf16[1216,256]{1,0:T(8,128)(2,1)S(1)}, u32[]{:S(2)}, u32[]{:S(2)}) collective-permute-start(bf16[1216,256]{1,0:T(8,128)(2,1)} %collective-permute-done.1.refs_7_), channel_id=1, source_target_pairs={{0,3},{1,0},{2,1},{3,2},{4,7},{5,4},{6,5},{7,6},{8,11},{9,8},{10,9... | collective-permute-start | bytes 1867784 | tf_op jit(solution)/shard_map/ppermute | solution.py:26
  42.6 16.9 %collective-permute-start.6 = (bf16[1216,256]{1,0:T(8,128)(2,1)}, bf16[1216,256]{1,0:T(8,128)(2,1)S(1)}, u32[]{:S(2)}, u32[]{:S(2)}) collective-permute-start(bf16[1216,256]{1,0:T(8,128)(2,1)} %collective-permute-done.refs_2_), channel_id=1, source_target_pairs={{0,1},{1,2},{2,3},{3,0},{4,5},{5,6},{6,7},{7,4},{8,9},{9,10},{10,1... | collective-permute-start | bytes 1867784 | tf_op jit(solution)/shard_map/ppermute | solution.py:26
  43.3 16.8 %copy-start.26 = (s32[8]{0:T(128)S(1)}, s32[8]{0:T(128)}, u32[]{:S(2)}) copy-start(s32[8]{0:T(128)} %param.12) | copy-start | bytes 100
  59.5 3.1 %copy-start.18 = (bf16[1216,256]{1,0:T(8,128)(2,1)}, bf16[1216,256]{1,0:T(8,128)(2,1)S(1)}, u32[]{:S(2)}) copy-start(bf16[1216,256]{1,0:T(8,128)(2,1)S(1)} %collective-permute-done.7.refs_3_) | copy-start | bytes 1867780
  59.5 3.0 %copy-start.19 = (bf16[1216,256]{1,0:T(8,128)(2,1)}, bf16[1216,256]{1,0:T(8,128)(2,1)S(1)}, u32[]{:S(2)}) copy-start(bf16[1216,256]{1,0:T(8,128)(2,1)S(1)} %collective-permute-done.6.refs_2_) | copy-start | bytes 1867780
  59.5 2.1 collective-permute-start.10
  59.6 2.9 %collective-permute-start.11 = (bf16[1216,256]{1,0:T(8,128)(2,1)S(1)}, bf16[1216,256]{1,0:T(8,128)(2,1)S(1)}, u32[]{:S(2)}, u32[]{:S(2)}) collective-permute-start(bf16[1216,256]{1,0:T(8,128)(2,1)S(1)} %collective-permute-done.7.refs_3_), channel_id=1, source_target_pairs={{0,4},{4,0},{1,5},{5,1},{2,6},{6,2},{3,7},{7,3},{8,12},{12,8},{9,1... | collective-permute-start | bytes 1867784 | tf_op jit(solution)/shard_map/ppermute | solution.py:26
  61.7 0.9 copy-start.24
  62.6 0.8 copy-start.25
  106.4 0.9 copy-start.27
  112.7 27.4 %copy-start.28 = (bf16[768,1024]{1,0:T(8,128)(2,1)S(1)}, bf16[768,1024]{1,0:T(8,128)(2,1)}, u32[]{:S(2)}) copy-start(bf16[768,1024]{1,0:T(8,128)(2,1)} %get-tuple-element.100) | copy-start | bytes 4718596
  112.8 27.4 %all-to-all-start.1 = ((bf16[32,32,768]{2,1,0:T(8,128)(2,1)}), bf16[32,32,768]{2,1,0:T(8,128)(2,1)S(1)}, u32[]{:S(2)}, u32[]{:S(2)}) async-start(bf16[32,32,768]{2,1,0:T(8,128)(2,1)} %bitcast.18), calls=%async_computation.1 | async-start | bytes 3145728 | tf_op jit(solution)/shard_map/all_to_all | solution.py:462
  140.1 3.1 %copy-start.16 = (bf16[32,32,768]{2,1,0:T(8,128)(2,1)}, bf16[32,32,768]{2,1,0:T(8,128)(2,1)S(1)}, u32[]{:S(2)}) copy-start(bf16[32,32,768]{2,1,0:T(8,128)(2,1)S(1)} %all-to-all-done.1) | copy-start | bytes 4718596
  155.3 10.3 %collective-permute-start.12 = (bf16[4,384,1024]{2,1,0:T(8,128)(2,1)}, bf16[4,384,1024]{2,1,0:T(8,128)(2,1)S(1)}, u32[]{:S(2)}, u32[]{:S(2)}) collective-permute-start(bf16[4,384,1024]{2,1,0:T(8,128)(2,1)} %get-tuple-element.103), channel_id=1, source_target_pairs={{0,4},{4,0},{1,5},{5,1},{2,6},{6,2},{3,7},{7,3},{8,12},{12,8},{9,1... | collective-permute-start | bytes 9437192 | tf_op jit(solution)/shard_map/ppermute | solution.py:26
  155.3 10.2 %copy-start.14 = (bf16[4,384,1024]{2,1,0:T(8,128)(2,1)S(1)}, bf16[4,384,1024]{2,1,0:T(8,128)(2,1)}, u32[]{:S(2)}) copy-start(bf16[4,384,1024]{2,1,0:T(8,128)(2,1)} %get-tuple-element.110) | copy-start | bytes 9437188
  165.1 4.4 %collective-permute-start.13 = (bf16[1,512,1024]{2,1,0:T(8,128)(2,1)}, bf16[1,512,1024]{2,1,0:T(8,128)(2,1)S(1)}, u32[]{:S(2)}, u32[]{:S(2)}) collective-permute-start(bf16[1,512,1024]{2,1,0:T(8,128)(2,1)} %get-tuple-element.109), channel_id=1, source_target_pairs={{0,4},{4,0},{1,5},{5,1},{2,6},{6,2},{3,7},{7,3},{8,12},{12,8},{9,1... | collective-permute-start | bytes 3145736 | tf_op jit(solution)/shard_map/ppermute | solution.py:26
  167.6 1.9 copy-start.17
  170.9 21.9 %all-to-all-start.2 = ((bf16[16,32,1024]{2,1,0:T(8,128)(2,1)}), bf16[16,32,1024]{2,1,0:T(8,128)(2,1)S(1)}, u32[]{:S(2)}, u32[]{:S(2)}) async-start(bf16[16,32,1024]{2,1,0:T(8,128)(2,1)} %bitcast.28), calls=%async_computation.2 | async-start | bytes 2097152 | tf_op jit(solution)/shard_map/all_to_all | solution.py:482
  192.8 3.2 %collective-permute-start.15 = (bf16[1,512,1024]{2,1,0:T(8,128)(2,1)}, bf16[1,512,1024]{2,1,0:T(8,128)(2,1)}, u32[]{:S(2)}, u32[]{:S(2)}) collective-permute-start(bf16[1,512,1024]{2,1,0:T(8,128)(2,1)} %get-tuple-element.115), channel_id=1, source_target_pairs={{0,4},{4,0},{1,5},{5,1},{2,6},{6,2},{3,7},{7,3},{8,12},{12,8},{9,1... | collective-permute-start | bytes 3145736 | tf_op jit(solution)/shard_map/ppermute | solution.py:26
  192.8 20.3 %collective-permute-start.14 = (bf16[2,8,24,1024]{3,2,1,0:T(8,128)(2,1)}, bf16[2,8,24,1024]{3,2,1,0:T(8,128)(2,1)}, u32[]{:S(2)}, u32[]{:S(2)}) collective-permute-start(bf16[2,8,24,1024]{3,2,1,0:T(8,128)(2,1)} %bitcast.109), channel_id=1, source_target_pairs={{0,1},{1,0},{2,3},{3,2},{4,5},{5,4},{6,7},{7,6},{8,9},{9,8},{10,11... | collective-permute-start | bytes 2359304 | tf_op jit(solution)/shard_map/ppermute | solution.py:327
  192.8 25.0 %collective-permute-start.16 = (bf16[2,8,24,1024]{3,2,0,1:T(8,128)(2,1)}, bf16[2,8,24,1024]{3,2,0,1:T(8,128)(2,1)}, u32[]{:S(2)}, u32[]{:S(2)}) collective-permute-start(bf16[2,8,24,1024]{3,2,0,1:T(8,128)(2,1)} %dynamic-slice_bitcast_fusion), channel_id=1, source_target_pairs={{0,3},{3,0},{1,2},{2,1},{4,7},{7,4},{5,6},{6,5},{8,11},{11,8},{9,1... | collective-permute-start | bytes 2359304 | tf_op jit(solution)/shard_map/ppermute | solution.py:327
  198.9 32.1 %all-to-all-start.3 = ((bf16[16,32,1024]{2,1,0:T(8,128)(2,1)}), bf16[16,32,1024]{2,1,0:T(8,128)(2,1)}, u32[]{:S(2)}, u32[]{:S(2)}) async-start(bf16[16,32,1024]{2,1,0:T(8,128)(2,1)} %bitcast.32), calls=%async_computation.3 | async-start | bytes 2097152 | tf_op jit(solution)/shard_map/all_to_all | solution.py:486
  214.6 12.3 %collective-permute-start.20 = (bf16[8,24,1024]{2,1,0:T(8,128)(2,1)S(1)}, bf16[8,24,1024]{2,1,0:T(8,128)(2,1)S(1)}, u32[]{:S(2)}, u32[]{:S(2)}) collective-permute-start(bf16[8,24,1024]{2,1,0:T(8,128)(2,1)S(1)} %dynamic-slice_bitcast_fusion.2), channel_id=1, source_target_pairs={{0,3},{3,0},{1,2},{2,1},{4,7},{7,4},{5,6},{6,5},{8,11},{11,8},{9,1... | collective-permute-start | bytes 1179656 | tf_op jit(solution)/shard_map/ppermute | solution.py:327
  219.3 10.5 %collective-permute-start.21 = (bf16[8,24,1024]{2,1,0:T(8,128)(2,1)S(1)}, bf16[8,24,1024]{2,1,0:T(8,128)(2,1)S(1)}, u32[]{:S(2)}, u32[]{:S(2)}) collective-permute-start(bf16[8,24,1024]{2,1,0:T(8,128)(2,1)S(1)} %dynamic-slice_bitcast_fusion.1), channel_id=1, source_target_pairs={{0,1},{1,0},{2,3},{3,2},{4,5},{5,4},{6,7},{7,6},{8,9},{9,8},{10,11... | collective-permute-start | bytes 1179656 | tf_op jit(solution)/shard_map/ppermute | solution.py:327
  231.0 16.9 %all-to-all-start.4 = ((bf16[16,24,1024]{2,1,0:T(8,128)(2,1)}), bf16[16,24,1024]{2,1,0:T(8,128)(2,1)S(1)}, u32[]{:S(2)}, u32[]{:S(2)}) async-start(bf16[16,24,1024]{2,1,0:T(8,128)(2,1)} %pad_maximum_fusion), calls=%async_computation.4 | async-start | bytes 1572864 | tf_op jit(solution)/shard_map/all_to_all | solution.py:494
  234.6 18.7 %copy-start.1 = (f32[8,768]{1,0:T(8,128)S(1)}, f32[8,768]{1,0:T(8,128)}, u32[]{:S(2)}) copy-start(f32[8,768]{1,0:T(8,128)} %param.11) | copy-start | bytes 73732
  236.1 6.2 %collective-permute-start.17 = (f32[2,8,1024]{2,1,0:T(8,128)S(1)}, f32[2,8,1024]{2,1,0:T(8,128)S(1)}, u32[]{:S(2)}, u32[]{:S(2)}) collective-permute-start(f32[2,8,1024]{2,1,0:T(8,128)S(1)} %get-tuple-element.134), channel_id=1, source_target_pairs={{0,1},{1,2},{2,3},{3,0},{4,5},{5,6},{6,7},{7,4},{8,9},{9,10},{10,1... | collective-permute-start | bytes 196616 | tf_op jit(solution)/shard_map/ppermute | solution.py:26
  236.4 5.9 %collective-permute-start.18 = (f32[2,8,1024]{2,1,0:T(8,128)S(1)}, f32[2,8,1024]{2,1,0:T(8,128)S(1)}, u32[]{:S(2)}, u32[]{:S(2)}) collective-permute-start(f32[2,8,1024]{2,1,0:T(8,128)S(1)} %get-tuple-element.135), channel_id=1, source_target_pairs={{0,2},{1,3},{2,0},{3,1},{4,6},{5,7},{6,4},{7,5},{8,10},{9,11},{10,... | collective-permute-start | bytes 196616 | tf_op jit(solution)/shard_map/ppermute | solution.py:26
  237.9 5.3 %collective-permute-start.19 = (f32[2,8,1024]{2,1,0:T(8,128)S(1)}, f32[2,8,1024]{2,1,0:T(8,128)S(1)}, u32[]{:S(2)}, u32[]{:S(2)}) collective-permute-start(f32[2,8,1024]{2,1,0:T(8,128)S(1)} %get-tuple-element.136), channel_id=1, source_target_pairs={{0,3},{1,0},{2,1},{3,2},{4,7},{5,4},{6,5},{7,6},{8,11},{9,8},{10,9... | collective-permute-start | bytes 196616 | tf_op jit(solution)/shard_map/ppermute | solution.py:26

commit v10 on v8

--- a/solution.py
+++ b/solution.py
@@ -261,12 +261,15 @@
     )(place, hidden, resid_grad, residual, grad_rows, scalars)
 
 
-def late_kernel(place, resid_grad, second, slope, tokens, keep, send):
+def late_kernel(gray, place, resid_grad, second, slope, tokens, keep, send):
     hidden_grad = dot(resid_grad[...], second[...], ((1,), (1,)))
     preact_grad = (slope[...].astype(F32) * hidden_grad).astype(BF16)
     first = dot(tokens[...], preact_grad, ((0,), (0,)))
     cols = first.shape[1]
-    store_halves(place[1], first.reshape(16, 2, -1, cols), keep, send)
+    parts = first.reshape(16, 2, RING, -1, cols)
+    if gray:
+        parts = jnp.stack([parts[:, :, i] for i in (0, 3, 1, 2)], 2)
+    store_halves(place[1], parts.reshape(16, 2, -1, cols), keep, send)
 
 
 def late_grads(place, part, resid_grad, second, slope, tokens):
@@ -275,7 +278,7 @@
     steps = width // tile
     out = pl.BlockSpec((1, width // 2, tile), lambda j, s: (0, 0, j))
     return pl.pallas_call(
-        late_kernel,
+        functools.partial(late_kernel, part == 1),
         grid_spec=pltpu.PrefetchScalarGridSpec(
             num_scalar_prefetch=1,
             grid=(steps,),
@@ -481,26 +484,32 @@
     a = add(after(late[0], *early_sent), a_in).reshape(16, RING * n, width)
     a_all = lax.all_to_all(a, group, 0, 0, tiled=True)
     late = late_grads(at, 1, after(resid_grad, a), second, slope, tokens)
-    b_in = shift(after(late[1], a_all, *early_in), "c", 1)
+    b_in = shift(after(late[1], *early_in), "c", 1)
     early = [kept_plus(x, v, s[0]) for x, v, s in zip(early, early_in, steps)]
     early_sent = [outgoing(x, s[1]) for x, s in zip(early, steps)]
     early_in = [sent_along(x, s[1]) for x, s in zip(early_sent, steps)]
-    b = add(after(late[0], *early_sent), b_in).reshape(16, RING * n, width)
-    b_all = lax.all_to_all(b, group, 0, 0, tiled=True)
-    a = jnp.sum(after(a_all, b).astype(F32), 0)
-    early = [kept_plus(x, after(v, b), s[1]) for x, v, s in zip(early, early_in, steps)]
-    early = jnp.concatenate(early)
-    b = jnp.sum(b_all.astype(F32), 0)
-    early = lax.all_to_all(after(early, b_all), group, 0, 0, tiled=True)
-    first = summed_over_y(jnp.stack([a, b]).reshape(2, RING, n, width))
+    b = add(after(late[0], *early_sent), b_in).reshape(2, -1, width)
+    b = [by_ring(v, n) for v in (b[0], b[1])]
+    b_sent = [outgoing(x, s[0]) for x, s in zip(b, steps)]
+    b_in = [sent_along(x, s[0]) for x, s in zip(b_sent, steps)]
+    a = jnp.sum(after(a_all, *b_sent).astype(F32), 0)
+    first = summed_over_y(a.reshape(1, RING, n, width))
+    early = [kept_plus(x, after(v, *b_sent), s[1]) for x, v, s in zip(early, early_in, steps)]
+    b = [kept_plus(x, after(v, *early), s[0]) for x, v, s in zip(b, b_in, steps)]
+    b_sent = [outgoing(x, s[1]) for x, s in zip(b, steps)]
+    b_in = [sent_along(x, s[1]) for x, s in zip(b_sent, steps)]
+    b = [kept_plus(x, v, s[1]) for x, v, s in zip(b, b_in, steps)]
+    early = jnp.concatenate([jnp.concatenate(early), jnp.concatenate(b)], 1)
+    early = lax.all_to_all(early, group, 0, 0, tiled=True)
     early = jnp.sum(early.astype(F32), 0)
+    early, b = early[:-n], early[-n:]
     n_second = shard * RING // 128
     ride = jnp.sum(early[n_second:, out_width:], 1)
     score_total = ride[0] + ride[1] + ride[2]
     valid_total = jnp.maximum(ride[3], 1.0)
     scale = 1.0 / valid_total
     return (
-        jnp.concatenate([first[0], first[1]], 1) * scale,
+        jnp.concatenate([first[0], b], 1) * scale,
         early[:n_second] * scale,
         early[n_second:, :out_width] * scale,
         score_total / valid_total,

time: 255 us -> 252 us (0.988)
  other arithmetic: 17.8 us -> 14.9 us
    ppermute x4 -> x8, waiting for transfers between devices: 11 us -> 21.9 us  [sent_along(): return lax.ppermute(x, step[1], step[0])]
    all_to_all x2 -> x1, waiting for transfers between devices: 18 us -> 8.05 us  [per_device(): early = lax.all_to_all(early, group, 0, 0, tiled=True)]
    ppermute x4 -> x8, starting transfers between devices: 5.71 us -> 9.8 us  [sent_along(): return lax.ppermute(x, step[1], step[0])]
    all_to_all x2 -> x1, starting transfers between devices: 10.4 us -> 6.87 us  [per_device(): early = lax.all_to_all(early, group, 0, 0, tiled=True)]
    convert_element_type x7 -> x11, other arithmetic: 9.68 us -> 6.78 us  [add(): return (a.astype(F32) + b.astype(F32)).astype(BF16)]
    unnamed x67 -> x66, local copies, waits for them, and re-layouts: 8.97 us -> 9.48 us
  transfers between devices with their start and end apart: 26 -> 29, of which waited for: 12 -> 17; matrix products, arithmetic and copies ran while one was open for 7% -> 6% of each run, Pallas kernels for 18% -> 18%
where the time goes in v10:
time: 252 us; the launch traced here: 251 us
  waiting for transfers between devices  69.6 us (28%)
  Pallas kernels  68 us (27%)
  starting transfers between devices  39.6 us (16%)
  blocking collectives  30.5 us (12%)
  local copies, waits for them, and re-layouts  16.3 us (6%)
  other arithmetic  14.9 us (6%)
  matrix products  6.83 us (3%)
  between operations  5.05 us (2%)
    pallas_call x3, Pallas kernels, forward_part(): pl.pallas_call(functools.partial(forward_kernel, groups, first_call, last...  36.5 us
    all_to_all x1, blocking collectives, per_device(): gathered = lax.all_to_all(forecast, group, 0, 0, tiled=True)  30.5 us
    ppermute x8, waiting for transfers between devices, sent_along(): return lax.ppermute(x, step[1], step[0])  21.9 us
    all_to_all x1, waiting for transfers between devices, per_device(): lax.all_to_all(grad_raw.reshape(32, members * own, out_width), group, 0,...  21.2 us
    pallas_call x2, Pallas kernels, late_grads(): pl.pallas_call(functools.partial(late_kernel, part == 1), grid_spec=pltpu...  19.3 us
    ppermute x18, waiting for transfers between devices, shift(): return lax.ppermute(x, axis, [(i, (i + by) % size) for i in range(size)])  18.5 us
    ppermute x18, starting transfers between devices, shift(): return lax.ppermute(x, axis, [(i, (i + by) % size) for i in range(size)])  15.1 us
    pallas_call x1, Pallas kernels, early_grads(): pl.pallas_call(early_kernel, grid_spec=pltpu.PrefetchScalarGridSpec(num_s...  12 us
  transfers between devices with their start and end apart: 29, of which 17 were waited for; matrix products, arithmetic and copies ran while one was open for 6% of the time, Pallas kernels for 18%

profile of v10, /device:TPU:0, one launch (start us, length us, event | category | flops | bytes accessed | tf_op | source)
XLA Modules:
  0.0 250.8 jit_solution(18328595197304176441)
XLA Ops:
  0.7 1.2 copy-done.2
  1.9 1.2 copy-done.4
  3.1 1.0 copy-done.6
  4.2 1.7 collective-permute-start
  5.9 1.6 collective-permute-start.1
  7.5 1.6 copy.26
  9.1 0.7 copy-done.5
  10.0 0.8 copy-done.12
  10.8 0.8 copy-done.13
  12.9 9.1 %forward_part.3 = (bf16[1024,2048]{1,0:T(8,128)(2,1)}, bf16[1024,2048]{1,0:T(8,128)(2,1)}, bf16[2048,1024]{1,0:T(8,128)(2,1)}, bf16[768,1024]{1,0:T(8,128)(2,1)}, f32[1024,1024]{1,0:T(8,128)}) custom-call(s32[4]{0:T(128)} %pad_add_fusion.refs_0_.place, bf16[1024,1024]{1,0:T(8,128)(2,1)} %bitcast.121, bf16[1216,256]{1,0:T(8,128)(2,1)} %copy-done.8, ...), custom_call_target="tpu_custom_call" | custom-call | flops 2147483648 | bytes 12582912 | tf_op jit(solution)/shard_map/forward_part/pallas_call | solution.py:166
  22.0 1.2 collective-permute-start.3
  23.1 2.1 collective-permute-start.2
  25.8 12.9 %collective-permute-done.3.refs_3_ = bf16[1216,256]{1,0:T(8,128)(2,1)S(1)} collective-permute-done((bf16[1216,256]{1,0:T(8,128)(2,1)S(1)}, bf16[1216,256]{1,0:T(8,128)(2,1)S(1)}, u32[]{:S(2)}, u32[]{:S(2)}) %collective-permute-start.3) | collective-permute-done | bytes 622624 | tf_op jit(solution)/shard_map/ppermute | solution.py:26
  38.8 0.8 copy-done.26
  39.6 2.9 %collective-permute-start.7 = (bf16[1216,256]{1,0:T(8,128)(2,1)}, bf16[1216,256]{1,0:T(8,128)(2,1)S(1)}, u32[]{:S(2)}, u32[]{:S(2)}) collective-permute-start(bf16[1216,256]{1,0:T(8,128)(2,1)} %collective-permute-done.1.refs_7_), channel_id=1, source_target_pairs={{0,3},{1,0},{2,1},{3,2},{4,7},{5,4},{6,5},{7,6},{8,11},{9,8},{10,9... | collective-permute-start | bytes 1867784 | tf_op jit(solution)/shard_map/ppermute | solution.py:26
  42.6 0.7 stack.59.refs_0_
  43.3 16.3 %forward_part.4 = (bf16[1024,2048]{1,0:T(8,128)(2,1)}, bf16[1024,2048]{1,0:T(8,128)(2,1)}, bf16[2048,1024]{1,0:T(8,128)(2,1)}, bf16[768,1024]{1,0:T(8,128)(2,1)}, f32[1024,1024]{1,0:T(8,128)}) custom-call(s32[5]{0:T(128)} %stack.59.refs_0_, ...), custom_call_target="tpu_custom_call", output_to_operand_aliasing={{0}: (11, {}), {1}: (12, {}), {2}: (13, {}), {3}: (14, {})} | custom-call | flops 4294967296 | bytes 12582912 | tf_op jit(solution)/shard_map/forward_part/pallas_call | solution.py:166
  61.4 0.9 collective-permute-done.10.refs_4_
  62.2 0.9 collective-permute-done.11.refs_5_
  63.1 0.8 copy-done.28
  63.9 11.1 %forward_part.5 = (bf16[1024,2048]{1,0:T(8,128)(2,1)}, bf16[1024,2048]{1,0:T(8,128)(2,1)}, bf16[2048,1024]{1,0:T(8,128)(2,1)}, bf16[768,1024]{1,0:T(8,128)(2,1)}...) custom-call(s32[4]{0:T(128)} %get-tuple-element.132.refs_0_, ...), custom_call_target="tpu_custom_call", output_to_operand_aliasing={{0}: (7, {}), {1}: (8, {}), {2}: (9, {})} | custom-call | flops 2147483648 | bytes 12582912 | tf_op jit(solution)/shard_map/forward_part/pallas_call | solution.py:166
  75.1 30.5 %all_to_all.20 = bf16[32,32,768]{2,1,0:T(8,128)(2,1)S(1)} all-to-all(bf16[32,32,768]{2,1,0:T(8,128)(2,1)} %bitcast.138), channel_id=1, replica_groups=mesh['x'=4,'z'=4,'c'=2,'y'=4] {'x','z','c'}, dimensions={0} | all-to-all | bytes 3145728 | tf_op jit(solution)/shard_map/all_to_all | solution.py:462
  105.8 0.8 fusion.6
  106.9 0.9 fusion.37
  107.9 0.6 multiply_reduce_fusion
  108.5 2.8 %fusion.8 = bf16[128,8,768]{2,0,1:T(8,128)(2,1)S(1)} fusion(f32[128,8]{0,1:T(8,128)S(1)} %bitcast.144, f32[128,8]{0,1:T(8,128)S(1)} %copy.29, f32[8,768]{1,0:T(8,128)S(1)} %broadcast_select_fusion, f32[8]{0:T(128)S(1)} %get-tuple-element.151, bf16[128,8,768]{2,1,0:T(8,128)(2,1)S(1)} %bitcast.130, f32[8,128,128]{1,2,0:T(8,128)S(1)} %get-tuple-element.152), kind=kOutput, calls=%fused_computation.14 | convolution fusion | flops 1215168512 | bytes 3702816 | tf_op jit(solution)/shard_map/pmn,npo->mpo/dot_general | solution.py:399
  111.3 2.0 copy.36
  113.3 4.2 %all-to-all-start.1 = ((bf16[32,32,768]{2,1,0:T(8,128)(2,1)}), bf16[32,32,768]{2,1,0:T(8,128)(2,1)S(1)}, u32[]{:S(2)}, u32[]{:S(2)}) async-start(bf16[32,32,768]{2,1,0:T(8,128)(2,1)} %bitcast.18), calls=%async_computation.1 | async-start | bytes 3145728 | tf_op jit(solution)/shard_map/all_to_all | solution.py:465
  117.5 1.9 pad_maximum_fusion.scalars
  119.4 21.2 %all-to-all-done.1 = bf16[32,32,768]{2,1,0:T(8,128)(2,1)S(1)} async-done(((bf16[32,32,768]{2,1,0:T(8,128)(2,1)}), bf16[32,32,768]{2,1,0:T(8,128)(2,1)S(1)}, u32[]{:S(2)}, u32[]{:S(2)}) %all-to-all-start.1) | async-done | bytes 1572896 | tf_op jit(solution)/shard_map/all_to_all | solution.py:465
  140.7 3.1 %convolution_convert_fusion.resid_grad = bf16[1024,1024]{1,0:T(8,128)(2,1)} fusion(bf16[1024,768]{1,0:T(8,128)(2,1)S(1)} %bitcast.136, bf16[768,1024]{1,0:T(8,128)(2,1)S(1)} %copy-done.31), kind=kOutput, calls=%fused_computation.19 | convolution fusion | flops 1611661312 | bytes 5242880 | tf_op jit(solution)/shard_map/dot_general | solution.py:30
  143.8 12.0 %early_grads.1 = (bf16[4,384,1024]{2,1,0:T(8,128)(2,1)}, bf16[4,384,1024]{2,1,0:T(8,128)(2,1)}) custom-call(s32[4]{0:T(128)} %pad_add_fusion.refs_0_.place, bf16[1024,2048]{1,0:T(8,128)(2,1)} %get-tuple-element.103.hidden, bf16[1024,1024]{1,0:T(8,128)(2,1)} %convolution_convert_fusion.resid_grad, bf16[1024,1024]{1,0:T(8,128)(2,1)} %get-tuple-element.104.residual, ...), custom_call_target="tpu_custom_call" | custom-call | flops 5905580032 | bytes 18874368 | tf_op jit(solution)/shard_map/early_grads/pallas_call | solution.py:241
  155.9 9.7 %late_grads.2 = (bf16[1,512,1024]{2,1,0:T(8,128)(2,1)}, bf16[1,512,1024]{2,1,0:T(8,128)(2,1)}) custom-call(s32[4]{0:T(128)} %pad_add_fusion.refs_0_.place, bf16[1024,1024]{1,0:T(8,128)(2,1)} %convolution_convert_fusion.resid_grad, bf16[2048,1024]{1,0:T(8,128)(2,1)} %get-tuple-element.107.second, bf16[1024,2048]{1,0:T(8,128)(2,1)} %get-tuple-element.108.slope, ...), custom_call_target="tpu_custom_call" | custom-call | flops 4294967296 | bytes 12582912 | tf_op jit(solution)/shard_map/late_grads/pallas_call | solution.py:280
  166.1 1.6 add_convert_fusion
  168.1 2.8 %collective-permute-start.15 = (bf16[2,8,24,1024]{3,2,0,1:T(8,128)(2,1)S(1)}, bf16[2,8,24,1024]{3,2,0,1:T(8,128)(2,1)}, u32[]{:S(2)}, u32[]{:S(2)}) collective-permute-start(bf16[2,8,24,1024]{3,2,0,1:T(8,128)(2,1)S(1)} %dynamic-slice_bitcast_fusion), channel_id=1, source_target_pairs={{0,3},{3,0},{1,2},{2,1},{4,7},{7,4},{5,6},{6,5},{8,11},{11,8},{9,1... | collective-permute-start | bytes 2359304 | tf_op jit(solution)/shard_map/ppermute | solution.py:330
  171.2 0.9 copy-done.18
  172.1 1.4 add_convert_fusion.2
  173.5 9.6 %late_grads.3 = (bf16[1,512,1024]{2,1,0:T(8,128)(2,1)}, bf16[1,512,1024]{2,1,0:T(8,128)(2,1)}) custom-call(s32[4]{0:T(128)} %pad_add_fusion.refs_0_.place, bf16[1024,1024]{1,0:T(8,128)(2,1)} %convolution_convert_fusion.resid_grad, bf16[2048,1024]{1,0:T(8,128)(2,1)} %get-tuple-element.107.second, bf16[1024,2048]{1,0:T(8,128)(2,1)} %get-tuple-element.108.slope, ...), custom_call_target="tpu_custom_call" | custom-call | flops 4294967296 | bytes 12582912 | tf_op jit(solution)/shard_map/late_grads/pallas_call | solution.py:280
  183.1 5.9 %collective-permute-done.15 = bf16[2,8,24,1024]{3,2,0,1:T(8,128)(2,1)} collective-permute-done((bf16[2,8,24,1024]{3,2,0,1:T(8,128)(2,1)S(1)}, bf16[2,8,24,1024]{3,2,0,1:T(8,128)(2,1)}, u32[]{:S(2)}, u32[]{:S(2)}) %collective-permute-start.15) | collective-permute-done | bytes 786464 | tf_op jit(solution)/shard_map/ppermute | solution.py:330
  189.0 1.4 collective-permute-done.14
  190.4 0.9 copy-done.19
  191.3 3.7 %all-to-all-start.2 = ((bf16[16,32,1024]{2,1,0:T(8,128)(2,1)}), bf16[16,32,1024]{2,1,0:T(8,128)(2,1)S(1)}, u32[]{:S(2)}, u32[]{:S(2)}) async-start(bf16[16,32,1024]{2,1,0:T(8,128)(2,1)} %bitcast.28), calls=%async_computation.2 | async-start | bytes 2097152 | tf_op jit(solution)/shard_map/all_to_all | solution.py:485
  195.0 1.5 fusion.9
  197.3 1.1 collective-permute-start.20
  198.4 1.5 add_convert_fusion.1
  200.1 1.5 collective-permute-start.22
  201.6 2.0 collective-permute-start.24
  203.6 4.9 %collective-permute-done.21 = bf16[8,24,1024]{2,1,0:T(8,128)(2,1)S(1)} collective-permute-done((bf16[8,24,1024]{2,1,0:T(8,128)(2,1)S(1)}, bf16[8,24,1024]{2,1,0:T(8,128)(2,1)S(1)}, u32[]{:S(2)}, u32[]{:S(2)}) %collective-permute-start.21) | collective-permute-done | bytes 393248 | tf_op jit(solution)/shard_map/ppermute | solution.py:330
  208.7 1.8 collective-permute-done.20
  210.6 3.1 %collective-permute-done.22 = bf16[2,8,8,1024]{3,2,1,0:T(8,128)(2,1)S(1)} collective-permute-done((bf16[2,8,8,1024]{3,2,1,0:T(8,128)(2,1)S(1)}, bf16[2,8,8,1024]{3,2,1,0:T(8,128)(2,1)S(1)}, u32[]{:S(2)}, u32[]{:S(2)}) %collective-permute-start.22) | collective-permute-done | bytes 262176 | tf_op jit(solution)/shard_map/ppermute | solution.py:330
  213.9 1.4 collective-permute-start.23
  216.1 4.2 %collective-permute-done.23 = bf16[8,8,1024]{2,1,0:T(8,128)(2,1)S(1)} collective-permute-done((bf16[8,8,1024]{2,1,0:T(8,128)(2,1)S(1)}, bf16[8,8,1024]{2,1,0:T(8,128)(2,1)S(1)}, u32[]{:S(2)}, u32[]{:S(2)}) %collective-permute-start.23) | collective-permute-done | bytes 131104 | tf_op jit(solution)/shard_map/ppermute | solution.py:330
  220.6 1.1 maximum_maximum_fusion
  221.7 6.9 %all-to-all-start.3 = ((bf16[16,32,1024]{2,1,0:T(8,128)(2,1)}), bf16[16,32,1024]{2,1,0:T(8,128)(2,1)S(1)}, u32[]{:S(2)}, u32[]{:S(2)}) async-start(bf16[16,32,1024]{2,1,0:T(8,128)(2,1)} %maximum_maximum_fusion), calls=%async_computation.3 | async-start | bytes 2097152 | tf_op jit(solution)/shard_map/all_to_all | solution.py:503
  229.4 2.7 %collective-permute-start.18 = (f32[1,8,1024]{2,1,0:T(8,128)S(1)}, f32[1,8,1024]{2,1,0:T(8,128)S(1)}, u32[]{:S(2)}, u32[]{:S(2)}) collective-permute-start(f32[1,8,1024]{2,1,0:T(8,128)S(1)} %get-tuple-element.144), channel_id=1, source_target_pairs={{0,2},{1,3},{2,0},{3,1},{4,6},{5,7},{6,4},{7,5},{8,10},{9,11},{10,... | collective-permute-start | bytes 98312 | tf_op jit(solution)/shard_map/ppermute | solution.py:26
  232.1 0.7 collective-permute-start.19
  232.8 1.3 collective-permute-done.17
  234.0 0.8 collective-permute-done.18
  234.8 1.2 collective-permute-done.19
  236.1 8.1 %all-to-all-done.3 = bf16[16,32,1024]{2,1,0:T(8,128)(2,1)S(1)} async-done(((bf16[16,32,1024]{2,1,0:T(8,128)(2,1)}), bf16[16,32,1024]{2,1,0:T(8,128)(2,1)S(1)}, u32[]{:S(2)}, u32[]{:S(2)}) %all-to-all-start.3) | async-done | bytes 1048608 | tf_op jit(solution)/shard_map/all_to_all | solution.py:503
  244.4 0.7 fusion.41
  245.8 0.6 slice_multiply_fusion.1
  246.4 0.6 slice_multiply_fusion
  249.0 0.6 maximum_multiply_fusion
  (123 shorter events, 9.1 us)
Async XLA Ops:
  0.6 60.1 %copy-start = (f32[8,768]{1,0:T(8,128)S(1)}, f32[8,768]{1,0:T(8,128)}, u32[]{:S(2)}) copy-start(f32[8,768]{1,0:T(8,128)} %param.11) | copy-start | bytes 73732
  0.7 1.2 copy-start.2
  1.9 1.2 copy-start.4
  3.1 1.0 copy-start.6
  4.1 3.4 %copy-start.15 = (bf16[4,256,1024]{2,1,0:T(8,128)(2,1)S(1)}, bf16[4,256,1024]{2,1,0:T(8,128)(2,1)}, u32[]{:S(2)}) copy-start(bf16[4,256,1024]{2,1,0:T(8,128)(2,1)} %param.7) | copy-start | bytes 6291460
  4.2 4.9 %copy-start.8 = (bf16[1216,256]{1,0:T(8,128)(2,1)}, bf16[1216,256]{1,0:T(8,128)(2,1)S(1)}, u32[]{:S(2)}) copy-start(bf16[1216,256]{1,0:T(8,128)(2,1)S(1)} %get-tuple-element.75.refs_2_) | copy-start | bytes 1867780
  4.2 4.9 %copy-start.10 = (bf16[1216,256]{1,0:T(8,128)(2,1)}, bf16[1216,256]{1,0:T(8,128)(2,1)S(1)}, u32[]{:S(2)}) copy-start(bf16[1216,256]{1,0:T(8,128)(2,1)S(1)} %get-tuple-element.76.refs_3_) | copy-start | bytes 1867780
  4.2 17.7 %collective-permute-start = (bf16[1216,256]{1,0:T(8,128)(2,1)S(1)}, bf16[1216,256]{1,0:T(8,128)(2,1)}, u32[]{:S(2)}, u32[]{:S(2)}) collective-permute-start(bf16[1216,256]{1,0:T(8,128)(2,1)S(1)} %get-tuple-element.75.refs_2_), channel_id=1, source_target_pairs={{0,1},{1,2},{2,3},{3,0},{4,5},{5,6},{6,7},{7,4},{8,9},{9,10},{10,1... | collective-permute-start | bytes 1867784 | tf_op jit(solution)/shard_map/ppermute | solution.py:26
  5.9 16.0 %collective-permute-start.1 = (bf16[1216,256]{1,0:T(8,128)(2,1)S(1)}, bf16[1216,256]{1,0:T(8,128)(2,1)}, u32[]{:S(2)}, u32[]{:S(2)}) collective-permute-start(bf16[1216,256]{1,0:T(8,128)(2,1)S(1)} %get-tuple-element.76.refs_3_), channel_id=1, source_target_pairs={{0,3},{1,0},{2,1},{3,2},{4,7},{5,4},{6,5},{7,6},{8,11},{9,8},{10,9... | collective-permute-start | bytes 1867784 | tf_op jit(solution)/shard_map/ppermute | solution.py:26
  7.5 1.6 copy-start.3
  7.5 2.3 copy-start.5
  7.5 2.4 copy-start.7
  10.0 0.8 copy-start.12
  10.8 0.8 copy-start.13
  12.9 9.1 %copy-start.11 = (bf16[1216,256]{1,0:T(8,128)(2,1)S(1)}, bf16[1216,256]{1,0:T(8,128)(2,1)}, u32[]{:S(2)}) copy-start(bf16[1216,256]{1,0:T(8,128)(2,1)} %copy-done.10) | copy-start | bytes 1867780
  12.9 10.3 %copy-start.9 = (bf16[1216,256]{1,0:T(8,128)(2,1)S(1)}, bf16[1216,256]{1,0:T(8,128)(2,1)}, u32[]{:S(2)}) copy-start(bf16[1216,256]{1,0:T(8,128)(2,1)} %copy-done.8) | copy-start | bytes 1867780
  22.0 16.7 %collective-permute-start.3 = (bf16[1216,256]{1,0:T(8,128)(2,1)S(1)}, bf16[1216,256]{1,0:T(8,128)(2,1)S(1)}, u32[]{:S(2)}, u32[]{:S(2)}) collective-permute-start(bf16[1216,256]{1,0:T(8,128)(2,1)S(1)} %copy-done.11), channel_id=1, source_target_pairs={{0,1},{1,2},{2,3},{3,0},{4,5},{5,6},{6,7},{7,4},{8,9},{9,10},{10,1... | collective-permute-start | bytes 1867784 | tf_op jit(solution)/shard_map/ppermute | solution.py:26
  23.1 15.6 %collective-permute-start.2 = (bf16[1216,256]{1,0:T(8,128)(2,1)S(1)}, bf16[1216,256]{1,0:T(8,128)(2,1)S(1)}, u32[]{:S(2)}, u32[]{:S(2)}) collective-permute-start(bf16[1216,256]{1,0:T(8,128)(2,1)S(1)} %copy-done.9), channel_id=1, source_target_pairs={{0,3},{1,0},{2,1},{3,2},{4,7},{5,4},{6,5},{7,6},{8,11},{9,8},{10,9... | collective-permute-start | bytes 1867784 | tf_op jit(solution)/shard_map/ppermute | solution.py:26
  25.3 13.4 %collective-permute-start.4 = (bf16[1216,256]{1,0:T(8,128)(2,1)}, bf16[1216,256]{1,0:T(8,128)(2,1)S(1)}, u32[]{:S(2)}, u32[]{:S(2)}) collective-permute-start(bf16[1216,256]{1,0:T(8,128)(2,1)} %collective-permute-done.refs_2_), channel_id=1, source_target_pairs={{0,4},{4,0},{1,5},{5,1},{2,6},{6,2},{3,7},{7,3},{8,12},{12,8},{9,1... | collective-permute-start | bytes 1867784 | tf_op jit(solution)/shard_map/ppermute | solution.py:26
  25.3 13.4 %collective-permute-start.5 = (bf16[1216,256]{1,0:T(8,128)(2,1)}, bf16[1216,256]{1,0:T(8,128)(2,1)S(1)}, u32[]{:S(2)}, u32[]{:S(2)}) collective-permute-start(bf16[1216,256]{1,0:T(8,128)(2,1)} %collective-permute-done.1.refs_7_), channel_id=1, source_target_pairs={{0,4},{4,0},{1,5},{5,1},{2,6},{6,2},{3,7},{7,3},{8,12},{12,8},{9,1... | collective-permute-start | bytes 1867784 | tf_op jit(solution)/shard_map/ppermute | solution.py:26
  38.7 4.6 %copy-start.23 = (bf16[1216,256]{1,0:T(8,128)(2,1)}, bf16[1216,256]{1,0:T(8,128)(2,1)S(1)}, u32[]{:S(2)}) copy-start(bf16[1216,256]{1,0:T(8,128)(2,1)S(1)} %collective-permute-done.3.refs_3_) | copy-start | bytes 1867780
  38.7 4.6 %copy-start.24 = (bf16[1216,256]{1,0:T(8,128)(2,1)}, bf16[1216,256]{1,0:T(8,128)(2,1)S(1)}, u32[]{:S(2)}) copy-start(bf16[1216,256]{1,0:T(8,128)(2,1)S(1)} %collective-permute-done.2.refs_6_) | copy-start | bytes 1867780
  38.7 4.6 %copy-start.25 = (bf16[1216,256]{1,0:T(8,128)(2,1)}, bf16[1216,256]{1,0:T(8,128)(2,1)S(1)}, u32[]{:S(2)}) copy-start(bf16[1216,256]{1,0:T(8,128)(2,1)S(1)} %collective-permute-done.4.refs_4_) | copy-start | bytes 1867780
  38.7 0.9 copy-start.26
  38.7 4.6 %collective-permute-start.8 = (bf16[1216,256]{1,0:T(8,128)(2,1)S(1)}, bf16[1216,256]{1,0:T(8,128)(2,1)}, u32[]{:S(2)}, u32[]{:S(2)}) collective-permute-start(bf16[1216,256]{1,0:T(8,128)(2,1)S(1)} %collective-permute-done.3.refs_3_), channel_id=1, source_target_pairs={{0,4},{4,0},{1,5},{5,1},{2,6},{6,2},{3,7},{7,3},{8,12},{12,8},{9,1... | collective-permute-start | bytes 1867784 | tf_op jit(solution)/shard_map/ppermute | solution.py:26
  39.6 3.6 %collective-permute-start.9 = (bf16[1216,256]{1,0:T(8,128)(2,1)S(1)}, bf16[1216,256]{1,0:T(8,128)(2,1)}, u32[]{:S(2)}, u32[]{:S(2)}) collective-permute-start(bf16[1216,256]{1,0:T(8,128)(2,1)S(1)} %collective-permute-done.2.refs_6_), channel_id=1, source_target_pairs={{0,4},{4,0},{1,5},{5,1},{2,6},{6,2},{3,7},{7,3},{8,12},{12,8},{9,1... | collective-permute-start | bytes 1867784 | tf_op jit(solution)/shard_map/ppermute | solution.py:26
  39.6 20.0 %collective-permute-start.7 = (bf16[1216,256]{1,0:T(8,128)(2,1)}, bf16[1216,256]{1,0:T(8,128)(2,1)S(1)}, u32[]{:S(2)}, u32[]{:S(2)}) collective-permute-start(bf16[1216,256]{1,0:T(8,128)(2,1)} %collective-permute-done.1.refs_7_), channel_id=1, source_target_pairs={{0,3},{1,0},{2,1},{3,2},{4,7},{5,4},{6,5},{7,6},{8,11},{9,8},{10,9... | collective-permute-start | bytes 1867784 | tf_op jit(solution)/shard_map/ppermute | solution.py:26
  42.6 17.6 %collective-permute-start.6 = (bf16[1216,256]{1,0:T(8,128)(2,1)}, bf16[1216,256]{1,0:T(8,128)(2,1)S(1)}, u32[]{:S(2)}, u32[]{:S(2)}) collective-permute-start(bf16[1216,256]{1,0:T(8,128)(2,1)} %collective-permute-done.refs_2_), channel_id=1, source_target_pairs={{0,1},{1,2},{2,3},{3,0},{4,5},{5,6},{6,7},{7,4},{8,9},{9,10},{10,1... | collective-permute-start | bytes 1867784 | tf_op jit(solution)/shard_map/ppermute | solution.py:26
  43.3 17.4 %copy-start.29 = (s32[8]{0:T(128)S(1)}, s32[8]{0:T(128)}, u32[]{:S(2)}) copy-start(s32[8]{0:T(128)} %param.12) | copy-start | bytes 100
  59.6 3.5 %copy-start.21 = (bf16[1216,256]{1,0:T(8,128)(2,1)}, bf16[1216,256]{1,0:T(8,128)(2,1)S(1)}, u32[]{:S(2)}) copy-start(bf16[1216,256]{1,0:T(8,128)(2,1)S(1)} %collective-permute-done.7.refs_3_) | copy-start | bytes 1867780
  60.2 3.0 %copy-start.22 = (bf16[1216,256]{1,0:T(8,128)(2,1)}, bf16[1216,256]{1,0:T(8,128)(2,1)S(1)}, u32[]{:S(2)}) copy-start(bf16[1216,256]{1,0:T(8,128)(2,1)S(1)} %collective-permute-done.6.refs_2_) | copy-start | bytes 1867780
  60.2 2.1 collective-permute-start.10
  60.2 2.9 %collective-permute-start.11 = (bf16[1216,256]{1,0:T(8,128)(2,1)S(1)}, bf16[1216,256]{1,0:T(8,128)(2,1)S(1)}, u32[]{:S(2)}, u32[]{:S(2)}) collective-permute-start(bf16[1216,256]{1,0:T(8,128)(2,1)S(1)} %collective-permute-done.7.refs_3_), channel_id=1, source_target_pairs={{0,4},{4,0},{1,5},{5,1},{2,6},{6,2},{3,7},{7,3},{8,12},{12,8},{9,1... | collective-permute-start | bytes 1867784 | tf_op jit(solution)/shard_map/ppermute | solution.py:26
  62.2 0.9 copy-start.27
  63.1 0.8 copy-start.28
  106.9 1.0 copy-start.30
  113.3 27.4 %copy-start.31 = (bf16[768,1024]{1,0:T(8,128)(2,1)S(1)}, bf16[768,1024]{1,0:T(8,128)(2,1)}, u32[]{:S(2)}) copy-start(bf16[768,1024]{1,0:T(8,128)(2,1)} %get-tuple-element.102) | copy-start | bytes 4718596
  113.3 27.4 %all-to-all-start.1 = ((bf16[32,32,768]{2,1,0:T(8,128)(2,1)}), bf16[32,32,768]{2,1,0:T(8,128)(2,1)S(1)}, u32[]{:S(2)}, u32[]{:S(2)}) async-start(bf16[32,32,768]{2,1,0:T(8,128)(2,1)} %bitcast.18), calls=%async_computation.1 | async-start | bytes 3145728 | tf_op jit(solution)/shard_map/all_to_all | solution.py:465
  140.7 3.1 %copy-start.16 = (bf16[32,32,768]{2,1,0:T(8,128)(2,1)}, bf16[32,32,768]{2,1,0:T(8,128)(2,1)S(1)}, u32[]{:S(2)}) copy-start(bf16[32,32,768]{2,1,0:T(8,128)(2,1)S(1)} %all-to-all-done.1) | copy-start | bytes 4718596
  155.8 10.3 %collective-permute-start.12 = (bf16[4,384,1024]{2,1,0:T(8,128)(2,1)}, bf16[4,384,1024]{2,1,0:T(8,128)(2,1)S(1)}, u32[]{:S(2)}, u32[]{:S(2)}) collective-permute-start(bf16[4,384,1024]{2,1,0:T(8,128)(2,1)} %get-tuple-element.105), channel_id=1, source_target_pairs={{0,4},{4,0},{1,5},{5,1},{2,6},{6,2},{3,7},{7,3},{8,12},{12,8},{9,1... | collective-permute-start | bytes 9437192 | tf_op jit(solution)/shard_map/ppermute | solution.py:26
  155.9 10.2 %copy-start.14 = (bf16[4,384,1024]{2,1,0:T(8,128)(2,1)S(1)}, bf16[4,384,1024]{2,1,0:T(8,128)(2,1)}, u32[]{:S(2)}) copy-start(bf16[4,384,1024]{2,1,0:T(8,128)(2,1)} %get-tuple-element.112) | copy-start | bytes 9437188
  165.6 5.6 %collective-permute-start.13 = (bf16[1,512,1024]{2,1,0:T(8,128)(2,1)}, bf16[1,512,1024]{2,1,0:T(8,128)(2,1)S(1)}, u32[]{:S(2)}, u32[]{:S(2)}) collective-permute-start(bf16[1,512,1024]{2,1,0:T(8,128)(2,1)} %get-tuple-element.111), channel_id=1, source_target_pairs={{0,4},{4,0},{1,5},{5,1},{2,6},{6,2},{3,7},{7,3},{8,12},{12,8},{9,1... | collective-permute-start | bytes 3145736 | tf_op jit(solution)/shard_map/ppermute | solution.py:26
  168.1 20.9 %collective-permute-start.15 = (bf16[2,8,24,1024]{3,2,0,1:T(8,128)(2,1)S(1)}, bf16[2,8,24,1024]{3,2,0,1:T(8,128)(2,1)}, u32[]{:S(2)}, u32[]{:S(2)}) collective-permute-start(bf16[2,8,24,1024]{3,2,0,1:T(8,128)(2,1)S(1)} %dynamic-slice_bitcast_fusion), channel_id=1, source_target_pairs={{0,3},{3,0},{1,2},{2,1},{4,7},{7,4},{5,6},{6,5},{8,11},{11,8},{9,1... | collective-permute-start | bytes 2359304 | tf_op jit(solution)/shard_map/ppermute | solution.py:330
  170.9 1.2 copy-start.18
  171.1 19.3 %collective-permute-start.14 = (bf16[2,8,24,1024]{3,2,1,0:T(8,128)(2,1)S(1)}, bf16[2,8,24,1024]{3,2,1,0:T(8,128)(2,1)S(1)}, u32[]{:S(2)}, u32[]{:S(2)}) collective-permute-start(bf16[2,8,24,1024]{3,2,1,0:T(8,128)(2,1)S(1)} %bitcast.139), channel_id=1, source_target_pairs={{0,1},{1,0},{2,3},{3,2},{4,5},{5,4},{6,7},{7,6},{8,9},{9,8},{10,11... | collective-permute-start | bytes 2359304 | tf_op jit(solution)/shard_map/ppermute | solution.py:330
  190.4 0.9 copy-start.19
  191.3 7.1 %collective-permute-start.16 = (bf16[1,512,1024]{2,1,0:T(8,128)(2,1)}, bf16[1,512,1024]{2,1,0:T(8,128)(2,1)}, u32[]{:S(2)}, u32[]{:S(2)}) collective-permute-start(bf16[1,512,1024]{2,1,0:T(8,128)(2,1)} %get-tuple-element.118), channel_id=1, source_target_pairs={{0,4},{4,0},{1,5},{5,1},{2,6},{6,2},{3,7},{7,3},{8,12},{12,8},{9,1... | collective-permute-start | bytes 3145736 | tf_op jit(solution)/shard_map/ppermute | solution.py:26
  191.3 30.4 %all-to-all-start.2 = ((bf16[16,32,1024]{2,1,0:T(8,128)(2,1)}), bf16[16,32,1024]{2,1,0:T(8,128)(2,1)S(1)}, u32[]{:S(2)}, u32[]{:S(2)}) async-start(bf16[16,32,1024]{2,1,0:T(8,128)(2,1)} %bitcast.28), calls=%async_computation.2 | async-start | bytes 2097152 | tf_op jit(solution)/shard_map/all_to_all | solution.py:485
  195.0 1.9 copy-start.20
  196.5 1.9 copy-start.17
  196.5 12.0 %collective-permute-start.21 = (bf16[8,24,1024]{2,1,0:T(8,128)(2,1)S(1)}, bf16[8,24,1024]{2,1,0:T(8,128)(2,1)S(1)}, u32[]{:S(2)}, u32[]{:S(2)}) collective-permute-start(bf16[8,24,1024]{2,1,0:T(8,128)(2,1)S(1)} %dynamic-slice_bitcast_fusion.1), channel_id=1, source_target_pairs={{0,1},{1,0},{2,3},{3,2},{4,5},{5,4},{6,7},{7,6},{8,9},{9,8},{10,11... | collective-permute-start | bytes 1179656 | tf_op jit(solution)/shard_map/ppermute | solution.py:330
  197.3 13.2 %collective-permute-start.20 = (bf16[8,24,1024]{2,1,0:T(8,128)(2,1)S(1)}, bf16[8,24,1024]{2,1,0:T(8,128)(2,1)S(1)}, u32[]{:S(2)}, u32[]{:S(2)}) collective-permute-start(bf16[8,24,1024]{2,1,0:T(8,128)(2,1)S(1)} %dynamic-slice_bitcast_fusion.2), channel_id=1, source_target_pairs={{0,3},{3,0},{1,2},{2,1},{4,7},{7,4},{5,6},{6,5},{8,11},{11,8},{9,1... | collective-permute-start | bytes 1179656 | tf_op jit(solution)/shard_map/ppermute | solution.py:330
  200.1 13.7 %collective-permute-start.22 = (bf16[2,8,8,1024]{3,2,1,0:T(8,128)(2,1)S(1)}, bf16[2,8,8,1024]{3,2,1,0:T(8,128)(2,1)S(1)}, u32[]{:S(2)}, u32[]{:S(2)}) collective-permute-start(bf16[2,8,8,1024]{3,2,1,0:T(8,128)(2,1)S(1)} %bitcast.143), channel_id=1, source_target_pairs={{0,1},{1,0},{2,3},{3,2},{4,5},{5,4},{6,7},{7,6},{8,9},{9,8},{10,11... | collective-permute-start | bytes 786440 | tf_op jit(solution)/shard_map/ppermute | solution.py:330
  201.6 13.9 %collective-permute-start.24 = (bf16[2,8,8,1024]{3,2,0,1:T(8,128)(2,1)S(1)}, bf16[2,8,8,1024]{3,2,0,1:T(8,128)(2,1)S(1)}, u32[]{:S(2)}, u32[]{:S(2)}) collective-permute-start(bf16[2,8,8,1024]{3,2,0,1:T(8,128)(2,1)S(1)} %dynamic-slice_bitcast_fusion.3), channel_id=1, source_target_pairs={{0,3},{3,0},{1,2},{2,1},{4,7},{7,4},{5,6},{6,5},{8,11},{11,8},{9,1... | collective-permute-start | bytes 786440 | tf_op jit(solution)/shard_map/ppermute | solution.py:330
  213.9 6.4 %collective-permute-start.23 = (bf16[8,8,1024]{2,1,0:T(8,128)(2,1)S(1)}, bf16[8,8,1024]{2,1,0:T(8,128)(2,1)S(1)}, u32[]{:S(2)}, u32[]{:S(2)}) collective-permute-start(bf16[8,8,1024]{2,1,0:T(8,128)(2,1)S(1)} %dynamic-slice_bitcast_fusion.5), channel_id=1, source_target_pairs={{0,3},{3,0},{1,2},{2,1},{4,7},{7,4},{5,6},{6,5},{8,11},{11,8},{9,1... | collective-permute-start | bytes 393224 | tf_op jit(solution)/shard_map/ppermute | solution.py:330
  215.5 5.0 %collective-permute-start.25 = (bf16[8,8,1024]{2,1,0:T(8,128)(2,1)S(1)}, bf16[8,8,1024]{2,1,0:T(8,128)(2,1)S(1)}, u32[]{:S(2)}, u32[]{:S(2)}) collective-permute-start(bf16[8,8,1024]{2,1,0:T(8,128)(2,1)S(1)} %dynamic-slice_bitcast_fusion.4), channel_id=1, source_target_pairs={{0,1},{1,0},{2,3},{3,2},{4,5},{5,4},{6,7},{7,6},{8,9},{9,8},{10,11... | collective-permute-start | bytes 393224 | tf_op jit(solution)/shard_map/ppermute | solution.py:330
  221.7 22.4 %all-to-all-start.3 = ((bf16[16,32,1024]{2,1,0:T(8,128)(2,1)}), bf16[16,32,1024]{2,1,0:T(8,128)(2,1)S(1)}, u32[]{:S(2)}, u32[]{:S(2)}) async-start(bf16[16,32,1024]{2,1,0:T(8,128)(2,1)} %maximum_maximum_fusion), calls=%async_computation.3 | async-start | bytes 2097152 | tf_op jit(solution)/shard_map/all_to_all | solution.py:503
  228.6 21.1 %copy-start.1 = (f32[8,768]{1,0:T(8,128)S(1)}, f32[8,768]{1,0:T(8,128)}, u32[]{:S(2)}) copy-start(f32[8,768]{1,0:T(8,128)} %param.11) | copy-start | bytes 73732
  228.8 5.2 %collective-permute-start.17 = (f32[1,8,1024]{2,1,0:T(8,128)S(1)}, f32[1,8,1024]{2,1,0:T(8,128)S(1)}, u32[]{:S(2)}, u32[]{:S(2)}) collective-permute-start(f32[1,8,1024]{2,1,0:T(8,128)S(1)} %get-tuple-element.142), channel_id=1, source_target_pairs={{0,1},{1,2},{2,3},{3,0},{4,5},{5,6},{6,7},{7,4},{8,9},{9,10},{10,1... | collective-permute-start | bytes 98312 | tf_op jit(solution)/shard_map/ppermute | solution.py:26
  229.4 5.4 %collective-permute-start.18 = (f32[1,8,1024]{2,1,0:T(8,128)S(1)}, f32[1,8,1024]{2,1,0:T(8,128)S(1)}, u32[]{:S(2)}, u32[]{:S(2)}) collective-permute-start(f32[1,8,1024]{2,1,0:T(8,128)S(1)} %get-tuple-element.144), channel_id=1, source_target_pairs={{0,2},{1,3},{2,0},{3,1},{4,6},{5,7},{6,4},{7,5},{8,10},{9,11},{10,... | collective-permute-start | bytes 98312 | tf_op jit(solution)/shard_map/ppermute | solution.py:26
  232.1 3.9 %collective-permute-start.19 = (f32[1,8,1024]{2,1,0:T(8,128)S(1)}, f32[1,8,1024]{2,1,0:T(8,128)S(1)}, u32[]{:S(2)}, u32[]{:S(2)}) collective-permute-start(f32[1,8,1024]{2,1,0:T(8,128)S(1)} %get-tuple-element.143), channel_id=1, source_target_pairs={{0,3},{1,0},{2,1},{3,2},{4,7},{5,4},{6,5},{7,6},{8,11},{9,8},{10,9... | collective-permute-start | bytes 98312 | tf_op jit(solution)/shard_map/ppermute | solution.py:26

commit v11 on v10

--- a/solution.py
+++ b/solution.py
@@ -220,23 +220,17 @@
     return jnp.where(lane == 2 * place[0] + place[1], out, 0.0)
 
 
-def early_kernel(place, hidden, resid_grad, residual, grad_rows, scalars, keep, send):
+def early_kernel(place, hidden, resid_grad, keep, send):
     second = dot(hidden[...], resid_grad[...], ((0,), (0,)))
-    head = dot(residual[...], grad_rows[...], ((0,), (0,)))
-    width, out_width = second.shape[1], head.shape[1]
-    second = second.reshape(RING, 2, RING, -1, width)
-    head = head.reshape(RING, 2, RING, -1, out_width)
-    blank = riders(place, scalars, (head.shape[3], width - out_width))
-    blank = jnp.broadcast_to(blank, (*head.shape[:3], *blank.shape))
-    both = jnp.concatenate([second, jnp.concatenate([head, blank], 4)], 3)
-    both = jnp.stack([both[:, :, i] for i in (0, 3, 1, 2)], 2)
-    store_halves(place[1], both.reshape(RING, 2, -1, width), keep, send)
-
-
-def early_grads(place, hidden, resid_grad, residual, grad_rows, scalars):
+    parts = second.reshape(RING, 2, RING, -1, second.shape[1])
+    parts = jnp.stack([parts[:, :, i] for i in (0, 3, 1, 2)], 2)
+    store_halves(place[1], parts.reshape(RING, 2, -1, second.shape[1]), keep, send)
+
+
+def early_grads(place, hidden, resid_grad):
     rows, hid = hidden.shape
-    width, out_width = residual.shape[1], grad_rows.shape[1]
-    lines = (hid + width) // RING // 2
+    width = resid_grad.shape[1]
+    lines = hid // RING // 2
     out = pl.BlockSpec((1, lines, width), lambda i, s: (i, 0, 0))
     return pl.pallas_call(
         early_kernel,
@@ -246,39 +240,59 @@
             in_specs=[
                 pl.BlockSpec((rows, hid // RING), lambda i, s: (0, i)),
                 once((rows, width)),
-                pl.BlockSpec((rows, width // RING), lambda i, s: (0, i)),
-                once((rows, out_width)),
-                pl.BlockSpec(memory_space=pltpu.SMEM),
             ],
             out_specs=[out, out],
         ),
         out_shape=[jax.ShapeDtypeStruct((RING, lines, width), BF16)] * 2,
         compiler_params=params(56),
         cost_estimate=pl.CostEstimate(
-            flops=2 * rows * width * (hid + out_width), bytes_accessed=18 * MIB, transcendentals=0
+            flops=2 * rows * width * hid, bytes_accessed=12 * MIB, transcendentals=0
         ),
         name="early_grads",
-    )(place, hidden, resid_grad, residual, grad_rows, scalars)
-
-
-def late_kernel(gray, place, resid_grad, second, slope, tokens, keep, send):
+    )(place, hidden, resid_grad)
+
+
+def late_kernel(steps, place, resid_grad, second, slope, tokens, *refs):
+    keep, send = refs[-2:]
     hidden_grad = dot(resid_grad[...], second[...], ((1,), (1,)))
     preact_grad = (slope[...].astype(F32) * hidden_grad).astype(BF16)
     first = dot(tokens[...], preact_grad, ((0,), (0,)))
     cols = first.shape[1]
-    parts = first.reshape(16, 2, RING, -1, cols)
-    if gray:
-        parts = jnp.stack([parts[:, :, i] for i in (0, 3, 1, 2)], 2)
-    store_halves(place[1], parts.reshape(16, 2, -1, cols), keep, send)
-
-
-def late_grads(place, part, resid_grad, second, slope, tokens):
+
+    def store(*grads):
+        parts = jnp.concatenate([g.reshape(16, 2, RING, -1, cols) for g in grads], 3)
+        if len(refs) == 2:
+            parts = jnp.stack([parts[:, :, i] for i in (0, 3, 1, 2)], 2)
+        store_halves(place[1], parts.reshape(16, 2, -1, cols), keep, send)
+
+    if len(refs) == 2:
+        store(first)
+        return
+    residual, grad_rows, scalars = refs[:3]
+    width, out_width = residual.shape[1], grad_rows.shape[1]
+    for j in range(steps):
+
+        @pl.when(pl.program_id(0) == j)
+        def _(j=j):
+            head = dot(residual[...], grad_rows[:, j * cols : (j + 1) * cols], ((0,), (0,)))
+            if j == steps - 1:
+                blank = riders(place, scalars, (8, width - out_width))
+                blank = jnp.broadcast_to(blank, (width // 8, *blank.shape))
+                head = jnp.concatenate([head, blank.reshape(width, -1)], 1)
+            store(first, head)
+
+
+def late_grads(place, part, resid_grad, second, slope, tokens, *head):
     rows, width = resid_grad.shape
     tile = 2 * LANES
     steps = width // tile
-    out = pl.BlockSpec((1, width // 2, tile), lambda j, s: (0, 0, j))
+    lines = width if head else width // 2
+    out = pl.BlockSpec((1, lines, tile), lambda j, s: (0, 0, j))
+    specs = []
+    if head:
+        specs = [once(head[0].shape), once(head[1].shape), pl.BlockSpec(memory_space=pltpu.SMEM)]
     return pl.pallas_call(
-        functools.partial(late_kernel, part == 1),
+        functools.partial(late_kernel, steps),
         grid_spec=pltpu.PrefetchScalarGridSpec(
             num_scalar_prefetch=1,
             grid=(steps,),
@@ -287,16 +301,17 @@
                 pl.BlockSpec((tile, width), lambda j, s: (part * steps + j, 0)),
                 pl.BlockSpec((rows, tile), lambda j, s: (0, part * steps + j)),
                 once((rows, width)),
+                *specs,
             ],
             out_specs=[out, out],
         ),
-        out_shape=[jax.ShapeDtypeStruct((1, width // 2, width), BF16)] * 2,
+        out_shape=[jax.ShapeDtypeStruct((1, lines, width), BF16)] * 2,
         compiler_params=params(56),
         cost_estimate=pl.CostEstimate(
             flops=4 * rows * width * width, bytes_accessed=12 * MIB, transcendentals=0
         ),
         name="late_grads",
-    )(place, resid_grad, second, slope, tokens)
+    )(place, resid_grad, second, slope, tokens, *head)
 
 
 def add(a, b):
@@ -469,9 +484,19 @@
     at = place(0)
     scalars = jnp.stack([score_part, count_part])
     resid_grad = dot(grad_rows, head).astype(BF16)
-    early = early_grads(at, hidden, resid_grad, residual, grad_rows, scalars)
+    early = early_grads(at, hidden, resid_grad)
     early_in = shift(early[1], "c", 1)
-    late = late_grads(at, 0, after(resid_grad, early[1]), second, slope, tokens)
+    late = late_grads(
+        at,
+        0,
+        after(resid_grad, early[1]),
+        second,
+        slope,
+        tokens,
+        residual,
+        grad_rows,
+        scalars,
+    )
     a_in = shift(late[1], "c", 1)
     steps = [ring_chain("y", True), ring_chain("y", False)]
     group = ("x", "z")
@@ -481,7 +506,7 @@
     early = [by_ring(v, lines) for v in (early[:2], early[2:])]
     early_sent = [outgoing(x, s[0]) for x, s in zip(early, steps)]
     early_in = [sent_along(x, s[0]) for x, s in zip(early_sent, steps)]
-    a = add(after(late[0], *early_sent), a_in).reshape(16, RING * n, width)
+    a = add(after(late[0], *early_sent), a_in).reshape(16, 2 * RING * n, width)
     a_all = lax.all_to_all(a, group, 0, 0, tiled=True)
     late = late_grads(at, 1, after(resid_grad, a), second, slope, tokens)
     b_in = shift(after(late[1], *early_in), "c", 1)
@@ -493,7 +518,7 @@
     b_sent = [outgoing(x, s[0]) for x, s in zip(b, steps)]
     b_in = [sent_along(x, s[0]) for x, s in zip(b_sent, steps)]
     a = jnp.sum(after(a_all, *b_sent).astype(F32), 0)
-    first = summed_over_y(a.reshape(1, RING, n, width))
+    first = summed_over_y(a.reshape(1, RING, 2 * n, width))[0]
     early = [kept_plus(x, after(v, *b_sent), s[1]) for x, v, s in zip(early, early_in, steps)]
     b = [kept_plus(x, after(v, *early), s[0]) for x, v, s in zip(b, b_in, steps)]
     b_sent = [outgoing(x, s[1]) for x, s in zip(b, steps)]
@@ -503,15 +528,15 @@
     early = lax.all_to_all(early, group, 0, 0, tiled=True)
     early = jnp.sum(early.astype(F32), 0)
     early, b = early[:-n], early[-n:]
-    n_second = shard * RING // 128
-    ride = jnp.sum(early[n_second:, out_width:], 1)
+    first, head = first[:n], first[n:]
+    ride = jnp.sum(head[:, out_width:], 1)
     score_total = ride[0] + ride[1] + ride[2]
     valid_total = jnp.maximum(ride[3], 1.0)
     scale = 1.0 / valid_total
     return (
-        jnp.concatenate([first[0], b], 1) * scale,
-        early[:n_second] * scale,
-        early[n_second:, :out_width] * scale,
+        jnp.concatenate([first, b], 1) * scale,
+        early * scale,
+        head[:, :out_width] * scale,
         score_total / valid_total,
     )
 

time: 252 us -> 253 us (level)
  blocking collectives: 30.5 us -> 57 us
  waiting for transfers between devices: 69.6 us -> 45.2 us
  other arithmetic: 14.9 us -> 20.1 us
  starting transfers between devices: 39.6 us -> 34.5 us
    all_to_all x0 -> x1, blocking collectives: none -> 26.4 us  [per_device(): lax.all_to_all(grad_raw.reshape(32, members * own, out_width), group, 0,...]
    all_to_all x1 -> x0, waiting for transfers between devices: 21.2 us -> none  [per_device(): lax.all_to_all(grad_raw.reshape(32, members * own, out_width), group, 0,...]
    ppermute x8, waiting for transfers between devices: 21.9 us -> 9.85 us  [sent_along(): return lax.ppermute(x, step[1], step[0])]
    all_to_all x1, waiting for transfers between devices: 0.01 us -> 11 us  [per_device(): a_all = lax.all_to_all(a, group, 0, 0, tiled=True)]
    convert_element_type x11, other arithmetic: 6.78 us -> 11.9 us  [add(): return (a.astype(F32) + b.astype(F32)).astype(BF16)]
    all_to_all x1 -> x0, starting transfers between devices: 4.24 us -> none  [per_device(): lax.all_to_all(grad_raw.reshape(32, members * own, out_width), group, 0,...]
    ppermute x18, waiting for transfers between devices: 18.5 us -> 14.8 us  [shift(): return lax.ppermute(x, axis, [(i, (i + by) % size) for i in range(size)])]
    pallas_call x2, Pallas kernels: 19.3 us -> 22.8 us  [late_grads(): pl.pallas_call(functools.partial(late_kernel, steps), grid_spec=pltpu.Pre...]
  transfers between devices with their start and end apart: 29 -> 28, of which waited for: 17 -> 11; matrix products, arithmetic and copies ran while one was open for 6% -> 9% of each run, Pallas kernels for 18% -> 19%
where the time goes in v11:
time: 253 us; the launch traced here: 252 us
  Pallas kernels  68.6 us (27%)
  blocking collectives  57 us (23%)
  waiting for transfers between devices  45.2 us (18%)
  starting transfers between devices  34.5 us (14%)
  other arithmetic  20.1 us (8%)
  local copies, waits for them, and re-layouts  14.5 us (6%)
  matrix products  6.87 us (3%)
  between operations  5.04 us (2%)
    pallas_call x3, Pallas kernels, forward_part(): pl.pallas_call(functools.partial(forward_kernel, groups, first_call, last...  36.3 us
    all_to_all x1, blocking collectives, per_device(): gathered = lax.all_to_all(forecast, group, 0, 0, tiled=True)  30.5 us
    all_to_all x1, blocking collectives, per_device(): lax.all_to_all(grad_raw.reshape(32, members * own, out_width), group, 0,...  26.4 us
    pallas_call x2, Pallas kernels, late_grads(): pl.pallas_call(functools.partial(late_kernel, steps), grid_spec=pltpu.Pre...  22.8 us
    ppermute x18, starting transfers between devices, shift(): return lax.ppermute(x, axis, [(i, (i + by) % size) for i in range(size)])  15.2 us
    ppermute x18, waiting for transfers between devices, shift(): return lax.ppermute(x, axis, [(i, (i + by) % size) for i in range(size)])  14.8 us
    convert_element_type x11, other arithmetic, add(): return (a.astype(F32) + b.astype(F32)).astype(BF16)  11.9 us
    all_to_all x1, waiting for transfers between devices, per_device(): a_all = lax.all_to_all(a, group, 0, 0, tiled=True)  11 us
  transfers between devices with their start and end apart: 28, of which 11 were waited for; matrix products, arithmetic and copies ran while one was open for 9% of the time, Pallas kernels for 19%

profile of v11, /device:TPU:0, one launch (start us, length us, event | category | flops | bytes accessed | tf_op | source)
XLA Modules:
  0.0 251.8 jit_solution(3952278960670048013)
XLA Ops:
  0.7 1.2 copy-done.2
  1.9 1.2 copy-done.4
  3.1 1.0 copy-done.6
  4.2 1.7 collective-permute-start
  5.9 1.6 collective-permute-start.1
  7.5 1.6 copy.26
  9.1 0.7 copy-done.5
  10.0 0.8 copy-done.12
  10.8 0.8 copy-done.13
  11.6 0.7 pad_add_fusion.2
  12.3 0.7 pad_add_fusion.refs_0_.place
  13.0 9.1 %forward_part.3 = (bf16[1024,2048]{1,0:T(8,128)(2,1)}, bf16[1024,2048]{1,0:T(8,128)(2,1)}, bf16[2048,1024]{1,0:T(8,128)(2,1)}, bf16[768,1024]{1,0:T(8,128)(2,1)}, f32[1024,1024]{1,0:T(8,128)}) custom-call(s32[4]{0:T(128)} %pad_add_fusion.refs_0_.place, bf16[1024,1024]{1,0:T(8,128)(2,1)} %bitcast.121, bf16[1216,256]{1,0:T(8,128)(2,1)} %copy-done.8, ...), custom_call_target="tpu_custom_call" | custom-call | flops 2147483648 | bytes 12582912 | tf_op jit(solution)/shard_map/forward_part/pallas_call | solution.py:166
  22.1 1.0 collective-permute-start.3
  23.1 2.3 collective-permute-start.2
  25.9 12.9 %collective-permute-done.3.refs_3_ = bf16[1216,256]{1,0:T(8,128)(2,1)S(1)} collective-permute-done((bf16[1216,256]{1,0:T(8,128)(2,1)S(1)}, bf16[1216,256]{1,0:T(8,128)(2,1)S(1)}, u32[]{:S(2)}, u32[]{:S(2)}) %collective-permute-start.3) | collective-permute-done | bytes 622624 | tf_op jit(solution)/shard_map/ppermute | solution.py:26
  39.8 2.9 %collective-permute-start.7 = (bf16[1216,256]{1,0:T(8,128)(2,1)}, bf16[1216,256]{1,0:T(8,128)(2,1)S(1)}, u32[]{:S(2)}, u32[]{:S(2)}) collective-permute-start(bf16[1216,256]{1,0:T(8,128)(2,1)} %collective-permute-done.1.refs_7_), channel_id=1, source_target_pairs={{0,3},{1,0},{2,1},{3,2},{4,7},{5,4},{6,5},{7,6},{8,11},{9,8},{10,9... | collective-permute-start | bytes 1867784 | tf_op jit(solution)/shard_map/ppermute | solution.py:26
  42.7 0.6 stack.59.refs_0_
  43.3 16.1 %forward_part.4 = (bf16[1024,2048]{1,0:T(8,128)(2,1)}, bf16[1024,2048]{1,0:T(8,128)(2,1)}, bf16[2048,1024]{1,0:T(8,128)(2,1)}, bf16[768,1024]{1,0:T(8,128)(2,1)}, f32[1024,1024]{1,0:T(8,128)}) custom-call(s32[5]{0:T(128)} %stack.59.refs_0_, ...), custom_call_target="tpu_custom_call", output_to_operand_aliasing={{0}: (11, {}), {1}: (12, {}), {2}: (13, {}), {3}: (14, {})} | custom-call | flops 4294967296 | bytes 12582912 | tf_op jit(solution)/shard_map/forward_part/pallas_call | solution.py:166
  60.7 0.9 collective-permute-done.10.refs_4_
  61.6 0.9 collective-permute-done.11.refs_5_
  62.5 0.8 copy-done.26
  63.3 11.1 %forward_part.5 = (bf16[1024,2048]{1,0:T(8,128)(2,1)}, bf16[1024,2048]{1,0:T(8,128)(2,1)}, bf16[2048,1024]{1,0:T(8,128)(2,1)}, bf16[768,1024]{1,0:T(8,128)(2,1)}...) custom-call(s32[4]{0:T(128)} %get-tuple-element.132.refs_0_, ...), custom_call_target="tpu_custom_call", output_to_operand_aliasing={{0}: (7, {}), {1}: (8, {}), {2}: (9, {})} | custom-call | flops 2147483648 | bytes 12582912 | tf_op jit(solution)/shard_map/forward_part/pallas_call | solution.py:166
  74.5 30.5 %all_to_all.20 = bf16[32,32,768]{2,1,0:T(8,128)(2,1)S(1)} all-to-all(bf16[32,32,768]{2,1,0:T(8,128)(2,1)} %bitcast.139), channel_id=1, replica_groups=mesh['x'=4,'z'=4,'c'=2,'y'=4] {'x','z','c'}, dimensions={0} | all-to-all | bytes 3145728 | tf_op jit(solution)/shard_map/all_to_all | solution.py:477
  105.2 0.8 fusion.6
  106.3 0.9 fusion.36
  107.2 0.6 multiply_reduce_fusion
  107.9 2.8 %fusion.8 = bf16[128,8,768]{2,0,1:T(8,128)(2,1)S(1)} fusion(f32[128,8]{0,1:T(8,128)S(1)} %bitcast.145, f32[128,8]{0,1:T(8,128)S(1)} %copy.29, f32[8,768]{1,0:T(8,128)S(1)} %broadcast_select_fusion, f32[8]{0:T(128)S(1)} %get-tuple-element.153, bf16[128,8,768]{2,1,0:T(8,128)(2,1)S(1)} %bitcast.131, f32[8,128,128]{1,2,0:T(8,128)S(1)} %get-tuple-element.154), kind=kOutput, calls=%fused_computation.16 | convolution fusion | flops 1215168512 | bytes 3702816 | tf_op jit(solution)/shard_map/pmn,npo->mpo/dot_general | solution.py:414
  110.7 0.9 copy.36
  111.5 26.4 %all_to_all.21 = bf16[32,32,768]{2,1,0:T(8,128)(2,1)S(1)} all-to-all(bf16[32,32,768]{2,1,0:T(8,128)(2,1)S(1)} %bitcast.129), channel_id=1, replica_groups=mesh['x'=4,'z'=4,'c'=2,'y'=4] {'x','z','c'}, dimensions={0} | all-to-all | bytes 3145728 | tf_op jit(solution)/shard_map/all_to_all | solution.py:480
  138.0 3.1 %convolution_convert_fusion.resid_grad = bf16[1024,1024]{1,0:T(8,128)(2,1)} fusion(bf16[1024,768]{1,0:T(8,128)(2,1)S(1)} %bitcast.127, bf16[768,1024]{1,0:T(8,128)(2,1)S(1)} %copy-done.29), kind=kOutput, calls=%fused_computation.18 | convolution fusion | flops 1611661312 | bytes 5242880 | tf_op jit(solution)/shard_map/dot_general | solution.py:30
  141.1 9.4 %early_grads.1 = (bf16[4,256,1024]{2,1,0:T(8,128)(2,1)}, bf16[4,256,1024]{2,1,0:T(8,128)(2,1)}) custom-call(s32[4]{0:T(128)} %pad_add_fusion.refs_0_.place, bf16[1024,2048]{1,0:T(8,128)(2,1)} %get-tuple-element.103.hidden, bf16[1024,1024]{1,0:T(8,128)(2,1)} %convolution_convert_fusion.resid_grad), custom_call_target="tpu_custom_call" | custom-call | flops 4294967296 | bytes 12582912 | tf_op jit(solution)/shard_map/early_grads/pallas_call | solution.py:235
  150.5 0.8 collective-permute-start.12
  151.3 1.9 pad_maximum_fusion.refs_2_
  153.2 13.2 %late_grads.2 = (bf16[1,1024,1024]{2,1,0:T(8,128)(2,1)}, bf16[1,1024,1024]{2,1,0:T(8,128)(2,1)}) custom-call(s32[4]{0:T(128)} %pad_add_fusion.refs_0_.place, bf16[1024,1024]{1,0:T(8,128)(2,1)} %convolution_convert_fusion.resid_grad, bf16[2048,1024]{1,0:T(8,128)(2,1)} %get-tuple-element.106.second, bf16[1024,2048]{1,0:T(8,128)(2,1)} %get-tuple-element.107.slope, ...), custom_call_target="tpu_custom_call" | custom-call | flops 4294967296 | bytes 12582912 | tf_op jit(solution)/shard_map/late_grads/pallas_call | solution.py:294
  166.4 3.2 %add_convert_fusion.1 = bf16[4,256,1024]{2,1,0:T(8,128)(2,1)S(1)} fusion(bf16[4,256,1024]{2,1,0:T(8,128)(2,1)} %collective-permute-done.12, bf16[4,256,1024]{2,1,0:T(8,128)(2,1)} %get-tuple-element.112), kind=kLoop, calls=%fused_computation.3 | loop fusion | flops 4194304 | bytes 6291456 | tf_op jit(solution)/shard_map/convert_element_type | solution.py:318
  169.9 3.3 %collective-permute-start.15 = (bf16[2,8,16,1024]{3,2,0,1:T(8,128)(2,1)S(1)}, bf16[2,8,16,1024]{3,2,0,1:T(8,128)(2,1)}, u32[]{:S(2)}, u32[]{:S(2)}) collective-permute-start(bf16[2,8,16,1024]{3,2,0,1:T(8,128)(2,1)S(1)} %dynamic-slice_bitcast_fusion), channel_id=1, source_target_pairs={{0,3},{3,0},{1,2},{2,1},{4,7},{7,4},{5,6},{6,5},{8,11},{11,8},{9,1... | collective-permute-start | bytes 1572872 | tf_op jit(solution)/shard_map/ppermute | solution.py:345
  173.2 0.9 constant_dynamic-slice_fusion.2
  174.2 2.4 add_convert_fusion
  176.6 9.6 %late_grads.3 = (bf16[1,512,1024]{2,1,0:T(8,128)(2,1)}, bf16[1,512,1024]{2,1,0:T(8,128)(2,1)}) custom-call(s32[4]{0:T(128)} %pad_add_fusion.refs_0_.place, bf16[1024,1024]{1,0:T(8,128)(2,1)} %convolution_convert_fusion.resid_grad, bf16[2048,1024]{1,0:T(8,128)(2,1)} %get-tuple-element.106.second, bf16[1024,2048]{1,0:T(8,128)(2,1)} %get-tuple-element.107.slope, ...), custom_call_target="tpu_custom_call" | custom-call | flops 4294967296 | bytes 12582912 | tf_op jit(solution)/shard_map/late_grads/pallas_call | solution.py:294
  186.2 2.2 collective-permute-done.14
  188.3 3.7 %all-to-all-start.2 = ((bf16[16,64,1024]{2,1,0:T(8,128)(2,1)}), bf16[16,64,1024]{2,1,0:T(8,128)(2,1)S(1)}, u32[]{:S(2)}, u32[]{:S(2)}) async-start(bf16[16,64,1024]{2,1,0:T(8,128)(2,1)} %bitcast.28), calls=%async_computation.2 | async-start | bytes 4194304 | tf_op jit(solution)/shard_map/all_to_all | solution.py:510
  192.1 1.4 fusion.24
  193.8 1.2 fusion.25
  195.5 1.5 add_convert_fusion.2
  197.2 1.5 collective-permute-start.22
  198.8 2.6 %collective-permute-start.24 = (bf16[2,8,8,1024]{3,2,0,1:T(8,128)(2,1)S(1)}, bf16[2,8,8,1024]{3,2,0,1:T(8,128)(2,1)S(1)}, u32[]{:S(2)}, u32[]{:S(2)}) collective-permute-start(bf16[2,8,8,1024]{3,2,0,1:T(8,128)(2,1)S(1)} %dynamic-slice_bitcast_fusion.1), channel_id=1, source_target_pairs={{0,3},{3,0},{1,2},{2,1},{4,7},{7,4},{5,6},{6,5},{8,11},{11,8},{9,1... | collective-permute-start | bytes 786440 | tf_op jit(solution)/shard_map/ppermute | solution.py:345
  201.4 1.3 collective-permute-done.21
  202.7 2.8 %collective-permute-done.20 = bf16[8,16,1024]{2,1,0:T(8,128)(2,1)S(1)} collective-permute-done((bf16[8,16,1024]{2,1,0:T(8,128)(2,1)S(1)}, bf16[8,16,1024]{2,1,0:T(8,128)(2,1)S(1)}, u32[]{:S(2)}, u32[]{:S(2)}) %collective-permute-start.20) | collective-permute-done | bytes 262176 | tf_op jit(solution)/shard_map/ppermute | solution.py:345
  205.6 2.3 collective-permute-done.22
  207.9 0.7 dynamic-slice_bitcast_fusion.5
  209.1 1.3 collective-permute-done.24
  210.5 0.7 dynamic-slice_bitcast_fusion.4
  211.7 11.0 %all-to-all-done.2 = bf16[16,64,1024]{2,1,0:T(8,128)(2,1)S(1)} async-done(((bf16[16,64,1024]{2,1,0:T(8,128)(2,1)}), bf16[16,64,1024]{2,1,0:T(8,128)(2,1)S(1)}, u32[]{:S(2)}, u32[]{:S(2)}) %all-to-all-start.2) | async-done | bytes 2097184 | tf_op jit(solution)/shard_map/all_to_all | solution.py:510
  223.5 1.7 collective-permute-start.18
  225.2 1.3 collective-permute-start.19
  226.5 0.9 fusion.31
  227.5 1.0 fusion.30
  228.4 1.0 maximum_maximum_fusion
  229.4 6.3 %all-to-all-start.3 = ((bf16[16,24,1024]{2,1,0:T(8,128)(2,1)}), bf16[16,24,1024]{2,1,0:T(8,128)(2,1)S(1)}, u32[]{:S(2)}, u32[]{:S(2)}) async-start(bf16[16,24,1024]{2,1,0:T(8,128)(2,1)} %maximum_maximum_fusion), calls=%async_computation.3 | async-start | bytes 1572864 | tf_op jit(solution)/shard_map/all_to_all | solution.py:528
  235.8 0.6 fusion.40
  239.1 0.6 slice_multiply_fusion.1
  239.7 9.6 %all-to-all-done.3 = bf16[16,24,1024]{2,1,0:T(8,128)(2,1)S(1)} async-done(((bf16[16,24,1024]{2,1,0:T(8,128)(2,1)}), bf16[16,24,1024]{2,1,0:T(8,128)(2,1)S(1)}, u32[]{:S(2)}, u32[]{:S(2)}) %all-to-all-start.3) | async-done | bytes 786464 | tf_op jit(solution)/shard_map/all_to_all | solution.py:528
  249.4 0.6 slice_multiply_fusion
  250.0 0.6 maximum_multiply_fusion
  (119 shorter events, 7.3 us)
Async XLA Ops:
  0.6 59.4 %copy-start = (f32[8,768]{1,0:T(8,128)S(1)}, f32[8,768]{1,0:T(8,128)}, u32[]{:S(2)}) copy-start(f32[8,768]{1,0:T(8,128)} %param.11) | copy-start | bytes 73732
  0.7 1.2 copy-start.2
  1.9 1.2 copy-start.4
  3.1 1.0 copy-start.6
  4.1 3.4 %copy-start.16 = (bf16[4,256,1024]{2,1,0:T(8,128)(2,1)S(1)}, bf16[4,256,1024]{2,1,0:T(8,128)(2,1)}, u32[]{:S(2)}) copy-start(bf16[4,256,1024]{2,1,0:T(8,128)(2,1)} %param.7) | copy-start | bytes 6291460
  4.2 5.0 %copy-start.8 = (bf16[1216,256]{1,0:T(8,128)(2,1)}, bf16[1216,256]{1,0:T(8,128)(2,1)S(1)}, u32[]{:S(2)}) copy-start(bf16[1216,256]{1,0:T(8,128)(2,1)S(1)} %get-tuple-element.75.refs_2_) | copy-start | bytes 1867780
  4.2 4.9 %copy-start.10 = (bf16[1216,256]{1,0:T(8,128)(2,1)}, bf16[1216,256]{1,0:T(8,128)(2,1)S(1)}, u32[]{:S(2)}) copy-start(bf16[1216,256]{1,0:T(8,128)(2,1)S(1)} %get-tuple-element.76.refs_3_) | copy-start | bytes 1867780
  4.2 17.8 %collective-permute-start = (bf16[1216,256]{1,0:T(8,128)(2,1)S(1)}, bf16[1216,256]{1,0:T(8,128)(2,1)}, u32[]{:S(2)}, u32[]{:S(2)}) collective-permute-start(bf16[1216,256]{1,0:T(8,128)(2,1)S(1)} %get-tuple-element.75.refs_2_), channel_id=1, source_target_pairs={{0,1},{1,2},{2,3},{3,0},{4,5},{5,6},{6,7},{7,4},{8,9},{9,10},{10,1... | collective-permute-start | bytes 1867784 | tf_op jit(solution)/shard_map/ppermute | solution.py:26
  5.9 16.1 %collective-permute-start.1 = (bf16[1216,256]{1,0:T(8,128)(2,1)S(1)}, bf16[1216,256]{1,0:T(8,128)(2,1)}, u32[]{:S(2)}, u32[]{:S(2)}) collective-permute-start(bf16[1216,256]{1,0:T(8,128)(2,1)S(1)} %get-tuple-element.76.refs_3_), channel_id=1, source_target_pairs={{0,3},{1,0},{2,1},{3,2},{4,7},{5,4},{6,5},{7,6},{8,11},{9,8},{10,9... | collective-permute-start | bytes 1867784 | tf_op jit(solution)/shard_map/ppermute | solution.py:26
  7.5 1.6 copy-start.3
  7.5 2.3 copy-start.5
  7.5 2.4 copy-start.7
  10.0 0.8 copy-start.12
  10.8 0.8 copy-start.13
  12.9 9.1 %copy-start.11 = (bf16[1216,256]{1,0:T(8,128)(2,1)S(1)}, bf16[1216,256]{1,0:T(8,128)(2,1)}, u32[]{:S(2)}) copy-start(bf16[1216,256]{1,0:T(8,128)(2,1)} %copy-done.10) | copy-start | bytes 1867780
  13.0 10.2 %copy-start.9 = (bf16[1216,256]{1,0:T(8,128)(2,1)S(1)}, bf16[1216,256]{1,0:T(8,128)(2,1)}, u32[]{:S(2)}) copy-start(bf16[1216,256]{1,0:T(8,128)(2,1)} %copy-done.8) | copy-start | bytes 1867780
  22.1 16.7 %collective-permute-start.3 = (bf16[1216,256]{1,0:T(8,128)(2,1)S(1)}, bf16[1216,256]{1,0:T(8,128)(2,1)S(1)}, u32[]{:S(2)}, u32[]{:S(2)}) collective-permute-start(bf16[1216,256]{1,0:T(8,128)(2,1)S(1)} %copy-done.11), channel_id=1, source_target_pairs={{0,1},{1,2},{2,3},{3,0},{4,5},{5,6},{6,7},{7,4},{8,9},{9,10},{10,1... | collective-permute-start | bytes 1867784 | tf_op jit(solution)/shard_map/ppermute | solution.py:26
  23.1 15.7 %collective-permute-start.2 = (bf16[1216,256]{1,0:T(8,128)(2,1)S(1)}, bf16[1216,256]{1,0:T(8,128)(2,1)S(1)}, u32[]{:S(2)}, u32[]{:S(2)}) collective-permute-start(bf16[1216,256]{1,0:T(8,128)(2,1)S(1)} %copy-done.9), channel_id=1, source_target_pairs={{0,3},{1,0},{2,1},{3,2},{4,7},{5,4},{6,5},{7,6},{8,11},{9,8},{10,9... | collective-permute-start | bytes 1867784 | tf_op jit(solution)/shard_map/ppermute | solution.py:26
  25.4 13.4 %collective-permute-start.4 = (bf16[1216,256]{1,0:T(8,128)(2,1)}, bf16[1216,256]{1,0:T(8,128)(2,1)S(1)}, u32[]{:S(2)}, u32[]{:S(2)}) collective-permute-start(bf16[1216,256]{1,0:T(8,128)(2,1)} %collective-permute-done.refs_2_), channel_id=1, source_target_pairs={{0,4},{4,0},{1,5},{5,1},{2,6},{6,2},{3,7},{7,3},{8,12},{12,8},{9,1... | collective-permute-start | bytes 1867784 | tf_op jit(solution)/shard_map/ppermute | solution.py:26
  25.4 13.4 %collective-permute-start.5 = (bf16[1216,256]{1,0:T(8,128)(2,1)}, bf16[1216,256]{1,0:T(8,128)(2,1)S(1)}, u32[]{:S(2)}, u32[]{:S(2)}) collective-permute-start(bf16[1216,256]{1,0:T(8,128)(2,1)} %collective-permute-done.1.refs_7_), channel_id=1, source_target_pairs={{0,4},{4,0},{1,5},{5,1},{2,6},{6,2},{3,7},{7,3},{8,12},{12,8},{9,1... | collective-permute-start | bytes 1867784 | tf_op jit(solution)/shard_map/ppermute | solution.py:26
  38.8 4.5 %copy-start.21 = (bf16[1216,256]{1,0:T(8,128)(2,1)}, bf16[1216,256]{1,0:T(8,128)(2,1)S(1)}, u32[]{:S(2)}) copy-start(bf16[1216,256]{1,0:T(8,128)(2,1)S(1)} %collective-permute-done.3.refs_3_) | copy-start | bytes 1867780
  38.8 4.5 %copy-start.22 = (bf16[1216,256]{1,0:T(8,128)(2,1)}, bf16[1216,256]{1,0:T(8,128)(2,1)S(1)}, u32[]{:S(2)}) copy-start(bf16[1216,256]{1,0:T(8,128)(2,1)S(1)} %collective-permute-done.2.refs_6_) | copy-start | bytes 1867780
  38.8 4.5 %copy-start.23 = (bf16[1216,256]{1,0:T(8,128)(2,1)}, bf16[1216,256]{1,0:T(8,128)(2,1)S(1)}, u32[]{:S(2)}) copy-start(bf16[1216,256]{1,0:T(8,128)(2,1)S(1)} %collective-permute-done.4.refs_4_) | copy-start | bytes 1867780
  38.8 0.9 copy-start.24
  38.8 4.5 %collective-permute-start.8 = (bf16[1216,256]{1,0:T(8,128)(2,1)S(1)}, bf16[1216,256]{1,0:T(8,128)(2,1)}, u32[]{:S(2)}, u32[]{:S(2)}) collective-permute-start(bf16[1216,256]{1,0:T(8,128)(2,1)S(1)} %collective-permute-done.3.refs_3_), channel_id=1, source_target_pairs={{0,4},{4,0},{1,5},{5,1},{2,6},{6,2},{3,7},{7,3},{8,12},{12,8},{9,1... | collective-permute-start | bytes 1867784 | tf_op jit(solution)/shard_map/ppermute | solution.py:26
  38.9 4.4 %collective-permute-start.9 = (bf16[1216,256]{1,0:T(8,128)(2,1)S(1)}, bf16[1216,256]{1,0:T(8,128)(2,1)}, u32[]{:S(2)}, u32[]{:S(2)}) collective-permute-start(bf16[1216,256]{1,0:T(8,128)(2,1)S(1)} %collective-permute-done.2.refs_6_), channel_id=1, source_target_pairs={{0,4},{4,0},{1,5},{5,1},{2,6},{6,2},{3,7},{7,3},{8,12},{12,8},{9,1... | collective-permute-start | bytes 1867784 | tf_op jit(solution)/shard_map/ppermute | solution.py:26
  39.8 19.7 %collective-permute-start.7 = (bf16[1216,256]{1,0:T(8,128)(2,1)}, bf16[1216,256]{1,0:T(8,128)(2,1)S(1)}, u32[]{:S(2)}, u32[]{:S(2)}) collective-permute-start(bf16[1216,256]{1,0:T(8,128)(2,1)} %collective-permute-done.1.refs_7_), channel_id=1, source_target_pairs={{0,3},{1,0},{2,1},{3,2},{4,7},{5,4},{6,5},{7,6},{8,11},{9,8},{10,9... | collective-permute-start | bytes 1867784 | tf_op jit(solution)/shard_map/ppermute | solution.py:26
  42.7 16.8 %collective-permute-start.6 = (bf16[1216,256]{1,0:T(8,128)(2,1)}, bf16[1216,256]{1,0:T(8,128)(2,1)S(1)}, u32[]{:S(2)}, u32[]{:S(2)}) collective-permute-start(bf16[1216,256]{1,0:T(8,128)(2,1)} %collective-permute-done.refs_2_), channel_id=1, source_target_pairs={{0,1},{1,2},{2,3},{3,0},{4,5},{5,6},{6,7},{7,4},{8,9},{9,10},{10,1... | collective-permute-start | bytes 1867784 | tf_op jit(solution)/shard_map/ppermute | solution.py:26
  43.3 16.7 %copy-start.27 = (s32[8]{0:T(128)S(1)}, s32[8]{0:T(128)}, u32[]{:S(2)}) copy-start(s32[8]{0:T(128)} %param.12) | copy-start | bytes 100
  59.4 3.1 %copy-start.19 = (bf16[1216,256]{1,0:T(8,128)(2,1)}, bf16[1216,256]{1,0:T(8,128)(2,1)S(1)}, u32[]{:S(2)}) copy-start(bf16[1216,256]{1,0:T(8,128)(2,1)S(1)} %collective-permute-done.7.refs_3_) | copy-start | bytes 1867780
  59.5 3.0 %copy-start.20 = (bf16[1216,256]{1,0:T(8,128)(2,1)}, bf16[1216,256]{1,0:T(8,128)(2,1)S(1)}, u32[]{:S(2)}) copy-start(bf16[1216,256]{1,0:T(8,128)(2,1)S(1)} %collective-permute-done.6.refs_2_) | copy-start | bytes 1867780
  59.5 2.1 collective-permute-start.10
  59.6 2.9 %collective-permute-start.11 = (bf16[1216,256]{1,0:T(8,128)(2,1)S(1)}, bf16[1216,256]{1,0:T(8,128)(2,1)S(1)}, u32[]{:S(2)}, u32[]{:S(2)}) collective-permute-start(bf16[1216,256]{1,0:T(8,128)(2,1)S(1)} %collective-permute-done.7.refs_3_), channel_id=1, source_target_pairs={{0,4},{4,0},{1,5},{5,1},{2,6},{6,2},{3,7},{7,3},{8,12},{12,8},{9,1... | collective-permute-start | bytes 1867784 | tf_op jit(solution)/shard_map/ppermute | solution.py:26
  61.6 0.9 copy-start.25
  62.5 0.8 copy-start.26
  106.3 0.9 copy-start.28
  111.5 26.4 %copy-start.29 = (bf16[768,1024]{1,0:T(8,128)(2,1)S(1)}, bf16[768,1024]{1,0:T(8,128)(2,1)}, u32[]{:S(2)}) copy-start(bf16[768,1024]{1,0:T(8,128)(2,1)} %get-tuple-element.102) | copy-start | bytes 4718596
  138.0 3.1 %copy-start.14 = (bf16[32,32,768]{2,1,0:T(8,128)(2,1)}, bf16[32,32,768]{2,1,0:T(8,128)(2,1)S(1)}, u32[]{:S(2)}) copy-start(bf16[32,32,768]{2,1,0:T(8,128)(2,1)S(1)} %all_to_all.21) | copy-start | bytes 4718596
  150.5 15.9 %collective-permute-start.12 = (bf16[4,256,1024]{2,1,0:T(8,128)(2,1)}, bf16[4,256,1024]{2,1,0:T(8,128)(2,1)}, u32[]{:S(2)}, u32[]{:S(2)}) collective-permute-start(bf16[4,256,1024]{2,1,0:T(8,128)(2,1)} %get-tuple-element.104), channel_id=1, source_target_pairs={{0,4},{4,0},{1,5},{5,1},{2,6},{6,2},{3,7},{7,3},{8,12},{12,8},{9,1... | collective-permute-start | bytes 6291464 | tf_op jit(solution)/shard_map/ppermute | solution.py:26
  166.4 7.9 %collective-permute-start.13 = (bf16[1,1024,1024]{2,1,0:T(8,128)(2,1)}, bf16[1,1024,1024]{2,1,0:T(8,128)(2,1)S(1)}, u32[]{:S(2)}, u32[]{:S(2)}) collective-permute-start(bf16[1,1024,1024]{2,1,0:T(8,128)(2,1)} %get-tuple-element.111), channel_id=1, source_target_pairs={{0,4},{4,0},{1,5},{5,1},{2,6},{6,2},{3,7},{7,3},{8,12},{12,8},{9,1... | collective-permute-start | bytes 6291464 | tf_op jit(solution)/shard_map/ppermute | solution.py:26
  169.9 4.4 %copy-start.15 = (bf16[1,1024,1024]{2,1,0:T(8,128)(2,1)S(1)}, bf16[1,1024,1024]{2,1,0:T(8,128)(2,1)}, u32[]{:S(2)}) copy-start(bf16[1,1024,1024]{2,1,0:T(8,128)(2,1)} %get-tuple-element.113) | copy-start | bytes 6291460
  169.9 16.2 %collective-permute-start.15 = (bf16[2,8,16,1024]{3,2,0,1:T(8,128)(2,1)S(1)}, bf16[2,8,16,1024]{3,2,0,1:T(8,128)(2,1)}, u32[]{:S(2)}, u32[]{:S(2)}) collective-permute-start(bf16[2,8,16,1024]{3,2,0,1:T(8,128)(2,1)S(1)} %dynamic-slice_bitcast_fusion), channel_id=1, source_target_pairs={{0,3},{3,0},{1,2},{2,1},{4,7},{7,4},{5,6},{6,5},{8,11},{11,8},{9,1... | collective-permute-start | bytes 1572872 | tf_op jit(solution)/shard_map/ppermute | solution.py:345
  174.1 14.2 %collective-permute-start.14 = (bf16[2,8,16,1024]{3,2,1,0:T(8,128)(2,1)S(1)}, bf16[2,8,16,1024]{3,2,1,0:T(8,128)(2,1)}, u32[]{:S(2)}, u32[]{:S(2)}) collective-permute-start(bf16[2,8,16,1024]{3,2,1,0:T(8,128)(2,1)S(1)} %bitcast.142), channel_id=1, source_target_pairs={{0,1},{1,0},{2,3},{3,2},{4,5},{5,4},{6,7},{7,6},{8,9},{9,8},{10,11... | collective-permute-start | bytes 1572872 | tf_op jit(solution)/shard_map/ppermute | solution.py:345
  188.3 7.2 %collective-permute-start.16 = (bf16[1,512,1024]{2,1,0:T(8,128)(2,1)}, bf16[1,512,1024]{2,1,0:T(8,128)(2,1)}, u32[]{:S(2)}, u32[]{:S(2)}) collective-permute-start(bf16[1,512,1024]{2,1,0:T(8,128)(2,1)} %get-tuple-element.118), channel_id=1, source_target_pairs={{0,4},{4,0},{1,5},{5,1},{2,6},{6,2},{3,7},{7,3},{8,12},{12,8},{9,1... | collective-permute-start | bytes 3145736 | tf_op jit(solution)/shard_map/ppermute | solution.py:26
  188.3 34.4 %all-to-all-start.2 = ((bf16[16,64,1024]{2,1,0:T(8,128)(2,1)}), bf16[16,64,1024]{2,1,0:T(8,128)(2,1)S(1)}, u32[]{:S(2)}, u32[]{:S(2)}) async-start(bf16[16,64,1024]{2,1,0:T(8,128)(2,1)} %bitcast.28), calls=%async_computation.2 | async-start | bytes 4194304 | tf_op jit(solution)/shard_map/all_to_all | solution.py:510
  192.0 1.8 copy-start.17
  192.0 3.4 %copy-start.18 = (bf16[1,512,1024]{2,1,0:T(8,128)(2,1)S(1)}, bf16[1,512,1024]{2,1,0:T(8,128)(2,1)}, u32[]{:S(2)}) copy-start(bf16[1,512,1024]{2,1,0:T(8,128)(2,1)} %get-tuple-element.116) | copy-start | bytes 3145732
  193.5 9.2 %collective-permute-start.21 = (bf16[8,16,1024]{2,1,0:T(8,128)(2,1)S(1)}, bf16[8,16,1024]{2,1,0:T(8,128)(2,1)S(1)}, u32[]{:S(2)}, u32[]{:S(2)}) collective-permute-start(bf16[8,16,1024]{2,1,0:T(8,128)(2,1)S(1)} %dynamic-slice_bitcast_fusion.2), channel_id=1, source_target_pairs={{0,1},{1,0},{2,3},{3,2},{4,5},{5,4},{6,7},{7,6},{8,9},{9,8},{10,11... | collective-permute-start | bytes 786440 | tf_op jit(solution)/shard_map/ppermute | solution.py:345
  195.1 10.4 %collective-permute-start.20 = (bf16[8,16,1024]{2,1,0:T(8,128)(2,1)S(1)}, bf16[8,16,1024]{2,1,0:T(8,128)(2,1)S(1)}, u32[]{:S(2)}, u32[]{:S(2)}) collective-permute-start(bf16[8,16,1024]{2,1,0:T(8,128)(2,1)S(1)} %dynamic-slice_bitcast_fusion.3), channel_id=1, source_target_pairs={{0,3},{3,0},{1,2},{2,1},{4,7},{7,4},{5,6},{6,5},{8,11},{11,8},{9,1... | collective-permute-start | bytes 786440 | tf_op jit(solution)/shard_map/ppermute | solution.py:345
  197.2 10.7 %collective-permute-start.22 = (bf16[2,8,8,1024]{3,2,1,0:T(8,128)(2,1)S(1)}, bf16[2,8,8,1024]{3,2,1,0:T(8,128)(2,1)S(1)}, u32[]{:S(2)}, u32[]{:S(2)}) collective-permute-start(bf16[2,8,8,1024]{3,2,1,0:T(8,128)(2,1)S(1)} %bitcast.144), channel_id=1, source_target_pairs={{0,1},{1,0},{2,3},{3,2},{4,5},{5,4},{6,7},{7,6},{8,9},{9,8},{10,11... | collective-permute-start | bytes 786440 | tf_op jit(solution)/shard_map/ppermute | solution.py:345
  198.8 11.7 %collective-permute-start.24 = (bf16[2,8,8,1024]{3,2,0,1:T(8,128)(2,1)S(1)}, bf16[2,8,8,1024]{3,2,0,1:T(8,128)(2,1)S(1)}, u32[]{:S(2)}, u32[]{:S(2)}) collective-permute-start(bf16[2,8,8,1024]{3,2,0,1:T(8,128)(2,1)S(1)} %dynamic-slice_bitcast_fusion.1), channel_id=1, source_target_pairs={{0,3},{3,0},{1,2},{2,1},{4,7},{7,4},{5,6},{6,5},{8,11},{11,8},{9,1... | collective-permute-start | bytes 786440 | tf_op jit(solution)/shard_map/ppermute | solution.py:345
  208.6 17.9 %collective-permute-start.23 = (bf16[8,8,1024]{2,1,0:T(8,128)(2,1)}, bf16[8,8,1024]{2,1,0:T(8,128)(2,1)}, u32[]{:S(2)}, u32[]{:S(2)}) collective-permute-start(bf16[8,8,1024]{2,1,0:T(8,128)(2,1)} %dynamic-slice_bitcast_fusion.5), channel_id=1, source_target_pairs={{0,3},{3,0},{1,2},{2,1},{4,7},{7,4},{5,6},{6,5},{8,11},{11,8},{9,1... | collective-permute-start | bytes 393224 | tf_op jit(solution)/shard_map/ppermute | solution.py:345
  211.2 16.3 %collective-permute-start.25 = (bf16[8,8,1024]{2,1,0:T(8,128)(2,1)}, bf16[8,8,1024]{2,1,0:T(8,128)(2,1)}, u32[]{:S(2)}, u32[]{:S(2)}) collective-permute-start(bf16[8,8,1024]{2,1,0:T(8,128)(2,1)} %dynamic-slice_bitcast_fusion.4), channel_id=1, source_target_pairs={{0,1},{1,0},{2,3},{3,2},{4,5},{5,4},{6,7},{7,6},{8,9},{9,8},{10,11... | collective-permute-start | bytes 393224 | tf_op jit(solution)/shard_map/ppermute | solution.py:345
  223.2 12.5 %collective-permute-start.17 = (f32[1,16,1024]{2,1,0:T(8,128)S(1)}, f32[1,16,1024]{2,1,0:T(8,128)S(1)}, u32[]{:S(2)}, u32[]{:S(2)}) collective-permute-start(f32[1,16,1024]{2,1,0:T(8,128)S(1)} %get-tuple-element.142), channel_id=1, source_target_pairs={{0,1},{1,2},{2,3},{3,0},{4,5},{5,6},{6,7},{7,4},{8,9},{9,10},{10,1... | collective-permute-start | bytes 196616 | tf_op jit(solution)/shard_map/ppermute | solution.py:26
  223.5 12.1 %collective-permute-start.18 = (f32[1,16,1024]{2,1,0:T(8,128)S(1)}, f32[1,16,1024]{2,1,0:T(8,128)S(1)}, u32[]{:S(2)}, u32[]{:S(2)}) collective-permute-start(f32[1,16,1024]{2,1,0:T(8,128)S(1)} %get-tuple-element.144), channel_id=1, source_target_pairs={{0,2},{1,3},{2,0},{3,1},{4,6},{5,7},{6,4},{7,5},{8,10},{9,11},{10,... | collective-permute-start | bytes 196616 | tf_op jit(solution)/shard_map/ppermute | solution.py:26
  225.2 10.4 %collective-permute-start.19 = (f32[1,16,1024]{2,1,0:T(8,128)S(1)}, f32[1,16,1024]{2,1,0:T(8,128)S(1)}, u32[]{:S(2)}, u32[]{:S(2)}) collective-permute-start(f32[1,16,1024]{2,1,0:T(8,128)S(1)} %get-tuple-element.143), channel_id=1, source_target_pairs={{0,3},{1,0},{2,1},{3,2},{4,7},{5,4},{6,5},{7,6},{8,11},{9,8},{10,9... | collective-permute-start | bytes 196616 | tf_op jit(solution)/shard_map/ppermute | solution.py:26
  227.5 23.2 %copy-start.1 = (f32[8,768]{1,0:T(8,128)S(1)}, f32[8,768]{1,0:T(8,128)}, u32[]{:S(2)}) copy-start(f32[8,768]{1,0:T(8,128)} %param.11) | copy-start | bytes 73732
  229.4 19.9 %all-to-all-start.3 = ((bf16[16,24,1024]{2,1,0:T(8,128)(2,1)}), bf16[16,24,1024]{2,1,0:T(8,128)(2,1)S(1)}, u32[]{:S(2)}, u32[]{:S(2)}) async-start(bf16[16,24,1024]{2,1,0:T(8,128)(2,1)} %maximum_maximum_fusion), calls=%async_computation.3 | async-start | bytes 1572864 | tf_op jit(solution)/shard_map/all_to_all | solution.py:528

commit v12 on v10

--- a/solution.py
+++ b/solution.py
@@ -299,6 +299,36 @@
     )(place, resid_grad, second, slope, tokens)
 
 
+def finish_kernel(arrived, half, first, second, head, loss):
+    total = jnp.sum(arrived[...].astype(F32), 0)
+    n, width = half.shape
+    out_width = head.shape[1]
+    lines = second.shape[0]
+    ride = total[lines : lines + n, out_width:]
+    line = lax.broadcasted_iota(jnp.int32, ride.shape, 0)
+    score = jnp.sum(jnp.where(line < 3, ride, 0.0), axis=(0, 1), keepdims=True)
+    count = jnp.sum(jnp.where(line == 3, ride, 0.0), axis=(0, 1), keepdims=True)
+    valid = jnp.maximum(count, 1.0)
+    scale = 1.0 / valid
+    first[:, :width] = half[...] * scale
+    first[:, width:] = total[lines + n :] * scale
+    second[...] = total[:lines] * scale
+    head[...] = total[lines : lines + n, :out_width] * scale
+    loss[...] = score / valid
+
+
+def finish(arrived, half, out_width):
+    n, width = half.shape
+    shapes = [(n, 2 * width), (arrived.shape[1] - 2 * n, width), (n, out_width), (1, 1)]
+    first, second, head, loss = pl.pallas_call(
+        finish_kernel,
+        out_shape=[jax.ShapeDtypeStruct(v, F32) for v in shapes],
+        compiler_params=pltpu.CompilerParams(vmem_limit_bytes=8 * MIB),
+        name="finish",
+    )(arrived, half)
+    return first, second, head, loss[0, 0]
+
+
 def add(a, b):
     return (a.astype(F32) + b.astype(F32)).astype(BF16)
 
@@ -501,19 +531,7 @@
     b = [kept_plus(x, v, s[1]) for x, v, s in zip(b, b_in, steps)]
     early = jnp.concatenate([jnp.concatenate(early), jnp.concatenate(b)], 1)
     early = lax.all_to_all(early, group, 0, 0, tiled=True)
-    early = jnp.sum(early.astype(F32), 0)
-    early, b = early[:-n], early[-n:]
-    n_second = shard * RING // 128
-    ride = jnp.sum(early[n_second:, out_width:], 1)
-    score_total = ride[0] + ride[1] + ride[2]
-    valid_total = jnp.maximum(ride[3], 1.0)
-    scale = 1.0 / valid_total
-    return (
-        jnp.concatenate([first[0], b], 1) * scale,
-        early[:n_second] * scale,
-        early[n_second:, :out_width] * scale,
-        score_total / valid_total,
-    )
+    return finish(early, first[0], out_width)
 
 
 def solution(mesh):

time: 252 us -> 246 us (0.976)
  between operations: 5.05 us -> 1.28 us
  other arithmetic: 14.9 us -> 11.5 us
    unnamed x66 -> x68, local copies, waits for them, and re-layouts: 9.48 us -> 8.1 us
    convert_element_type x11 -> x10, other arithmetic: 6.78 us -> 5.62 us  [add(): return (a.astype(F32) + b.astype(F32)).astype(BF16)]
  transfers between devices with their start and end apart: 29 -> 29, of which waited for: 17 -> 15; matrix products, arithmetic and copies ran while one was open for 6% -> 6% of each run, Pallas kernels for 18% -> 18%
where the time goes in v12:
time: 246 us; the launch traced here: 245 us
  waiting for transfers between devices  70.4 us (29%)
  Pallas kernels  68.9 us (28%)
  starting transfers between devices  40.9 us (17%)
  blocking collectives  30.5 us (12%)
  local copies, waits for them, and re-layouts  14.3 us (6%)
  other arithmetic  11.5 us (5%)
  matrix products  6.82 us (3%)
    pallas_call x3, Pallas kernels, forward_part(): pl.pallas_call(functools.partial(forward_kernel, groups, first_call, last...  36.4 us
    all_to_all x1, blocking collectives, per_device(): gathered = lax.all_to_all(forecast, group, 0, 0, tiled=True)  30.5 us
    ppermute x8, waiting for transfers between devices, sent_along(): return lax.ppermute(x, step[1], step[0])  23.8 us
    all_to_all x1, waiting for transfers between devices, per_device(): lax.all_to_all(grad_raw.reshape(32, members * own, out_width), group, 0,...  21.2 us
    pallas_call x2, Pallas kernels, late_grads(): pl.pallas_call(functools.partial(late_kernel, part == 1), grid_spec=pltpu...  19.4 us
    ppermute x18, waiting for transfers between devices, shift(): return lax.ppermute(x, axis, [(i, (i + by) % size) for i in range(size)])  18 us
    ppermute x18, starting transfers between devices, shift(): return lax.ppermute(x, axis, [(i, (i + by) % size) for i in range(size)])  15.9 us
    pallas_call x1, Pallas kernels, early_grads(): pl.pallas_call(early_kernel, grid_spec=pltpu.PrefetchScalarGridSpec(num_s...  12 us
  transfers between devices with their start and end apart: 29, of which 15 were waited for; matrix products, arithmetic and copies ran while one was open for 6% of the time, Pallas kernels for 18%

profile of v12, /device:TPU:0, one launch (start us, length us, event | category | flops | bytes accessed | tf_op | source)
XLA Modules:
  0.0 244.6 jit_solution(16117007974182540233)
XLA Ops:
  0.7 1.2 copy-done.2
  1.9 1.2 copy-done.4
  3.1 1.0 copy-done.6
  4.2 1.7 collective-permute-start
  5.9 1.6 collective-permute-start.1
  7.5 1.6 copy.20
  9.1 0.7 copy-done.5
  10.0 0.8 copy-done.12
  10.8 0.8 copy-done.13
  11.6 0.6 pad_add_fusion.2
  12.2 0.6 pad_add_fusion.refs_0_.place
  12.8 9.1 %forward_part.3 = (bf16[1024,2048]{1,0:T(8,128)(2,1)}, bf16[1024,2048]{1,0:T(8,128)(2,1)}, bf16[2048,1024]{1,0:T(8,128)(2,1)}, bf16[768,1024]{1,0:T(8,128)(2,1)}, f32[1024,1024]{1,0:T(8,128)}) custom-call(s32[4]{0:T(128)} %pad_add_fusion.refs_0_.place, bf16[1024,1024]{1,0:T(8,128)(2,1)} %bitcast.118, bf16[1216,256]{1,0:T(8,128)(2,1)} %copy-done.8, ...), custom_call_target="tpu_custom_call" | custom-call | flops 2147483648 | bytes 12582912 | tf_op jit(solution)/shard_map/forward_part/pallas_call | solution.py:166
  21.9 1.2 collective-permute-start.3
  23.1 2.1 collective-permute-start.2
  25.2 0.5 collective-permute-start.5
  25.7 12.9 %collective-permute-done.3.refs_3_ = bf16[1216,256]{1,0:T(8,128)(2,1)S(1)} collective-permute-done((bf16[1216,256]{1,0:T(8,128)(2,1)S(1)}, bf16[1216,256]{1,0:T(8,128)(2,1)S(1)}, u32[]{:S(2)}, u32[]{:S(2)}) %collective-permute-start.3) | collective-permute-done | bytes 622624 | tf_op jit(solution)/shard_map/ppermute | solution.py:26
  38.7 0.5 collective-permute-start.9
  39.5 2.9 %collective-permute-start.7 = (bf16[1216,256]{1,0:T(8,128)(2,1)}, bf16[1216,256]{1,0:T(8,128)(2,1)S(1)}, u32[]{:S(2)}, u32[]{:S(2)}) collective-permute-start(bf16[1216,256]{1,0:T(8,128)(2,1)} %collective-permute-done.1.refs_7_), channel_id=1, source_target_pairs={{0,3},{1,0},{2,1},{3,2},{4,7},{5,4},{6,5},{7,6},{8,11},{9,8},{10,9... | collective-permute-start | bytes 1867784 | tf_op jit(solution)/shard_map/ppermute | solution.py:26
  42.4 0.7 stack.59.refs_0_
  43.2 16.2 %forward_part.4 = (bf16[1024,2048]{1,0:T(8,128)(2,1)}, bf16[1024,2048]{1,0:T(8,128)(2,1)}, bf16[2048,1024]{1,0:T(8,128)(2,1)}, bf16[768,1024]{1,0:T(8,128)(2,1)}, f32[1024,1024]{1,0:T(8,128)}) custom-call(s32[5]{0:T(128)} %stack.59.refs_0_, ...), custom_call_target="tpu_custom_call", output_to_operand_aliasing={{0}: (11, {}), {1}: (12, {}), {2}: (13, {}), {3}: (14, {})} | custom-call | flops 4294967296 | bytes 12582912 | tf_op jit(solution)/shard_map/forward_part/pallas_call | solution.py:166
  59.5 0.5 collective-permute-start.11
  60.1 0.6 gather_fusion
  60.7 0.9 collective-permute-done.10.refs_4_
  61.6 0.9 collective-permute-done.11.refs_5_
  62.5 0.8 copy-done.28
  63.3 11.1 %forward_part.5 = (bf16[1024,2048]{1,0:T(8,128)(2,1)}, bf16[1024,2048]{1,0:T(8,128)(2,1)}, bf16[2048,1024]{1,0:T(8,128)(2,1)}, bf16[768,1024]{1,0:T(8,128)(2,1)}...) custom-call(s32[4]{0:T(128)} %get-tuple-element.140.refs_0_, ...), custom_call_target="tpu_custom_call", output_to_operand_aliasing={{0}: (7, {}), {1}: (8, {}), {2}: (9, {})} | custom-call | flops 2147483648 | bytes 12582912 | tf_op jit(solution)/shard_map/forward_part/pallas_call | solution.py:166
  74.4 30.5 %all_to_all.20 = bf16[32,32,768]{2,1,0:T(8,128)(2,1)S(1)} all-to-all(bf16[32,32,768]{2,1,0:T(8,128)(2,1)} %bitcast.133), channel_id=1, replica_groups=mesh['x'=4,'z'=4,'c'=2,'y'=4] {'x','z','c'}, dimensions={0} | all-to-all | bytes 3145728 | tf_op jit(solution)/shard_map/all_to_all | solution.py:492
  105.2 0.8 fusion.6
  106.3 0.9 fusion.37
  107.2 0.6 multiply_reduce_fusion
  107.8 2.8 %fusion.8 = bf16[128,8,768]{2,0,1:T(8,128)(2,1)S(1)} fusion(f32[128,8]{0,1:T(8,128)S(1)} %bitcast.141, f32[128,8]{0,1:T(8,128)S(1)} %copy.23, f32[8,768]{1,0:T(8,128)S(1)} %broadcast_select_fusion, f32[8]{0:T(128)S(1)} %get-tuple-element.159, bf16[128,8,768]{2,1,0:T(8,128)(2,1)S(1)} %bitcast.125, f32[8,128,128]{1,2,0:T(8,128)S(1)} %get-tuple-element.160), kind=kOutput, calls=%fused_computation.14 | convolution fusion | flops 1215168512 | bytes 3702816 | tf_op jit(solution)/shard_map/pmn,npo->mpo/dot_general | solution.py:429
  110.6 2.0 copy.30
  112.6 4.2 %all-to-all-start.1 = ((bf16[32,32,768]{2,1,0:T(8,128)(2,1)}), bf16[32,32,768]{2,1,0:T(8,128)(2,1)S(1)}, u32[]{:S(2)}, u32[]{:S(2)}) async-start(bf16[32,32,768]{2,1,0:T(8,128)(2,1)} %bitcast.18), calls=%async_computation.1 | async-start | bytes 3145728 | tf_op jit(solution)/shard_map/all_to_all | solution.py:495
  116.9 1.9 pad_maximum_fusion.scalars
  118.8 21.2 %all-to-all-done.1 = bf16[32,32,768]{2,1,0:T(8,128)(2,1)S(1)} async-done(((bf16[32,32,768]{2,1,0:T(8,128)(2,1)}), bf16[32,32,768]{2,1,0:T(8,128)(2,1)S(1)}, u32[]{:S(2)}, u32[]{:S(2)}) %all-to-all-start.1) | async-done | bytes 1572896 | tf_op jit(solution)/shard_map/all_to_all | solution.py:495
  140.0 3.1 %convolution_convert_fusion.resid_grad = bf16[1024,1024]{1,0:T(8,128)(2,1)} fusion(bf16[1024,768]{1,0:T(8,128)(2,1)S(1)} %bitcast.131, bf16[768,1024]{1,0:T(8,128)(2,1)S(1)} %copy-done.31), kind=kOutput, calls=%fused_computation.18 | convolution fusion | flops 1611661312 | bytes 5242880 | tf_op jit(solution)/shard_map/dot_general | solution.py:30
  143.1 12.0 %early_grads.1 = (bf16[4,384,1024]{2,1,0:T(8,128)(2,1)}, bf16[4,384,1024]{2,1,0:T(8,128)(2,1)}) custom-call(s32[4]{0:T(128)} %pad_add_fusion.refs_0_.place, bf16[1024,2048]{1,0:T(8,128)(2,1)} %get-tuple-element.103.hidden, bf16[1024,1024]{1,0:T(8,128)(2,1)} %convolution_convert_fusion.resid_grad, bf16[1024,1024]{1,0:T(8,128)(2,1)} %get-tuple-element.108.residual, ...), custom_call_target="tpu_custom_call" | custom-call | flops 5905580032 | bytes 18874368 | tf_op jit(solution)/shard_map/early_grads/pallas_call | solution.py:241
  155.2 9.8 %late_grads.2 = (bf16[1,512,1024]{2,1,0:T(8,128)(2,1)}, bf16[1,512,1024]{2,1,0:T(8,128)(2,1)}) custom-call(s32[4]{0:T(128)} %pad_add_fusion.refs_0_.place, bf16[1024,1024]{1,0:T(8,128)(2,1)} %convolution_convert_fusion.resid_grad, bf16[2048,1024]{1,0:T(8,128)(2,1)} %get-tuple-element.112.second, bf16[1024,2048]{1,0:T(8,128)(2,1)} %get-tuple-element.113.slope, ...), custom_call_target="tpu_custom_call" | custom-call | flops 4294967296 | bytes 12582912 | tf_op jit(solution)/shard_map/late_grads/pallas_call | solution.py:280
  165.5 1.6 add_convert_fusion
  167.6 3.3 %collective-permute-start.16 = (bf16[2,8,24,1024]{3,2,1,0:T(8,128)(2,1)S(1)}, bf16[2,8,24,1024]{3,2,1,0:T(8,128)(2,1)S(1)}, u32[]{:S(2)}, u32[]{:S(2)}) collective-permute-start(bf16[2,8,24,1024]{3,2,1,0:T(8,128)(2,1)S(1)} %bitcast.134), channel_id=1, source_target_pairs={{0,3},{3,0},{1,2},{2,1},{4,7},{7,4},{5,6},{6,5},{8,11},{11,8},{9,1... | collective-permute-start | bytes 2359304 | tf_op jit(solution)/shard_map/ppermute | solution.py:360
  171.3 0.9 copy-done.18
  172.2 1.4 add_convert_fusion.2
  173.6 9.6 %late_grads.3 = (bf16[1,512,1024]{2,1,0:T(8,128)(2,1)}, bf16[1,512,1024]{2,1,0:T(8,128)(2,1)}) custom-call(s32[4]{0:T(128)} %pad_add_fusion.refs_0_.place, bf16[1024,1024]{1,0:T(8,128)(2,1)} %convolution_convert_fusion.resid_grad, bf16[2048,1024]{1,0:T(8,128)(2,1)} %get-tuple-element.112.second, bf16[1024,2048]{1,0:T(8,128)(2,1)} %get-tuple-element.113.slope, ...), custom_call_target="tpu_custom_call" | custom-call | flops 4294967296 | bytes 12582912 | tf_op jit(solution)/shard_map/late_grads/pallas_call | solution.py:280
  183.1 5.6 %collective-permute-done.16 = bf16[2,8,24,1024]{3,2,1,0:T(8,128)(2,1)S(1)} collective-permute-done((bf16[2,8,24,1024]{3,2,1,0:T(8,128)(2,1)S(1)}, bf16[2,8,24,1024]{3,2,1,0:T(8,128)(2,1)S(1)}, u32[]{:S(2)}, u32[]{:S(2)}) %collective-permute-start.16) | collective-permute-done | bytes 786464 | tf_op jit(solution)/shard_map/ppermute | solution.py:360
  188.7 1.8 collective-permute-done.13
  190.5 3.7 %all-to-all-start.3 = ((bf16[16,32,1024]{2,1,0:T(8,128)(2,1)}), bf16[16,32,1024]{2,1,0:T(8,128)(2,1)S(1)}, u32[]{:S(2)}, u32[]{:S(2)}) async-start(bf16[16,32,1024]{2,1,0:T(8,128)(2,1)} %bitcast.33), calls=%async_computation.3 | async-start | bytes 2097152 | tf_op jit(solution)/shard_map/all_to_all | solution.py:515
  194.5 2.2 collective-permute-start.14
  197.2 1.5 add_convert_fusion.1
  198.9 2.1 collective-permute-start.19
  201.0 1.2 collective-permute-start.21
  202.2 5.6 %collective-permute-done.14 = bf16[8,24,1024]{2,1,0:T(8,128)(2,1)S(1)} collective-permute-done((bf16[8,24,1024]{2,1,0:T(8,128)(2,1)S(1)}, bf16[8,24,1024]{2,1,0:T(8,128)(2,1)S(1)}, u32[]{:S(2)}, u32[]{:S(2)}) %collective-permute-start.14) | collective-permute-done | bytes 393248 | tf_op jit(solution)/shard_map/ppermute | solution.py:360
  207.7 1.3 collective-permute-done.18
  209.4 4.6 %collective-permute-done.19 = bf16[2,8,8,1024]{3,2,1,0:T(8,128)(2,1)S(1)} collective-permute-done((bf16[2,8,8,1024]{3,2,1,0:T(8,128)(2,1)S(1)}, bf16[2,8,8,1024]{3,2,1,0:T(8,128)(2,1)S(1)}, u32[]{:S(2)}, u32[]{:S(2)}) %collective-permute-start.19) | collective-permute-done | bytes 262176 | tf_op jit(solution)/shard_map/ppermute | solution.py:360
  214.1 1.2 collective-permute-start.20
  215.5 4.8 %collective-permute-done.20 = bf16[8,8,1024]{2,1,0:T(8,128)(2,1)S(1)} collective-permute-done((bf16[8,8,1024]{2,1,0:T(8,128)(2,1)S(1)}, bf16[8,8,1024]{2,1,0:T(8,128)(2,1)S(1)}, u32[]{:S(2)}, u32[]{:S(2)}) %collective-permute-start.20) | collective-permute-done | bytes 131104 | tf_op jit(solution)/shard_map/ppermute | solution.py:360
  220.5 1.1 maximum_maximum_fusion
  221.7 6.9 %all-to-all-start.2 = ((bf16[16,32,1024]{2,1,0:T(8,128)(2,1)}), bf16[16,32,1024]{2,1,0:T(8,128)(2,1)S(1)}, u32[]{:S(2)}, u32[]{:S(2)}) async-start(bf16[16,32,1024]{2,1,0:T(8,128)(2,1)} %maximum_maximum_fusion), calls=%async_computation.2 | async-start | bytes 2097152 | tf_op jit(solution)/shard_map/all_to_all | solution.py:533
  228.9 3.5 %collective-permute-start.24 = (f32[1,8,1024]{2,1,0:T(8,128)S(1)}, f32[1,8,1024]{2,1,0:T(8,128)S(1)}, u32[]{:S(2)}, u32[]{:S(2)}) collective-permute-start(f32[1,8,1024]{2,1,0:T(8,128)S(1)} %get-tuple-element.156), channel_id=1, source_target_pairs={{0,2},{1,3},{2,0},{3,1},{4,6},{5,7},{6,4},{7,5},{8,10},{9,11},{10,... | collective-permute-start | bytes 98312 | tf_op jit(solution)/shard_map/ppermute | solution.py:26
  232.4 0.6 collective-permute-start.25
  233.0 1.0 collective-permute-done.23
  234.0 0.7 collective-permute-done.24
  234.6 1.7 collective-permute-done.25
  236.3 7.4 %all-to-all-done.2.arrived = bf16[16,32,1024]{2,1,0:T(8,128)(2,1)S(1)} async-done(((bf16[16,32,1024]{2,1,0:T(8,128)(2,1)}), bf16[16,32,1024]{2,1,0:T(8,128)(2,1)S(1)}, u32[]{:S(2)}, u32[]{:S(2)}) %all-to-all-start.2) | async-done | bytes 1048608 | tf_op jit(solution)/shard_map/all_to_all | solution.py:533
  243.7 0.8 finish.1
  (118 shorter events, 4.7 us)
Async XLA Ops:
  0.6 59.4 %copy-start = (f32[8,768]{1,0:T(8,128)S(1)}, f32[8,768]{1,0:T(8,128)}, u32[]{:S(2)}) copy-start(f32[8,768]{1,0:T(8,128)} %param.11) | copy-start | bytes 73732
  0.7 1.2 copy-start.2
  1.9 1.2 copy-start.4
  3.1 1.0 copy-start.6
  4.1 3.4 %copy-start.15 = (bf16[4,256,1024]{2,1,0:T(8,128)(2,1)S(1)}, bf16[4,256,1024]{2,1,0:T(8,128)(2,1)}, u32[]{:S(2)}) copy-start(bf16[4,256,1024]{2,1,0:T(8,128)(2,1)} %param.7) | copy-start | bytes 6291460
  4.2 4.9 %copy-start.8 = (bf16[1216,256]{1,0:T(8,128)(2,1)}, bf16[1216,256]{1,0:T(8,128)(2,1)S(1)}, u32[]{:S(2)}) copy-start(bf16[1216,256]{1,0:T(8,128)(2,1)S(1)} %get-tuple-element.79.refs_2_) | copy-start | bytes 1867780
  4.2 4.9 %copy-start.10 = (bf16[1216,256]{1,0:T(8,128)(2,1)}, bf16[1216,256]{1,0:T(8,128)(2,1)S(1)}, u32[]{:S(2)}) copy-start(bf16[1216,256]{1,0:T(8,128)(2,1)S(1)} %get-tuple-element.80.refs_3_) | copy-start | bytes 1867780
  4.2 17.7 %collective-permute-start = (bf16[1216,256]{1,0:T(8,128)(2,1)S(1)}, bf16[1216,256]{1,0:T(8,128)(2,1)}, u32[]{:S(2)}, u32[]{:S(2)}) collective-permute-start(bf16[1216,256]{1,0:T(8,128)(2,1)S(1)} %get-tuple-element.79.refs_2_), channel_id=1, source_target_pairs={{0,1},{1,2},{2,3},{3,0},{4,5},{5,6},{6,7},{7,4},{8,9},{9,10},{10,1... | collective-permute-start | bytes 1867784 | tf_op jit(solution)/shard_map/ppermute | solution.py:26
  5.9 15.9 %collective-permute-start.1 = (bf16[1216,256]{1,0:T(8,128)(2,1)S(1)}, bf16[1216,256]{1,0:T(8,128)(2,1)}, u32[]{:S(2)}, u32[]{:S(2)}) collective-permute-start(bf16[1216,256]{1,0:T(8,128)(2,1)S(1)} %get-tuple-element.80.refs_3_), channel_id=1, source_target_pairs={{0,3},{1,0},{2,1},{3,2},{4,7},{5,4},{6,5},{7,6},{8,11},{9,8},{10,9... | collective-permute-start | bytes 1867784 | tf_op jit(solution)/shard_map/ppermute | solution.py:26
  7.5 1.6 copy-start.3
  7.5 2.3 copy-start.5
  7.5 2.4 copy-start.7
  10.0 0.8 copy-start.12
  10.8 0.8 copy-start.13
  12.8 9.1 %copy-start.11 = (bf16[1216,256]{1,0:T(8,128)(2,1)S(1)}, bf16[1216,256]{1,0:T(8,128)(2,1)}, u32[]{:S(2)}) copy-start(bf16[1216,256]{1,0:T(8,128)(2,1)} %copy-done.10) | copy-start | bytes 1867780
  12.8 10.3 %copy-start.9 = (bf16[1216,256]{1,0:T(8,128)(2,1)S(1)}, bf16[1216,256]{1,0:T(8,128)(2,1)}, u32[]{:S(2)}) copy-start(bf16[1216,256]{1,0:T(8,128)(2,1)} %copy-done.8) | copy-start | bytes 1867780
  21.9 16.7 %collective-permute-start.3 = (bf16[1216,256]{1,0:T(8,128)(2,1)S(1)}, bf16[1216,256]{1,0:T(8,128)(2,1)S(1)}, u32[]{:S(2)}, u32[]{:S(2)}) collective-permute-start(bf16[1216,256]{1,0:T(8,128)(2,1)S(1)} %copy-done.11), channel_id=1, source_target_pairs={{0,1},{1,2},{2,3},{3,0},{4,5},{5,6},{6,7},{7,4},{8,9},{9,10},{10,1... | collective-permute-start | bytes 1867784 | tf_op jit(solution)/shard_map/ppermute | solution.py:26
  23.1 15.5 %collective-permute-start.2 = (bf16[1216,256]{1,0:T(8,128)(2,1)S(1)}, bf16[1216,256]{1,0:T(8,128)(2,1)S(1)}, u32[]{:S(2)}, u32[]{:S(2)}) collective-permute-start(bf16[1216,256]{1,0:T(8,128)(2,1)S(1)} %copy-done.9), channel_id=1, source_target_pairs={{0,3},{1,0},{2,1},{3,2},{4,7},{5,4},{6,5},{7,6},{8,11},{9,8},{10,9... | collective-permute-start | bytes 1867784 | tf_op jit(solution)/shard_map/ppermute | solution.py:26
  25.2 13.4 %collective-permute-start.4 = (bf16[1216,256]{1,0:T(8,128)(2,1)}, bf16[1216,256]{1,0:T(8,128)(2,1)S(1)}, u32[]{:S(2)}, u32[]{:S(2)}) collective-permute-start(bf16[1216,256]{1,0:T(8,128)(2,1)} %collective-permute-done.refs_2_), channel_id=1, source_target_pairs={{0,4},{4,0},{1,5},{5,1},{2,6},{6,2},{3,7},{7,3},{8,12},{12,8},{9,1... | collective-permute-start | bytes 1867784 | tf_op jit(solution)/shard_map/ppermute | solution.py:26
  25.2 13.4 %collective-permute-start.5 = (bf16[1216,256]{1,0:T(8,128)(2,1)}, bf16[1216,256]{1,0:T(8,128)(2,1)S(1)}, u32[]{:S(2)}, u32[]{:S(2)}) collective-permute-start(bf16[1216,256]{1,0:T(8,128)(2,1)} %collective-permute-done.1.refs_7_), channel_id=1, source_target_pairs={{0,4},{4,0},{1,5},{5,1},{2,6},{6,2},{3,7},{7,3},{8,12},{12,8},{9,1... | collective-permute-start | bytes 1867784 | tf_op jit(solution)/shard_map/ppermute | solution.py:26
  38.6 4.5 %copy-start.23 = (bf16[1216,256]{1,0:T(8,128)(2,1)}, bf16[1216,256]{1,0:T(8,128)(2,1)S(1)}, u32[]{:S(2)}) copy-start(bf16[1216,256]{1,0:T(8,128)(2,1)S(1)} %collective-permute-done.3.refs_3_) | copy-start | bytes 1867780
  38.6 4.5 %copy-start.24 = (bf16[1216,256]{1,0:T(8,128)(2,1)}, bf16[1216,256]{1,0:T(8,128)(2,1)S(1)}, u32[]{:S(2)}) copy-start(bf16[1216,256]{1,0:T(8,128)(2,1)S(1)} %collective-permute-done.2.refs_6_) | copy-start | bytes 1867780
  38.6 4.5 %copy-start.25 = (bf16[1216,256]{1,0:T(8,128)(2,1)}, bf16[1216,256]{1,0:T(8,128)(2,1)S(1)}, u32[]{:S(2)}) copy-start(bf16[1216,256]{1,0:T(8,128)(2,1)S(1)} %collective-permute-done.4.refs_4_) | copy-start | bytes 1867780
  38.6 0.9 copy-start.26
  38.6 4.5 %collective-permute-start.8 = (bf16[1216,256]{1,0:T(8,128)(2,1)S(1)}, bf16[1216,256]{1,0:T(8,128)(2,1)}, u32[]{:S(2)}, u32[]{:S(2)}) collective-permute-start(bf16[1216,256]{1,0:T(8,128)(2,1)S(1)} %collective-permute-done.3.refs_3_), channel_id=1, source_target_pairs={{0,4},{4,0},{1,5},{5,1},{2,6},{6,2},{3,7},{7,3},{8,12},{12,8},{9,1... | collective-permute-start | bytes 1867784 | tf_op jit(solution)/shard_map/ppermute | solution.py:26
  38.7 4.4 %collective-permute-start.9 = (bf16[1216,256]{1,0:T(8,128)(2,1)S(1)}, bf16[1216,256]{1,0:T(8,128)(2,1)}, u32[]{:S(2)}, u32[]{:S(2)}) collective-permute-start(bf16[1216,256]{1,0:T(8,128)(2,1)S(1)} %collective-permute-done.2.refs_6_), channel_id=1, source_target_pairs={{0,4},{4,0},{1,5},{5,1},{2,6},{6,2},{3,7},{7,3},{8,12},{12,8},{9,1... | collective-permute-start | bytes 1867784 | tf_op jit(solution)/shard_map/ppermute | solution.py:26
  39.5 19.9 %collective-permute-start.7 = (bf16[1216,256]{1,0:T(8,128)(2,1)}, bf16[1216,256]{1,0:T(8,128)(2,1)S(1)}, u32[]{:S(2)}, u32[]{:S(2)}) collective-permute-start(bf16[1216,256]{1,0:T(8,128)(2,1)} %collective-permute-done.1.refs_7_), channel_id=1, source_target_pairs={{0,3},{1,0},{2,1},{3,2},{4,7},{5,4},{6,5},{7,6},{8,11},{9,8},{10,9... | collective-permute-start | bytes 1867784 | tf_op jit(solution)/shard_map/ppermute | solution.py:26
  42.4 17.0 %collective-permute-start.6 = (bf16[1216,256]{1,0:T(8,128)(2,1)}, bf16[1216,256]{1,0:T(8,128)(2,1)S(1)}, u32[]{:S(2)}, u32[]{:S(2)}) collective-permute-start(bf16[1216,256]{1,0:T(8,128)(2,1)} %collective-permute-done.refs_2_), channel_id=1, source_target_pairs={{0,1},{1,2},{2,3},{3,0},{4,5},{5,6},{6,7},{7,4},{8,9},{9,10},{10,1... | collective-permute-start | bytes 1867784 | tf_op jit(solution)/shard_map/ppermute | solution.py:26
  43.1 16.9 %copy-start.29 = (s32[8]{0:T(128)S(1)}, s32[8]{0:T(128)}, u32[]{:S(2)}) copy-start(s32[8]{0:T(128)} %param.12) | copy-start | bytes 100
  59.4 3.1 %copy-start.21 = (bf16[1216,256]{1,0:T(8,128)(2,1)}, bf16[1216,256]{1,0:T(8,128)(2,1)S(1)}, u32[]{:S(2)}) copy-start(bf16[1216,256]{1,0:T(8,128)(2,1)S(1)} %collective-permute-done.7.refs_3_) | copy-start | bytes 1867780
  59.4 3.0 %copy-start.22 = (bf16[1216,256]{1,0:T(8,128)(2,1)}, bf16[1216,256]{1,0:T(8,128)(2,1)S(1)}, u32[]{:S(2)}) copy-start(bf16[1216,256]{1,0:T(8,128)(2,1)S(1)} %collective-permute-done.6.refs_2_) | copy-start | bytes 1867780
  59.4 2.1 collective-permute-start.10
  59.5 2.9 %collective-permute-start.11 = (bf16[1216,256]{1,0:T(8,128)(2,1)S(1)}, bf16[1216,256]{1,0:T(8,128)(2,1)S(1)}, u32[]{:S(2)}, u32[]{:S(2)}) collective-permute-start(bf16[1216,256]{1,0:T(8,128)(2,1)S(1)} %collective-permute-done.7.refs_3_), channel_id=1, source_target_pairs={{0,4},{4,0},{1,5},{5,1},{2,6},{6,2},{3,7},{7,3},{8,12},{12,8},{9,1... | collective-permute-start | bytes 1867784 | tf_op jit(solution)/shard_map/ppermute | solution.py:26
  61.6 0.9 copy-start.27
  62.4 0.8 copy-start.28
  106.3 1.0 copy-start.30
  112.6 27.4 %copy-start.31 = (bf16[768,1024]{1,0:T(8,128)(2,1)S(1)}, bf16[768,1024]{1,0:T(8,128)(2,1)}, u32[]{:S(2)}) copy-start(bf16[768,1024]{1,0:T(8,128)(2,1)} %get-tuple-element.107) | copy-start | bytes 4718596
  112.6 27.4 %all-to-all-start.1 = ((bf16[32,32,768]{2,1,0:T(8,128)(2,1)}), bf16[32,32,768]{2,1,0:T(8,128)(2,1)S(1)}, u32[]{:S(2)}, u32[]{:S(2)}) async-start(bf16[32,32,768]{2,1,0:T(8,128)(2,1)} %bitcast.18), calls=%async_computation.1 | async-start | bytes 3145728 | tf_op jit(solution)/shard_map/all_to_all | solution.py:495
  140.0 3.1 %copy-start.16 = (bf16[32,32,768]{2,1,0:T(8,128)(2,1)}, bf16[32,32,768]{2,1,0:T(8,128)(2,1)S(1)}, u32[]{:S(2)}) copy-start(bf16[32,32,768]{2,1,0:T(8,128)(2,1)S(1)} %all-to-all-done.1) | copy-start | bytes 4718596
  155.1 10.4 %collective-permute-start.12 = (bf16[4,384,1024]{2,1,0:T(8,128)(2,1)}, bf16[4,384,1024]{2,1,0:T(8,128)(2,1)S(1)}, u32[]{:S(2)}, u32[]{:S(2)}) collective-permute-start(bf16[4,384,1024]{2,1,0:T(8,128)(2,1)} %get-tuple-element.110), channel_id=1, source_target_pairs={{0,4},{4,0},{1,5},{5,1},{2,6},{6,2},{3,7},{7,3},{8,12},{12,8},{9,1... | collective-permute-start | bytes 9437192 | tf_op jit(solution)/shard_map/ppermute | solution.py:26
  155.2 10.3 %copy-start.14 = (bf16[4,384,1024]{2,1,0:T(8,128)(2,1)S(1)}, bf16[4,384,1024]{2,1,0:T(8,128)(2,1)}, u32[]{:S(2)}) copy-start(bf16[4,384,1024]{2,1,0:T(8,128)(2,1)} %get-tuple-element.115) | copy-start | bytes 9437188
  165.0 6.3 %collective-permute-start.15 = (bf16[1,512,1024]{2,1,0:T(8,128)(2,1)}, bf16[1,512,1024]{2,1,0:T(8,128)(2,1)S(1)}, u32[]{:S(2)}, u32[]{:S(2)}) collective-permute-start(bf16[1,512,1024]{2,1,0:T(8,128)(2,1)} %get-tuple-element.114), channel_id=1, source_target_pairs={{0,4},{4,0},{1,5},{5,1},{2,6},{6,2},{3,7},{7,3},{8,12},{12,8},{9,1... | collective-permute-start | bytes 3145736 | tf_op jit(solution)/shard_map/ppermute | solution.py:26
  167.6 21.1 %collective-permute-start.16 = (bf16[2,8,24,1024]{3,2,1,0:T(8,128)(2,1)S(1)}, bf16[2,8,24,1024]{3,2,1,0:T(8,128)(2,1)S(1)}, u32[]{:S(2)}, u32[]{:S(2)}) collective-permute-start(bf16[2,8,24,1024]{3,2,1,0:T(8,128)(2,1)S(1)} %bitcast.134), channel_id=1, source_target_pairs={{0,3},{3,0},{1,2},{2,1},{4,7},{7,4},{5,6},{6,5},{8,11},{11,8},{9,1... | collective-permute-start | bytes 2359304 | tf_op jit(solution)/shard_map/ppermute | solution.py:360
  171.0 1.2 copy-start.18
  171.2 19.3 %collective-permute-start.13 = (bf16[2,8,24,1024]{3,2,1,0:T(8,128)(2,1)S(1)}, bf16[2,8,24,1024]{3,2,1,0:T(8,128)(2,1)S(1)}, u32[]{:S(2)}, u32[]{:S(2)}) collective-permute-start(bf16[2,8,24,1024]{3,2,1,0:T(8,128)(2,1)S(1)} %bitcast.135), channel_id=1, source_target_pairs={{0,1},{1,0},{2,3},{3,2},{4,5},{5,4},{6,7},{7,6},{8,9},{9,8},{10,11... | collective-permute-start | bytes 2359304 | tf_op jit(solution)/shard_map/ppermute | solution.py:360
  188.7 1.8 copy-start.19
  190.5 6.7 %collective-permute-start.17 = (bf16[1,512,1024]{2,1,0:T(8,128)(2,1)}, bf16[1,512,1024]{2,1,0:T(8,128)(2,1)}, u32[]{:S(2)}, u32[]{:S(2)}) collective-permute-start(bf16[1,512,1024]{2,1,0:T(8,128)(2,1)} %get-tuple-element.122), channel_id=1, source_target_pairs={{0,4},{4,0},{1,5},{5,1},{2,6},{6,2},{3,7},{7,3},{8,12},{12,8},{9,1... | collective-permute-start | bytes 3145736 | tf_op jit(solution)/shard_map/ppermute | solution.py:26
  190.5 31.2 %all-to-all-start.3 = ((bf16[16,32,1024]{2,1,0:T(8,128)(2,1)}), bf16[16,32,1024]{2,1,0:T(8,128)(2,1)S(1)}, u32[]{:S(2)}, u32[]{:S(2)}) async-start(bf16[16,32,1024]{2,1,0:T(8,128)(2,1)} %bitcast.33), calls=%async_computation.3 | async-start | bytes 2097152 | tf_op jit(solution)/shard_map/all_to_all | solution.py:515
  194.2 2.5 %copy-start.20 = (bf16[2,8,24,1024]{3,2,1,0:T(8,128)(2,1)S(1)}, bf16[2,8,24,1024]{3,2,1,0:T(8,128)(2,1)}, u32[]{:S(2)}) copy-start(bf16[2,8,24,1024]{3,2,1,0:T(8,128)(2,1)} %copy-done.19) | copy-start | bytes 2359300
  194.5 2.7 %copy-start.17 = (bf16[1,512,1024]{2,1,0:T(8,128)(2,1)S(1)}, bf16[1,512,1024]{2,1,0:T(8,128)(2,1)}, u32[]{:S(2)}) copy-start(bf16[1,512,1024]{2,1,0:T(8,128)(2,1)} %get-tuple-element.120) | copy-start | bytes 3145732
  194.5 13.2 %collective-permute-start.14 = (bf16[8,24,1024]{2,1,0:T(8,128)(2,1)S(1)}, bf16[8,24,1024]{2,1,0:T(8,128)(2,1)S(1)}, u32[]{:S(2)}, u32[]{:S(2)}) collective-permute-start(bf16[8,24,1024]{2,1,0:T(8,128)(2,1)S(1)} %dynamic-slice_bitcast_fusion.1), channel_id=1, source_target_pairs={{0,3},{3,0},{1,2},{2,1},{4,7},{7,4},{5,6},{6,5},{8,11},{11,8},{9,1... | collective-permute-start | bytes 1179656 | tf_op jit(solution)/shard_map/ppermute | solution.py:360
  197.1 12.0 %collective-permute-start.18 = (bf16[8,24,1024]{2,1,0:T(8,128)(2,1)S(1)}, bf16[8,24,1024]{2,1,0:T(8,128)(2,1)S(1)}, u32[]{:S(2)}, u32[]{:S(2)}) collective-permute-start(bf16[8,24,1024]{2,1,0:T(8,128)(2,1)S(1)} %dynamic-slice_bitcast_fusion), channel_id=1, source_target_pairs={{0,1},{1,0},{2,3},{3,2},{4,5},{5,4},{6,7},{7,6},{8,9},{9,8},{10,11... | collective-permute-start | bytes 1179656 | tf_op jit(solution)/shard_map/ppermute | solution.py:360
  198.9 15.1 %collective-permute-start.19 = (bf16[2,8,8,1024]{3,2,1,0:T(8,128)(2,1)S(1)}, bf16[2,8,8,1024]{3,2,1,0:T(8,128)(2,1)S(1)}, u32[]{:S(2)}, u32[]{:S(2)}) collective-permute-start(bf16[2,8,8,1024]{3,2,1,0:T(8,128)(2,1)S(1)} %bitcast.140), channel_id=1, source_target_pairs={{0,1},{1,0},{2,3},{3,2},{4,5},{5,4},{6,7},{7,6},{8,9},{9,8},{10,11... | collective-permute-start | bytes 786440 | tf_op jit(solution)/shard_map/ppermute | solution.py:360
  201.0 14.3 %collective-permute-start.21 = (bf16[2,8,8,1024]{3,2,1,0:T(8,128)(2,1)S(1)}, bf16[2,8,8,1024]{3,2,1,0:T(8,128)(2,1)S(1)}, u32[]{:S(2)}, u32[]{:S(2)}) collective-permute-start(bf16[2,8,8,1024]{3,2,1,0:T(8,128)(2,1)S(1)} %bitcast.139), channel_id=1, source_target_pairs={{0,3},{3,0},{1,2},{2,1},{4,7},{7,4},{5,6},{6,5},{8,11},{11,8},{9,1... | collective-permute-start | bytes 786440 | tf_op jit(solution)/shard_map/ppermute | solution.py:360
  214.1 6.3 %collective-permute-start.20 = (bf16[8,8,1024]{2,1,0:T(8,128)(2,1)S(1)}, bf16[8,8,1024]{2,1,0:T(8,128)(2,1)S(1)}, u32[]{:S(2)}, u32[]{:S(2)}) collective-permute-start(bf16[8,8,1024]{2,1,0:T(8,128)(2,1)S(1)} %dynamic-slice_bitcast_fusion.3), channel_id=1, source_target_pairs={{0,3},{3,0},{1,2},{2,1},{4,7},{7,4},{5,6},{6,5},{8,11},{11,8},{9,1... | collective-permute-start | bytes 393224 | tf_op jit(solution)/shard_map/ppermute | solution.py:360
  215.4 5.0 %collective-permute-start.22 = (bf16[8,8,1024]{2,1,0:T(8,128)(2,1)S(1)}, bf16[8,8,1024]{2,1,0:T(8,128)(2,1)S(1)}, u32[]{:S(2)}, u32[]{:S(2)}) collective-permute-start(bf16[8,8,1024]{2,1,0:T(8,128)(2,1)S(1)} %dynamic-slice_bitcast_fusion.2), channel_id=1, source_target_pairs={{0,1},{1,0},{2,3},{3,2},{4,5},{5,4},{6,7},{7,6},{8,9},{9,8},{10,11... | collective-permute-start | bytes 393224 | tf_op jit(solution)/shard_map/ppermute | solution.py:360
  220.5 24.0 %copy-start.1 = (f32[8,768]{1,0:T(8,128)S(1)}, f32[8,768]{1,0:T(8,128)}, u32[]{:S(2)}) copy-start(f32[8,768]{1,0:T(8,128)} %param.11) | copy-start | bytes 73732
  221.7 22.0 %all-to-all-start.2 = ((bf16[16,32,1024]{2,1,0:T(8,128)(2,1)}), bf16[16,32,1024]{2,1,0:T(8,128)(2,1)S(1)}, u32[]{:S(2)}, u32[]{:S(2)}) async-start(bf16[16,32,1024]{2,1,0:T(8,128)(2,1)} %maximum_maximum_fusion), calls=%async_computation.2 | async-start | bytes 2097152 | tf_op jit(solution)/shard_map/all_to_all | solution.py:533
  228.8 5.2 %collective-permute-start.23 = (f32[1,8,1024]{2,1,0:T(8,128)S(1)}, f32[1,8,1024]{2,1,0:T(8,128)S(1)}, u32[]{:S(2)}, u32[]{:S(2)}) collective-permute-start(f32[1,8,1024]{2,1,0:T(8,128)S(1)} %get-tuple-element.154), channel_id=1, source_target_pairs={{0,1},{1,2},{2,3},{3,0},{4,5},{5,6},{6,7},{7,4},{8,9},{9,10},{10,1... | collective-permute-start | bytes 98312 | tf_op jit(solution)/shard_map/ppermute | solution.py:26
  228.9 5.8 %collective-permute-start.24 = (f32[1,8,1024]{2,1,0:T(8,128)S(1)}, f32[1,8,1024]{2,1,0:T(8,128)S(1)}, u32[]{:S(2)}, u32[]{:S(2)}) collective-permute-start(f32[1,8,1024]{2,1,0:T(8,128)S(1)} %get-tuple-element.156), channel_id=1, source_target_pairs={{0,2},{1,3},{2,0},{3,1},{4,6},{5,7},{6,4},{7,5},{8,10},{9,11},{10,... | collective-permute-start | bytes 98312 | tf_op jit(solution)/shard_map/ppermute | solution.py:26
  232.4 3.9 %collective-permute-start.25 = (f32[1,8,1024]{2,1,0:T(8,128)S(1)}, f32[1,8,1024]{2,1,0:T(8,128)S(1)}, u32[]{:S(2)}, u32[]{:S(2)}) collective-permute-start(f32[1,8,1024]{2,1,0:T(8,128)S(1)} %get-tuple-element.155), channel_id=1, source_target_pairs={{0,3},{1,0},{2,1},{3,2},{4,7},{5,4},{6,5},{7,6},{8,11},{9,8},{10,9... | collective-permute-start | bytes 98312 | tf_op jit(solution)/shard_map/ppermute | solution.py:26

commit v13 on v12

--- a/solution.py
+++ b/solution.py
@@ -114,7 +114,7 @@
     hid = 2 * half * RING
     head_rows = out_width // RING
     first_call = carried is None
-    block_rows = min(rows, 256)
+    block_rows = min(rows, 512)
     whole = lambda shape: pl.BlockSpec(
         shape, lambda g, i, s: (0,) * len(shape), pipeline_mode=pl.Buffered(1)
     )
@@ -412,7 +412,7 @@
             out_specs=[out, out],
         ),
         out_shape=[jax.ShapeDtypeStruct((lines, LANES), BF16)] * 2,
-        compiler_params=params(8),
+        compiler_params=params(56),
         name="packed",
     )(side, first, second, head)
 

time: 246 us -> 243 us (0.988)
  local copies, waits for them, and re-layouts: 14.3 us -> 8.39 us
  Pallas kernels: 68.9 us -> 72.6 us
    unnamed x68 -> x50, local copies, waits for them, and re-layouts: 8.1 us -> 2.2 us
    pallas_call x2, Pallas kernels: 0.16 us -> 4.89 us  [packed(): pl.pallas_call(pack_kernel, grid_spec=pltpu.PrefetchScalarGridSpec(num_sc...]
  transfers between devices with their start and end apart: 29 -> 29, of which waited for: 15 -> 17; matrix products, arithmetic and copies ran while one was open for 6% -> 6% of each run, Pallas kernels for 18% -> 19%
where the time goes in v13:
time: 243 us; the launch traced here: 242 us
  Pallas kernels  72.6 us (30%)
  waiting for transfers between devices  70.8 us (29%)
  starting transfers between devices  40.3 us (17%)
  blocking collectives  30.5 us (13%)
  other arithmetic  11.5 us (5%)
  local copies, waits for them, and re-layouts  8.39 us (3%)
  matrix products  6.83 us (3%)
    pallas_call x3, Pallas kernels, forward_part(): pl.pallas_call(functools.partial(forward_kernel, groups, first_call, last...  35.4 us
    all_to_all x1, blocking collectives, per_device(): gathered = lax.all_to_all(forecast, group, 0, 0, tiled=True)  30.5 us
    ppermute x8, waiting for transfers between devices, sent_along(): return lax.ppermute(x, step[1], step[0])  23.8 us
    all_to_all x1, waiting for transfers between devices, per_device(): lax.all_to_all(grad_raw.reshape(32, members * own, out_width), group, 0,...  21.2 us
    pallas_call x2, Pallas kernels, late_grads(): pl.pallas_call(functools.partial(late_kernel, part == 1), grid_spec=pltpu...  19.4 us
    ppermute x18, waiting for transfers between devices, shift(): return lax.ppermute(x, axis, [(i, (i + by) % size) for i in range(size)])  18.4 us
    ppermute x18, starting transfers between devices, shift(): return lax.ppermute(x, axis, [(i, (i + by) % size) for i in range(size)])  15.8 us
    pallas_call x1, Pallas kernels, early_grads(): pl.pallas_call(early_kernel, grid_spec=pltpu.PrefetchScalarGridSpec(num_s...  12.1 us
  transfers between devices with their start and end apart: 29, of which 17 were waited for; matrix products, arithmetic and copies ran while one was open for 6% of the time, Pallas kernels for 19%

profile of v13, /device:TPU:0, one launch (start us, length us, event | category | flops | bytes accessed | tf_op | source)
XLA Modules:
  0.0 242.2 jit_solution(8707666520257916605)
XLA Ops:
  0.7 2.5 %packed.2 = (bf16[1216,256]{1,0:T(8,128)(2,1)}, bf16[1216,256]{1,0:T(8,128)(2,1)}) custom-call(s32[1]{0:T(128)} %bitcast.1.side, bf16[1024,512]{1,0:T(8,128)(2,1)} %first.3, bf16[512,1024]{1,0:T(8,128)(2,1)} %second.3, bf16[192,1024]{1,0:T(8,128)(2,1)} %bitcast.132), custom_call_target="tpu_custom_call" | custom-call | tf_op jit(solution)/shard_map/packed/pallas_call | solution.py:402
  3.2 1.7 collective-permute-start
  4.8 1.6 collective-permute-start.1
  6.4 1.6 copy.20
  8.0 2.4 packed.3
  10.4 0.6 pad_add_fusion.2
  11.0 0.6 pad_add_fusion.refs_0_.place
  11.6 8.9 %forward_part.3 = (bf16[1024,2048]{1,0:T(8,128)(2,1)}, bf16[1024,2048]{1,0:T(8,128)(2,1)}, bf16[2048,1024]{1,0:T(8,128)(2,1)}, bf16[768,1024]{1,0:T(8,128)(2,1)}, f32[1024,1024]{1,0:T(8,128)}) custom-call(s32[4]{0:T(128)} %pad_add_fusion.refs_0_.place, bf16[1024,1024]{1,0:T(8,128)(2,1)} %bitcast.116, bf16[1216,256]{1,0:T(8,128)(2,1)} %get-tuple-element.79.refs_2_, ...), custom_call_target="tpu_custom_call" | custom-call | flops 2147483648 | bytes 12582912 | tf_op jit(solution)/shard_map/forward_part/pallas_call | solution.py:166
  20.5 1.6 collective-permute-start.3
  22.1 1.7 collective-permute-start.2
  23.8 0.5 collective-permute-start.5
  24.3 12.8 %collective-permute-done.3.refs_3_ = bf16[1216,256]{1,0:T(8,128)(2,1)S(1)} collective-permute-done((bf16[1216,256]{1,0:T(8,128)(2,1)S(1)}, bf16[1216,256]{1,0:T(8,128)(2,1)S(1)}, u32[]{:S(2)}, u32[]{:S(2)}) %collective-permute-start.3) | collective-permute-done | bytes 622624 | tf_op jit(solution)/shard_map/ppermute | solution.py:26
  37.3 0.5 collective-permute-start.9
  38.0 3.0 %collective-permute-start.7 = (bf16[1216,256]{1,0:T(8,128)(2,1)S(1)}, bf16[1216,256]{1,0:T(8,128)(2,1)S(1)}, u32[]{:S(2)}, u32[]{:S(2)}) collective-permute-start(bf16[1216,256]{1,0:T(8,128)(2,1)S(1)} %collective-permute-done.1.refs_7_), channel_id=1, source_target_pairs={{0,3},{1,0},{2,1},{3,2},{4,7},{5,4},{6,5},{7,6},{8,11},{9,8},{10,9... | collective-permute-start | bytes 1867784 | tf_op jit(solution)/shard_map/ppermute | solution.py:26
  41.0 0.7 stack.59.refs_0_
  41.8 15.5 %forward_part.4 = (bf16[1024,2048]{1,0:T(8,128)(2,1)}, bf16[1024,2048]{1,0:T(8,128)(2,1)}, bf16[2048,1024]{1,0:T(8,128)(2,1)}, bf16[768,1024]{1,0:T(8,128)(2,1)}, f32[1024,1024]{1,0:T(8,128)}) custom-call(s32[5]{0:T(128)} %stack.59.refs_0_, ...), custom_call_target="tpu_custom_call", output_to_operand_aliasing={{0}: (11, {}), {1}: (12, {}), {2}: (13, {}), {3}: (14, {})} | custom-call | flops 4294967296 | bytes 12582912 | tf_op jit(solution)/shard_map/forward_part/pallas_call | solution.py:166
  57.3 0.5 collective-permute-done.6.refs_2_
  57.8 0.5 collective-permute-start.11
  58.3 0.6 gather_fusion
  59.0 0.9 collective-permute-done.10.refs_4_
  59.8 0.9 collective-permute-done.11.refs_5_
  60.7 0.8 copy-done.17
  61.5 11.0 %forward_part.5 = (bf16[1024,2048]{1,0:T(8,128)(2,1)}, bf16[1024,2048]{1,0:T(8,128)(2,1)}, bf16[2048,1024]{1,0:T(8,128)(2,1)}, bf16[768,1024]{1,0:T(8,128)(2,1)}...) custom-call(s32[4]{0:T(128)} %get-tuple-element.140.refs_0_, ...), custom_call_target="tpu_custom_call", output_to_operand_aliasing={{0}: (7, {}), {1}: (8, {}), {2}: (9, {})} | custom-call | flops 2147483648 | bytes 12582912 | tf_op jit(solution)/shard_map/forward_part/pallas_call | solution.py:166
  72.5 30.5 %all_to_all.20 = bf16[32,32,768]{2,1,0:T(8,128)(2,1)S(1)} all-to-all(bf16[32,32,768]{2,1,0:T(8,128)(2,1)} %bitcast.131), channel_id=1, replica_groups=mesh['x'=4,'z'=4,'c'=2,'y'=4] {'x','z','c'}, dimensions={0} | all-to-all | bytes 3145728 | tf_op jit(solution)/shard_map/all_to_all | solution.py:492
  103.3 0.8 fusion.6
  104.4 0.9 fusion.37
  105.3 0.6 multiply_reduce_fusion
  105.9 2.8 %fusion.8 = bf16[128,8,768]{2,0,1:T(8,128)(2,1)S(1)} fusion(f32[128,8]{0,1:T(8,128)S(1)} %bitcast.141, f32[128,8]{0,1:T(8,128)S(1)} %copy.23, f32[8,768]{1,0:T(8,128)S(1)} %broadcast_select_fusion, f32[8]{0:T(128)S(1)} %get-tuple-element.159, bf16[128,8,768]{2,1,0:T(8,128)(2,1)S(1)} %bitcast.123, f32[8,128,128]{1,2,0:T(8,128)S(1)} %get-tuple-element.160), kind=kOutput, calls=%fused_computation.14 | convolution fusion | flops 1215168512 | bytes 3702816 | tf_op jit(solution)/shard_map/pmn,npo->mpo/dot_general | solution.py:429
  108.7 2.0 copy.30
  110.8 4.2 %all-to-all-start.1 = ((bf16[32,32,768]{2,1,0:T(8,128)(2,1)}), bf16[32,32,768]{2,1,0:T(8,128)(2,1)S(1)}, u32[]{:S(2)}, u32[]{:S(2)}) async-start(bf16[32,32,768]{2,1,0:T(8,128)(2,1)} %bitcast.18), calls=%async_computation.1 | async-start | bytes 3145728 | tf_op jit(solution)/shard_map/all_to_all | solution.py:495
  115.0 1.9 pad_maximum_fusion.scalars
  116.9 21.2 %all-to-all-done.1 = bf16[32,32,768]{2,1,0:T(8,128)(2,1)S(1)} async-done(((bf16[32,32,768]{2,1,0:T(8,128)(2,1)}), bf16[32,32,768]{2,1,0:T(8,128)(2,1)S(1)}, u32[]{:S(2)}, u32[]{:S(2)}) %all-to-all-start.1) | async-done | bytes 1572896 | tf_op jit(solution)/shard_map/all_to_all | solution.py:495
  138.1 3.1 %convolution_convert_fusion.resid_grad = bf16[1024,1024]{1,0:T(8,128)(2,1)} fusion(bf16[1024,768]{1,0:T(8,128)(2,1)S(1)} %bitcast.129, bf16[768,1024]{1,0:T(8,128)(2,1)S(1)} %copy-done.20), kind=kOutput, calls=%fused_computation.18 | convolution fusion | flops 1611661312 | bytes 5242880 | tf_op jit(solution)/shard_map/dot_general | solution.py:30
  141.2 12.1 %early_grads.1 = (bf16[4,384,1024]{2,1,0:T(8,128)(2,1)}, bf16[4,384,1024]{2,1,0:T(8,128)(2,1)}) custom-call(s32[4]{0:T(128)} %pad_add_fusion.refs_0_.place, bf16[1024,2048]{1,0:T(8,128)(2,1)} %get-tuple-element.103.hidden, bf16[1024,1024]{1,0:T(8,128)(2,1)} %convolution_convert_fusion.resid_grad, bf16[1024,1024]{1,0:T(8,128)(2,1)} %get-tuple-element.108.residual, ...), custom_call_target="tpu_custom_call" | custom-call | flops 5905580032 | bytes 18874368 | tf_op jit(solution)/shard_map/early_grads/pallas_call | solution.py:241
  153.4 9.8 %late_grads.2 = (bf16[1,512,1024]{2,1,0:T(8,128)(2,1)}, bf16[1,512,1024]{2,1,0:T(8,128)(2,1)}) custom-call(s32[4]{0:T(128)} %pad_add_fusion.refs_0_.place, bf16[1024,1024]{1,0:T(8,128)(2,1)} %convolution_convert_fusion.resid_grad, bf16[2048,1024]{1,0:T(8,128)(2,1)} %get-tuple-element.112.second, bf16[1024,2048]{1,0:T(8,128)(2,1)} %get-tuple-element.113.slope, ...), custom_call_target="tpu_custom_call" | custom-call | flops 4294967296 | bytes 12582912 | tf_op jit(solution)/shard_map/late_grads/pallas_call | solution.py:280
  163.2 0.4 collective-permute-start.15
  163.7 1.6 add_convert_fusion
  165.3 0.3 fusion.38
  165.8 2.8 %collective-permute-start.16 = (bf16[2,8,24,1024]{3,2,1,0:T(8,128)(2,1)S(1)}, bf16[2,8,24,1024]{3,2,1,0:T(8,128)(2,1)S(1)}, u32[]{:S(2)}, u32[]{:S(2)}) collective-permute-start(bf16[2,8,24,1024]{3,2,1,0:T(8,128)(2,1)S(1)} %bitcast.134), channel_id=1, source_target_pairs={{0,3},{3,0},{1,2},{2,1},{4,7},{7,4},{5,6},{6,5},{8,11},{11,8},{9,1... | collective-permute-start | bytes 2359304 | tf_op jit(solution)/shard_map/ppermute | solution.py:360
  169.0 0.9 copy-done.6
  169.9 1.4 add_convert_fusion.2
  171.2 9.6 %late_grads.3 = (bf16[1,512,1024]{2,1,0:T(8,128)(2,1)}, bf16[1,512,1024]{2,1,0:T(8,128)(2,1)}) custom-call(s32[4]{0:T(128)} %pad_add_fusion.refs_0_.place, bf16[1024,1024]{1,0:T(8,128)(2,1)} %convolution_convert_fusion.resid_grad, bf16[2048,1024]{1,0:T(8,128)(2,1)} %get-tuple-element.112.second, bf16[1024,2048]{1,0:T(8,128)(2,1)} %get-tuple-element.113.slope, ...), custom_call_target="tpu_custom_call" | custom-call | flops 4294967296 | bytes 12582912 | tf_op jit(solution)/shard_map/late_grads/pallas_call | solution.py:280
  180.8 5.8 %collective-permute-done.16 = bf16[2,8,24,1024]{3,2,1,0:T(8,128)(2,1)S(1)} collective-permute-done((bf16[2,8,24,1024]{3,2,1,0:T(8,128)(2,1)S(1)}, bf16[2,8,24,1024]{3,2,1,0:T(8,128)(2,1)S(1)}, u32[]{:S(2)}, u32[]{:S(2)}) %collective-permute-start.16) | collective-permute-done | bytes 786464 | tf_op jit(solution)/shard_map/ppermute | solution.py:360
  186.6 1.6 collective-permute-done.13
  188.2 3.7 %all-to-all-start.3 = ((bf16[16,32,1024]{2,1,0:T(8,128)(2,1)}), bf16[16,32,1024]{2,1,0:T(8,128)(2,1)S(1)}, u32[]{:S(2)}, u32[]{:S(2)}) async-start(bf16[16,32,1024]{2,1,0:T(8,128)(2,1)} %bitcast.33), calls=%async_computation.3 | async-start | bytes 2097152 | tf_op jit(solution)/shard_map/all_to_all | solution.py:515
  192.2 2.1 collective-permute-start.14
  194.8 1.5 add_convert_fusion.1
  196.6 2.1 collective-permute-start.19
  198.7 1.2 collective-permute-start.21
  199.8 5.6 %collective-permute-done.14 = bf16[8,24,1024]{2,1,0:T(8,128)(2,1)S(1)} collective-permute-done((bf16[8,24,1024]{2,1,0:T(8,128)(2,1)S(1)}, bf16[8,24,1024]{2,1,0:T(8,128)(2,1)S(1)}, u32[]{:S(2)}, u32[]{:S(2)}) %collective-permute-start.14) | collective-permute-done | bytes 393248 | tf_op jit(solution)/shard_map/ppermute | solution.py:360
  205.4 1.3 collective-permute-done.18
  206.7 0.3 fusion.26
  207.1 4.6 %collective-permute-done.19 = bf16[2,8,8,1024]{3,2,1,0:T(8,128)(2,1)S(1)} collective-permute-done((bf16[2,8,8,1024]{3,2,1,0:T(8,128)(2,1)S(1)}, bf16[2,8,8,1024]{3,2,1,0:T(8,128)(2,1)S(1)}, u32[]{:S(2)}, u32[]{:S(2)}) %collective-permute-start.19) | collective-permute-done | bytes 262176 | tf_op jit(solution)/shard_map/ppermute | solution.py:360
  211.7 1.3 collective-permute-start.20
  213.2 4.8 %collective-permute-done.20 = bf16[8,8,1024]{2,1,0:T(8,128)(2,1)S(1)} collective-permute-done((bf16[8,8,1024]{2,1,0:T(8,128)(2,1)S(1)}, bf16[8,8,1024]{2,1,0:T(8,128)(2,1)S(1)}, u32[]{:S(2)}, u32[]{:S(2)}) %collective-permute-start.20) | collective-permute-done | bytes 131104 | tf_op jit(solution)/shard_map/ppermute | solution.py:360
  218.2 1.1 maximum_maximum_fusion
  219.3 6.9 %all-to-all-start.2 = ((bf16[16,32,1024]{2,1,0:T(8,128)(2,1)}), bf16[16,32,1024]{2,1,0:T(8,128)(2,1)S(1)}, u32[]{:S(2)}, u32[]{:S(2)}) async-start(bf16[16,32,1024]{2,1,0:T(8,128)(2,1)} %maximum_maximum_fusion), calls=%async_computation.2 | async-start | bytes 2097152 | tf_op jit(solution)/shard_map/all_to_all | solution.py:533
  226.5 3.5 %collective-permute-start.24 = (f32[1,8,1024]{2,1,0:T(8,128)S(1)}, f32[1,8,1024]{2,1,0:T(8,128)S(1)}, u32[]{:S(2)}, u32[]{:S(2)}) collective-permute-start(f32[1,8,1024]{2,1,0:T(8,128)S(1)} %get-tuple-element.156), channel_id=1, source_target_pairs={{0,2},{1,3},{2,0},{3,1},{4,6},{5,7},{6,4},{7,5},{8,10},{9,11},{10,... | collective-permute-start | bytes 98312 | tf_op jit(solution)/shard_map/ppermute | solution.py:26
  230.0 0.6 collective-permute-start.25
  230.6 1.0 collective-permute-done.23
  231.6 0.6 collective-permute-done.24
  232.3 1.7 collective-permute-done.25
  233.9 7.4 %all-to-all-done.2.arrived = bf16[16,32,1024]{2,1,0:T(8,128)(2,1)S(1)} async-done(((bf16[16,32,1024]{2,1,0:T(8,128)(2,1)}), bf16[16,32,1024]{2,1,0:T(8,128)(2,1)S(1)}, u32[]{:S(2)}, u32[]{:S(2)}) %all-to-all-start.2) | async-done | bytes 1048608 | tf_op jit(solution)/shard_map/all_to_all | solution.py:533
  241.3 0.8 finish.1
  (100 shorter events, 3.4 us)
Async XLA Ops:
  0.6 57.7 %copy-start = (f32[8,768]{1,0:T(8,128)S(1)}, f32[8,768]{1,0:T(8,128)}, u32[]{:S(2)}) copy-start(f32[8,768]{1,0:T(8,128)} %param.11) | copy-start | bytes 73732
  0.6 5.8 %copy-start.3 = (bf16[4,256,1024]{2,1,0:T(8,128)(2,1)S(1)}, bf16[4,256,1024]{2,1,0:T(8,128)(2,1)}, u32[]{:S(2)}) copy-start(bf16[4,256,1024]{2,1,0:T(8,128)(2,1)} %param.7) | copy-start | bytes 6291460
  3.2 17.3 %collective-permute-start = (bf16[1216,256]{1,0:T(8,128)(2,1)}, bf16[1216,256]{1,0:T(8,128)(2,1)S(1)}, u32[]{:S(2)}, u32[]{:S(2)}) collective-permute-start(bf16[1216,256]{1,0:T(8,128)(2,1)} %get-tuple-element.79.refs_2_), channel_id=1, source_target_pairs={{0,1},{1,2},{2,3},{3,0},{4,5},{5,6},{6,7},{7,4},{8,9},{9,10},{10,1... | collective-permute-start | bytes 1867784 | tf_op jit(solution)/shard_map/ppermute | solution.py:26
  4.8 15.7 %collective-permute-start.1 = (bf16[1216,256]{1,0:T(8,128)(2,1)}, bf16[1216,256]{1,0:T(8,128)(2,1)S(1)}, u32[]{:S(2)}, u32[]{:S(2)}) collective-permute-start(bf16[1216,256]{1,0:T(8,128)(2,1)} %get-tuple-element.80.refs_3_), channel_id=1, source_target_pairs={{0,3},{1,0},{2,1},{3,2},{4,7},{5,4},{6,5},{7,6},{8,11},{9,8},{10,9... | collective-permute-start | bytes 1867784 | tf_op jit(solution)/shard_map/ppermute | solution.py:26
  11.6 9.0 %copy-start.22 = (bf16[1216,256]{1,0:T(8,128)(2,1)S(1)}, bf16[1216,256]{1,0:T(8,128)(2,1)}, u32[]{:S(2)}) copy-start(bf16[1216,256]{1,0:T(8,128)(2,1)} %get-tuple-element.80.refs_3_) | copy-start | bytes 1867780
  11.6 10.6 %copy-start.21 = (bf16[1216,256]{1,0:T(8,128)(2,1)S(1)}, bf16[1216,256]{1,0:T(8,128)(2,1)}, u32[]{:S(2)}) copy-start(bf16[1216,256]{1,0:T(8,128)(2,1)} %get-tuple-element.79.refs_2_) | copy-start | bytes 1867780
  20.5 21.2 %copy-start.9 = (bf16[1216,256]{1,0:T(8,128)(2,1)}, bf16[1216,256]{1,0:T(8,128)(2,1)S(1)}, u32[]{:S(2)}) copy-start(bf16[1216,256]{1,0:T(8,128)(2,1)S(1)} %collective-permute-done.refs_2_) | copy-start | bytes 1867780
  20.5 21.2 %copy-start.10 = (bf16[1216,256]{1,0:T(8,128)(2,1)}, bf16[1216,256]{1,0:T(8,128)(2,1)S(1)}, u32[]{:S(2)}) copy-start(bf16[1216,256]{1,0:T(8,128)(2,1)S(1)} %collective-permute-done.1.refs_7_) | copy-start | bytes 1867780
  20.5 16.6 %collective-permute-start.3 = (bf16[1216,256]{1,0:T(8,128)(2,1)S(1)}, bf16[1216,256]{1,0:T(8,128)(2,1)S(1)}, u32[]{:S(2)}, u32[]{:S(2)}) collective-permute-start(bf16[1216,256]{1,0:T(8,128)(2,1)S(1)} %copy-done.22), channel_id=1, source_target_pairs={{0,1},{1,2},{2,3},{3,0},{4,5},{5,6},{6,7},{7,4},{8,9},{9,10},{10,1... | collective-permute-start | bytes 1867784 | tf_op jit(solution)/shard_map/ppermute | solution.py:26
  22.1 15.0 %collective-permute-start.2 = (bf16[1216,256]{1,0:T(8,128)(2,1)S(1)}, bf16[1216,256]{1,0:T(8,128)(2,1)}, u32[]{:S(2)}, u32[]{:S(2)}) collective-permute-start(bf16[1216,256]{1,0:T(8,128)(2,1)S(1)} %copy-done.21), channel_id=1, source_target_pairs={{0,3},{1,0},{2,1},{3,2},{4,7},{5,4},{6,5},{7,6},{8,11},{9,8},{10,9... | collective-permute-start | bytes 1867784 | tf_op jit(solution)/shard_map/ppermute | solution.py:26
  23.8 13.3 %collective-permute-start.4 = (bf16[1216,256]{1,0:T(8,128)(2,1)S(1)}, bf16[1216,256]{1,0:T(8,128)(2,1)S(1)}, u32[]{:S(2)}, u32[]{:S(2)}) collective-permute-start(bf16[1216,256]{1,0:T(8,128)(2,1)S(1)} %collective-permute-done.refs_2_), channel_id=1, source_target_pairs={{0,4},{4,0},{1,5},{5,1},{2,6},{6,2},{3,7},{7,3},{8,12},{12,8},{9,1... | collective-permute-start | bytes 1867784 | tf_op jit(solution)/shard_map/ppermute | solution.py:26
  23.8 13.3 %collective-permute-start.5 = (bf16[1216,256]{1,0:T(8,128)(2,1)S(1)}, bf16[1216,256]{1,0:T(8,128)(2,1)S(1)}, u32[]{:S(2)}, u32[]{:S(2)}) collective-permute-start(bf16[1216,256]{1,0:T(8,128)(2,1)S(1)} %collective-permute-done.1.refs_7_), channel_id=1, source_target_pairs={{0,4},{4,0},{1,5},{5,1},{2,6},{6,2},{3,7},{7,3},{8,12},{12,8},{9,1... | collective-permute-start | bytes 1867784 | tf_op jit(solution)/shard_map/ppermute | solution.py:26
  37.1 4.6 %copy-start.13 = (bf16[1216,256]{1,0:T(8,128)(2,1)}, bf16[1216,256]{1,0:T(8,128)(2,1)S(1)}, u32[]{:S(2)}) copy-start(bf16[1216,256]{1,0:T(8,128)(2,1)S(1)} %collective-permute-done.3.refs_3_) | copy-start | bytes 1867780
  37.1 0.9 copy-start.14
  37.2 3.9 %copy-start.15 = (bf16[1216,256]{1,0:T(8,128)(2,1)}, bf16[1216,256]{1,0:T(8,128)(2,1)S(1)}, u32[]{:S(2)}) copy-start(bf16[1216,256]{1,0:T(8,128)(2,1)S(1)} %collective-permute-done.5.refs_9_) | copy-start | bytes 1867780
  37.2 4.6 %collective-permute-start.8 = (bf16[1216,256]{1,0:T(8,128)(2,1)S(1)}, bf16[1216,256]{1,0:T(8,128)(2,1)}, u32[]{:S(2)}, u32[]{:S(2)}) collective-permute-start(bf16[1216,256]{1,0:T(8,128)(2,1)S(1)} %collective-permute-done.3.refs_3_), channel_id=1, source_target_pairs={{0,4},{4,0},{1,5},{5,1},{2,6},{6,2},{3,7},{7,3},{8,12},{12,8},{9,1... | collective-permute-start | bytes 1867784 | tf_op jit(solution)/shard_map/ppermute | solution.py:26
  37.3 4.5 %collective-permute-start.9 = (bf16[1216,256]{1,0:T(8,128)(2,1)}, bf16[1216,256]{1,0:T(8,128)(2,1)}, u32[]{:S(2)}, u32[]{:S(2)}) collective-permute-start(bf16[1216,256]{1,0:T(8,128)(2,1)} %collective-permute-done.2.refs_6_), channel_id=1, source_target_pairs={{0,4},{4,0},{1,5},{5,1},{2,6},{6,2},{3,7},{7,3},{8,12},{12,8},{9,1... | collective-permute-start | bytes 1867784 | tf_op jit(solution)/shard_map/ppermute | solution.py:26
  38.0 19.3 %collective-permute-start.7 = (bf16[1216,256]{1,0:T(8,128)(2,1)S(1)}, bf16[1216,256]{1,0:T(8,128)(2,1)S(1)}, u32[]{:S(2)}, u32[]{:S(2)}) collective-permute-start(bf16[1216,256]{1,0:T(8,128)(2,1)S(1)} %collective-permute-done.1.refs_7_), channel_id=1, source_target_pairs={{0,3},{1,0},{2,1},{3,2},{4,7},{5,4},{6,5},{7,6},{8,11},{9,8},{10,9... | collective-permute-start | bytes 1867784 | tf_op jit(solution)/shard_map/ppermute | solution.py:26
  41.0 16.7 %collective-permute-start.6 = (bf16[1216,256]{1,0:T(8,128)(2,1)S(1)}, bf16[1216,256]{1,0:T(8,128)(2,1)S(1)}, u32[]{:S(2)}, u32[]{:S(2)}) collective-permute-start(bf16[1216,256]{1,0:T(8,128)(2,1)S(1)} %collective-permute-done.refs_2_), channel_id=1, source_target_pairs={{0,1},{1,2},{2,3},{3,0},{4,5},{5,6},{6,7},{7,4},{8,9},{9,10},{10,1... | collective-permute-start | bytes 1867784 | tf_op jit(solution)/shard_map/ppermute | solution.py:26
  41.7 16.5 %copy-start.18 = (s32[8]{0:T(128)S(1)}, s32[8]{0:T(128)}, u32[]{:S(2)}) copy-start(s32[8]{0:T(128)} %param.12) | copy-start | bytes 100
  57.3 3.4 %copy-start.11 = (bf16[1216,256]{1,0:T(8,128)(2,1)}, bf16[1216,256]{1,0:T(8,128)(2,1)S(1)}, u32[]{:S(2)}) copy-start(bf16[1216,256]{1,0:T(8,128)(2,1)S(1)} %collective-permute-done.7.refs_3_) | copy-start | bytes 1867780
  57.8 3.0 %copy-start.12 = (bf16[1216,256]{1,0:T(8,128)(2,1)}, bf16[1216,256]{1,0:T(8,128)(2,1)S(1)}, u32[]{:S(2)}) copy-start(bf16[1216,256]{1,0:T(8,128)(2,1)S(1)} %collective-permute-done.6.refs_2_) | copy-start | bytes 1867780
  57.8 2.1 collective-permute-start.10
  57.8 2.9 %collective-permute-start.11 = (bf16[1216,256]{1,0:T(8,128)(2,1)S(1)}, bf16[1216,256]{1,0:T(8,128)(2,1)S(1)}, u32[]{:S(2)}, u32[]{:S(2)}) collective-permute-start(bf16[1216,256]{1,0:T(8,128)(2,1)S(1)} %collective-permute-done.7.refs_3_), channel_id=1, source_target_pairs={{0,4},{4,0},{1,5},{5,1},{2,6},{6,2},{3,7},{7,3},{8,12},{12,8},{9,1... | collective-permute-start | bytes 1867784 | tf_op jit(solution)/shard_map/ppermute | solution.py:26
  59.8 0.9 copy-start.16
  60.7 0.8 copy-start.17
  104.4 0.9 copy-start.19
  110.8 27.4 %copy-start.20 = (bf16[768,1024]{1,0:T(8,128)(2,1)S(1)}, bf16[768,1024]{1,0:T(8,128)(2,1)}, u32[]{:S(2)}) copy-start(bf16[768,1024]{1,0:T(8,128)(2,1)} %get-tuple-element.107) | copy-start | bytes 4718596
  110.8 27.4 %all-to-all-start.1 = ((bf16[32,32,768]{2,1,0:T(8,128)(2,1)}), bf16[32,32,768]{2,1,0:T(8,128)(2,1)S(1)}, u32[]{:S(2)}, u32[]{:S(2)}) async-start(bf16[32,32,768]{2,1,0:T(8,128)(2,1)} %bitcast.18), calls=%async_computation.1 | async-start | bytes 3145728 | tf_op jit(solution)/shard_map/all_to_all | solution.py:495
  138.1 3.1 %copy-start.4 = (bf16[32,32,768]{2,1,0:T(8,128)(2,1)}, bf16[32,32,768]{2,1,0:T(8,128)(2,1)S(1)}, u32[]{:S(2)}) copy-start(bf16[32,32,768]{2,1,0:T(8,128)(2,1)S(1)} %all-to-all-done.1) | copy-start | bytes 4718596
  153.3 10.3 %collective-permute-start.12 = (bf16[4,384,1024]{2,1,0:T(8,128)(2,1)}, bf16[4,384,1024]{2,1,0:T(8,128)(2,1)S(1)}, u32[]{:S(2)}, u32[]{:S(2)}) collective-permute-start(bf16[4,384,1024]{2,1,0:T(8,128)(2,1)} %get-tuple-element.110), channel_id=1, source_target_pairs={{0,4},{4,0},{1,5},{5,1},{2,6},{6,2},{3,7},{7,3},{8,12},{12,8},{9,1... | collective-permute-start | bytes 9437192 | tf_op jit(solution)/shard_map/ppermute | solution.py:26
  153.4 10.3 %copy-start.2 = (bf16[4,384,1024]{2,1,0:T(8,128)(2,1)S(1)}, bf16[4,384,1024]{2,1,0:T(8,128)(2,1)}, u32[]{:S(2)}) copy-start(bf16[4,384,1024]{2,1,0:T(8,128)(2,1)} %get-tuple-element.115) | copy-start | bytes 9437188
  163.2 5.7 %collective-permute-start.15 = (bf16[1,512,1024]{2,1,0:T(8,128)(2,1)}, bf16[1,512,1024]{2,1,0:T(8,128)(2,1)S(1)}, u32[]{:S(2)}, u32[]{:S(2)}) collective-permute-start(bf16[1,512,1024]{2,1,0:T(8,128)(2,1)} %get-tuple-element.114), channel_id=1, source_target_pairs={{0,4},{4,0},{1,5},{5,1},{2,6},{6,2},{3,7},{7,3},{8,12},{12,8},{9,1... | collective-permute-start | bytes 3145736 | tf_op jit(solution)/shard_map/ppermute | solution.py:26
  165.8 20.8 %collective-permute-start.16 = (bf16[2,8,24,1024]{3,2,1,0:T(8,128)(2,1)S(1)}, bf16[2,8,24,1024]{3,2,1,0:T(8,128)(2,1)S(1)}, u32[]{:S(2)}, u32[]{:S(2)}) collective-permute-start(bf16[2,8,24,1024]{3,2,1,0:T(8,128)(2,1)S(1)} %bitcast.134), channel_id=1, source_target_pairs={{0,3},{3,0},{1,2},{2,1},{4,7},{7,4},{5,6},{6,5},{8,11},{11,8},{9,1... | collective-permute-start | bytes 2359304 | tf_op jit(solution)/shard_map/ppermute | solution.py:360
  168.6 1.2 copy-start.6
  168.9 19.3 %collective-permute-start.13 = (bf16[2,8,24,1024]{3,2,1,0:T(8,128)(2,1)S(1)}, bf16[2,8,24,1024]{3,2,1,0:T(8,128)(2,1)S(1)}, u32[]{:S(2)}, u32[]{:S(2)}) collective-permute-start(bf16[2,8,24,1024]{3,2,1,0:T(8,128)(2,1)S(1)} %bitcast.135), channel_id=1, source_target_pairs={{0,1},{1,0},{2,3},{3,2},{4,5},{5,4},{6,7},{7,6},{8,9},{9,8},{10,11... | collective-permute-start | bytes 2359304 | tf_op jit(solution)/shard_map/ppermute | solution.py:360
  186.6 1.6 copy-start.7
  188.2 6.6 %collective-permute-start.17 = (bf16[1,512,1024]{2,1,0:T(8,128)(2,1)}, bf16[1,512,1024]{2,1,0:T(8,128)(2,1)}, u32[]{:S(2)}, u32[]{:S(2)}) collective-permute-start(bf16[1,512,1024]{2,1,0:T(8,128)(2,1)} %get-tuple-element.122), channel_id=1, source_target_pairs={{0,4},{4,0},{1,5},{5,1},{2,6},{6,2},{3,7},{7,3},{8,12},{12,8},{9,1... | collective-permute-start | bytes 3145736 | tf_op jit(solution)/shard_map/ppermute | solution.py:26
  188.2 31.1 %all-to-all-start.3 = ((bf16[16,32,1024]{2,1,0:T(8,128)(2,1)}), bf16[16,32,1024]{2,1,0:T(8,128)(2,1)S(1)}, u32[]{:S(2)}, u32[]{:S(2)}) async-start(bf16[16,32,1024]{2,1,0:T(8,128)(2,1)} %bitcast.33), calls=%async_computation.3 | async-start | bytes 2097152 | tf_op jit(solution)/shard_map/all_to_all | solution.py:515
  191.8 2.5 %copy-start.8 = (bf16[2,8,24,1024]{3,2,1,0:T(8,128)(2,1)S(1)}, bf16[2,8,24,1024]{3,2,1,0:T(8,128)(2,1)}, u32[]{:S(2)}) copy-start(bf16[2,8,24,1024]{3,2,1,0:T(8,128)(2,1)} %copy-done.7) | copy-start | bytes 2359300
  192.2 2.7 %copy-start.5 = (bf16[1,512,1024]{2,1,0:T(8,128)(2,1)S(1)}, bf16[1,512,1024]{2,1,0:T(8,128)(2,1)}, u32[]{:S(2)}) copy-start(bf16[1,512,1024]{2,1,0:T(8,128)(2,1)} %get-tuple-element.120) | copy-start | bytes 3145732
  192.2 13.2 %collective-permute-start.14 = (bf16[8,24,1024]{2,1,0:T(8,128)(2,1)S(1)}, bf16[8,24,1024]{2,1,0:T(8,128)(2,1)S(1)}, u32[]{:S(2)}, u32[]{:S(2)}) collective-permute-start(bf16[8,24,1024]{2,1,0:T(8,128)(2,1)S(1)} %dynamic-slice_bitcast_fusion.1), channel_id=1, source_target_pairs={{0,3},{3,0},{1,2},{2,1},{4,7},{7,4},{5,6},{6,5},{8,11},{11,8},{9,1... | collective-permute-start | bytes 1179656 | tf_op jit(solution)/shard_map/ppermute | solution.py:360
  194.7 12.0 %collective-permute-start.18 = (bf16[8,24,1024]{2,1,0:T(8,128)(2,1)S(1)}, bf16[8,24,1024]{2,1,0:T(8,128)(2,1)S(1)}, u32[]{:S(2)}, u32[]{:S(2)}) collective-permute-start(bf16[8,24,1024]{2,1,0:T(8,128)(2,1)S(1)} %dynamic-slice_bitcast_fusion), channel_id=1, source_target_pairs={{0,1},{1,0},{2,3},{3,2},{4,5},{5,4},{6,7},{7,6},{8,9},{9,8},{10,11... | collective-permute-start | bytes 1179656 | tf_op jit(solution)/shard_map/ppermute | solution.py:360
  196.6 15.1 %collective-permute-start.19 = (bf16[2,8,8,1024]{3,2,1,0:T(8,128)(2,1)S(1)}, bf16[2,8,8,1024]{3,2,1,0:T(8,128)(2,1)S(1)}, u32[]{:S(2)}, u32[]{:S(2)}) collective-permute-start(bf16[2,8,8,1024]{3,2,1,0:T(8,128)(2,1)S(1)} %bitcast.140), channel_id=1, source_target_pairs={{0,1},{1,0},{2,3},{3,2},{4,5},{5,4},{6,7},{7,6},{8,9},{9,8},{10,11... | collective-permute-start | bytes 786440 | tf_op jit(solution)/shard_map/ppermute | solution.py:360
  198.7 14.3 %collective-permute-start.21 = (bf16[2,8,8,1024]{3,2,1,0:T(8,128)(2,1)S(1)}, bf16[2,8,8,1024]{3,2,1,0:T(8,128)(2,1)S(1)}, u32[]{:S(2)}, u32[]{:S(2)}) collective-permute-start(bf16[2,8,8,1024]{3,2,1,0:T(8,128)(2,1)S(1)} %bitcast.139), channel_id=1, source_target_pairs={{0,3},{3,0},{1,2},{2,1},{4,7},{7,4},{5,6},{6,5},{8,11},{11,8},{9,1... | collective-permute-start | bytes 786440 | tf_op jit(solution)/shard_map/ppermute | solution.py:360
  211.7 6.3 %collective-permute-start.20 = (bf16[8,8,1024]{2,1,0:T(8,128)(2,1)S(1)}, bf16[8,8,1024]{2,1,0:T(8,128)(2,1)S(1)}, u32[]{:S(2)}, u32[]{:S(2)}) collective-permute-start(bf16[8,8,1024]{2,1,0:T(8,128)(2,1)S(1)} %dynamic-slice_bitcast_fusion.3), channel_id=1, source_target_pairs={{0,3},{3,0},{1,2},{2,1},{4,7},{7,4},{5,6},{6,5},{8,11},{11,8},{9,1... | collective-permute-start | bytes 393224 | tf_op jit(solution)/shard_map/ppermute | solution.py:360
  213.1 5.0 %collective-permute-start.22 = (bf16[8,8,1024]{2,1,0:T(8,128)(2,1)S(1)}, bf16[8,8,1024]{2,1,0:T(8,128)(2,1)S(1)}, u32[]{:S(2)}, u32[]{:S(2)}) collective-permute-start(bf16[8,8,1024]{2,1,0:T(8,128)(2,1)S(1)} %dynamic-slice_bitcast_fusion.2), channel_id=1, source_target_pairs={{0,1},{1,0},{2,3},{3,2},{4,5},{5,4},{6,7},{7,6},{8,9},{9,8},{10,11... | collective-permute-start | bytes 393224 | tf_op jit(solution)/shard_map/ppermute | solution.py:360
  218.2 24.0 %copy-start.1 = (f32[8,768]{1,0:T(8,128)S(1)}, f32[8,768]{1,0:T(8,128)}, u32[]{:S(2)}) copy-start(f32[8,768]{1,0:T(8,128)} %param.11) | copy-start | bytes 73732
  219.3 22.0 %all-to-all-start.2 = ((bf16[16,32,1024]{2,1,0:T(8,128)(2,1)}), bf16[16,32,1024]{2,1,0:T(8,128)(2,1)S(1)}, u32[]{:S(2)}, u32[]{:S(2)}) async-start(bf16[16,32,1024]{2,1,0:T(8,128)(2,1)} %maximum_maximum_fusion), calls=%async_computation.2 | async-start | bytes 2097152 | tf_op jit(solution)/shard_map/all_to_all | solution.py:533
  226.4 5.2 %collective-permute-start.23 = (f32[1,8,1024]{2,1,0:T(8,128)S(1)}, f32[1,8,1024]{2,1,0:T(8,128)S(1)}, u32[]{:S(2)}, u32[]{:S(2)}) collective-permute-start(f32[1,8,1024]{2,1,0:T(8,128)S(1)} %get-tuple-element.154), channel_id=1, source_target_pairs={{0,1},{1,2},{2,3},{3,0},{4,5},{5,6},{6,7},{7,4},{8,9},{9,10},{10,1... | collective-permute-start | bytes 98312 | tf_op jit(solution)/shard_map/ppermute | solution.py:26
  226.5 5.8 %collective-permute-start.24 = (f32[1,8,1024]{2,1,0:T(8,128)S(1)}, f32[1,8,1024]{2,1,0:T(8,128)S(1)}, u32[]{:S(2)}, u32[]{:S(2)}) collective-permute-start(f32[1,8,1024]{2,1,0:T(8,128)S(1)} %get-tuple-element.156), channel_id=1, source_target_pairs={{0,2},{1,3},{2,0},{3,1},{4,6},{5,7},{6,4},{7,5},{8,10},{9,11},{10,... | collective-permute-start | bytes 98312 | tf_op jit(solution)/shard_map/ppermute | solution.py:26
  230.0 3.9 %collective-permute-start.25 = (f32[1,8,1024]{2,1,0:T(8,128)S(1)}, f32[1,8,1024]{2,1,0:T(8,128)S(1)}, u32[]{:S(2)}, u32[]{:S(2)}) collective-permute-start(f32[1,8,1024]{2,1,0:T(8,128)S(1)} %get-tuple-element.155), channel_id=1, source_target_pairs={{0,3},{1,0},{2,1},{3,2},{4,7},{5,4},{6,5},{7,6},{8,11},{9,8},{10,9... | collective-permute-start | bytes 98312 | tf_op jit(solution)/shard_map/ppermute | solution.py:26
